TPU v7x, 256 devices: a whole 4x4x8 slice. The times are simulated.
256 devices in a mesh: row: 32 (over z_hi, x, core), col: 8 (over y, z_lo).
Axes of the slice: x: 4, y: 4, z: 8 (z_hi: 4, z_lo: 2; z = z_hi * 2 + z_lo), core: 2. Of those that a mesh axis runs over, the one named last changes fastest.
Arguments:
- amplitudes: float32 [2, 32, 8, 262144], P(None, 'row', 'col'), may hold values from -6 to 6
- gate_matrices: float32 [5, 4, 2, 128, 128], replicated, may hold values from -0.375 to 0.375
- permutation: int32 [32], replicated, may hold values from 0 to 31, each once
Outputs:
- evolved: float32 [2, 32, 8, 262144], P(None, 'row', 'col')
Inputs may be any that keep to these rules, and one draw needn't show every extreme that they name: `permutation`: each value from 0 to 31 appears once.
All inputs are finite; a program needn't handle non-finite values.
Results may differ from a plain program's by a relative error of at most 0.00014.
Values sent between devices are 32-bit elements; how exact they have to be, the bound alone decides.
No kernel may reach another device: no remote copies, remote signals or barrier semaphores. Data moves between devices by JAX's collectives and lax.ppermute only.
A program may use at most 64 MiB of HBM per device.

v0:
```python
import functools

import jax
import jax.numpy as jnp
from jax import lax
from jax.experimental import pallas as pl
from jax.experimental.pallas import tpu as pltpu
from jax.sharding import PartitionSpec as P


HIGHEST = lax.Precision.HIGHEST
F32 = jnp.float32
BF16 = jnp.bfloat16
GD = 128
HALF = 64
LIMIT = 16 << 20
STATE = (16, 16, 8, 128)
PART = (8, 16, 8, 128)


def split(value):
    high = value.astype(BF16)
    return high, (value - high.astype(F32)).astype(BF16)


def onehot(kind, ids_ref, perm_ref):
    new = lax.broadcasted_iota(jnp.int32, (GD, GD), 0)
    old = lax.broadcasted_iota(jnp.int32, (GD, GD), 1)
    z_own, x_own, c_own = ids_ref[0], ids_ref[1], ids_ref[2]
    rest, core, block = new & 3, (new >> 2) & 1, new >> 3
    if kind == "mid":
        want = ((new & 7) << 4) | (new >> 3)
    elif kind[:3] == "xor":
        want = new ^ (ids_ref[int(kind[3:])] << 6)
    elif kind == "dest":
        x = ((block >> 2) + x_own) & 3
        z = ((block & 3) + z_own) & 3
        want = (((((z << 2) | x) << 1) | (core ^ c_own)) << 2) | rest
    else:
        z = (z_own - (block >> 2)) & 3
        x = (x_own - (block & 3)) & 3
        want = (((((z << 2) | x) << 1) | (core ^ c_own)) << 2) | rest
        old = jnp.broadcast_to(perm_ref[...], (GD, GD))
    return jnp.where(want == old, 1.0, 0.0).astype(BF16)


def weight_kernel(kinds, ids_ref, gates_ref, perm_ref, out_ref):
    made = {}
    for number, (rows, cols) in enumerate(kinds):
        for kind in (rows, cols):
            if kind is not None and kind not in made:
                made[kind] = onehot(kind, ids_ref, perm_ref)
        slot = (0, 1, 3)[number]
        real_high, real_low = split(gates_ref[0, slot, 0])
        imag_high, imag_low = split(gates_ref[0, slot, 1])
        wide = jnp.concatenate([real_high, imag_high, real_low, imag_low], axis=1)
        if rows is not None:
            wide = jnp.dot(made[rows], wide, preferred_element_type=F32).astype(BF16)
        parts = [wide[:, GD * i : GD * (i + 1)] for i in range(4)]
        if cols is not None:
            tall = lax.dot_general(
                jnp.concatenate(parts, axis=0),
                made[cols],
                (((1,), (1,)), ((), ())),
                preferred_element_type=F32,
            ).astype(BF16)
            parts = [tall[GD * i : GD * (i + 1)] for i in range(4)]
        out_ref[number, 0:GD, 0:GD] = parts[0]
        out_ref[number, 0:GD, GD:] = parts[1]
        out_ref[number, GD:, 0:GD] = parts[2]
        out_ref[number, GD:, GD:] = parts[3]


def weights(gate_matrices, seg, kinds, ids, perm_row):
    return pl.pallas_call(
        functools.partial(weight_kernel, kinds),
        out_shape=jax.ShapeDtypeStruct((3, 256, 256), BF16),
        grid_spec=pltpu.PrefetchScalarGridSpec(
            num_scalar_prefetch=1,
            grid=(1,),
            in_specs=[
                pl.BlockSpec((1, 4, 2, GD, GD), lambda i, ids: (seg, 0, 0, 0, 0)),
                pl.BlockSpec((1, GD), lambda i, ids: (0, 0)),
            ],
            out_specs=pl.BlockSpec((3, 256, 256), lambda i, ids: (0, 0, 0)),
        ),
        cost_estimate=pl.CostEstimate(
            flops=3 * 2 * 640 * 128 * 512, bytes_accessed=1 << 20, transcendentals=0
        ),
    )(ids, gate_matrices, perm_row)


def gate_step(first, second, w_high_low, w_high, sign):
    state = jnp.concatenate([first, second], axis=1)
    turned = jnp.concatenate(
        [pltpu.roll(first, HALF, 1) * sign, pltpu.roll(second, HALF, 1) * sign], axis=1
    )
    high, low = split(jnp.concatenate([state, turned], axis=0))
    both = jnp.dot(w_high_low, high, preferred_element_type=F32)
    small = jnp.dot(w_high, low, preferred_element_type=F32)
    return both[:GD] + (both[GD:] + small)


def segment_kernel(source, target, n_in, n_after, *refs):
    w_ref = refs[0]
    ins = refs[1 : 1 + n_in]
    outs = refs[1 + n_in + n_after : -2]
    one, two = refs[-2:]
    lane = lax.broadcasted_iota(jnp.int32, (1, GD), 1)
    sign = jnp.where(lane < HALF, -1.0, 1.0)
    upper = lax.broadcasted_iota(jnp.int32, (1, 8, GD), 1) >= 4

    def load_start(i):
        blocks = []
        for p in (2 * i, 2 * i + 1):
            re = ins[0][0, pl.ds(p, GD, stride=16), :]
            im = ins[0][1, pl.ds(p, GD, stride=16), :]
            if source[1] == 0:
                blocks.append(jnp.where(lane < HALF, re, pltpu.roll(im, HALF, 1)))
            else:
                blocks.append(jnp.where(lane < HALF, pltpu.roll(re, HALF, 1), im))
        return blocks

    def load_pair(i):
        return [
            jnp.concatenate(
                [ins[0][:, p].reshape(HALF, GD), ins[1][:, p].reshape(HALF, GD)], axis=0
            )
            for p in (2 * i, 2 * i + 1)
        ]

    def load_remap(i):
        near = jnp.concatenate([ref[:, 0, i] for ref in ins[:4]], axis=0)
        far = jnp.concatenate([ref[:, 1, i] for ref in ins[:4]], axis=0)
        even = jnp.where(upper, pltpu.roll(far, 4, 1), near)
        odd = jnp.where(upper, far, pltpu.roll(near, 4, 1))
        return [even.reshape(GD, GD), odd.reshape(GD, GD)]

    load = {"start": load_start, "pair": load_pair, "remap": load_remap}[source[0]]

    def top_first(i, carry):
        first, second = load(i)
        result = gate_step(first, second, w_ref[0], w_ref[0, :GD], sign)
        one[:, 2 * i] = result[:, :GD].reshape(16, 8, GD)
        one[:, 2 * i + 1] = result[:, GD:].reshape(16, 8, GD)
        return carry

    def mid(i, carry):
        first = one[2 * i].reshape(GD, GD)
        second = one[2 * i + 1].reshape(GD, GD)
        result = gate_step(first, second, w_ref[1], w_ref[1, :GD], sign)
        two[2 * i] = result[:, :GD].reshape(16, 8, GD)
        two[2 * i + 1] = result[:, GD:].reshape(16, 8, GD)
        return carry

    def top_last(i, carry):
        first = two[:, 2 * i].reshape(GD, GD)
        second = two[:, 2 * i + 1].reshape(GD, GD)
        result = gate_step(first, second, w_ref[2], w_ref[2, :GD], sign)
        pieces = (result[:, :GD], result[:, GD:])
        if target == "pair":
            for p, piece in zip((2 * i, 2 * i + 1), pieces):
                outs[0][:, p] = piece[:HALF].reshape(8, 8, GD)
                outs[1][:, p] = piece[HALF:].reshape(8, 8, GD)
        elif target == "remap":
            even, odd = (piece.reshape(16, 8, GD) for piece in pieces)
            near = jnp.where(upper, pltpu.roll(odd, 4, 1), even)
            far = jnp.where(upper, odd, pltpu.roll(even, 4, 1))
            for x in range(4):
                outs[2 * x][:, i] = near[4 * x : 4 * x + 4]
                outs[2 * x + 1][:, i] = far[4 * x : 4 * x + 4]
        elif target == "plain":
            for p, piece in zip((2 * i, 2 * i + 1), pieces):
                outs[0][:, p] = piece.reshape(16, 8, GD)
        else:
            other_ref, low_ref = ins[n_in - 2], ins[n_in - 1]
            for p, piece in zip((2 * i, 2 * i + 1), pieces):
                rows = jnp.concatenate([other_ref[:, p].reshape(GD, GD), piece], axis=1)
                high, low = split(rows)
                done = jnp.dot(high, low_ref[0], preferred_element_type=F32) + (
                    jnp.dot(high, low_ref[1], preferred_element_type=F32)
                    + jnp.dot(low, low_ref[0], preferred_element_type=F32)
                )
                outs[0][0, pl.ds(p, GD, stride=16), :] = done[:, :GD]
                outs[0][1, pl.ds(p, GD, stride=16), :] = done[:, GD:]
        return carry

    for step in (top_first, mid, top_last):
        lax.fori_loop(0, 8, step, 0)


def run_segment(source, target, w, ins, extra=(), after=()):
    if target == "pair":
        out_shape = [jax.ShapeDtypeStruct(PART, F32)] * 2
    elif target == "remap":
        out_shape = [jax.ShapeDtypeStruct((4, 8, 8, 128), F32)] * 8
    elif target == "plain":
        out_shape = [jax.ShapeDtypeStruct(STATE, F32)]
    else:
        out_shape = [jax.ShapeDtypeStruct((2, 2048, 128), F32)]
    args = list(ins) + list(extra)
    vmem = pl.BlockSpec(memory_space=pltpu.VMEM)
    return pl.pallas_call(
        functools.partial(segment_kernel, source, target, len(args), len(after)),
        out_shape=out_shape,
        in_specs=[vmem] * (1 + len(args)) + [pl.BlockSpec(memory_space=pl.ANY)] * len(after),
        out_specs=[vmem] * len(out_shape),
        scratch_shapes=[pltpu.VMEM(STATE, F32)] * 2,
        cost_estimate=pl.CostEstimate(
            flops=3 * 3 * 2 * 128 * 256 * 2048, bytes_accessed=3 << 20, transcendentals=0
        ),
        compiler_params=pltpu.CompilerParams(vmem_limit_bytes=LIMIT),
    )(w, *args, *after)


def regroup_kernel(*refs):
    ins, outs = refs[:8], refs[8:]
    for z in range(4):
        for x in range(4):
            for c in range(2):
                outs[z][x, c] = ins[2 * x + c][z]


def regroup(blocks):
    vmem = pl.BlockSpec(memory_space=pltpu.VMEM)
    return pl.pallas_call(
        regroup_kernel,
        out_shape=[jax.ShapeDtypeStruct((4, 2, 8, 8, 128), F32)] * 4,
        in_specs=[vmem] * 8,
        out_specs=[vmem] * 4,
        cost_estimate=pl.CostEstimate(flops=0, bytes_accessed=2 << 20, transcendentals=0),
        compiler_params=pltpu.CompilerParams(vmem_limit_bytes=LIMIT),
    )(*blocks)


def flip(value, axis, mask):
    return lax.ppermute(value, axis, [(s, s ^ mask) for s in range(lax.axis_size(axis))])


def shift_row(value, z, x, c):
    pairs = []
    for s in range(32):
        to = ((((s >> 3) + z) & 3) << 3) | ((((s >> 1) + x) & 3) << 1) | ((s & 1) ^ c)
        pairs.append((s, to))
    return lax.ppermute(value, "row", pairs)


def stacked(gate_mat):
    real_part = gate_mat[0]
    imag_part = gate_mat[1]
    top_rows = jnp.concatenate([real_part, -imag_part], axis=1)
    bottom_rows = jnp.concatenate([imag_part, real_part], axis=1)
    return jnp.concatenate([top_rows, bottom_rows], axis=0)


def low_weights(gate_matrices):
    total = stacked(gate_matrices[0, 2])
    for seg in range(1, gate_matrices.shape[0]):
        total = jnp.dot(stacked(gate_matrices[seg, 2]), total, precision=HIGHEST)
    rows = total.T.reshape(2, 2, HALF, 256).transpose(1, 0, 2, 3).reshape(256, 256)
    high = lax.reduce_precision(rows, 8, 7)
    return jnp.stack([high.astype(BF16), (rows - high).astype(BF16)])


def circuit(amplitudes, gate_matrices, permutation):
    state = amplitudes.reshape(2, 2048, 128)
    row = lax.axis_index("row")
    col = lax.axis_index("col")
    ids = jnp.stack([row >> 3, (row >> 1) & 3, row & 1, row >> 4, col >> 2]).astype(jnp.int32)
    perm_row = (permutation[:, None] * 4 + jnp.arange(4, dtype=jnp.int32)).reshape(1, GD)
    mid = ("mid", "mid")
    kinds = (
        ((None, None), mid, ("xor2", None)),
        ((None, "xor2"), mid, ("xor3", None)),
        ((None, "xor3"), mid, ("dest", None)),
        ((None, "src"), mid, ("xor4", None)),
        ((None, "xor4"), mid, (None, None)),
    )
    w = [weights(gate_matrices, seg, kinds[seg], ids, perm_row) for seg in range(5)]
    low = low_weights(gate_matrices)
    halves = (0, 1)
    kept, sent = {}, {}
    after = ()
    for h in halves:
        kept[h], out = run_segment(("start", h), "pair", w[0], [state], after=after)
        after = (out,)
        sent[h] = flip(out, "row", 1)
    after = ()
    for h in halves:
        kept[h], out = run_segment(("pair",), "pair", w[1], [kept[h], sent[h]], after=after)
        after = (out,)
        sent[h] = flip(out, "row", 16)
    got = {}
    after = ()
    for h in halves:
        blocks = run_segment(("pair",), "remap", w[2], [kept[h], sent[h]], after=after)
        moved = [
            block if k == 0 else shift_row(block, 0, k >> 1, k & 1)
            for k, block in enumerate(blocks)
        ]
        groups = regroup(moved)
        after = (groups[0],)
        got[h] = [groups[0]]
        for z in range(1, 4):
            got[h].append(shift_row(groups[z], z, 0, 0))
    after = ()
    for h in halves:
        kept[h], out = run_segment(("remap",), "pair", w[3], got[h], after=after)
        after = (out,)
        sent[h] = flip(out, "col", 4)
    (first,) = run_segment(("pair",), "plain", w[4], [kept[0], sent[0]])
    (out,) = run_segment(("pair",), "low", w[4], [kept[1], sent[1]], [first, low])
    return out.reshape(amplitudes.shape)


def solution(mesh):
    placed = (P(None, "row", "col", None), P(), P())
    return jax.shard_map(
        circuit, mesh=mesh, in_specs=placed, out_specs=P(None, "row", "col", None), check_vma=False
    )
```

profile of v0, /device:TPU:1, one launch (start us, length us, event | category | flops | bytes accessed | tf_op | source)
XLA Modules:
  0.0 207.6 jit_solution(17127103523773340202)
XLA Ops:
  2.1 2.8 %shard_map.41.refs_0_ = bf16[3,256,256]{2,1,0:T(8,128)(2,1)} custom-call(s32[5]{0:T(128)} %stack.28.ids_ref, f32[5,4,2,128,128]{4,3,2,1,0:T(8,128)} %gates_ref.9, s32[1,128]{1,0:T(1,128)} %add.26.perm_ref), custom_call_target="tpu_custom_call" | custom-call | flops 251658240 | bytes 1048576 | tf_op jit(solution)/shard_map/pallas_call | solution.py:75
  5.9 8.5 %shard_map.42 = (f32[8,16,8,128]{3,2,1,0:T(8,128)S(1)}, f32[8,16,8,128]{3,2,1,0:T(8,128)}) custom-call(bf16[3,256,256]{2,1,0:T(8,128)(2,1)S(1)} %copy-done.5, f32[2,2048,128]{2,1,0:T(8,128)S(1)} %bitcast.44), custom_call_target="tpu_custom_call" | custom-call | flops 1207959552 | bytes 3145728 | tf_op jit(solution)/shard_map/pallas_call | solution.py:203
  15.2 3.2 %collective-permute-start.1 = (f32[8,16,8,128]{3,2,1,0:T(8,128)}, f32[8,16,8,128]{3,2,1,0:T(8,128)S(1)}, u32[]{:S(2)}, u32[]{:S(2)}) collective-permute-start(f32[8,16,8,128]{3,2,1,0:T(8,128)} %get-tuple-element.41.refs_2_), channel_id=1, source_target_pairs={{0,8},{8,0},{16,24},{24,16},{32,40},{40,32},{48,56},{56,48},{64,72... | collective-permute-start | bytes 1572872 | tf_op jit(solution)/shard_map/ppermute | solution.py:237
  18.4 7.7 %shard_map.43 = (f32[8,16,8,128]{3,2,1,0:T(8,128)S(1)}, f32[8,16,8,128]{3,2,1,0:T(8,128)S(1)}) custom-call(bf16[3,256,256]{2,1,0:T(8,128)(2,1)S(1)} %copy-done.5, f32[2,2048,128]{2,1,0:T(8,128)S(1)} %bitcast.45, f32[8,16,8,128]{3,2,1,0:T(8,128)} %get-tuple-element.41.refs_2_), custom_call_target="tpu_custom_call" | custom-call | flops 1207959552 | bytes 3145728 | tf_op jit(solution)/shard_map/pallas_call | solution.py:203
  27.0 2.9 %shard_map.40.refs_0_ = bf16[3,256,256]{2,1,0:T(8,128)(2,1)} custom-call(s32[5]{0:T(128)} %stack.28.ids_ref, f32[5,4,2,128,128]{4,3,2,1,0:T(8,128)} %gates_ref.9, s32[1,128]{1,0:T(1,128)} %add.26.perm_ref), custom_call_target="tpu_custom_call" | custom-call | flops 251658240 | bytes 1048576 | tf_op jit(solution)/shard_map/pallas_call | solution.py:75
  30.9 7.1 %shard_map.44 = (f32[8,16,8,128]{3,2,1,0:T(8,128)S(1)}, f32[8,16,8,128]{3,2,1,0:T(8,128)S(1)}) custom-call(bf16[3,256,256]{2,1,0:T(8,128)(2,1)S(1)} %copy-done.4, f32[8,16,8,128]{3,2,1,0:T(8,128)S(1)} %copy-done.12, f32[8,16,8,128]{3,2,1,0:T(8,128)S(1)} %collective-permute-done.1.refs_2_), custom_call_target="tpu_custom_call" | custom-call | flops 1207959552 | bytes 3145728 | tf_op jit(solution)/shard_map/pallas_call | solution.py:203
  38.1 5.3 %collective-permute-start.3 = (f32[8,16,8,128]{3,2,1,0:T(8,128)S(1)}, f32[8,16,8,128]{3,2,1,0:T(8,128)S(1)}, u32[]{:S(2)}, u32[]{:S(2)}) collective-permute-start(f32[8,16,8,128]{3,2,1,0:T(8,128)S(1)} %get-tuple-element.45.refs_3_), channel_id=1, source_target_pairs={{0,128},{8,136},{16,144},{24,152},{32,160},{40,168},{48,176},{56,1... | collective-permute-start | bytes 1572872 | tf_op jit(solution)/shard_map/ppermute | solution.py:237
  43.4 7.1 %shard_map.45 = (f32[8,16,8,128]{3,2,1,0:T(8,128)S(1)}, f32[8,16,8,128]{3,2,1,0:T(8,128)S(1)}) custom-call(bf16[3,256,256]{2,1,0:T(8,128)(2,1)S(1)} %copy-done.4, f32[8,16,8,128]{3,2,1,0:T(8,128)S(1)} %copy-done.8, f32[8,16,8,128]{3,2,1,0:T(8,128)S(1)} %collective-permute-done.refs_2_, f32[8,16,8,128]{3,2,1,0:T(8,128)S(1)} %get-tuple-element.45.refs_3_), custom_call_target="tpu_custom_call" | custom-call | flops 1207959552 | bytes 3145728 | tf_op jit(solution)/shard_map/pallas_call | solution.py:203
  50.8 2.8 %shard_map.39.refs_0_ = bf16[3,256,256]{2,1,0:T(8,128)(2,1)} custom-call(s32[5]{0:T(128)} %stack.28.ids_ref, f32[5,4,2,128,128]{4,3,2,1,0:T(8,128)} %gates_ref.9, s32[1,128]{1,0:T(1,128)} %add.26.perm_ref), custom_call_target="tpu_custom_call" | custom-call | flops 251658240 | bytes 1048576 | tf_op jit(solution)/shard_map/pallas_call | solution.py:75
  53.6 3.7 %collective-permute-done.3.refs_2_ = f32[8,16,8,128]{3,2,1,0:T(8,128)S(1)} collective-permute-done((f32[8,16,8,128]{3,2,1,0:T(8,128)S(1)}, f32[8,16,8,128]{3,2,1,0:T(8,128)S(1)}, u32[]{:S(2)}, u32[]{:S(2)}) %collective-permute-start.3) | collective-permute-done | bytes 524320 | tf_op jit(solution)/shard_map/ppermute | solution.py:237
  58.3 7.1 %shard_map.46 = (f32[4,8,8,128]{3,2,1,0:T(8,128)S(1)}, f32[4,8,8,128]{3,2,1,0:T(8,128)S(1)}, f32[4,8,8,128]{3,2,1,0:T(8,128)S(1)}, f32[4,8,8,128]{3,2,1,0:T(8,12...) custom-call(bf16[3,256,256]{2,1,0:T(8,128)(2,1)S(1)} %copy-done.1, ...), custom_call_target="tpu_custom_call" | custom-call | flops 1207959552 | bytes 3145728 | tf_op jit(solution)/shard_map/pallas_call | solution.py:203
  65.5 2.3 %collective-permute-start.4 = (f32[4,8,8,128]{3,2,1,0:T(8,128)S(1)}, f32[4,8,8,128]{3,2,1,0:T(8,128)S(1)}, u32[]{:S(2)}, u32[]{:S(2)}) collective-permute-start(f32[4,8,8,128]{3,2,1,0:T(8,128)S(1)} %get-tuple-element.50), channel_id=1, source_target_pairs={{0,8},{8,0},{16,24},{24,16},{32,40},{40,32},{48,56},{56,48},{64,72... | collective-permute-start | bytes 393224 | tf_op jit(solution)/shard_map/ppermute | solution.py:245
  74.7 2.3 %collective-permute-done.6.refs_3_ = f32[4,8,8,128]{3,2,1,0:T(8,128)S(1)} collective-permute-done((f32[4,8,8,128]{3,2,1,0:T(8,128)S(1)}, f32[4,8,8,128]{3,2,1,0:T(8,128)S(1)}, u32[]{:S(2)}, u32[]{:S(2)}) %collective-permute-start.6) | collective-permute-done | bytes 131104 | tf_op jit(solution)/shard_map/ppermute | solution.py:245
  80.1 3.1 %collective-permute-done.8.refs_5_ = f32[4,8,8,128]{3,2,1,0:T(8,128)S(1)} collective-permute-done((f32[4,8,8,128]{3,2,1,0:T(8,128)S(1)}, f32[4,8,8,128]{3,2,1,0:T(8,128)S(1)}, u32[]{:S(2)}, u32[]{:S(2)}) %collective-permute-start.8) | collective-permute-done | bytes 131104 | tf_op jit(solution)/shard_map/ppermute | solution.py:245
  84.4 7.2 %shard_map.48 = (f32[4,8,8,128]{3,2,1,0:T(8,128)S(1)}, f32[4,8,8,128]{3,2,1,0:T(8,128)S(1)}, f32[4,8,8,128]{3,2,1,0:T(8,128)S(1)}, f32[4,8,8,128]{3,2,1,0:T(8,12...) custom-call(bf16[3,256,256]{2,1,0:T(8,128)(2,1)S(1)} %copy-done.2, ...), custom_call_target="tpu_custom_call" | custom-call | flops 1207959552 | bytes 3145728 | tf_op jit(solution)/shard_map/pallas_call | solution.py:203
  91.7 5.5 %collective-permute-start.12 = (f32[4,8,8,128]{3,2,1,0:T(8,128)S(1)}, f32[4,8,8,128]{3,2,1,0:T(8,128)S(1)}, u32[]{:S(2)}, u32[]{:S(2)}) collective-permute-start(f32[4,8,8,128]{3,2,1,0:T(8,128)S(1)} %get-tuple-element.60), channel_id=1, source_target_pairs={{0,16},{8,24},{16,32},{24,40},{32,48},{40,56},{48,0},{56,8},{64,80... | collective-permute-start | bytes 393224 | tf_op jit(solution)/shard_map/ppermute | solution.py:245
  103.6 17.8 %collective-permute-start.21 = (f32[4,2,8,8,128]{4,3,2,1,0:T(8,128)S(1)}, f32[4,2,8,8,128]{4,3,2,1,0:T(8,128)S(1)}, u32[]{:S(2)}, u32[]{:S(2)}) collective-permute-start(f32[4,2,8,8,128]{4,3,2,1,0:T(8,128)S(1)} %get-tuple-element.70), channel_id=1, source_target_pairs={{0,64},{8,72},{16,80},{24,88},{32,96},{40,104},{48,112},{56,120},{... | collective-permute-start | bytes 786440 | tf_op jit(solution)/shard_map/ppermute | solution.py:245
  121.8 2.6 %collective-permute-start.16 = (f32[4,8,8,128]{3,2,1,0:T(8,128)S(1)}, f32[4,8,8,128]{3,2,1,0:T(8,128)S(1)}, u32[]{:S(2)}, u32[]{:S(2)}) collective-permute-start(f32[4,8,8,128]{3,2,1,0:T(8,128)S(1)} %get-tuple-element.64), channel_id=1, source_target_pairs={{0,48},{8,56},{16,0},{24,8},{32,16},{40,24},{48,32},{56,40},{64,11... | collective-permute-start | bytes 393224 | tf_op jit(solution)/shard_map/ppermute | solution.py:245
  124.9 4.8 %collective-permute-start.22 = (f32[4,2,8,8,128]{4,3,2,1,0:T(8,128)S(1)}, f32[4,2,8,8,128]{4,3,2,1,0:T(8,128)S(1)}, u32[]{:S(2)}, u32[]{:S(2)}) collective-permute-start(f32[4,2,8,8,128]{4,3,2,1,0:T(8,128)S(1)} %get-tuple-element.71), channel_id=1, source_target_pairs={{0,128},{8,136},{16,144},{24,152},{32,160},{40,168},{48,176},{56,1... | collective-permute-start | bytes 786440 | tf_op jit(solution)/shard_map/ppermute | solution.py:245
  129.7 2.9 %collective-permute-start.23 = (f32[4,2,8,8,128]{4,3,2,1,0:T(8,128)S(1)}, f32[4,2,8,8,128]{4,3,2,1,0:T(8,128)S(1)}, u32[]{:S(2)}, u32[]{:S(2)}) collective-permute-start(f32[4,2,8,8,128]{4,3,2,1,0:T(8,128)S(1)} %get-tuple-element.72), channel_id=1, source_target_pairs={{0,192},{8,200},{16,208},{24,216},{32,224},{40,232},{48,240},{56,2... | collective-permute-start | bytes 786440 | tf_op jit(solution)/shard_map/ppermute | solution.py:245
  133.0 2.8 %shard_map.38.refs_0_ = bf16[3,256,256]{2,1,0:T(8,128)(2,1)} custom-call(s32[5]{0:T(128)} %stack.28.ids_ref, f32[5,4,2,128,128]{4,3,2,1,0:T(8,128)} %gates_ref.9, s32[1,128]{1,0:T(1,128)} %add.26.perm_ref), custom_call_target="tpu_custom_call" | custom-call | flops 251658240 | bytes 1048576 | tf_op jit(solution)/shard_map/pallas_call | solution.py:75
  136.0 2.2 %collective-permute-start.19 = (f32[4,2,8,8,128]{4,3,2,1,0:T(8,128)S(1)}, f32[4,2,8,8,128]{4,3,2,1,0:T(8,128)S(1)}, u32[]{:S(2)}, u32[]{:S(2)}) collective-permute-start(f32[4,2,8,8,128]{4,3,2,1,0:T(8,128)S(1)} %get-tuple-element.68), channel_id=1, source_target_pairs={{0,128},{8,136},{16,144},{24,152},{32,160},{40,168},{48,176},{56,1... | collective-permute-start | bytes 786440 | tf_op jit(solution)/shard_map/ppermute | solution.py:245
  138.2 3.5 %collective-permute-start.20 = (f32[4,2,8,8,128]{4,3,2,1,0:T(8,128)S(1)}, f32[4,2,8,8,128]{4,3,2,1,0:T(8,128)S(1)}, u32[]{:S(2)}, u32[]{:S(2)}) collective-permute-start(f32[4,2,8,8,128]{4,3,2,1,0:T(8,128)S(1)} %get-tuple-element.69), channel_id=1, source_target_pairs={{0,192},{8,200},{16,208},{24,216},{32,224},{40,232},{48,240},{56,2... | collective-permute-start | bytes 786440 | tf_op jit(solution)/shard_map/ppermute | solution.py:245
  143.0 8.5 %collective-permute-done.22.refs_3_ = f32[4,2,8,8,128]{4,3,2,1,0:T(8,128)S(1)} collective-permute-done((f32[4,2,8,8,128]{4,3,2,1,0:T(8,128)S(1)}, f32[4,2,8,8,128]{4,3,2,1,0:T(8,128)S(1)}, u32[]{:S(2)}, u32[]{:S(2)}) %collective-permute-start.22) | collective-permute-done | bytes 262176 | tf_op jit(solution)/shard_map/ppermute | solution.py:245
  151.5 11.5 %collective-permute-done.23.refs_4_ = f32[4,2,8,8,128]{4,3,2,1,0:T(8,128)S(1)} collective-permute-done((f32[4,2,8,8,128]{4,3,2,1,0:T(8,128)S(1)}, f32[4,2,8,8,128]{4,3,2,1,0:T(8,128)S(1)}, u32[]{:S(2)}, u32[]{:S(2)}) %collective-permute-start.23) | collective-permute-done | bytes 262176 | tf_op jit(solution)/shard_map/ppermute | solution.py:245
  164.0 7.1 %shard_map.50 = (f32[8,16,8,128]{3,2,1,0:T(8,128)S(1)}, f32[8,16,8,128]{3,2,1,0:T(8,128)S(1)}) custom-call(bf16[3,256,256]{2,1,0:T(8,128)(2,1)S(1)} %copy-done.3, f32[4,2,8,8,128]{4,3,2,1,0:T(8,128)S(1)} %get-tuple-element.57.refs_3_.refs_1_, f32[4,2,8,8,128]{4,3,2,1,0:T(8,128)S(1)} %collective-permute-done.21.refs_2_, ...), custom_call_target="tpu_custom_call" | custom-call | flops 1207959552 | bytes 3145728 | tf_op jit(solution)/shard_map/pallas_call | solution.py:203
  171.2 3.0 %collective-permute-start.25 = (f32[8,16,8,128]{3,2,1,0:T(8,128)S(1)}, f32[8,16,8,128]{3,2,1,0:T(8,128)S(1)}, u32[]{:S(2)}, u32[]{:S(2)}) collective-permute-start(f32[8,16,8,128]{3,2,1,0:T(8,128)S(1)} %get-tuple-element.73.refs_5_), channel_id=1, source_target_pairs={{0,4},{1,5},{2,6},{3,7},{4,0},{5,1},{6,2},{7,3},{8,12},{9,13},{10,... | collective-permute-start | bytes 1572872 | tf_op jit(solution)/shard_map/ppermute | solution.py:237
  174.2 7.2 %shard_map.51 = (f32[8,16,8,128]{3,2,1,0:T(8,128)S(1)}, f32[8,16,8,128]{3,2,1,0:T(8,128)S(1)}) custom-call(bf16[3,256,256]{2,1,0:T(8,128)(2,1)S(1)} %copy-done.3, f32[4,2,8,8,128]{4,3,2,1,0:T(8,128)S(1)} %get-tuple-element.66.refs_1_, f32[4,2,8,8,128]{4,3,2,1,0:T(8,128)S(1)} %collective-permute-done.18.refs_2_, ...), custom_call_target="tpu_custom_call" | custom-call | flops 1207959552 | bytes 3145728 | tf_op jit(solution)/shard_map/pallas_call | solution.py:203
  182.2 2.8 %shard_map.37.refs_0_ = bf16[3,256,256]{2,1,0:T(8,128)(2,1)} custom-call(s32[5]{0:T(128)} %stack.28.ids_ref, f32[5,4,2,128,128]{4,3,2,1,0:T(8,128)} %gates_ref.9, s32[1,128]{1,0:T(1,128)} %add.26.perm_ref), custom_call_target="tpu_custom_call" | custom-call | flops 251658240 | bytes 1048576 | tf_op jit(solution)/shard_map/pallas_call | solution.py:75
  186.6 7.1 %shard_map.52.refs_3_ = f32[16,16,8,128]{3,2,1,0:T(8,128)S(1)} custom-call(bf16[3,256,256]{2,1,0:T(8,128)(2,1)S(1)} %copy-done, f32[8,16,8,128]{3,2,1,0:T(8,128)S(1)} %copy-done.10, f32[8,16,8,128]{3,2,1,0:T(8,128)S(1)} %collective-permute-done.25.refs_2_), custom_call_target="tpu_custom_call" | custom-call | flops 1207959552 | bytes 3145728 | tf_op jit(solution)/shard_map/pallas_call | solution.py:203
  193.8 3.2 %collective-permute-done.24.refs_2_ = f32[8,16,8,128]{3,2,1,0:T(8,128)S(1)} collective-permute-done((f32[8,16,8,128]{3,2,1,0:T(8,128)S(1)}, f32[8,16,8,128]{3,2,1,0:T(8,128)S(1)}, u32[]{:S(2)}, u32[]{:S(2)}) %collective-permute-start.24) | collective-permute-done | bytes 524320 | tf_op jit(solution)/shard_map/ppermute | solution.py:237
  196.9 10.7 %shard_map.53 = f32[2,2048,128]{2,1,0:T(8,128)} custom-call(bf16[3,256,256]{2,1,0:T(8,128)(2,1)S(1)} %copy-done, f32[8,16,8,128]{3,2,1,0:T(8,128)S(1)} %get-tuple-element.74.refs_1_, f32[8,16,8,128]{3,2,1,0:T(8,128)S(1)} %collective-permute-done.24.refs_2_, f32[16,16,8,128]{3,2,1,0:T(8,128)S(1)} %shard_map.52.refs_3_, ...), custom_call_target="tpu_custom_call" | custom-call | flops 1207959552 | bytes 3145728 | tf_op jit(solution)/shard_map/pallas_call | solution.py:203
  (82 shorter events, 30.9 us)
Async XLA Ops:
  15.2 14.7 %collective-permute-start.1 = (f32[8,16,8,128]{3,2,1,0:T(8,128)}, f32[8,16,8,128]{3,2,1,0:T(8,128)S(1)}, u32[]{:S(2)}, u32[]{:S(2)}) collective-permute-start(f32[8,16,8,128]{3,2,1,0:T(8,128)} %get-tuple-element.41.refs_2_), channel_id=1, source_target_pairs={{0,8},{8,0},{16,24},{24,16},{32,40},{40,32},{48,56},{56,48},{64,72... | collective-permute-start | bytes 1572872 | tf_op jit(solution)/shard_map/ppermute | solution.py:237
  27.0 16.4 %collective-permute-start = (f32[8,16,8,128]{3,2,1,0:T(8,128)S(1)}, f32[8,16,8,128]{3,2,1,0:T(8,128)S(1)}, u32[]{:S(2)}, u32[]{:S(2)}) collective-permute-start(f32[8,16,8,128]{3,2,1,0:T(8,128)S(1)} %get-tuple-element.43), channel_id=1, source_target_pairs={{0,8},{8,0},{16,24},{24,16},{32,40},{40,32},{48,56},{56,48},{64,72... | collective-permute-start | bytes 1572872 | tf_op jit(solution)/shard_map/ppermute | solution.py:237
  30.9 12.5 %copy-start.8 = (f32[8,16,8,128]{3,2,1,0:T(8,128)S(1)}, f32[8,16,8,128]{3,2,1,0:T(8,128)}, u32[]{:S(2)}) copy-start(f32[8,16,8,128]{3,2,1,0:T(8,128)} %copy-done.7) | copy-start | bytes 1572868
  38.1 12.5 %copy-start.13 = (f32[8,16,8,128]{3,2,1,0:T(8,128)}, f32[8,16,8,128]{3,2,1,0:T(8,128)S(1)}, u32[]{:S(2)}) copy-start(f32[8,16,8,128]{3,2,1,0:T(8,128)S(1)} %get-tuple-element.48.refs_1_) | copy-start | bytes 1572868
  38.1 19.3 %collective-permute-start.3 = (f32[8,16,8,128]{3,2,1,0:T(8,128)S(1)}, f32[8,16,8,128]{3,2,1,0:T(8,128)S(1)}, u32[]{:S(2)}, u32[]{:S(2)}) collective-permute-start(f32[8,16,8,128]{3,2,1,0:T(8,128)S(1)} %get-tuple-element.45.refs_3_), channel_id=1, source_target_pairs={{0,128},{8,136},{16,144},{24,152},{32,160},{40,168},{48,176},{56,1... | collective-permute-start | bytes 1572872 | tf_op jit(solution)/shard_map/ppermute | solution.py:237
  50.5 6.8 %copy-start.14 = (f32[8,16,8,128]{3,2,1,0:T(8,128)S(1)}, f32[8,16,8,128]{3,2,1,0:T(8,128)}, u32[]{:S(2)}) copy-start(f32[8,16,8,128]{3,2,1,0:T(8,128)} %copy-done.13) | copy-start | bytes 1572868
  50.5 33.8 %collective-permute-start.2 = (f32[8,16,8,128]{3,2,1,0:T(8,128)S(1)}, f32[8,16,8,128]{3,2,1,0:T(8,128)S(1)}, u32[]{:S(2)}, u32[]{:S(2)}) collective-permute-start(f32[8,16,8,128]{3,2,1,0:T(8,128)S(1)} %get-tuple-element.47), channel_id=1, source_target_pairs={{0,128},{8,136},{16,144},{24,152},{32,160},{40,168},{48,176},{56,1... | collective-permute-start | bytes 1572872 | tf_op jit(solution)/shard_map/ppermute | solution.py:237
  58.3 26.0 %copy-start.2 = (bf16[3,256,256]{2,1,0:T(8,128)(2,1)S(1)}, bf16[3,256,256]{2,1,0:T(8,128)(2,1)}, u32[]{:S(2)}) copy-start(bf16[3,256,256]{2,1,0:T(8,128)(2,1)} %shard_map.39.refs_0_) | copy-start | bytes 1179652
  65.5 6.4 %collective-permute-start.4 = (f32[4,8,8,128]{3,2,1,0:T(8,128)S(1)}, f32[4,8,8,128]{3,2,1,0:T(8,128)S(1)}, u32[]{:S(2)}, u32[]{:S(2)}) collective-permute-start(f32[4,8,8,128]{3,2,1,0:T(8,128)S(1)} %get-tuple-element.50), channel_id=1, source_target_pairs={{0,8},{8,0},{16,24},{24,16},{32,40},{40,32},{48,56},{56,48},{64,72... | collective-permute-start | bytes 393224 | tf_op jit(solution)/shard_map/ppermute | solution.py:245
  67.8 6.2 %collective-permute-start.5 = (f32[4,8,8,128]{3,2,1,0:T(8,128)S(1)}, f32[4,8,8,128]{3,2,1,0:T(8,128)S(1)}, u32[]{:S(2)}, u32[]{:S(2)}) collective-permute-start(f32[4,8,8,128]{3,2,1,0:T(8,128)S(1)} %get-tuple-element.51), channel_id=1, source_target_pairs={{0,16},{8,24},{16,32},{24,40},{32,48},{40,56},{48,0},{56,8},{64,80... | collective-permute-start | bytes 393224 | tf_op jit(solution)/shard_map/ppermute | solution.py:245
  68.5 8.5 %collective-permute-start.6 = (f32[4,8,8,128]{3,2,1,0:T(8,128)S(1)}, f32[4,8,8,128]{3,2,1,0:T(8,128)S(1)}, u32[]{:S(2)}, u32[]{:S(2)}) collective-permute-start(f32[4,8,8,128]{3,2,1,0:T(8,128)S(1)} %get-tuple-element.52), channel_id=1, source_target_pairs={{0,24},{8,16},{16,40},{24,32},{32,56},{40,48},{48,8},{56,0},{64,88... | collective-permute-start | bytes 393224 | tf_op jit(solution)/shard_map/ppermute | solution.py:245
  70.0 10.1 %collective-permute-start.7 = (f32[4,8,8,128]{3,2,1,0:T(8,128)S(1)}, f32[4,8,8,128]{3,2,1,0:T(8,128)S(1)}, u32[]{:S(2)}, u32[]{:S(2)}) collective-permute-start(f32[4,8,8,128]{3,2,1,0:T(8,128)S(1)} %get-tuple-element.53), channel_id=1, source_target_pairs={{0,32},{8,40},{16,48},{24,56},{32,0},{40,8},{48,16},{56,24},{64,96... | collective-permute-start | bytes 393224 | tf_op jit(solution)/shard_map/ppermute | solution.py:245
  71.9 11.3 %collective-permute-start.8 = (f32[4,8,8,128]{3,2,1,0:T(8,128)S(1)}, f32[4,8,8,128]{3,2,1,0:T(8,128)S(1)}, u32[]{:S(2)}, u32[]{:S(2)}) collective-permute-start(f32[4,8,8,128]{3,2,1,0:T(8,128)S(1)} %get-tuple-element.54), channel_id=1, source_target_pairs={{0,40},{8,32},{16,56},{24,48},{32,8},{40,0},{48,24},{56,16},{64,10... | collective-permute-start | bytes 393224 | tf_op jit(solution)/shard_map/ppermute | solution.py:245
  73.9 9.2 %collective-permute-start.9 = (f32[4,8,8,128]{3,2,1,0:T(8,128)S(1)}, f32[4,8,8,128]{3,2,1,0:T(8,128)S(1)}, u32[]{:S(2)}, u32[]{:S(2)}) collective-permute-start(f32[4,8,8,128]{3,2,1,0:T(8,128)S(1)} %get-tuple-element.55), channel_id=1, source_target_pairs={{0,48},{8,56},{16,0},{24,8},{32,16},{40,24},{48,32},{56,40},{64,11... | collective-permute-start | bytes 393224 | tf_op jit(solution)/shard_map/ppermute | solution.py:245
  77.0 7.2 %collective-permute-start.10 = (f32[4,8,8,128]{3,2,1,0:T(8,128)S(1)}, f32[4,8,8,128]{3,2,1,0:T(8,128)S(1)}, u32[]{:S(2)}, u32[]{:S(2)}) collective-permute-start(f32[4,8,8,128]{3,2,1,0:T(8,128)S(1)} %get-tuple-element.56), channel_id=1, source_target_pairs={{0,56},{8,48},{16,8},{24,0},{32,24},{40,16},{48,40},{56,32},{64,12... | collective-permute-start | bytes 393224 | tf_op jit(solution)/shard_map/ppermute | solution.py:245
  91.5 12.1 %collective-permute-start.11 = (f32[4,8,8,128]{3,2,1,0:T(8,128)S(1)}, f32[4,8,8,128]{3,2,1,0:T(8,128)S(1)}, u32[]{:S(2)}, u32[]{:S(2)}) collective-permute-start(f32[4,8,8,128]{3,2,1,0:T(8,128)S(1)} %get-tuple-element.59), channel_id=1, source_target_pairs={{0,8},{8,0},{16,24},{24,16},{32,40},{40,32},{48,56},{56,48},{64,72... | collective-permute-start | bytes 393224 | tf_op jit(solution)/shard_map/ppermute | solution.py:245
  91.7 30.1 %collective-permute-start.12 = (f32[4,8,8,128]{3,2,1,0:T(8,128)S(1)}, f32[4,8,8,128]{3,2,1,0:T(8,128)S(1)}, u32[]{:S(2)}, u32[]{:S(2)}) collective-permute-start(f32[4,8,8,128]{3,2,1,0:T(8,128)S(1)} %get-tuple-element.60), channel_id=1, source_target_pairs={{0,16},{8,24},{16,32},{24,40},{32,48},{40,56},{48,0},{56,8},{64,80... | collective-permute-start | bytes 393224 | tf_op jit(solution)/shard_map/ppermute | solution.py:245
  97.2 27.2 %collective-permute-start.13 = (f32[4,8,8,128]{3,2,1,0:T(8,128)S(1)}, f32[4,8,8,128]{3,2,1,0:T(8,128)S(1)}, u32[]{:S(2)}, u32[]{:S(2)}) collective-permute-start(f32[4,8,8,128]{3,2,1,0:T(8,128)S(1)} %get-tuple-element.61), channel_id=1, source_target_pairs={{0,24},{8,16},{16,40},{24,32},{32,56},{40,48},{48,8},{56,0},{64,88... | collective-permute-start | bytes 393224 | tf_op jit(solution)/shard_map/ppermute | solution.py:245
  98.8 26.1 %collective-permute-start.14 = (f32[4,8,8,128]{3,2,1,0:T(8,128)S(1)}, f32[4,8,8,128]{3,2,1,0:T(8,128)S(1)}, u32[]{:S(2)}, u32[]{:S(2)}) collective-permute-start(f32[4,8,8,128]{3,2,1,0:T(8,128)S(1)} %get-tuple-element.62), channel_id=1, source_target_pairs={{0,32},{8,40},{16,48},{24,56},{32,0},{40,8},{48,16},{56,24},{64,96... | collective-permute-start | bytes 393224 | tf_op jit(solution)/shard_map/ppermute | solution.py:245
  99.9 29.8 %collective-permute-start.15 = (f32[4,8,8,128]{3,2,1,0:T(8,128)S(1)}, f32[4,8,8,128]{3,2,1,0:T(8,128)S(1)}, u32[]{:S(2)}, u32[]{:S(2)}) collective-permute-start(f32[4,8,8,128]{3,2,1,0:T(8,128)S(1)} %get-tuple-element.63), channel_id=1, source_target_pairs={{0,40},{8,32},{16,56},{24,48},{32,8},{40,0},{48,24},{56,16},{64,10... | collective-permute-start | bytes 393224 | tf_op jit(solution)/shard_map/ppermute | solution.py:245
  103.6 34.6 %collective-permute-start.21 = (f32[4,2,8,8,128]{4,3,2,1,0:T(8,128)S(1)}, f32[4,2,8,8,128]{4,3,2,1,0:T(8,128)S(1)}, u32[]{:S(2)}, u32[]{:S(2)}) collective-permute-start(f32[4,2,8,8,128]{4,3,2,1,0:T(8,128)S(1)} %get-tuple-element.70), channel_id=1, source_target_pairs={{0,64},{8,72},{16,80},{24,88},{32,96},{40,104},{48,112},{56,120},{... | collective-permute-start | bytes 786440 | tf_op jit(solution)/shard_map/ppermute | solution.py:245
  121.8 14.0 %collective-permute-start.16 = (f32[4,8,8,128]{3,2,1,0:T(8,128)S(1)}, f32[4,8,8,128]{3,2,1,0:T(8,128)S(1)}, u32[]{:S(2)}, u32[]{:S(2)}) collective-permute-start(f32[4,8,8,128]{3,2,1,0:T(8,128)S(1)} %get-tuple-element.64), channel_id=1, source_target_pairs={{0,48},{8,56},{16,0},{24,8},{32,16},{40,24},{48,32},{56,40},{64,11... | collective-permute-start | bytes 393224 | tf_op jit(solution)/shard_map/ppermute | solution.py:245
  124.4 11.5 %collective-permute-start.17 = (f32[4,8,8,128]{3,2,1,0:T(8,128)S(1)}, f32[4,8,8,128]{3,2,1,0:T(8,128)S(1)}, u32[]{:S(2)}, u32[]{:S(2)}) collective-permute-start(f32[4,8,8,128]{3,2,1,0:T(8,128)S(1)} %get-tuple-element.65), channel_id=1, source_target_pairs={{0,56},{8,48},{16,8},{24,0},{32,24},{40,16},{48,40},{56,32},{64,12... | collective-permute-start | bytes 393224 | tf_op jit(solution)/shard_map/ppermute | solution.py:245
  124.9 26.6 %collective-permute-start.22 = (f32[4,2,8,8,128]{4,3,2,1,0:T(8,128)S(1)}, f32[4,2,8,8,128]{4,3,2,1,0:T(8,128)S(1)}, u32[]{:S(2)}, u32[]{:S(2)}) collective-permute-start(f32[4,2,8,8,128]{4,3,2,1,0:T(8,128)S(1)} %get-tuple-element.71), channel_id=1, source_target_pairs={{0,128},{8,136},{16,144},{24,152},{32,160},{40,168},{48,176},{56,1... | collective-permute-start | bytes 786440 | tf_op jit(solution)/shard_map/ppermute | solution.py:245
  129.7 33.3 %collective-permute-start.23 = (f32[4,2,8,8,128]{4,3,2,1,0:T(8,128)S(1)}, f32[4,2,8,8,128]{4,3,2,1,0:T(8,128)S(1)}, u32[]{:S(2)}, u32[]{:S(2)}) collective-permute-start(f32[4,2,8,8,128]{4,3,2,1,0:T(8,128)S(1)} %get-tuple-element.72), channel_id=1, source_target_pairs={{0,192},{8,200},{16,208},{24,216},{32,224},{40,232},{48,240},{56,2... | collective-permute-start | bytes 786440 | tf_op jit(solution)/shard_map/ppermute | solution.py:245
  135.9 38.3 %collective-permute-start.18 = (f32[4,2,8,8,128]{4,3,2,1,0:T(8,128)S(1)}, f32[4,2,8,8,128]{4,3,2,1,0:T(8,128)S(1)}, u32[]{:S(2)}, u32[]{:S(2)}) collective-permute-start(f32[4,2,8,8,128]{4,3,2,1,0:T(8,128)S(1)} %get-tuple-element.67), channel_id=1, source_target_pairs={{0,64},{8,72},{16,80},{24,88},{32,96},{40,104},{48,112},{56,120},{... | collective-permute-start | bytes 786440 | tf_op jit(solution)/shard_map/ppermute | solution.py:245
  136.0 38.3 %collective-permute-start.19 = (f32[4,2,8,8,128]{4,3,2,1,0:T(8,128)S(1)}, f32[4,2,8,8,128]{4,3,2,1,0:T(8,128)S(1)}, u32[]{:S(2)}, u32[]{:S(2)}) collective-permute-start(f32[4,2,8,8,128]{4,3,2,1,0:T(8,128)S(1)} %get-tuple-element.68), channel_id=1, source_target_pairs={{0,128},{8,136},{16,144},{24,152},{32,160},{40,168},{48,176},{56,1... | collective-permute-start | bytes 786440 | tf_op jit(solution)/shard_map/ppermute | solution.py:245
  138.2 36.0 %collective-permute-start.20 = (f32[4,2,8,8,128]{4,3,2,1,0:T(8,128)S(1)}, f32[4,2,8,8,128]{4,3,2,1,0:T(8,128)S(1)}, u32[]{:S(2)}, u32[]{:S(2)}) collective-permute-start(f32[4,2,8,8,128]{4,3,2,1,0:T(8,128)S(1)} %get-tuple-element.69), channel_id=1, source_target_pairs={{0,192},{8,200},{16,208},{24,216},{32,224},{40,232},{48,240},{56,2... | collective-permute-start | bytes 786440 | tf_op jit(solution)/shard_map/ppermute | solution.py:245
  171.2 10.4 %copy-start.9 = (f32[8,16,8,128]{3,2,1,0:T(8,128)}, f32[8,16,8,128]{3,2,1,0:T(8,128)S(1)}, u32[]{:S(2)}) copy-start(f32[8,16,8,128]{3,2,1,0:T(8,128)S(1)} %get-tuple-element.76.refs_1_) | copy-start | bytes 1572868
  171.2 10.3 %copy-start.15 = (f32[128,128]{1,0:T(8,128)S(1)}, f32[128,128]{1,0:T(8,128)}, u32[]{:S(2)}) copy-start(f32[128,128]{1,0:T(8,128)} %get-tuple-element.77) | copy-start | bytes 196612
  171.2 14.4 %collective-permute-start.25 = (f32[8,16,8,128]{3,2,1,0:T(8,128)S(1)}, f32[8,16,8,128]{3,2,1,0:T(8,128)S(1)}, u32[]{:S(2)}, u32[]{:S(2)}) collective-permute-start(f32[8,16,8,128]{3,2,1,0:T(8,128)S(1)} %get-tuple-element.73.refs_5_), channel_id=1, source_target_pairs={{0,4},{1,5},{2,6},{3,7},{4,0},{5,1},{6,2},{7,3},{8,12},{9,13},{10,... | collective-permute-start | bytes 1572872 | tf_op jit(solution)/shard_map/ppermute | solution.py:237
  181.4 15.5 %collective-permute-start.24 = (f32[8,16,8,128]{3,2,1,0:T(8,128)S(1)}, f32[8,16,8,128]{3,2,1,0:T(8,128)S(1)}, u32[]{:S(2)}, u32[]{:S(2)}) collective-permute-start(f32[8,16,8,128]{3,2,1,0:T(8,128)S(1)} %get-tuple-element.75), channel_id=1, source_target_pairs={{0,4},{1,5},{2,6},{3,7},{4,0},{5,1},{6,2},{7,3},{8,12},{9,13},{10,... | collective-permute-start | bytes 1572872 | tf_op jit(solution)/shard_map/ppermute | solution.py:237
  (10 other events, 18.5 us)
where the time goes:
time: 208 us
  Pallas kernels  91.2 us (44%)
  starting transfers between devices  66.1 us (32%)
  waiting for transfers between devices  35.1 us (17%)
  local copies, waits for them, and re-layouts  9.68 us (5%)
  matrix products  2.66 us (1%)
  other arithmetic  2.58 us (1%)
    pallas_call x10, Pallas kernels, run_segment(): pl.pallas_call(functools.partial(segment_kernel, source, target, len(args...  76.9 us
    ppermute x20, starting transfers between devices, shift_row(): return lax.ppermute(value, 'row', pairs)  54.2 us
    ppermute x20, waiting for transfers between devices, shift_row(): return lax.ppermute(value, 'row', pairs)  27.6 us
    pallas_call x5, Pallas kernels, weights(): pl.pallas_call(functools.partial(weight_kernel, kinds), out_shape=jax.Sha...  14.2 us
    ppermute x6, starting transfers between devices, flip(): lax.ppermute(value, axis, [(s, s ^ mask) for s in range(lax.axis_size(axi...  11.9 us
    ppermute x6, waiting for transfers between devices, flip(): lax.ppermute(value, axis, [(s, s ^ mask) for s in range(lax.axis_size(axi...  7.46 us
    unnamed x32, local copies, waits for them, and re-layouts  6.6 us
  transfers between devices with their start and end apart: 26, of which 10 were waited for; matrix products, arithmetic and copies ran while one was open for 3% of the time, Pallas kernels for 30%

commit v1 on v0

--- a/solution.py
+++ b/solution.py
@@ -8,7 +8,6 @@
 from jax.sharding import PartitionSpec as P
 
 
-HIGHEST = lax.Precision.HIGHEST
 F32 = jnp.float32
 BF16 = jnp.bfloat16
 GD = 128
@@ -23,15 +22,17 @@
     return high, (value - high.astype(F32)).astype(BF16)
 
 
-def onehot(kind, ids_ref, perm_ref):
+def onehot(kind, perm_ref):
+    row = lax.axis_index("row")
+    col = lax.axis_index("col")
     new = lax.broadcasted_iota(jnp.int32, (GD, GD), 0)
     old = lax.broadcasted_iota(jnp.int32, (GD, GD), 1)
-    z_own, x_own, c_own = ids_ref[0], ids_ref[1], ids_ref[2]
+    z_own, x_own, c_own = row >> 3, (row >> 1) & 3, row & 1
     rest, core, block = new & 3, (new >> 2) & 1, new >> 3
     if kind == "mid":
         want = ((new & 7) << 4) | (new >> 3)
     elif kind[:3] == "xor":
-        want = new ^ (ids_ref[int(kind[3:])] << 6)
+        want = new ^ ({"xor2": c_own, "xor3": row >> 4, "xor4": col >> 2}[kind] << 6)
     elif kind == "dest":
         x = ((block >> 2) + x_own) & 3
         z = ((block & 3) + z_own) & 3
@@ -40,16 +41,20 @@
         z = (z_own - (block >> 2)) & 3
         x = (x_own - (block & 3)) & 3
         want = (((((z << 2) | x) << 1) | (core ^ c_own)) << 2) | rest
-        old = jnp.broadcast_to(perm_ref[...], (GD, GD))
+        state = lax.broadcasted_iota(jnp.int32, (1, GD), 1)
+        moved = state & 3
+        for t in range(32):
+            moved += jnp.where(state >> 2 == t, perm_ref[t] * 4, 0)
+        old = jnp.broadcast_to(moved, (GD, GD))
     return jnp.where(want == old, 1.0, 0.0).astype(BF16)
 
 
-def weight_kernel(kinds, ids_ref, gates_ref, perm_ref, out_ref):
+def weight_kernel(kinds, perm_ref, gates_ref, out_ref):
     made = {}
     for number, (rows, cols) in enumerate(kinds):
         for kind in (rows, cols):
             if kind is not None and kind not in made:
-                made[kind] = onehot(kind, ids_ref, perm_ref)
+                made[kind] = onehot(kind, perm_ref)
         slot = (0, 1, 3)[number]
         real_high, real_low = split(gates_ref[0, slot, 0])
         imag_high, imag_low = split(gates_ref[0, slot, 1])
@@ -71,23 +76,64 @@
         out_ref[number, GD:, GD:] = parts[3]
 
 
-def weights(gate_matrices, seg, kinds, ids, perm_row):
+def weights(gate_matrices, seg, kinds, permutation):
     return pl.pallas_call(
         functools.partial(weight_kernel, kinds),
         out_shape=jax.ShapeDtypeStruct((3, 256, 256), BF16),
         grid_spec=pltpu.PrefetchScalarGridSpec(
             num_scalar_prefetch=1,
             grid=(1,),
-            in_specs=[
-                pl.BlockSpec((1, 4, 2, GD, GD), lambda i, ids: (seg, 0, 0, 0, 0)),
-                pl.BlockSpec((1, GD), lambda i, ids: (0, 0)),
-            ],
-            out_specs=pl.BlockSpec((3, 256, 256), lambda i, ids: (0, 0, 0)),
+            in_specs=[pl.BlockSpec((1, 4, 2, GD, GD), lambda i, perm: (seg, 0, 0, 0, 0))],
+            out_specs=pl.BlockSpec(memory_space=pltpu.VMEM),
         ),
         cost_estimate=pl.CostEstimate(
             flops=3 * 2 * 640 * 128 * 512, bytes_accessed=1 << 20, transcendentals=0
         ),
-    )(ids, gate_matrices, perm_row)
+        compiler_params=pltpu.CompilerParams(vmem_limit_bytes=LIMIT),
+    )(permutation, gate_matrices)
+
+
+def low_kernel(gates_ref, out_ref, total_ref):
+    seg = pl.program_id(0)
+    real, imag = gates_ref[0, 0, 0], gates_ref[0, 0, 1]
+    form = jnp.concatenate(
+        [jnp.concatenate([real, -imag], axis=1), jnp.concatenate([imag, real], axis=1)], axis=0
+    )
+
+    @pl.when(seg == 0)
+    def _():
+        new = lax.broadcasted_iota(jnp.int32, (256, 256), 0)
+        old = lax.broadcasted_iota(jnp.int32, (256, 256), 1)
+        want = (((new >> 6) & 1) << 7) | ((new >> 7) << 6) | (new & 63)
+        total_ref[...] = jnp.where(want == old, 1.0, 0.0)
+
+    high, low = split(total_ref[...])
+    form_high, form_low = split(form)
+
+    def times(left, right):
+        return lax.dot_general(
+            left, right, (((1,), (1,)), ((), ())), preferred_element_type=F32
+        )
+
+    total = times(high, form_high) + (times(high, form_low) + times(low, form_high))
+    total_ref[...] = total
+    out_ref[0], out_ref[1] = split(total)
+
+
+def low_weights(gate_matrices):
+    return pl.pallas_call(
+        low_kernel,
+        out_shape=jax.ShapeDtypeStruct((2, 256, 256), BF16),
+        grid=(gate_matrices.shape[0],),
+        in_specs=[pl.BlockSpec((1, 1, 2, GD, GD), lambda i: (i, 2, 0, 0, 0))],
+        out_specs=pl.BlockSpec(memory_space=pltpu.VMEM),
+        scratch_shapes=[pltpu.VMEM((256, 256), F32)],
+        cost_estimate=pl.CostEstimate(
+            flops=5 * 3 * 2 * 256**3, bytes_accessed=1 << 20, transcendentals=0
+        ),
+        compiler_params=pltpu.CompilerParams(vmem_limit_bytes=LIMIT),
+        name="low_weights",
+    )(gate_matrices)
 
 
 def gate_step(first, second, w_high_low, w_high, sign):
@@ -101,10 +147,10 @@
     return both[:GD] + (both[GD:] + small)
 
 
-def segment_kernel(source, target, n_in, n_after, *refs):
+def segment_kernel(source, target, n_in, unroll, *refs):
     w_ref = refs[0]
     ins = refs[1 : 1 + n_in]
-    outs = refs[1 + n_in + n_after : -2]
+    outs = refs[1 + n_in : -2]
     one, two = refs[-2:]
     lane = lax.broadcasted_iota(jnp.int32, (1, GD), 1)
     sign = jnp.where(lane < HALF, -1.0, 1.0)
@@ -169,27 +215,39 @@
             for x in range(4):
                 outs[2 * x][:, i] = near[4 * x : 4 * x + 4]
                 outs[2 * x + 1][:, i] = far[4 * x : 4 * x + 4]
-        elif target == "plain":
+        else:
+            held = outs[0] if target == "plain" else one
             for p, piece in zip((2 * i, 2 * i + 1), pieces):
-                outs[0][:, p] = piece.reshape(16, 8, GD)
-        else:
-            other_ref, low_ref = ins[n_in - 2], ins[n_in - 1]
-            for p, piece in zip((2 * i, 2 * i + 1), pieces):
-                rows = jnp.concatenate([other_ref[:, p].reshape(GD, GD), piece], axis=1)
-                high, low = split(rows)
-                done = jnp.dot(high, low_ref[0], preferred_element_type=F32) + (
-                    jnp.dot(high, low_ref[1], preferred_element_type=F32)
-                    + jnp.dot(low, low_ref[0], preferred_element_type=F32)
-                )
-                outs[0][0, pl.ds(p, GD, stride=16), :] = done[:, :GD]
-                outs[0][1, pl.ds(p, GD, stride=16), :] = done[:, GD:]
+                held[:, p] = piece.reshape(16, 8, GD)
         return carry
 
+    def low_gate(i, carry):
+        other_ref, low_ref = ins[n_in - 2], ins[n_in - 1]
+        rows = [
+            jnp.concatenate(
+                [other_ref[:, p].reshape(GD, GD), one[:, p].reshape(GD, GD)], axis=1
+            )
+            for p in range(4 * i, 4 * i + 4)
+        ]
+        high, low = split(jnp.concatenate(rows, axis=0))
+        done = jnp.dot(high, low_ref[0], preferred_element_type=F32) + (
+            jnp.dot(high, low_ref[1], preferred_element_type=F32)
+            + jnp.dot(low, low_ref[0], preferred_element_type=F32)
+        )
+        for k in range(4):
+            piece = done[GD * k : GD * (k + 1)]
+            outs[0][0, pl.ds(4 * i + k, GD, stride=16), :] = piece[:, :GD]
+            outs[0][1, pl.ds(4 * i + k, GD, stride=16), :] = piece[:, GD:]
+        return carry
+
     for step in (top_first, mid, top_last):
-        lax.fori_loop(0, 8, step, 0)
-
-
-def run_segment(source, target, w, ins, extra=(), after=()):
+        lax.fori_loop(0, 8, step, 0, unroll=unroll)
+    if target == "low":
+        for i in range(4):
+            low_gate(i, 0)
+
+
+def run_segment(source, target, w, ins, extra=(), unroll=8):
     if target == "pair":
         out_shape = [jax.ShapeDtypeStruct(PART, F32)] * 2
     elif target == "remap":
@@ -201,16 +259,16 @@
     args = list(ins) + list(extra)
     vmem = pl.BlockSpec(memory_space=pltpu.VMEM)
     return pl.pallas_call(
-        functools.partial(segment_kernel, source, target, len(args), len(after)),
+        functools.partial(segment_kernel, source, target, len(args), unroll),
         out_shape=out_shape,
-        in_specs=[vmem] * (1 + len(args)) + [pl.BlockSpec(memory_space=pl.ANY)] * len(after),
+        in_specs=[vmem] * (1 + len(args)),
         out_specs=[vmem] * len(out_shape),
         scratch_shapes=[pltpu.VMEM(STATE, F32)] * 2,
         cost_estimate=pl.CostEstimate(
             flops=3 * 3 * 2 * 128 * 256 * 2048, bytes_accessed=3 << 20, transcendentals=0
         ),
         compiler_params=pltpu.CompilerParams(vmem_limit_bytes=LIMIT),
-    )(w, *args, *after)
+    )(w, *args)
 
 
 def regroup_kernel(*refs):
@@ -245,29 +303,8 @@
     return lax.ppermute(value, "row", pairs)
 
 
-def stacked(gate_mat):
-    real_part = gate_mat[0]
-    imag_part = gate_mat[1]
-    top_rows = jnp.concatenate([real_part, -imag_part], axis=1)
-    bottom_rows = jnp.concatenate([imag_part, real_part], axis=1)
-    return jnp.concatenate([top_rows, bottom_rows], axis=0)
-
-
-def low_weights(gate_matrices):
-    total = stacked(gate_matrices[0, 2])
-    for seg in range(1, gate_matrices.shape[0]):
-        total = jnp.dot(stacked(gate_matrices[seg, 2]), total, precision=HIGHEST)
-    rows = total.T.reshape(2, 2, HALF, 256).transpose(1, 0, 2, 3).reshape(256, 256)
-    high = lax.reduce_precision(rows, 8, 7)
-    return jnp.stack([high.astype(BF16), (rows - high).astype(BF16)])
-
-
 def circuit(amplitudes, gate_matrices, permutation):
     state = amplitudes.reshape(2, 2048, 128)
-    row = lax.axis_index("row")
-    col = lax.axis_index("col")
-    ids = jnp.stack([row >> 3, (row >> 1) & 3, row & 1, row >> 4, col >> 2]).astype(jnp.int32)
-    perm_row = (permutation[:, None] * 4 + jnp.arange(4, dtype=jnp.int32)).reshape(1, GD)
     mid = ("mid", "mid")
     kinds = (
         ((None, None), mid, ("xor2", None)),
@@ -276,39 +313,31 @@
         ((None, "src"), mid, ("xor4", None)),
         ((None, "xor4"), mid, (None, None)),
     )
-    w = [weights(gate_matrices, seg, kinds[seg], ids, perm_row) for seg in range(5)]
+    w = [weights(gate_matrices, seg, kinds[seg], permutation) for seg in range(5)]
     low = low_weights(gate_matrices)
     halves = (0, 1)
     kept, sent = {}, {}
-    after = ()
     for h in halves:
-        kept[h], out = run_segment(("start", h), "pair", w[0], [state], after=after)
-        after = (out,)
+        kept[h], out = run_segment(("start", h), "pair", w[0], [state])
         sent[h] = flip(out, "row", 1)
-    after = ()
     for h in halves:
-        kept[h], out = run_segment(("pair",), "pair", w[1], [kept[h], sent[h]], after=after)
-        after = (out,)
+        kept[h], out = run_segment(("pair",), "pair", w[1], [kept[h], sent[h]], unroll=(8, 4)[h])
         sent[h] = flip(out, "row", 16)
     got = {}
-    after = ()
     for h in halves:
-        blocks = run_segment(("pair",), "remap", w[2], [kept[h], sent[h]], after=after)
+        blocks = run_segment(("pair",), "remap", w[2], [kept[h], sent[h]], unroll=(8, 4)[h])
         moved = [
             block if k == 0 else shift_row(block, 0, k >> 1, k & 1)
             for k, block in enumerate(blocks)
         ]
         groups = regroup(moved)
-        after = (groups[0],)
         got[h] = [groups[0]]
         for z in range(1, 4):
             got[h].append(shift_row(groups[z], z, 0, 0))
-    after = ()
     for h in halves:
-        kept[h], out = run_segment(("remap",), "pair", w[3], got[h], after=after)
-        after = (out,)
+        kept[h], out = run_segment(("remap",), "pair", w[3], got[h], unroll=(4, 8)[h])
         sent[h] = flip(out, "col", 4)
-    (first,) = run_segment(("pair",), "plain", w[4], [kept[0], sent[0]])
+    (first,) = run_segment(("pair",), "plain", w[4], [kept[0], sent[0]], unroll=4)
     (out,) = run_segment(("pair",), "low", w[4], [kept[1], sent[1]], [first, low])
     return out.reshape(amplitudes.shape)
 

time: 208 us -> 163 us (0.78)
  Pallas kernels: 91.2 us -> 33.1 us
  waiting for transfers between devices: 35.1 us -> 60 us
  local copies, waits for them, and re-layouts: 9.68 us -> 3.09 us
  matrix products: 2.66 us -> 0 us
  other arithmetic: 2.58 us -> 0 us
    pallas_call x10, Pallas kernels: 76.9 us -> 26.8 us  [run_segment(): pl.pallas_call(functools.partial(segment_kernel, source, target, len(args...]
    ppermute x6, waiting for transfers between devices: 7.46 us -> 25.8 us  [flip(): lax.ppermute(value, axis, [(s, s ^ mask) for s in range(lax.axis_size(axi...]
    pallas_call x5, Pallas kernels: 14.2 us -> 4.42 us  [weights(): pl.pallas_call(functools.partial(weight_kernel, kinds), out_shape=jax.Sha...]
    ppermute x20, waiting for transfers between devices: 27.6 us -> 34.1 us  [shift_row(): return lax.ppermute(value, 'row', pairs)]
    unnamed x32 -> x10, local copies, waits for them, and re-layouts: 6.6 us -> 3.09 us
    dot_general x4 -> x0, matrix products: 2.66 us -> none  [low_weights(): total = jnp.dot(stacked(gate_matrices[seg, 2]), total, precision=HIGHEST)]
  transfers between devices with their start and end apart: 26 -> 26, of which waited for: 10 -> 10; matrix products, arithmetic and copies ran while one was open for 3% -> 0% of each run, Pallas kernels for 30% -> 16%
where the time goes in v1:
time: 163 us; the launch traced here: 162 us
  starting transfers between devices  66 us (40%)
  waiting for transfers between devices  60 us (37%)
  Pallas kernels  33.1 us (20%)
  local copies, waits for them, and re-layouts  3.09 us (2%)
    ppermute x20, starting transfers between devices, shift_row(): return lax.ppermute(value, 'row', pairs)  54 us
    ppermute x20, waiting for transfers between devices, shift_row(): return lax.ppermute(value, 'row', pairs)  34.1 us
    pallas_call x10, Pallas kernels, run_segment(): pl.pallas_call(functools.partial(segment_kernel, source, target, len(args...  26.8 us
    ppermute x6, waiting for transfers between devices, flip(): lax.ppermute(value, axis, [(s, s ^ mask) for s in range(lax.axis_size(axi...  25.8 us
    ppermute x6, starting transfers between devices, flip(): lax.ppermute(value, axis, [(s, s ^ mask) for s in range(lax.axis_size(axi...  12 us
    pallas_call x5, Pallas kernels, weights(): pl.pallas_call(functools.partial(weight_kernel, kinds), out_shape=jax.Sha...  4.42 us
  transfers between devices with their start and end apart: 26, of which 10 were waited for; matrix products, arithmetic and copies ran while one was open for 0% of the time, Pallas kernels for 16%

profile of v1, /device:TPU:1, one launch (start us, length us, event | category | flops | bytes accessed | tf_op | source)
XLA Modules:
  0.0 162.4 jit_solution(3863288127643159025)
XLA Ops:
  0.0 1.7 %copy-done = f32[5,4,2,128,128]{4,3,2,1,0:T(8,128)S(1)} copy-done((f32[5,4,2,128,128]{4,3,2,1,0:T(8,128)S(1)}, f32[5,4,2,128,128]{4,3,2,1,0:T(8,128)}, u32[]{:S(2)}) %copy-start) | copy-done | bytes 2621464
  4.0 2.3 %shard_map.47 = (f32[8,16,8,128]{3,2,1,0:T(8,128)S(1)}, f32[8,16,8,128]{3,2,1,0:T(8,128)S(1)}) custom-call(bf16[3,256,256]{2,1,0:T(8,128)(2,1)S(1)} %shard_map.41.refs_0_, f32[2,2048,128]{2,1,0:T(8,128)S(1)} %bitcast.2), custom_call_target="tpu_custom_call" | custom-call | flops 1207959552 | bytes 3145728 | tf_op jit(solution)/shard_map/pallas_call | solution.py:261
  6.3 3.3 %collective-permute-start.13 = (f32[8,16,8,128]{3,2,1,0:T(8,128)S(1)}, f32[8,16,8,128]{3,2,1,0:T(8,128)S(1)}, u32[]{:S(2)}, u32[]{:S(2)}) collective-permute-start(f32[8,16,8,128]{3,2,1,0:T(8,128)S(1)} %get-tuple-element.60), channel_id=1, source_target_pairs={{0,8},{8,0},{16,24},{24,16},{32,40},{40,32},{48,56},{56,48},{64,72... | collective-permute-start | bytes 1572872 | tf_op jit(solution)/shard_map/ppermute | solution.py:295
  9.6 2.3 %shard_map.42 = (f32[8,16,8,128]{3,2,1,0:T(8,128)S(1)}, f32[8,16,8,128]{3,2,1,0:T(8,128)S(1)}) custom-call(bf16[3,256,256]{2,1,0:T(8,128)(2,1)S(1)} %shard_map.41.refs_0_, f32[2,2048,128]{2,1,0:T(8,128)S(1)} %bitcast.3), custom_call_target="tpu_custom_call" | custom-call | flops 1207959552 | bytes 3145728 | tf_op jit(solution)/shard_map/pallas_call | solution.py:261
  12.9 2.0 %shard_map.48 = (f32[8,16,8,128]{3,2,1,0:T(8,128)S(1)}, f32[8,16,8,128]{3,2,1,0:T(8,128)S(1)}) custom-call(bf16[3,256,256]{2,1,0:T(8,128)(2,1)S(1)} %shard_map.40.refs_0_, f32[8,16,8,128]{3,2,1,0:T(8,128)S(1)} %get-tuple-element.59.refs_1_, f32[8,16,8,128]{3,2,1,0:T(8,128)S(1)} %collective-permute-done.13.refs_2_), custom_call_target="tpu_custom_call" | custom-call | flops 1207959552 | bytes 3145728 | tf_op jit(solution)/shard_map/pallas_call | solution.py:261
  14.9 5.3 %collective-permute-start.14 = (f32[8,16,8,128]{3,2,1,0:T(8,128)S(1)}, f32[8,16,8,128]{3,2,1,0:T(8,128)S(1)}, u32[]{:S(2)}, u32[]{:S(2)}) collective-permute-start(f32[8,16,8,128]{3,2,1,0:T(8,128)S(1)} %get-tuple-element.62), channel_id=1, source_target_pairs={{0,128},{8,136},{16,144},{24,152},{32,160},{40,168},{48,176},{56,1... | collective-permute-start | bytes 1572872 | tf_op jit(solution)/shard_map/ppermute | solution.py:295
  20.2 2.9 %shard_map.43 = (f32[8,16,8,128]{3,2,1,0:T(8,128)S(1)}, f32[8,16,8,128]{3,2,1,0:T(8,128)S(1)}) custom-call(bf16[3,256,256]{2,1,0:T(8,128)(2,1)S(1)} %shard_map.40.refs_0_, f32[8,16,8,128]{3,2,1,0:T(8,128)S(1)} %get-tuple-element.41.refs_1_, f32[8,16,8,128]{3,2,1,0:T(8,128)S(1)} %collective-permute-done.refs_2_), custom_call_target="tpu_custom_call" | custom-call | flops 1207959552 | bytes 3145728 | tf_op jit(solution)/shard_map/pallas_call | solution.py:261
  24.2 9.8 %collective-permute-done.14.refs_2_ = f32[8,16,8,128]{3,2,1,0:T(8,128)S(1)} collective-permute-done((f32[8,16,8,128]{3,2,1,0:T(8,128)S(1)}, f32[8,16,8,128]{3,2,1,0:T(8,128)S(1)}, u32[]{:S(2)}, u32[]{:S(2)}) %collective-permute-start.14) | collective-permute-done | bytes 524320 | tf_op jit(solution)/shard_map/ppermute | solution.py:295
  34.0 2.0 %shard_map.49 = (f32[4,8,8,128]{3,2,1,0:T(8,128)S(1)}, f32[4,8,8,128]{3,2,1,0:T(8,128)S(1)}, f32[4,8,8,128]{3,2,1,0:T(8,128)S(1)}, f32[4,8,8,128]{3,2,1,0:T(8,12...) custom-call(bf16[3,256,256]{2,1,0:T(8,128)(2,1)S(1)} %shard_map.39.r, ...), custom_call_target="tpu_custom_call" | custom-call | flops 1207959552 | bytes 3145728 | tf_op jit(solution)/shard_map/pallas_call | solution.py:261
  36.0 2.7 %collective-permute-start.15 = (f32[4,8,8,128]{3,2,1,0:T(8,128)S(1)}, f32[4,8,8,128]{3,2,1,0:T(8,128)S(1)}, u32[]{:S(2)}, u32[]{:S(2)}) collective-permute-start(f32[4,8,8,128]{3,2,1,0:T(8,128)S(1)} %get-tuple-element.64), channel_id=1, source_target_pairs={{0,8},{8,0},{16,24},{24,16},{32,40},{40,32},{48,56},{56,48},{64,72... | collective-permute-start | bytes 393224 | tf_op jit(solution)/shard_map/ppermute | solution.py:303
  40.9 1.9 %collective-permute-start.18 = (f32[4,8,8,128]{3,2,1,0:T(8,128)S(1)}, f32[4,8,8,128]{3,2,1,0:T(8,128)S(1)}, u32[]{:S(2)}, u32[]{:S(2)}) collective-permute-start(f32[4,8,8,128]{3,2,1,0:T(8,128)S(1)} %get-tuple-element.67), channel_id=1, source_target_pairs={{0,32},{8,40},{16,48},{24,56},{32,0},{40,8},{48,16},{56,24},{64,96... | collective-permute-start | bytes 393224 | tf_op jit(solution)/shard_map/ppermute | solution.py:303
  42.8 6.3 %collective-permute-done.1.refs_2_ = f32[8,16,8,128]{3,2,1,0:T(8,128)S(1)} collective-permute-done((f32[8,16,8,128]{3,2,1,0:T(8,128)S(1)}, f32[8,16,8,128]{3,2,1,0:T(8,128)S(1)}, u32[]{:S(2)}, u32[]{:S(2)}) %collective-permute-start.1) | collective-permute-done | bytes 524320 | tf_op jit(solution)/shard_map/ppermute | solution.py:295
  49.1 19.1 %collective-permute-start.19 = (f32[4,8,8,128]{3,2,1,0:T(8,128)S(1)}, f32[4,8,8,128]{3,2,1,0:T(8,128)S(1)}, u32[]{:S(2)}, u32[]{:S(2)}) collective-permute-start(f32[4,8,8,128]{3,2,1,0:T(8,128)S(1)} %get-tuple-element.68), channel_id=1, source_target_pairs={{0,40},{8,32},{16,56},{24,48},{32,8},{40,0},{48,24},{56,16},{64,10... | collective-permute-start | bytes 393224 | tf_op jit(solution)/shard_map/ppermute | solution.py:303
  69.0 2.9 %shard_map.44 = (f32[4,8,8,128]{3,2,1,0:T(8,128)S(1)}, f32[4,8,8,128]{3,2,1,0:T(8,128)S(1)}, f32[4,8,8,128]{3,2,1,0:T(8,128)S(1)}, f32[4,8,8,128]{3,2,1,0:T(8,12...) custom-call(bf16[3,256,256]{2,1,0:T(8,128)(2,1)S(1)} %shard_map.39.r, ...), custom_call_target="tpu_custom_call" | custom-call | flops 1207959552 | bytes 3145728 | tf_op jit(solution)/shard_map/pallas_call | solution.py:261
  76.0 4.0 %collective-permute-start.22 = (f32[4,2,8,8,128]{4,3,2,1,0:T(8,128)S(1)}, f32[4,2,8,8,128]{4,3,2,1,0:T(8,128)S(1)}, u32[]{:S(2)}, u32[]{:S(2)}) collective-permute-start(f32[4,2,8,8,128]{4,3,2,1,0:T(8,128)S(1)} %get-tuple-element.72), channel_id=1, source_target_pairs={{0,64},{8,72},{16,80},{24,88},{32,96},{40,104},{48,112},{56,120},{... | collective-permute-start | bytes 786440 | tf_op jit(solution)/shard_map/ppermute | solution.py:303
  80.0 1.7 %collective-permute-start.5 = (f32[4,8,8,128]{3,2,1,0:T(8,128)S(1)}, f32[4,8,8,128]{3,2,1,0:T(8,128)S(1)}, u32[]{:S(2)}, u32[]{:S(2)}) collective-permute-start(f32[4,8,8,128]{3,2,1,0:T(8,128)S(1)} %get-tuple-element.49), channel_id=1, source_target_pairs={{0,32},{8,40},{16,48},{24,56},{32,0},{40,8},{48,16},{56,24},{64,96... | collective-permute-start | bytes 393224 | tf_op jit(solution)/shard_map/ppermute | solution.py:303
  81.7 2.7 %collective-permute-start.6 = (f32[4,8,8,128]{3,2,1,0:T(8,128)S(1)}, f32[4,8,8,128]{3,2,1,0:T(8,128)S(1)}, u32[]{:S(2)}, u32[]{:S(2)}) collective-permute-start(f32[4,8,8,128]{3,2,1,0:T(8,128)S(1)} %get-tuple-element.50), channel_id=1, source_target_pairs={{0,40},{8,32},{16,56},{24,48},{32,8},{40,0},{48,24},{56,16},{64,10... | collective-permute-start | bytes 393224 | tf_op jit(solution)/shard_map/ppermute | solution.py:303
  84.4 2.4 %collective-permute-start.7 = (f32[4,8,8,128]{3,2,1,0:T(8,128)S(1)}, f32[4,8,8,128]{3,2,1,0:T(8,128)S(1)}, u32[]{:S(2)}, u32[]{:S(2)}) collective-permute-start(f32[4,8,8,128]{3,2,1,0:T(8,128)S(1)} %get-tuple-element.51), channel_id=1, source_target_pairs={{0,48},{8,56},{16,0},{24,8},{32,16},{40,24},{48,32},{56,40},{64,11... | collective-permute-start | bytes 393224 | tf_op jit(solution)/shard_map/ppermute | solution.py:303
  86.8 4.7 %collective-permute-start.23 = (f32[4,2,8,8,128]{4,3,2,1,0:T(8,128)S(1)}, f32[4,2,8,8,128]{4,3,2,1,0:T(8,128)S(1)}, u32[]{:S(2)}, u32[]{:S(2)}) collective-permute-start(f32[4,2,8,8,128]{4,3,2,1,0:T(8,128)S(1)} %get-tuple-element.73), channel_id=1, source_target_pairs={{0,128},{8,136},{16,144},{24,152},{32,160},{40,168},{48,176},{56,1... | collective-permute-start | bytes 786440 | tf_op jit(solution)/shard_map/ppermute | solution.py:303
  91.5 1.5 collective-permute-start.24
  93.1 2.9 %collective-permute-done.8.refs_7_ = f32[4,8,8,128]{3,2,1,0:T(8,128)S(1)} collective-permute-done((f32[4,8,8,128]{3,2,1,0:T(8,128)S(1)}, f32[4,8,8,128]{3,2,1,0:T(8,128)S(1)}, u32[]{:S(2)}, u32[]{:S(2)}) %collective-permute-start.8) | collective-permute-done | bytes 131104 | tf_op jit(solution)/shard_map/ppermute | solution.py:303
  96.1 4.9 %collective-permute-start.10 = (f32[4,2,8,8,128]{4,3,2,1,0:T(8,128)S(1)}, f32[4,2,8,8,128]{4,3,2,1,0:T(8,128)S(1)}, u32[]{:S(2)}, u32[]{:S(2)}) collective-permute-start(f32[4,2,8,8,128]{4,3,2,1,0:T(8,128)S(1)} %get-tuple-element.55), channel_id=1, source_target_pairs={{0,128},{8,136},{16,144},{24,152},{32,160},{40,168},{48,176},{56,1... | collective-permute-start | bytes 786440 | tf_op jit(solution)/shard_map/ppermute | solution.py:303
  104.3 5.1 %collective-permute-done.23.refs_3_ = f32[4,2,8,8,128]{4,3,2,1,0:T(8,128)S(1)} collective-permute-done((f32[4,2,8,8,128]{4,3,2,1,0:T(8,128)S(1)}, f32[4,2,8,8,128]{4,3,2,1,0:T(8,128)S(1)}, u32[]{:S(2)}, u32[]{:S(2)}) %collective-permute-start.23) | collective-permute-done | bytes 262176 | tf_op jit(solution)/shard_map/ppermute | solution.py:303
  109.4 19.8 %collective-permute-done.24.refs_4_ = f32[4,2,8,8,128]{4,3,2,1,0:T(8,128)S(1)} collective-permute-done((f32[4,2,8,8,128]{4,3,2,1,0:T(8,128)S(1)}, f32[4,2,8,8,128]{4,3,2,1,0:T(8,128)S(1)}, u32[]{:S(2)}, u32[]{:S(2)}) %collective-permute-start.24) | collective-permute-done | bytes 262176 | tf_op jit(solution)/shard_map/ppermute | solution.py:303
  129.2 2.9 %shard_map.51 = (f32[8,16,8,128]{3,2,1,0:T(8,128)S(1)}, f32[8,16,8,128]{3,2,1,0:T(8,128)S(1)}) custom-call(bf16[3,256,256]{2,1,0:T(8,128)(2,1)S(1)} %shard_map.38.refs_0_, f32[4,2,8,8,128]{4,3,2,1,0:T(8,128)S(1)} %get-tuple-element.71.refs_1_, f32[4,2,8,8,128]{4,3,2,1,0:T(8,128)S(1)} %collective-permute-done.22.refs_2_, ...), custom_call_target="tpu_custom_call" | custom-call | flops 1207959552 | bytes 3145728 | tf_op jit(solution)/shard_map/pallas_call | solution.py:261
  132.2 5.2 %collective-permute-done.11.refs_4_ = f32[4,2,8,8,128]{4,3,2,1,0:T(8,128)S(1)} collective-permute-done((f32[4,2,8,8,128]{4,3,2,1,0:T(8,128)S(1)}, f32[4,2,8,8,128]{4,3,2,1,0:T(8,128)S(1)}, u32[]{:S(2)}, u32[]{:S(2)}) %collective-permute-start.11) | collective-permute-done | bytes 262176 | tf_op jit(solution)/shard_map/ppermute | solution.py:303
  137.4 2.0 %shard_map.46 = (f32[8,16,8,128]{3,2,1,0:T(8,128)S(1)}, f32[8,16,8,128]{3,2,1,0:T(8,128)S(1)}) custom-call(bf16[3,256,256]{2,1,0:T(8,128)(2,1)S(1)} %shard_map.38.refs_0_, f32[4,2,8,8,128]{4,3,2,1,0:T(8,128)S(1)} %get-tuple-element.53.refs_1_, f32[4,2,8,8,128]{4,3,2,1,0:T(8,128)S(1)} %collective-permute-done.9.refs_2_, ...), custom_call_target="tpu_custom_call" | custom-call | flops 1207959552 | bytes 3145728 | tf_op jit(solution)/shard_map/pallas_call | solution.py:261
  139.4 3.0 %collective-permute-start.12 = (f32[8,16,8,128]{3,2,1,0:T(8,128)S(1)}, f32[8,16,8,128]{3,2,1,0:T(8,128)S(1)}, u32[]{:S(2)}, u32[]{:S(2)}) collective-permute-start(f32[8,16,8,128]{3,2,1,0:T(8,128)S(1)} %get-tuple-element.58), channel_id=1, source_target_pairs={{0,4},{1,5},{2,6},{3,7},{4,0},{5,1},{6,2},{7,3},{8,12},{9,13},{10,... | collective-permute-start | bytes 1572872 | tf_op jit(solution)/shard_map/ppermute | solution.py:295
  143.3 1.8 %low_weights.1.refs_4_ = bf16[2,256,256]{2,1,0:T(8,128)(2,1)S(1)} custom-call(f32[5,4,2,128,128]{4,3,2,1,0:T(8,128)S(1)} %copy-done.1), custom_call_target="tpu_custom_call" | custom-call | flops 503316480 | bytes 1048576 | tf_op jit(solution)/shard_map/low_weights/pallas_call | solution.py:124
  146.5 2.9 %shard_map.52.refs_3_ = f32[16,16,8,128]{3,2,1,0:T(8,128)S(1)} custom-call(bf16[3,256,256]{2,1,0:T(8,128)(2,1)S(1)} %shard_map.37.refs_0_, f32[8,16,8,128]{3,2,1,0:T(8,128)S(1)} %get-tuple-element.75.refs_1_, f32[8,16,8,128]{3,2,1,0:T(8,128)S(1)} %collective-permute-done.25.refs_2_), custom_call_target="tpu_custom_call" | custom-call | flops 1207959552 | bytes 3145728 | tf_op jit(solution)/shard_map/pallas_call | solution.py:261
  149.4 8.3 %collective-permute-done.12.refs_2_ = f32[8,16,8,128]{3,2,1,0:T(8,128)S(1)} collective-permute-done((f32[8,16,8,128]{3,2,1,0:T(8,128)S(1)}, f32[8,16,8,128]{3,2,1,0:T(8,128)S(1)}, u32[]{:S(2)}, u32[]{:S(2)}) %collective-permute-start.12) | collective-permute-done | bytes 524320 | tf_op jit(solution)/shard_map/ppermute | solution.py:295
  157.7 4.6 %shard_map.53 = f32[2,2048,128]{2,1,0:T(8,128)} custom-call(bf16[3,256,256]{2,1,0:T(8,128)(2,1)S(1)} %shard_map.37.refs_0_, f32[8,16,8,128]{3,2,1,0:T(8,128)S(1)} %get-tuple-element.57.refs_1_, f32[8,16,8,128]{3,2,1,0:T(8,128)S(1)} %collective-permute-done.12.refs_2_, f32[16,16,8,128]{3,2,1,0:T(8,128)S(1)} %shard_map.52.refs_3_, ...), custom_call_target="tpu_custom_call" | custom-call | flops 1207959552 | bytes 3145728 | tf_op jit(solution)/shard_map/pallas_call | solution.py:261
  (48 shorter events, 17.2 us)
Async XLA Ops:
  0.0 1.7 %copy-start = (f32[5,4,2,128,128]{4,3,2,1,0:T(8,128)S(1)}, f32[5,4,2,128,128]{4,3,2,1,0:T(8,128)}, u32[]{:S(2)}) copy-start(f32[5,4,2,128,128]{4,3,2,1,0:T(8,128)} %gates_ref.11) | copy-start | bytes 7864324
  1.7 0.7 copy-start.2
  2.4 1.6 copy-start.4
  6.3 5.7 %copy-start.1 = (f32[5,4,2,128,128]{4,3,2,1,0:T(8,128)S(1)}, f32[5,4,2,128,128]{4,3,2,1,0:T(8,128)}, u32[]{:S(2)}) copy-start(f32[5,4,2,128,128]{4,3,2,1,0:T(8,128)} %gates_ref.11) | copy-start | bytes 7864324
  6.3 6.6 %collective-permute-start.13 = (f32[8,16,8,128]{3,2,1,0:T(8,128)S(1)}, f32[8,16,8,128]{3,2,1,0:T(8,128)S(1)}, u32[]{:S(2)}, u32[]{:S(2)}) collective-permute-start(f32[8,16,8,128]{3,2,1,0:T(8,128)S(1)} %get-tuple-element.60), channel_id=1, source_target_pairs={{0,8},{8,0},{16,24},{24,16},{32,40},{40,32},{48,56},{56,48},{64,72... | collective-permute-start | bytes 1572872 | tf_op jit(solution)/shard_map/ppermute | solution.py:295
  11.9 8.3 %collective-permute-start = (f32[8,16,8,128]{3,2,1,0:T(8,128)S(1)}, f32[8,16,8,128]{3,2,1,0:T(8,128)S(1)}, u32[]{:S(2)}, u32[]{:S(2)}) collective-permute-start(f32[8,16,8,128]{3,2,1,0:T(8,128)S(1)} %get-tuple-element.42), channel_id=1, source_target_pairs={{0,8},{8,0},{16,24},{24,16},{32,40},{40,32},{48,56},{56,48},{64,72... | collective-permute-start | bytes 1572872 | tf_op jit(solution)/shard_map/ppermute | solution.py:295
  14.9 19.1 %collective-permute-start.14 = (f32[8,16,8,128]{3,2,1,0:T(8,128)S(1)}, f32[8,16,8,128]{3,2,1,0:T(8,128)S(1)}, u32[]{:S(2)}, u32[]{:S(2)}) collective-permute-start(f32[8,16,8,128]{3,2,1,0:T(8,128)S(1)} %get-tuple-element.62), channel_id=1, source_target_pairs={{0,128},{8,136},{16,144},{24,152},{32,160},{40,168},{48,176},{56,1... | collective-permute-start | bytes 1572872 | tf_op jit(solution)/shard_map/ppermute | solution.py:295
  23.1 26.0 %collective-permute-start.1 = (f32[8,16,8,128]{3,2,1,0:T(8,128)S(1)}, f32[8,16,8,128]{3,2,1,0:T(8,128)S(1)}, u32[]{:S(2)}, u32[]{:S(2)}) collective-permute-start(f32[8,16,8,128]{3,2,1,0:T(8,128)S(1)} %get-tuple-element.44), channel_id=1, source_target_pairs={{0,128},{8,136},{16,144},{24,152},{32,160},{40,168},{48,176},{56,1... | collective-permute-start | bytes 1572872 | tf_op jit(solution)/shard_map/ppermute | solution.py:295
  36.0 32.2 %collective-permute-start.15 = (f32[4,8,8,128]{3,2,1,0:T(8,128)S(1)}, f32[4,8,8,128]{3,2,1,0:T(8,128)S(1)}, u32[]{:S(2)}, u32[]{:S(2)}) collective-permute-start(f32[4,8,8,128]{3,2,1,0:T(8,128)S(1)} %get-tuple-element.64), channel_id=1, source_target_pairs={{0,8},{8,0},{16,24},{24,16},{32,40},{40,32},{48,56},{56,48},{64,72... | collective-permute-start | bytes 393224 | tf_op jit(solution)/shard_map/ppermute | solution.py:303
  38.7 30.3 %collective-permute-start.16 = (f32[4,8,8,128]{3,2,1,0:T(8,128)S(1)}, f32[4,8,8,128]{3,2,1,0:T(8,128)S(1)}, u32[]{:S(2)}, u32[]{:S(2)}) collective-permute-start(f32[4,8,8,128]{3,2,1,0:T(8,128)S(1)} %get-tuple-element.65), channel_id=1, source_target_pairs={{0,16},{8,24},{16,32},{24,40},{32,48},{40,56},{48,0},{56,8},{64,80... | collective-permute-start | bytes 393224 | tf_op jit(solution)/shard_map/ppermute | solution.py:303
  39.5 32.5 %collective-permute-start.17 = (f32[4,8,8,128]{3,2,1,0:T(8,128)S(1)}, f32[4,8,8,128]{3,2,1,0:T(8,128)S(1)}, u32[]{:S(2)}, u32[]{:S(2)}) collective-permute-start(f32[4,8,8,128]{3,2,1,0:T(8,128)S(1)} %get-tuple-element.66), channel_id=1, source_target_pairs={{0,24},{8,16},{16,40},{24,32},{32,56},{40,48},{48,8},{56,0},{64,88... | collective-permute-start | bytes 393224 | tf_op jit(solution)/shard_map/ppermute | solution.py:303
  40.9 31.6 %collective-permute-start.18 = (f32[4,8,8,128]{3,2,1,0:T(8,128)S(1)}, f32[4,8,8,128]{3,2,1,0:T(8,128)S(1)}, u32[]{:S(2)}, u32[]{:S(2)}) collective-permute-start(f32[4,8,8,128]{3,2,1,0:T(8,128)S(1)} %get-tuple-element.67), channel_id=1, source_target_pairs={{0,32},{8,40},{16,48},{24,56},{32,0},{40,8},{48,16},{56,24},{64,96... | collective-permute-start | bytes 393224 | tf_op jit(solution)/shard_map/ppermute | solution.py:303
  49.1 24.8 %collective-permute-start.19 = (f32[4,8,8,128]{3,2,1,0:T(8,128)S(1)}, f32[4,8,8,128]{3,2,1,0:T(8,128)S(1)}, u32[]{:S(2)}, u32[]{:S(2)}) collective-permute-start(f32[4,8,8,128]{3,2,1,0:T(8,128)S(1)} %get-tuple-element.68), channel_id=1, source_target_pairs={{0,40},{8,32},{16,56},{24,48},{32,8},{40,0},{48,24},{56,16},{64,10... | collective-permute-start | bytes 393224 | tf_op jit(solution)/shard_map/ppermute | solution.py:303
  68.2 6.7 %collective-permute-start.20 = (f32[4,8,8,128]{3,2,1,0:T(8,128)S(1)}, f32[4,8,8,128]{3,2,1,0:T(8,128)S(1)}, u32[]{:S(2)}, u32[]{:S(2)}) collective-permute-start(f32[4,8,8,128]{3,2,1,0:T(8,128)S(1)} %get-tuple-element.69), channel_id=1, source_target_pairs={{0,48},{8,56},{16,0},{24,8},{32,16},{40,24},{48,32},{56,40},{64,11... | collective-permute-start | bytes 393224 | tf_op jit(solution)/shard_map/ppermute | solution.py:303
  69.0 6.8 %collective-permute-start.21 = (f32[4,8,8,128]{3,2,1,0:T(8,128)S(1)}, f32[4,8,8,128]{3,2,1,0:T(8,128)S(1)}, u32[]{:S(2)}, u32[]{:S(2)}) collective-permute-start(f32[4,8,8,128]{3,2,1,0:T(8,128)S(1)} %get-tuple-element.70), channel_id=1, source_target_pairs={{0,56},{8,48},{16,8},{24,0},{32,24},{40,16},{48,40},{56,32},{64,12... | collective-permute-start | bytes 393224 | tf_op jit(solution)/shard_map/ppermute | solution.py:303
  71.9 31.4 %copy-start.3 = (s32[32]{0:T(128)S(1)}, s32[32]{0:T(128)}, u32[]{:S(2)}) copy-start(s32[32]{0:T(128)} %perm_ref.9) | copy-start | bytes 388
  72.0 9.7 %collective-permute-start.2 = (f32[4,8,8,128]{3,2,1,0:T(8,128)S(1)}, f32[4,8,8,128]{3,2,1,0:T(8,128)S(1)}, u32[]{:S(2)}, u32[]{:S(2)}) collective-permute-start(f32[4,8,8,128]{3,2,1,0:T(8,128)S(1)} %get-tuple-element.46), channel_id=1, source_target_pairs={{0,8},{8,0},{16,24},{24,16},{32,40},{40,32},{48,56},{56,48},{64,72... | collective-permute-start | bytes 393224 | tf_op jit(solution)/shard_map/ppermute | solution.py:303
  72.5 11.9 %collective-permute-start.3 = (f32[4,8,8,128]{3,2,1,0:T(8,128)S(1)}, f32[4,8,8,128]{3,2,1,0:T(8,128)S(1)}, u32[]{:S(2)}, u32[]{:S(2)}) collective-permute-start(f32[4,8,8,128]{3,2,1,0:T(8,128)S(1)} %get-tuple-element.47), channel_id=1, source_target_pairs={{0,16},{8,24},{16,32},{24,40},{32,48},{40,56},{48,0},{56,8},{64,80... | collective-permute-start | bytes 393224 | tf_op jit(solution)/shard_map/ppermute | solution.py:303
  73.9 12.9 %collective-permute-start.4 = (f32[4,8,8,128]{3,2,1,0:T(8,128)S(1)}, f32[4,8,8,128]{3,2,1,0:T(8,128)S(1)}, u32[]{:S(2)}, u32[]{:S(2)}) collective-permute-start(f32[4,8,8,128]{3,2,1,0:T(8,128)S(1)} %get-tuple-element.48), channel_id=1, source_target_pairs={{0,24},{8,16},{16,40},{24,32},{32,56},{40,48},{48,8},{56,0},{64,88... | collective-permute-start | bytes 393224 | tf_op jit(solution)/shard_map/ppermute | solution.py:303
  76.0 26.4 %collective-permute-start.22 = (f32[4,2,8,8,128]{4,3,2,1,0:T(8,128)S(1)}, f32[4,2,8,8,128]{4,3,2,1,0:T(8,128)S(1)}, u32[]{:S(2)}, u32[]{:S(2)}) collective-permute-start(f32[4,2,8,8,128]{4,3,2,1,0:T(8,128)S(1)} %get-tuple-element.72), channel_id=1, source_target_pairs={{0,64},{8,72},{16,80},{24,88},{32,96},{40,104},{48,112},{56,120},{... | collective-permute-start | bytes 786440 | tf_op jit(solution)/shard_map/ppermute | solution.py:303
  80.0 6.8 %collective-permute-start.5 = (f32[4,8,8,128]{3,2,1,0:T(8,128)S(1)}, f32[4,8,8,128]{3,2,1,0:T(8,128)S(1)}, u32[]{:S(2)}, u32[]{:S(2)}) collective-permute-start(f32[4,8,8,128]{3,2,1,0:T(8,128)S(1)} %get-tuple-element.49), channel_id=1, source_target_pairs={{0,32},{8,40},{16,48},{24,56},{32,0},{40,8},{48,16},{56,24},{64,96... | collective-permute-start | bytes 393224 | tf_op jit(solution)/shard_map/ppermute | solution.py:303
  81.7 9.8 %collective-permute-start.6 = (f32[4,8,8,128]{3,2,1,0:T(8,128)S(1)}, f32[4,8,8,128]{3,2,1,0:T(8,128)S(1)}, u32[]{:S(2)}, u32[]{:S(2)}) collective-permute-start(f32[4,8,8,128]{3,2,1,0:T(8,128)S(1)} %get-tuple-element.50), channel_id=1, source_target_pairs={{0,40},{8,32},{16,56},{24,48},{32,8},{40,0},{48,24},{56,16},{64,10... | collective-permute-start | bytes 393224 | tf_op jit(solution)/shard_map/ppermute | solution.py:303
  84.4 8.7 %collective-permute-start.7 = (f32[4,8,8,128]{3,2,1,0:T(8,128)S(1)}, f32[4,8,8,128]{3,2,1,0:T(8,128)S(1)}, u32[]{:S(2)}, u32[]{:S(2)}) collective-permute-start(f32[4,8,8,128]{3,2,1,0:T(8,128)S(1)} %get-tuple-element.51), channel_id=1, source_target_pairs={{0,48},{8,56},{16,0},{24,8},{32,16},{40,24},{48,32},{56,40},{64,11... | collective-permute-start | bytes 393224 | tf_op jit(solution)/shard_map/ppermute | solution.py:303
  86.8 9.2 %collective-permute-start.8 = (f32[4,8,8,128]{3,2,1,0:T(8,128)S(1)}, f32[4,8,8,128]{3,2,1,0:T(8,128)S(1)}, u32[]{:S(2)}, u32[]{:S(2)}) collective-permute-start(f32[4,8,8,128]{3,2,1,0:T(8,128)S(1)} %get-tuple-element.52), channel_id=1, source_target_pairs={{0,56},{8,48},{16,8},{24,0},{32,24},{40,16},{48,40},{56,32},{64,12... | collective-permute-start | bytes 393224 | tf_op jit(solution)/shard_map/ppermute | solution.py:303
  86.8 22.6 %collective-permute-start.23 = (f32[4,2,8,8,128]{4,3,2,1,0:T(8,128)S(1)}, f32[4,2,8,8,128]{4,3,2,1,0:T(8,128)S(1)}, u32[]{:S(2)}, u32[]{:S(2)}) collective-permute-start(f32[4,2,8,8,128]{4,3,2,1,0:T(8,128)S(1)} %get-tuple-element.73), channel_id=1, source_target_pairs={{0,128},{8,136},{16,144},{24,152},{32,160},{40,168},{48,176},{56,1... | collective-permute-start | bytes 786440 | tf_op jit(solution)/shard_map/ppermute | solution.py:303
  91.5 37.6 %collective-permute-start.24 = (f32[4,2,8,8,128]{4,3,2,1,0:T(8,128)S(1)}, f32[4,2,8,8,128]{4,3,2,1,0:T(8,128)S(1)}, u32[]{:S(2)}, u32[]{:S(2)}) collective-permute-start(f32[4,2,8,8,128]{4,3,2,1,0:T(8,128)S(1)} %get-tuple-element.74), channel_id=1, source_target_pairs={{0,192},{8,200},{16,208},{24,216},{32,224},{40,232},{48,240},{56,2... | collective-permute-start | bytes 786440 | tf_op jit(solution)/shard_map/ppermute | solution.py:303
  96.1 36.1 %collective-permute-start.10 = (f32[4,2,8,8,128]{4,3,2,1,0:T(8,128)S(1)}, f32[4,2,8,8,128]{4,3,2,1,0:T(8,128)S(1)}, u32[]{:S(2)}, u32[]{:S(2)}) collective-permute-start(f32[4,2,8,8,128]{4,3,2,1,0:T(8,128)S(1)} %get-tuple-element.55), channel_id=1, source_target_pairs={{0,128},{8,136},{16,144},{24,152},{32,160},{40,168},{48,176},{56,1... | collective-permute-start | bytes 786440 | tf_op jit(solution)/shard_map/ppermute | solution.py:303
  101.0 36.4 %collective-permute-start.11 = (f32[4,2,8,8,128]{4,3,2,1,0:T(8,128)S(1)}, f32[4,2,8,8,128]{4,3,2,1,0:T(8,128)S(1)}, u32[]{:S(2)}, u32[]{:S(2)}) collective-permute-start(f32[4,2,8,8,128]{4,3,2,1,0:T(8,128)S(1)} %get-tuple-element.56), channel_id=1, source_target_pairs={{0,192},{8,200},{16,208},{24,216},{32,224},{40,232},{48,240},{56,2... | collective-permute-start | bytes 786440 | tf_op jit(solution)/shard_map/ppermute | solution.py:303
  102.4 35.0 %collective-permute-start.9 = (f32[4,2,8,8,128]{4,3,2,1,0:T(8,128)S(1)}, f32[4,2,8,8,128]{4,3,2,1,0:T(8,128)S(1)}, u32[]{:S(2)}, u32[]{:S(2)}) collective-permute-start(f32[4,2,8,8,128]{4,3,2,1,0:T(8,128)S(1)} %get-tuple-element.54), channel_id=1, source_target_pairs={{0,64},{8,72},{16,80},{24,88},{32,96},{40,104},{48,112},{56,120},{... | collective-permute-start | bytes 786440 | tf_op jit(solution)/shard_map/ppermute | solution.py:303
  132.1 14.4 %collective-permute-start.25 = (f32[8,16,8,128]{3,2,1,0:T(8,128)S(1)}, f32[8,16,8,128]{3,2,1,0:T(8,128)S(1)}, u32[]{:S(2)}, u32[]{:S(2)}) collective-permute-start(f32[8,16,8,128]{3,2,1,0:T(8,128)S(1)} %get-tuple-element.76), channel_id=1, source_target_pairs={{0,4},{1,5},{2,6},{3,7},{4,0},{5,1},{6,2},{7,3},{8,12},{9,13},{10,... | collective-permute-start | bytes 1572872 | tf_op jit(solution)/shard_map/ppermute | solution.py:295
  139.4 18.3 %collective-permute-start.12 = (f32[8,16,8,128]{3,2,1,0:T(8,128)S(1)}, f32[8,16,8,128]{3,2,1,0:T(8,128)S(1)}, u32[]{:S(2)}, u32[]{:S(2)}) collective-permute-start(f32[8,16,8,128]{3,2,1,0:T(8,128)S(1)} %get-tuple-element.58), channel_id=1, source_target_pairs={{0,4},{1,5},{2,6},{3,7},{4,0},{5,1},{6,2},{7,3},{8,12},{9,13},{10,... | collective-permute-start | bytes 1572872 | tf_op jit(solution)/shard_map/ppermute | solution.py:295

commit v2 on v1

--- a/solution.py
+++ b/solution.py
@@ -49,7 +49,9 @@
     return jnp.where(want == old, 1.0, 0.0).astype(BF16)
 
 
-def weight_kernel(kinds, perm_ref, gates_ref, out_ref):
+def weight_kernel(kinds, *refs):
+    perm_ref = refs[0] if len(refs) == 3 else None
+    gates_ref, out_ref = refs[-2:]
     made = {}
     for number, (rows, cols) in enumerate(kinds):
         for kind in (rows, cols):
@@ -77,20 +79,24 @@
 
 
 def weights(gate_matrices, seg, kinds, permutation):
+    prefetch = () if permutation is None else (permutation,)
+    block = seg
+    if seg == 0:
+        block, gate_matrices = 0, gate_matrices[:1]
     return pl.pallas_call(
         functools.partial(weight_kernel, kinds),
         out_shape=jax.ShapeDtypeStruct((3, 256, 256), BF16),
         grid_spec=pltpu.PrefetchScalarGridSpec(
-            num_scalar_prefetch=1,
+            num_scalar_prefetch=len(prefetch),
             grid=(1,),
-            in_specs=[pl.BlockSpec((1, 4, 2, GD, GD), lambda i, perm: (seg, 0, 0, 0, 0))],
+            in_specs=[pl.BlockSpec((1, 4, 2, GD, GD), lambda i, *_: (block, 0, 0, 0, 0))],
             out_specs=pl.BlockSpec(memory_space=pltpu.VMEM),
         ),
         cost_estimate=pl.CostEstimate(
             flops=3 * 2 * 640 * 128 * 512, bytes_accessed=1 << 20, transcendentals=0
         ),
         compiler_params=pltpu.CompilerParams(vmem_limit_bytes=LIMIT),
-    )(permutation, gate_matrices)
+    )(*prefetch, gate_matrices)
 
 
 def low_kernel(gates_ref, out_ref, total_ref):
@@ -117,13 +123,17 @@
 
     total = times(high, form_high) + (times(high, form_low) + times(low, form_high))
     total_ref[...] = total
-    out_ref[0], out_ref[1] = split(total)
+    for k, piece in enumerate(split(total)):
+        for h in range(2):
+            rows = piece[GD * h : GD * (h + 1)]
+            out_ref[h, k, 0:GD] = rows
+            out_ref[h, k, GD:] = rows
 
 
 def low_weights(gate_matrices):
     return pl.pallas_call(
         low_kernel,
-        out_shape=jax.ShapeDtypeStruct((2, 256, 256), BF16),
+        out_shape=jax.ShapeDtypeStruct((2, 2, 256, 256), BF16),
         grid=(gate_matrices.shape[0],),
         in_specs=[pl.BlockSpec((1, 1, 2, GD, GD), lambda i: (i, 2, 0, 0, 0))],
         out_specs=pl.BlockSpec(memory_space=pltpu.VMEM),
@@ -176,8 +186,13 @@
         ]
 
     def load_remap(i):
-        near = jnp.concatenate([ref[:, 0, i] for ref in ins[:4]], axis=0)
-        far = jnp.concatenate([ref[:, 1, i] for ref in ins[:4]], axis=0)
+        def half(c):
+            if source[1] == "by_x":
+                blocks = [ins[x][z, c, i] for z in range(4) for x in range(4)]
+                return jnp.stack(blocks, axis=0)
+            return jnp.concatenate([ins[2 * z + c][:, i] for z in range(4)], axis=0)
+
+        near, far = half(0), half(1)
         even = jnp.where(upper, pltpu.roll(far, 4, 1), near)
         odd = jnp.where(upper, far, pltpu.roll(near, 4, 1))
         return [even.reshape(GD, GD), odd.reshape(GD, GD)]
@@ -208,32 +223,34 @@
             for p, piece in zip((2 * i, 2 * i + 1), pieces):
                 outs[0][:, p] = piece[:HALF].reshape(8, 8, GD)
                 outs[1][:, p] = piece[HALF:].reshape(8, 8, GD)
-        elif target == "remap":
+        elif target in ("by_x", "by_z"):
             even, odd = (piece.reshape(16, 8, GD) for piece in pieces)
             near = jnp.where(upper, pltpu.roll(odd, 4, 1), even)
             far = jnp.where(upper, odd, pltpu.roll(even, 4, 1))
             for x in range(4):
-                outs[2 * x][:, i] = near[4 * x : 4 * x + 4]
-                outs[2 * x + 1][:, i] = far[4 * x : 4 * x + 4]
+                if target == "by_x":
+                    outs[x][:, 0, i] = near[4 * x : 4 * x + 4]
+                    outs[x][:, 1, i] = far[4 * x : 4 * x + 4]
+                    continue
+                for z in range(4):
+                    outs[2 * z][x, i] = near[4 * x + z]
+                    outs[2 * z + 1][x, i] = far[4 * x + z]
         else:
-            held = outs[0] if target == "plain" else one
             for p, piece in zip((2 * i, 2 * i + 1), pieces):
-                held[:, p] = piece.reshape(16, 8, GD)
+                one[:, p] = piece.reshape(16, 8, GD)
         return carry
 
     def low_gate(i, carry):
-        other_ref, low_ref = ins[n_in - 2], ins[n_in - 1]
-        rows = [
-            jnp.concatenate(
-                [other_ref[:, p].reshape(GD, GD), one[:, p].reshape(GD, GD)], axis=1
-            )
-            for p in range(4 * i, 4 * i + 4)
-        ]
-        high, low = split(jnp.concatenate(rows, axis=0))
-        done = jnp.dot(high, low_ref[0], preferred_element_type=F32) + (
-            jnp.dot(high, low_ref[1], preferred_element_type=F32)
-            + jnp.dot(low, low_ref[0], preferred_element_type=F32)
+        low_ref = ins[-1]
+        rows = jnp.concatenate([one[:, 4 * i + k].reshape(GD, GD) for k in range(4)], axis=0)
+        pair = jnp.concatenate(split(rows), axis=1)
+        done = jnp.dot(pair, low_ref[source[1], 0], preferred_element_type=F32) + jnp.dot(
+            pair, low_ref[source[1], 1], preferred_element_type=F32
         )
+        if target == "share":
+            outs[0][i] = done
+            return carry
+        done = done + ins[-2][i]
         for k in range(4):
             piece = done[GD * k : GD * (k + 1)]
             outs[0][0, pl.ds(4 * i + k, GD, stride=16), :] = piece[:, :GD]
@@ -242,18 +259,19 @@
 
     for step in (top_first, mid, top_last):
         lax.fori_loop(0, 8, step, 0, unroll=unroll)
-    if target == "low":
-        for i in range(4):
-            low_gate(i, 0)
+    if target in ("share", "low"):
+        lax.fori_loop(0, 4, low_gate, 0, unroll=4 if unroll == 8 else 1)
 
 
 def run_segment(source, target, w, ins, extra=(), unroll=8):
     if target == "pair":
         out_shape = [jax.ShapeDtypeStruct(PART, F32)] * 2
-    elif target == "remap":
+    elif target == "by_x":
+        out_shape = [jax.ShapeDtypeStruct((4, 2, 8, 8, 128), F32)] * 4
+    elif target == "by_z":
         out_shape = [jax.ShapeDtypeStruct((4, 8, 8, 128), F32)] * 8
-    elif target == "plain":
-        out_shape = [jax.ShapeDtypeStruct(STATE, F32)]
+    elif target == "share":
+        out_shape = [jax.ShapeDtypeStruct((4, 512, 256), F32)]
     else:
         out_shape = [jax.ShapeDtypeStruct((2, 2048, 128), F32)]
     args = list(ins) + list(extra)
@@ -271,21 +289,27 @@
     )(w, *args)
 
 
-def regroup_kernel(*refs):
-    ins, outs = refs[:8], refs[8:]
+def regroup_kernel(target, *refs):
+    by_z, by_x = (refs[:8], refs[8:]) if target == "by_x" else (refs[4:], refs[:4])
     for z in range(4):
         for x in range(4):
             for c in range(2):
-                outs[z][x, c] = ins[2 * x + c][z]
-
-
-def regroup(blocks):
+                if target == "by_x":
+                    by_x[x][z, c] = by_z[2 * z + c][x]
+                else:
+                    by_z[2 * z + c][x] = by_x[x][z, c]
+
+
+def regroup(target, blocks):
     vmem = pl.BlockSpec(memory_space=pltpu.VMEM)
+    by_x = [jax.ShapeDtypeStruct((4, 2, 8, 8, 128), F32)] * 4
+    by_z = [jax.ShapeDtypeStruct((4, 8, 8, 128), F32)] * 8
+    out_shape = by_x if target == "by_x" else by_z
     return pl.pallas_call(
-        regroup_kernel,
-        out_shape=[jax.ShapeDtypeStruct((4, 2, 8, 8, 128), F32)] * 4,
-        in_specs=[vmem] * 8,
-        out_specs=[vmem] * 4,
+        functools.partial(regroup_kernel, target),
+        out_shape=out_shape,
+        in_specs=[vmem] * len(blocks),
+        out_specs=[vmem] * len(out_shape),
         cost_estimate=pl.CostEstimate(flops=0, bytes_accessed=2 << 20, transcendentals=0),
         compiler_params=pltpu.CompilerParams(vmem_limit_bytes=LIMIT),
     )(*blocks)
@@ -301,6 +325,20 @@
         to = ((((s >> 3) + z) & 3) << 3) | ((((s >> 1) + x) & 3) << 1) | ((s & 1) ^ c)
         pairs.append((s, to))
     return lax.ppermute(value, "row", pairs)
+
+
+def shift_x(blocks):
+    moved = [blocks[0]]
+    for x in range(1, 4):
+        moved.append(shift_row(blocks[x], 0, x, 0))
+    return moved
+
+
+def shift_z(blocks):
+    moved = [blocks[0]]
+    for k in range(1, 8):
+        moved.append(shift_row(blocks[k], k >> 1, 0, k & 1))
+    return moved
 
 
 def circuit(amplitudes, gate_matrices, permutation):
@@ -313,7 +351,10 @@
         ((None, "src"), mid, ("xor4", None)),
         ((None, "xor4"), mid, (None, None)),
     )
-    w = [weights(gate_matrices, seg, kinds[seg], permutation) for seg in range(5)]
+    w = [
+        weights(gate_matrices, seg, kinds[seg], permutation if seg == 3 else None)
+        for seg in range(5)
+    ]
     low = low_weights(gate_matrices)
     halves = (0, 1)
     kept, sent = {}, {}
@@ -324,21 +365,17 @@
         kept[h], out = run_segment(("pair",), "pair", w[1], [kept[h], sent[h]], unroll=(8, 4)[h])
         sent[h] = flip(out, "row", 16)
     got = {}
+    blocks = run_segment(("pair",), "by_z", w[2], [kept[0], sent[0]])
+    got[0] = shift_x(regroup("by_x", shift_z(blocks)))
+    blocks = run_segment(("pair",), "by_x", w[2], [kept[1], sent[1]])
+    got[1] = shift_z(regroup("by_z", shift_x(blocks)))
     for h in halves:
-        blocks = run_segment(("pair",), "remap", w[2], [kept[h], sent[h]], unroll=(8, 4)[h])
-        moved = [
-            block if k == 0 else shift_row(block, 0, k >> 1, k & 1)
-            for k, block in enumerate(blocks)
-        ]
-        groups = regroup(moved)
-        got[h] = [groups[0]]
-        for z in range(1, 4):
-            got[h].append(shift_row(groups[z], z, 0, 0))
-    for h in halves:
-        kept[h], out = run_segment(("remap",), "pair", w[3], got[h], unroll=(4, 8)[h])
+        kept[h], out = run_segment(
+            ("remap", ("by_x", "by_z")[h]), "pair", w[3], got[h], unroll=(4, 8)[h]
+        )
         sent[h] = flip(out, "col", 4)
-    (first,) = run_segment(("pair",), "plain", w[4], [kept[0], sent[0]], unroll=4)
-    (out,) = run_segment(("pair",), "low", w[4], [kept[1], sent[1]], [first, low])
+    (share,) = run_segment(("pair", 0), "share", w[4], [kept[0], sent[0]], [low], unroll=4)
+    (out,) = run_segment(("pair", 1), "low", w[4], [kept[1], sent[1]], [share, low])
     return out.reshape(amplitudes.shape)
 
 

time: 163 us -> 159 us (0.975)
  waiting for transfers between devices: 60 us -> 49.5 us
  starting transfers between devices: 66 us -> 75.1 us
  Pallas kernels: 33.1 us -> 31 us
    ppermute x6, waiting for transfers between devices: 25.8 us -> 15.7 us  [flip(): lax.ppermute(value, axis, [(s, s ^ mask) for s in range(lax.axis_size(axi...]
    ppermute x20, starting transfers between devices: 54 us -> 60.1 us  [shift_row(): return lax.ppermute(value, 'row', pairs)]
    ppermute x6, starting transfers between devices: 12 us -> 15 us  [flip(): lax.ppermute(value, axis, [(s, s ^ mask) for s in range(lax.axis_size(axi...]
    pallas_call x5, Pallas kernels: 4.42 us -> 2.25 us  [weights(): pl.pallas_call(functools.partial(weight_kernel, kinds), out_shape=jax.Sha...]
  transfers between devices with their start and end apart: 26 -> 26, of which waited for: 10 -> 11; matrix products, arithmetic and copies ran while one was open for 0% -> 0% of each run, Pallas kernels for 16% -> 15%
where the time goes in v2:
time: 159 us; the launch traced here: 158 us
  starting transfers between devices  75.1 us (47%)
  waiting for transfers between devices  49.5 us (31%)
  Pallas kernels  31 us (19%)
  local copies, waits for them, and re-layouts  2.67 us (2%)
    ppermute x20, starting transfers between devices, shift_row(): return lax.ppermute(value, 'row', pairs)  60.1 us
    ppermute x20, waiting for transfers between devices, shift_row(): return lax.ppermute(value, 'row', pairs)  33.8 us
    pallas_call x10, Pallas kernels, run_segment(): pl.pallas_call(functools.partial(segment_kernel, source, target, len(args...  26.8 us
    ppermute x6, waiting for transfers between devices, flip(): lax.ppermute(value, axis, [(s, s ^ mask) for s in range(lax.axis_size(axi...  15.7 us
    ppermute x6, starting transfers between devices, flip(): lax.ppermute(value, axis, [(s, s ^ mask) for s in range(lax.axis_size(axi...  15 us
  transfers between devices with their start and end apart: 26, of which 11 were waited for; matrix products, arithmetic and copies ran while one was open for 0% of the time, Pallas kernels for 15%

profile of v2, /device:TPU:1, one launch (start us, length us, event | category | flops | bytes accessed | tf_op | source)
XLA Modules:
  0.0 158.5 jit_solution(2033976854660148730)
XLA Ops:
  3.0 2.3 %shard_map.47 = (f32[8,16,8,128]{3,2,1,0:T(8,128)S(1)}, f32[8,16,8,128]{3,2,1,0:T(8,128)S(1)}) custom-call(bf16[3,256,256]{2,1,0:T(8,128)(2,1)S(1)} %shard_map.41.refs_0_, f32[2,2048,128]{2,1,0:T(8,128)S(1)} %bitcast.2), custom_call_target="tpu_custom_call" | custom-call | flops 1207959552 | bytes 3145728 | tf_op jit(solution)/shard_map/pallas_call | solution.py:279
  5.3 3.3 %collective-permute-start.13 = (f32[8,16,8,128]{3,2,1,0:T(8,128)S(1)}, f32[8,16,8,128]{3,2,1,0:T(8,128)S(1)}, u32[]{:S(2)}, u32[]{:S(2)}) collective-permute-start(f32[8,16,8,128]{3,2,1,0:T(8,128)S(1)} %get-tuple-element.60), channel_id=1, source_target_pairs={{0,8},{8,0},{16,24},{24,16},{32,40},{40,32},{48,56},{56,48},{64,72... | collective-permute-start | bytes 1572872 | tf_op jit(solution)/shard_map/ppermute | solution.py:319
  8.6 2.3 %shard_map.42 = (f32[8,16,8,128]{3,2,1,0:T(8,128)S(1)}, f32[8,16,8,128]{3,2,1,0:T(8,128)S(1)}) custom-call(bf16[3,256,256]{2,1,0:T(8,128)(2,1)S(1)} %shard_map.41.refs_0_, f32[2,2048,128]{2,1,0:T(8,128)S(1)} %bitcast.3), custom_call_target="tpu_custom_call" | custom-call | flops 1207959552 | bytes 3145728 | tf_op jit(solution)/shard_map/pallas_call | solution.py:279
  11.4 2.0 %shard_map.48 = (f32[8,16,8,128]{3,2,1,0:T(8,128)S(1)}, f32[8,16,8,128]{3,2,1,0:T(8,128)S(1)}) custom-call(bf16[3,256,256]{2,1,0:T(8,128)(2,1)S(1)} %shard_map.40.refs_0_, f32[8,16,8,128]{3,2,1,0:T(8,128)S(1)} %get-tuple-element.59.refs_1_, f32[8,16,8,128]{3,2,1,0:T(8,128)S(1)} %collective-permute-done.13.refs_2_), custom_call_target="tpu_custom_call" | custom-call | flops 1207959552 | bytes 3145728 | tf_op jit(solution)/shard_map/pallas_call | solution.py:279
  13.4 5.3 %collective-permute-start.14 = (f32[8,16,8,128]{3,2,1,0:T(8,128)S(1)}, f32[8,16,8,128]{3,2,1,0:T(8,128)S(1)}, u32[]{:S(2)}, u32[]{:S(2)}) collective-permute-start(f32[8,16,8,128]{3,2,1,0:T(8,128)S(1)} %get-tuple-element.62), channel_id=1, source_target_pairs={{0,128},{8,136},{16,144},{24,152},{32,160},{40,168},{48,176},{56,1... | collective-permute-start | bytes 1572872 | tf_op jit(solution)/shard_map/ppermute | solution.py:319
  18.7 2.9 %shard_map.43 = (f32[8,16,8,128]{3,2,1,0:T(8,128)S(1)}, f32[8,16,8,128]{3,2,1,0:T(8,128)S(1)}) custom-call(bf16[3,256,256]{2,1,0:T(8,128)(2,1)S(1)} %shard_map.40.refs_0_, f32[8,16,8,128]{3,2,1,0:T(8,128)S(1)} %get-tuple-element.41.refs_1_, f32[8,16,8,128]{3,2,1,0:T(8,128)S(1)} %collective-permute-done.refs_2_), custom_call_target="tpu_custom_call" | custom-call | flops 1207959552 | bytes 3145728 | tf_op jit(solution)/shard_map/pallas_call | solution.py:279
  22.2 10.3 %collective-permute-done.14.refs_2_ = f32[8,16,8,128]{3,2,1,0:T(8,128)S(1)} collective-permute-done((f32[8,16,8,128]{3,2,1,0:T(8,128)S(1)}, f32[8,16,8,128]{3,2,1,0:T(8,128)S(1)}, u32[]{:S(2)}, u32[]{:S(2)}) %collective-permute-start.14) | collective-permute-done | bytes 524320 | tf_op jit(solution)/shard_map/ppermute | solution.py:319
  32.5 2.0 %shard_map.49 = (f32[4,8,8,128]{3,2,1,0:T(8,128)S(1)}, f32[4,8,8,128]{3,2,1,0:T(8,128)S(1)}, f32[4,8,8,128]{3,2,1,0:T(8,128)S(1)}, f32[4,8,8,128]{3,2,1,0:T(8,12...) custom-call(bf16[3,256,256]{2,1,0:T(8,128)(2,1)S(1)} %shard_map.39.r, ...), custom_call_target="tpu_custom_call" | custom-call | flops 1207959552 | bytes 3145728 | tf_op jit(solution)/shard_map/pallas_call | solution.py:279
  34.5 2.7 %collective-permute-start.15 = (f32[4,8,8,128]{3,2,1,0:T(8,128)S(1)}, f32[4,8,8,128]{3,2,1,0:T(8,128)S(1)}, u32[]{:S(2)}, u32[]{:S(2)}) collective-permute-start(f32[4,8,8,128]{3,2,1,0:T(8,128)S(1)} %get-tuple-element.64), channel_id=1, source_target_pairs={{0,8},{8,0},{16,24},{24,16},{32,40},{40,32},{48,56},{56,48},{64,72... | collective-permute-start | bytes 393224 | tf_op jit(solution)/shard_map/ppermute | solution.py:327
  37.2 21.7 %collective-permute-start.16 = (f32[4,8,8,128]{3,2,1,0:T(8,128)S(1)}, f32[4,8,8,128]{3,2,1,0:T(8,128)S(1)}, u32[]{:S(2)}, u32[]{:S(2)}) collective-permute-start(f32[4,8,8,128]{3,2,1,0:T(8,128)S(1)} %get-tuple-element.65), channel_id=1, source_target_pairs={{0,64},{8,72},{16,80},{24,88},{32,96},{40,104},{48,112},{56,120},{... | collective-permute-start | bytes 393224 | tf_op jit(solution)/shard_map/ppermute | solution.py:327
  59.0 4.9 %collective-permute-start.18 = (f32[4,8,8,128]{3,2,1,0:T(8,128)S(1)}, f32[4,8,8,128]{3,2,1,0:T(8,128)S(1)}, u32[]{:S(2)}, u32[]{:S(2)}) collective-permute-start(f32[4,8,8,128]{3,2,1,0:T(8,128)S(1)} %get-tuple-element.67), channel_id=1, source_target_pairs={{0,128},{8,136},{16,144},{24,152},{32,160},{40,168},{48,176},{56,1... | collective-permute-start | bytes 393224 | tf_op jit(solution)/shard_map/ppermute | solution.py:327
  63.9 5.7 %collective-permute-start.19 = (f32[4,8,8,128]{3,2,1,0:T(8,128)S(1)}, f32[4,8,8,128]{3,2,1,0:T(8,128)S(1)}, u32[]{:S(2)}, u32[]{:S(2)}) collective-permute-start(f32[4,8,8,128]{3,2,1,0:T(8,128)S(1)} %get-tuple-element.68), channel_id=1, source_target_pairs={{0,136},{8,128},{16,152},{24,144},{32,168},{40,160},{48,184},{56,1... | collective-permute-start | bytes 393224 | tf_op jit(solution)/shard_map/ppermute | solution.py:327
  69.6 2.0 %shard_map.44 = (f32[4,2,8,8,128]{4,3,2,1,0:T(8,128)S(1)}, f32[4,2,8,8,128]{4,3,2,1,0:T(8,128)S(1)}, f32[4,2,8,8,128]{4,3,2,1,0:T(8,128)S(1)}, f32[4,2,8,8,128]{4,3,2,1,0:T(8,128)S(1)}) custom-call(bf16[3,256,256]{2,1,0:T(8,128)(2,1)S(1)} %shard_map.39.refs_0_, f32[8,16,8,128]{3,2,1,0:T(8,128)S(1)} %get-tuple-element.43.refs_1_, ...), custom_call_target="tpu_custom_call" | custom-call | flops 1207959552 | bytes 3145728 | tf_op jit(solution)/shard_map/pallas_call | solution.py:279
  71.6 2.1 %collective-permute-start.2 = (f32[4,2,8,8,128]{4,3,2,1,0:T(8,128)S(1)}, f32[4,2,8,8,128]{4,3,2,1,0:T(8,128)S(1)}, u32[]{:S(2)}, u32[]{:S(2)}) collective-permute-start(f32[4,2,8,8,128]{4,3,2,1,0:T(8,128)S(1)} %get-tuple-element.46), channel_id=1, source_target_pairs={{0,16},{8,24},{16,32},{24,40},{32,48},{40,56},{48,0},{56,8},{64,80... | collective-permute-start | bytes 786440 | tf_op jit(solution)/shard_map/ppermute | solution.py:327
  76.2 12.5 %collective-permute-done.18.refs_4_ = f32[4,8,8,128]{3,2,1,0:T(8,128)S(1)} collective-permute-done((f32[4,8,8,128]{3,2,1,0:T(8,128)S(1)}, f32[4,8,8,128]{3,2,1,0:T(8,128)S(1)}, u32[]{:S(2)}, u32[]{:S(2)}) %collective-permute-start.18) | collective-permute-done | bytes 131104 | tf_op jit(solution)/shard_map/ppermute | solution.py:327
  88.7 2.6 %collective-permute-start.3 = (f32[4,2,8,8,128]{4,3,2,1,0:T(8,128)S(1)}, f32[4,2,8,8,128]{4,3,2,1,0:T(8,128)S(1)}, u32[]{:S(2)}, u32[]{:S(2)}) collective-permute-start(f32[4,2,8,8,128]{4,3,2,1,0:T(8,128)S(1)} %get-tuple-element.47), channel_id=1, source_target_pairs={{0,32},{8,40},{16,48},{24,56},{32,0},{40,8},{48,16},{56,24},{64,96... | collective-permute-start | bytes 786440 | tf_op jit(solution)/shard_map/ppermute | solution.py:327
  91.5 2.3 %collective-permute-start.4 = (f32[4,2,8,8,128]{4,3,2,1,0:T(8,128)S(1)}, f32[4,2,8,8,128]{4,3,2,1,0:T(8,128)S(1)}, u32[]{:S(2)}, u32[]{:S(2)}) collective-permute-start(f32[4,2,8,8,128]{4,3,2,1,0:T(8,128)S(1)} %get-tuple-element.48), channel_id=1, source_target_pairs={{0,48},{8,56},{16,0},{24,8},{32,16},{40,24},{48,32},{56,40},{64,11... | collective-permute-start | bytes 786440 | tf_op jit(solution)/shard_map/ppermute | solution.py:327
  97.6 5.7 %collective-permute-done.4.refs_3_ = f32[4,2,8,8,128]{4,3,2,1,0:T(8,128)S(1)} collective-permute-done((f32[4,2,8,8,128]{4,3,2,1,0:T(8,128)S(1)}, f32[4,2,8,8,128]{4,3,2,1,0:T(8,128)S(1)}, u32[]{:S(2)}, u32[]{:S(2)}) %collective-permute-start.4) | collective-permute-done | bytes 262176 | tf_op jit(solution)/shard_map/ppermute | solution.py:327
  103.4 2.2 %collective-permute-start.5 = (f32[4,8,8,128]{3,2,1,0:T(8,128)S(1)}, f32[4,8,8,128]{3,2,1,0:T(8,128)S(1)}, u32[]{:S(2)}, u32[]{:S(2)}) collective-permute-start(f32[4,8,8,128]{3,2,1,0:T(8,128)S(1)} %get-tuple-element.50), channel_id=1, source_target_pairs={{0,8},{8,0},{16,24},{24,16},{32,40},{40,32},{48,56},{56,48},{64,72... | collective-permute-start | bytes 393224 | tf_op jit(solution)/shard_map/ppermute | solution.py:327
  108.9 2.7 %collective-permute-start.8 = (f32[4,8,8,128]{3,2,1,0:T(8,128)S(1)}, f32[4,8,8,128]{3,2,1,0:T(8,128)S(1)}, u32[]{:S(2)}, u32[]{:S(2)}) collective-permute-start(f32[4,8,8,128]{3,2,1,0:T(8,128)S(1)} %get-tuple-element.53), channel_id=1, source_target_pairs={{0,128},{8,136},{16,144},{24,152},{32,160},{40,168},{48,176},{56,1... | collective-permute-start | bytes 393224 | tf_op jit(solution)/shard_map/ppermute | solution.py:327
  111.5 2.9 %collective-permute-done.24.refs_4_ = f32[4,2,8,8,128]{4,3,2,1,0:T(8,128)S(1)} collective-permute-done((f32[4,2,8,8,128]{4,3,2,1,0:T(8,128)S(1)}, f32[4,2,8,8,128]{4,3,2,1,0:T(8,128)S(1)}, u32[]{:S(2)}, u32[]{:S(2)}) %collective-permute-start.24) | collective-permute-done | bytes 262176 | tf_op jit(solution)/shard_map/ppermute | solution.py:327
  114.5 1.9 %collective-permute-start.9 = (f32[4,8,8,128]{3,2,1,0:T(8,128)S(1)}, f32[4,8,8,128]{3,2,1,0:T(8,128)S(1)}, u32[]{:S(2)}, u32[]{:S(2)}) collective-permute-start(f32[4,8,8,128]{3,2,1,0:T(8,128)S(1)} %get-tuple-element.54), channel_id=1, source_target_pairs={{0,136},{8,128},{16,152},{24,144},{32,168},{40,160},{48,184},{56,1... | collective-permute-start | bytes 393224 | tf_op jit(solution)/shard_map/ppermute | solution.py:327
  116.4 4.3 %collective-permute-start.11 = (f32[4,8,8,128]{3,2,1,0:T(8,128)S(1)}, f32[4,8,8,128]{3,2,1,0:T(8,128)S(1)}, u32[]{:S(2)}, u32[]{:S(2)}) collective-permute-start(f32[4,8,8,128]{3,2,1,0:T(8,128)S(1)} %get-tuple-element.56), channel_id=1, source_target_pairs={{0,200},{8,192},{16,216},{24,208},{32,232},{40,224},{48,248},{56,2... | collective-permute-start | bytes 393224 | tf_op jit(solution)/shard_map/ppermute | solution.py:327
  121.6 2.9 %shard_map.51 = (f32[8,16,8,128]{3,2,1,0:T(8,128)S(1)}, f32[8,16,8,128]{3,2,1,0:T(8,128)S(1)}) custom-call(bf16[3,256,256]{2,1,0:T(8,128)(2,1)S(1)} %shard_map.38.refs_0_, f32[4,2,8,8,128]{4,3,2,1,0:T(8,128)S(1)} %get-tuple-element.71.refs_1_, f32[4,2,8,8,128]{4,3,2,1,0:T(8,128)S(1)} %collective-permute-done.22.refs_2_, ...), custom_call_target="tpu_custom_call" | custom-call | flops 1207959552 | bytes 3145728 | tf_op jit(solution)/shard_map/pallas_call | solution.py:279
  124.5 3.0 %collective-permute-start.25 = (f32[8,16,8,128]{3,2,1,0:T(8,128)S(1)}, f32[8,16,8,128]{3,2,1,0:T(8,128)S(1)}, u32[]{:S(2)}, u32[]{:S(2)}) collective-permute-start(f32[8,16,8,128]{3,2,1,0:T(8,128)S(1)} %get-tuple-element.76), channel_id=1, source_target_pairs={{0,4},{1,5},{2,6},{3,7},{4,0},{5,1},{6,2},{7,3},{8,12},{9,13},{10,... | collective-permute-start | bytes 1572872 | tf_op jit(solution)/shard_map/ppermute | solution.py:319
  128.9 5.7 %collective-permute-done.10.refs_7_ = f32[4,8,8,128]{3,2,1,0:T(8,128)S(1)} collective-permute-done((f32[4,8,8,128]{3,2,1,0:T(8,128)S(1)}, f32[4,8,8,128]{3,2,1,0:T(8,128)S(1)}, u32[]{:S(2)}, u32[]{:S(2)}) %collective-permute-start.10) | collective-permute-done | bytes 131104 | tf_op jit(solution)/shard_map/ppermute | solution.py:327
  134.6 2.8 %collective-permute-done.11.refs_8_ = f32[4,8,8,128]{3,2,1,0:T(8,128)S(1)} collective-permute-done((f32[4,8,8,128]{3,2,1,0:T(8,128)S(1)}, f32[4,8,8,128]{3,2,1,0:T(8,128)S(1)}, u32[]{:S(2)}, u32[]{:S(2)}) %collective-permute-start.11) | collective-permute-done | bytes 131104 | tf_op jit(solution)/shard_map/ppermute | solution.py:327
  137.4 2.0 %shard_map.46 = (f32[8,16,8,128]{3,2,1,0:T(8,128)S(1)}, f32[8,16,8,128]{3,2,1,0:T(8,128)S(1)}) custom-call(bf16[3,256,256]{2,1,0:T(8,128)(2,1)S(1)} %shard_map.38.refs_0_, f32[4,8,8,128]{3,2,1,0:T(8,128)S(1)} %get-tuple-element.49.refs_1_, f32[4,8,8,128]{3,2,1,0:T(8,128)S(1)} %collective-permute-done.5.refs_2_, ...), custom_call_target="tpu_custom_call" | custom-call | flops 1207959552 | bytes 3145728 | tf_op jit(solution)/shard_map/pallas_call | solution.py:279
  139.4 3.0 %collective-permute-start.12 = (f32[8,16,8,128]{3,2,1,0:T(8,128)S(1)}, f32[8,16,8,128]{3,2,1,0:T(8,128)S(1)}, u32[]{:S(2)}, u32[]{:S(2)}) collective-permute-start(f32[8,16,8,128]{3,2,1,0:T(8,128)S(1)} %get-tuple-element.58), channel_id=1, source_target_pairs={{0,4},{1,5},{2,6},{3,7},{4,0},{5,1},{6,2},{7,3},{8,12},{9,13},{10,... | collective-permute-start | bytes 1572872 | tf_op jit(solution)/shard_map/ppermute | solution.py:319
  144.6 4.1 %shard_map.52.refs_3_ = f32[4,512,256]{2,1,0:T(8,128)S(1)} custom-call(bf16[3,256,256]{2,1,0:T(8,128)(2,1)S(1)} %shard_map.37.refs_0_, f32[8,16,8,128]{3,2,1,0:T(8,128)S(1)} %get-tuple-element.75.refs_1_, f32[8,16,8,128]{3,2,1,0:T(8,128)S(1)} %collective-permute-done.25.refs_2_, bf16[2,2,256,256]{3,2,1,0:T(8,128)(2,1)S(1)} %low_weights.1.refs_3_.refs_4_), custom_call_target="tpu_custom_call" | custom-call | flops 1207959552 | bytes 3145728 | tf_op jit(solution)/shard_map/pallas_call | solution.py:279
  148.7 5.3 %collective-permute-done.12.refs_2_ = f32[8,16,8,128]{3,2,1,0:T(8,128)S(1)} collective-permute-done((f32[8,16,8,128]{3,2,1,0:T(8,128)S(1)}, f32[8,16,8,128]{3,2,1,0:T(8,128)S(1)}, u32[]{:S(2)}, u32[]{:S(2)}) %collective-permute-start.12) | collective-permute-done | bytes 524320 | tf_op jit(solution)/shard_map/ppermute | solution.py:319
  154.1 4.4 %shard_map.53 = f32[2,2048,128]{2,1,0:T(8,128)} custom-call(bf16[3,256,256]{2,1,0:T(8,128)(2,1)S(1)} %shard_map.37.refs_0_, f32[8,16,8,128]{3,2,1,0:T(8,128)S(1)} %get-tuple-element.57.refs_1_, f32[8,16,8,128]{3,2,1,0:T(8,128)S(1)} %collective-permute-done.12.refs_2_, f32[4,512,256]{2,1,0:T(8,128)S(1)} %shard_map.52.refs_3_, ...), custom_call_target="tpu_custom_call" | custom-call | flops 1207959552 | bytes 3145728 | tf_op jit(solution)/shard_map/pallas_call | solution.py:279
  (45 shorter events, 18.4 us)
Async XLA Ops:
  1.4 1.6 %copy-start.2 = (f32[2,1,1,262144]{3,2,1,0:T(1,128)S(1)}, f32[2,1,1,262144]{3,2,1,0:T(1,128)}, u32[]{:S(2)}) copy-start(f32[2,1,1,262144]{3,2,1,0:T(1,128)} %param.3) | copy-start | bytes 6291460
  5.3 5.7 %copy-start = (f32[5,4,2,128,128]{4,3,2,1,0:T(8,128)S(1)}, f32[5,4,2,128,128]{4,3,2,1,0:T(8,128)}, u32[]{:S(2)}) copy-start(f32[5,4,2,128,128]{4,3,2,1,0:T(8,128)} %gates_ref.1) | copy-start | bytes 7864324
  5.3 6.1 %collective-permute-start.13 = (f32[8,16,8,128]{3,2,1,0:T(8,128)S(1)}, f32[8,16,8,128]{3,2,1,0:T(8,128)S(1)}, u32[]{:S(2)}, u32[]{:S(2)}) collective-permute-start(f32[8,16,8,128]{3,2,1,0:T(8,128)S(1)} %get-tuple-element.60), channel_id=1, source_target_pairs={{0,8},{8,0},{16,24},{24,16},{32,40},{40,32},{48,56},{56,48},{64,72... | collective-permute-start | bytes 1572872 | tf_op jit(solution)/shard_map/ppermute | solution.py:319
  11.0 7.7 %collective-permute-start = (f32[8,16,8,128]{3,2,1,0:T(8,128)S(1)}, f32[8,16,8,128]{3,2,1,0:T(8,128)S(1)}, u32[]{:S(2)}, u32[]{:S(2)}) collective-permute-start(f32[8,16,8,128]{3,2,1,0:T(8,128)S(1)} %get-tuple-element.42), channel_id=1, source_target_pairs={{0,8},{8,0},{16,24},{24,16},{32,40},{40,32},{48,56},{56,48},{64,72... | collective-permute-start | bytes 1572872 | tf_op jit(solution)/shard_map/ppermute | solution.py:319
  13.4 19.1 %collective-permute-start.14 = (f32[8,16,8,128]{3,2,1,0:T(8,128)S(1)}, f32[8,16,8,128]{3,2,1,0:T(8,128)S(1)}, u32[]{:S(2)}, u32[]{:S(2)}) collective-permute-start(f32[8,16,8,128]{3,2,1,0:T(8,128)S(1)} %get-tuple-element.62), channel_id=1, source_target_pairs={{0,128},{8,136},{16,144},{24,152},{32,160},{40,168},{48,176},{56,1... | collective-permute-start | bytes 1572872 | tf_op jit(solution)/shard_map/ppermute | solution.py:319
  21.6 42.4 %collective-permute-start.1 = (f32[8,16,8,128]{3,2,1,0:T(8,128)S(1)}, f32[8,16,8,128]{3,2,1,0:T(8,128)S(1)}, u32[]{:S(2)}, u32[]{:S(2)}) collective-permute-start(f32[8,16,8,128]{3,2,1,0:T(8,128)S(1)} %get-tuple-element.44), channel_id=1, source_target_pairs={{0,128},{8,136},{16,144},{24,152},{32,160},{40,168},{48,176},{56,1... | collective-permute-start | bytes 1572872 | tf_op jit(solution)/shard_map/ppermute | solution.py:319
  34.5 37.1 %collective-permute-start.15 = (f32[4,8,8,128]{3,2,1,0:T(8,128)S(1)}, f32[4,8,8,128]{3,2,1,0:T(8,128)S(1)}, u32[]{:S(2)}, u32[]{:S(2)}) collective-permute-start(f32[4,8,8,128]{3,2,1,0:T(8,128)S(1)} %get-tuple-element.64), channel_id=1, source_target_pairs={{0,8},{8,0},{16,24},{24,16},{32,40},{40,32},{48,56},{56,48},{64,72... | collective-permute-start | bytes 393224 | tf_op jit(solution)/shard_map/ppermute | solution.py:327
  37.2 36.5 %collective-permute-start.16 = (f32[4,8,8,128]{3,2,1,0:T(8,128)S(1)}, f32[4,8,8,128]{3,2,1,0:T(8,128)S(1)}, u32[]{:S(2)}, u32[]{:S(2)}) collective-permute-start(f32[4,8,8,128]{3,2,1,0:T(8,128)S(1)} %get-tuple-element.65), channel_id=1, source_target_pairs={{0,64},{8,72},{16,80},{24,88},{32,96},{40,104},{48,112},{56,120},{... | collective-permute-start | bytes 393224 | tf_op jit(solution)/shard_map/ppermute | solution.py:327
  58.9 15.4 %collective-permute-start.17 = (f32[4,8,8,128]{3,2,1,0:T(8,128)S(1)}, f32[4,8,8,128]{3,2,1,0:T(8,128)S(1)}, u32[]{:S(2)}, u32[]{:S(2)}) collective-permute-start(f32[4,8,8,128]{3,2,1,0:T(8,128)S(1)} %get-tuple-element.66), channel_id=1, source_target_pairs={{0,72},{8,64},{16,88},{24,80},{32,104},{40,96},{48,120},{56,112},{... | collective-permute-start | bytes 393224 | tf_op jit(solution)/shard_map/ppermute | solution.py:327
  59.0 29.7 %collective-permute-start.18 = (f32[4,8,8,128]{3,2,1,0:T(8,128)S(1)}, f32[4,8,8,128]{3,2,1,0:T(8,128)S(1)}, u32[]{:S(2)}, u32[]{:S(2)}) collective-permute-start(f32[4,8,8,128]{3,2,1,0:T(8,128)S(1)} %get-tuple-element.67), channel_id=1, source_target_pairs={{0,128},{8,136},{16,144},{24,152},{32,160},{40,168},{48,176},{56,1... | collective-permute-start | bytes 393224 | tf_op jit(solution)/shard_map/ppermute | solution.py:327
  63.9 27.6 %collective-permute-start.19 = (f32[4,8,8,128]{3,2,1,0:T(8,128)S(1)}, f32[4,8,8,128]{3,2,1,0:T(8,128)S(1)}, u32[]{:S(2)}, u32[]{:S(2)}) collective-permute-start(f32[4,8,8,128]{3,2,1,0:T(8,128)S(1)} %get-tuple-element.68), channel_id=1, source_target_pairs={{0,136},{8,128},{16,152},{24,144},{32,168},{40,160},{48,184},{56,1... | collective-permute-start | bytes 393224 | tf_op jit(solution)/shard_map/ppermute | solution.py:327
  71.6 49.1 %copy-start.1 = (s32[32]{0:T(128)S(1)}, s32[32]{0:T(128)}, u32[]{:S(2)}) copy-start(s32[32]{0:T(128)} %refs_0_.5) | copy-start | bytes 388
  71.6 24.1 %collective-permute-start.2 = (f32[4,2,8,8,128]{4,3,2,1,0:T(8,128)S(1)}, f32[4,2,8,8,128]{4,3,2,1,0:T(8,128)S(1)}, u32[]{:S(2)}, u32[]{:S(2)}) collective-permute-start(f32[4,2,8,8,128]{4,3,2,1,0:T(8,128)S(1)} %get-tuple-element.46), channel_id=1, source_target_pairs={{0,16},{8,24},{16,32},{24,40},{32,48},{40,56},{48,0},{56,8},{64,80... | collective-permute-start | bytes 786440 | tf_op jit(solution)/shard_map/ppermute | solution.py:327
  73.7 20.1 %collective-permute-start.20 = (f32[4,8,8,128]{3,2,1,0:T(8,128)S(1)}, f32[4,8,8,128]{3,2,1,0:T(8,128)S(1)}, u32[]{:S(2)}, u32[]{:S(2)}) collective-permute-start(f32[4,8,8,128]{3,2,1,0:T(8,128)S(1)} %get-tuple-element.69), channel_id=1, source_target_pairs={{0,192},{8,200},{16,208},{24,216},{32,224},{40,232},{48,240},{56,2... | collective-permute-start | bytes 393224 | tf_op jit(solution)/shard_map/ppermute | solution.py:327
  74.3 19.5 %collective-permute-start.21 = (f32[4,8,8,128]{3,2,1,0:T(8,128)S(1)}, f32[4,8,8,128]{3,2,1,0:T(8,128)S(1)}, u32[]{:S(2)}, u32[]{:S(2)}) collective-permute-start(f32[4,8,8,128]{3,2,1,0:T(8,128)S(1)} %get-tuple-element.70), channel_id=1, source_target_pairs={{0,200},{8,192},{16,216},{24,208},{32,232},{40,224},{48,248},{56,2... | collective-permute-start | bytes 393224 | tf_op jit(solution)/shard_map/ppermute | solution.py:327
  88.7 8.9 %collective-permute-start.3 = (f32[4,2,8,8,128]{4,3,2,1,0:T(8,128)S(1)}, f32[4,2,8,8,128]{4,3,2,1,0:T(8,128)S(1)}, u32[]{:S(2)}, u32[]{:S(2)}) collective-permute-start(f32[4,2,8,8,128]{4,3,2,1,0:T(8,128)S(1)} %get-tuple-element.47), channel_id=1, source_target_pairs={{0,32},{8,40},{16,48},{24,56},{32,0},{40,8},{48,16},{56,24},{64,96... | collective-permute-start | bytes 786440 | tf_op jit(solution)/shard_map/ppermute | solution.py:327
  91.5 11.8 %collective-permute-start.4 = (f32[4,2,8,8,128]{4,3,2,1,0:T(8,128)S(1)}, f32[4,2,8,8,128]{4,3,2,1,0:T(8,128)S(1)}, u32[]{:S(2)}, u32[]{:S(2)}) collective-permute-start(f32[4,2,8,8,128]{4,3,2,1,0:T(8,128)S(1)} %get-tuple-element.48), channel_id=1, source_target_pairs={{0,48},{8,56},{16,0},{24,8},{32,16},{40,24},{48,32},{56,40},{64,11... | collective-permute-start | bytes 786440 | tf_op jit(solution)/shard_map/ppermute | solution.py:327
  93.9 11.7 %collective-permute-start.22 = (f32[4,2,8,8,128]{4,3,2,1,0:T(8,128)S(1)}, f32[4,2,8,8,128]{4,3,2,1,0:T(8,128)S(1)}, u32[]{:S(2)}, u32[]{:S(2)}) collective-permute-start(f32[4,2,8,8,128]{4,3,2,1,0:T(8,128)S(1)} %get-tuple-element.72), channel_id=1, source_target_pairs={{0,16},{8,24},{16,32},{24,40},{32,48},{40,56},{48,0},{56,8},{64,80... | collective-permute-start | bytes 786440 | tf_op jit(solution)/shard_map/ppermute | solution.py:327
  94.0 14.9 %collective-permute-start.23 = (f32[4,2,8,8,128]{4,3,2,1,0:T(8,128)S(1)}, f32[4,2,8,8,128]{4,3,2,1,0:T(8,128)S(1)}, u32[]{:S(2)}, u32[]{:S(2)}) collective-permute-start(f32[4,2,8,8,128]{4,3,2,1,0:T(8,128)S(1)} %get-tuple-element.73), channel_id=1, source_target_pairs={{0,32},{8,40},{16,48},{24,56},{32,0},{40,8},{48,16},{56,24},{64,96... | collective-permute-start | bytes 786440 | tf_op jit(solution)/shard_map/ppermute | solution.py:327
  95.7 18.7 %collective-permute-start.24 = (f32[4,2,8,8,128]{4,3,2,1,0:T(8,128)S(1)}, f32[4,2,8,8,128]{4,3,2,1,0:T(8,128)S(1)}, u32[]{:S(2)}, u32[]{:S(2)}) collective-permute-start(f32[4,2,8,8,128]{4,3,2,1,0:T(8,128)S(1)} %get-tuple-element.74), channel_id=1, source_target_pairs={{0,48},{8,56},{16,0},{24,8},{32,16},{40,24},{48,32},{56,40},{64,11... | collective-permute-start | bytes 786440 | tf_op jit(solution)/shard_map/ppermute | solution.py:327
  103.4 13.0 %collective-permute-start.5 = (f32[4,8,8,128]{3,2,1,0:T(8,128)S(1)}, f32[4,8,8,128]{3,2,1,0:T(8,128)S(1)}, u32[]{:S(2)}, u32[]{:S(2)}) collective-permute-start(f32[4,8,8,128]{3,2,1,0:T(8,128)S(1)} %get-tuple-element.50), channel_id=1, source_target_pairs={{0,8},{8,0},{16,24},{24,16},{32,40},{40,32},{48,56},{56,48},{64,72... | collective-permute-start | bytes 393224 | tf_op jit(solution)/shard_map/ppermute | solution.py:327
  105.6 10.8 %collective-permute-start.6 = (f32[4,8,8,128]{3,2,1,0:T(8,128)S(1)}, f32[4,8,8,128]{3,2,1,0:T(8,128)S(1)}, u32[]{:S(2)}, u32[]{:S(2)}) collective-permute-start(f32[4,8,8,128]{3,2,1,0:T(8,128)S(1)} %get-tuple-element.51), channel_id=1, source_target_pairs={{0,64},{8,72},{16,80},{24,88},{32,96},{40,104},{48,112},{56,120},{... | collective-permute-start | bytes 393224 | tf_op jit(solution)/shard_map/ppermute | solution.py:327
  105.6 18.9 %collective-permute-start.7 = (f32[4,8,8,128]{3,2,1,0:T(8,128)S(1)}, f32[4,8,8,128]{3,2,1,0:T(8,128)S(1)}, u32[]{:S(2)}, u32[]{:S(2)}) collective-permute-start(f32[4,8,8,128]{3,2,1,0:T(8,128)S(1)} %get-tuple-element.52), channel_id=1, source_target_pairs={{0,72},{8,64},{16,88},{24,80},{32,104},{40,96},{48,120},{56,112},{... | collective-permute-start | bytes 393224 | tf_op jit(solution)/shard_map/ppermute | solution.py:327
  108.9 18.6 %collective-permute-start.8 = (f32[4,8,8,128]{3,2,1,0:T(8,128)S(1)}, f32[4,8,8,128]{3,2,1,0:T(8,128)S(1)}, u32[]{:S(2)}, u32[]{:S(2)}) collective-permute-start(f32[4,8,8,128]{3,2,1,0:T(8,128)S(1)} %get-tuple-element.53), channel_id=1, source_target_pairs={{0,128},{8,136},{16,144},{24,152},{32,160},{40,168},{48,176},{56,1... | collective-permute-start | bytes 393224 | tf_op jit(solution)/shard_map/ppermute | solution.py:327
  114.5 14.4 %collective-permute-start.9 = (f32[4,8,8,128]{3,2,1,0:T(8,128)S(1)}, f32[4,8,8,128]{3,2,1,0:T(8,128)S(1)}, u32[]{:S(2)}, u32[]{:S(2)}) collective-permute-start(f32[4,8,8,128]{3,2,1,0:T(8,128)S(1)} %get-tuple-element.54), channel_id=1, source_target_pairs={{0,136},{8,128},{16,152},{24,144},{32,168},{40,160},{48,184},{56,1... | collective-permute-start | bytes 393224 | tf_op jit(solution)/shard_map/ppermute | solution.py:327
  116.4 18.2 %collective-permute-start.10 = (f32[4,8,8,128]{3,2,1,0:T(8,128)S(1)}, f32[4,8,8,128]{3,2,1,0:T(8,128)S(1)}, u32[]{:S(2)}, u32[]{:S(2)}) collective-permute-start(f32[4,8,8,128]{3,2,1,0:T(8,128)S(1)} %get-tuple-element.55), channel_id=1, source_target_pairs={{0,192},{8,200},{16,208},{24,216},{32,224},{40,232},{48,240},{56,2... | collective-permute-start | bytes 393224 | tf_op jit(solution)/shard_map/ppermute | solution.py:327
  116.4 21.0 %collective-permute-start.11 = (f32[4,8,8,128]{3,2,1,0:T(8,128)S(1)}, f32[4,8,8,128]{3,2,1,0:T(8,128)S(1)}, u32[]{:S(2)}, u32[]{:S(2)}) collective-permute-start(f32[4,8,8,128]{3,2,1,0:T(8,128)S(1)} %get-tuple-element.56), channel_id=1, source_target_pairs={{0,200},{8,192},{16,216},{24,208},{32,232},{40,224},{48,248},{56,2... | collective-permute-start | bytes 393224 | tf_op jit(solution)/shard_map/ppermute | solution.py:327
  124.5 20.1 %collective-permute-start.25 = (f32[8,16,8,128]{3,2,1,0:T(8,128)S(1)}, f32[8,16,8,128]{3,2,1,0:T(8,128)S(1)}, u32[]{:S(2)}, u32[]{:S(2)}) collective-permute-start(f32[8,16,8,128]{3,2,1,0:T(8,128)S(1)} %get-tuple-element.76), channel_id=1, source_target_pairs={{0,4},{1,5},{2,6},{3,7},{4,0},{5,1},{6,2},{7,3},{8,12},{9,13},{10,... | collective-permute-start | bytes 1572872 | tf_op jit(solution)/shard_map/ppermute | solution.py:319
  139.4 14.7 %collective-permute-start.12 = (f32[8,16,8,128]{3,2,1,0:T(8,128)S(1)}, f32[8,16,8,128]{3,2,1,0:T(8,128)S(1)}, u32[]{:S(2)}, u32[]{:S(2)}) collective-permute-start(f32[8,16,8,128]{3,2,1,0:T(8,128)S(1)} %get-tuple-element.58), channel_id=1, source_target_pairs={{0,4},{1,5},{2,6},{3,7},{4,0},{5,1},{6,2},{7,3},{8,12},{9,13},{10,... | collective-permute-start | bytes 1572872 | tf_op jit(solution)/shard_map/ppermute | solution.py:319

commit v3 on v2

--- a/solution.py
+++ b/solution.py
@@ -49,9 +49,9 @@
     return jnp.where(want == old, 1.0, 0.0).astype(BF16)
 
 
-def weight_kernel(kinds, *refs):
-    perm_ref = refs[0] if len(refs) == 3 else None
-    gates_ref, out_ref = refs[-2:]
+def weight_kernel(kinds, n_prefetch, *refs):
+    perm_ref = refs[0] if n_prefetch else None
+    gates_ref, out_ref = refs[n_prefetch], refs[-1]
     made = {}
     for number, (rows, cols) in enumerate(kinds):
         for kind in (rows, cols):
@@ -84,7 +84,7 @@
     if seg == 0:
         block, gate_matrices = 0, gate_matrices[:1]
     return pl.pallas_call(
-        functools.partial(weight_kernel, kinds),
+        functools.partial(weight_kernel, kinds, len(prefetch)),
         out_shape=jax.ShapeDtypeStruct((3, 256, 256), BF16),
         grid_spec=pltpu.PrefetchScalarGridSpec(
             num_scalar_prefetch=len(prefetch),
@@ -188,9 +188,8 @@
     def load_remap(i):
         def half(c):
             if source[1] == "by_x":
-                blocks = [ins[x][z, c, i] for z in range(4) for x in range(4)]
-                return jnp.stack(blocks, axis=0)
-            return jnp.concatenate([ins[2 * z + c][:, i] for z in range(4)], axis=0)
+                return jnp.stack([ins[x][c, z, i] for z in range(4) for x in range(4)], axis=0)
+            return jnp.concatenate([ins[z][c, :, i] for z in range(4)], axis=0)
 
         near, far = half(0), half(1)
         even = jnp.where(upper, pltpu.roll(far, 4, 1), near)
@@ -223,18 +222,10 @@
             for p, piece in zip((2 * i, 2 * i + 1), pieces):
                 outs[0][:, p] = piece[:HALF].reshape(8, 8, GD)
                 outs[1][:, p] = piece[HALF:].reshape(8, 8, GD)
-        elif target in ("by_x", "by_z"):
+        elif target == "remap":
             even, odd = (piece.reshape(16, 8, GD) for piece in pieces)
-            near = jnp.where(upper, pltpu.roll(odd, 4, 1), even)
-            far = jnp.where(upper, odd, pltpu.roll(even, 4, 1))
-            for x in range(4):
-                if target == "by_x":
-                    outs[x][:, 0, i] = near[4 * x : 4 * x + 4]
-                    outs[x][:, 1, i] = far[4 * x : 4 * x + 4]
-                    continue
-                for z in range(4):
-                    outs[2 * z][x, i] = near[4 * x + z]
-                    outs[2 * z + 1][x, i] = far[4 * x + z]
+            outs[0][:, i] = jnp.where(upper, pltpu.roll(odd, 4, 1), even)
+            outs[1][:, i] = jnp.where(upper, odd, pltpu.roll(even, 4, 1))
         else:
             for p, piece in zip((2 * i, 2 * i + 1), pieces):
                 one[:, p] = piece.reshape(16, 8, GD)
@@ -266,10 +257,8 @@
 def run_segment(source, target, w, ins, extra=(), unroll=8):
     if target == "pair":
         out_shape = [jax.ShapeDtypeStruct(PART, F32)] * 2
-    elif target == "by_x":
-        out_shape = [jax.ShapeDtypeStruct((4, 2, 8, 8, 128), F32)] * 4
-    elif target == "by_z":
-        out_shape = [jax.ShapeDtypeStruct((4, 8, 8, 128), F32)] * 8
+    elif target == "remap":
+        out_shape = [jax.ShapeDtypeStruct((16, 8, 8, 128), F32)] * 2
     elif target == "share":
         out_shape = [jax.ShapeDtypeStruct((4, 512, 256), F32)]
     else:
@@ -289,27 +278,24 @@
     )(w, *args)
 
 
-def regroup_kernel(target, *refs):
-    by_z, by_x = (refs[:8], refs[8:]) if target == "by_x" else (refs[4:], refs[:4])
-    for z in range(4):
-        for x in range(4):
+def regroup_kernel(order, *refs):
+    ins, outs = refs[:-4], refs[-4:]
+    for j in range(4):
+        for k in range(4):
             for c in range(2):
-                if target == "by_x":
-                    by_x[x][z, c] = by_z[2 * z + c][x]
+                if order == "swap":
+                    outs[j][c, k] = ins[k][c, j]
                 else:
-                    by_z[2 * z + c][x] = by_x[x][z, c]
-
-
-def regroup(target, blocks):
+                    outs[j][c, k] = ins[c][4 * j + k if order == "by_x" else 4 * k + j]
+
+
+def regroup(order, blocks):
     vmem = pl.BlockSpec(memory_space=pltpu.VMEM)
-    by_x = [jax.ShapeDtypeStruct((4, 2, 8, 8, 128), F32)] * 4
-    by_z = [jax.ShapeDtypeStruct((4, 8, 8, 128), F32)] * 8
-    out_shape = by_x if target == "by_x" else by_z
     return pl.pallas_call(
-        functools.partial(regroup_kernel, target),
-        out_shape=out_shape,
+        functools.partial(regroup_kernel, order),
+        out_shape=[jax.ShapeDtypeStruct((2, 4, 8, 8, 128), F32)] * 4,
         in_specs=[vmem] * len(blocks),
-        out_specs=[vmem] * len(out_shape),
+        out_specs=[vmem] * 4,
         cost_estimate=pl.CostEstimate(flops=0, bytes_accessed=2 << 20, transcendentals=0),
         compiler_params=pltpu.CompilerParams(vmem_limit_bytes=LIMIT),
     )(*blocks)
@@ -336,8 +322,8 @@
 
 def shift_z(blocks):
     moved = [blocks[0]]
-    for k in range(1, 8):
-        moved.append(shift_row(blocks[k], k >> 1, 0, k & 1))
+    for z in range(1, 4):
+        moved.append(shift_row(blocks[z], z, 0, 0))
     return moved
 
 
@@ -362,17 +348,20 @@
         kept[h], out = run_segment(("start", h), "pair", w[0], [state])
         sent[h] = flip(out, "row", 1)
     for h in halves:
-        kept[h], out = run_segment(("pair",), "pair", w[1], [kept[h], sent[h]], unroll=(8, 4)[h])
+        kept[h], out = run_segment(("pair",), "pair", w[1], [kept[h], sent[h]])
         sent[h] = flip(out, "row", 16)
     got = {}
-    blocks = run_segment(("pair",), "by_z", w[2], [kept[0], sent[0]])
-    got[0] = shift_x(regroup("by_x", shift_z(blocks)))
-    blocks = run_segment(("pair",), "by_x", w[2], [kept[1], sent[1]])
-    got[1] = shift_z(regroup("by_z", shift_x(blocks)))
     for h in halves:
-        kept[h], out = run_segment(
-            ("remap", ("by_x", "by_z")[h]), "pair", w[3], got[h], unroll=(4, 8)[h]
-        )
+        near, far = run_segment(("pair",), "remap", w[2], [kept[h], sent[h]])
+        pair = [near, flip(far, "row", 1)]
+        if h == 0:
+            moved = shift_z(regroup("by_z", pair))
+            got[h] = shift_x(regroup("swap", moved))
+        else:
+            moved = shift_x(regroup("by_x", pair))
+            got[h] = shift_z(regroup("swap", moved))
+    for h in halves:
+        kept[h], out = run_segment(("remap", ("by_x", "by_z")[h]), "pair", w[3], got[h])
         sent[h] = flip(out, "col", 4)
     (share,) = run_segment(("pair", 0), "share", w[4], [kept[0], sent[0]], [low], unroll=4)
     (out,) = run_segment(("pair", 1), "low", w[4], [kept[1], sent[1]], [share, low])

time: 159 us -> 150 us (0.943)
  the two profiles are of different devices: /device:TPU:1 before, /device:TPU:32 now
where the time goes in v3:
time: 150 us
  waiting for transfers between devices  63 us (42%)
  starting transfers between devices  54.9 us (37%)
  Pallas kernels  29.3 us (20%)
  local copies, waits for them, and re-layouts  2.67 us (2%)
    ppermute x8, waiting for transfers between devices, flip(): lax.ppermute(value, axis, [(s, s ^ mask) for s in range(lax.axis_size(axi...  45.4 us
    ppermute x12, starting transfers between devices, shift_row(): return lax.ppermute(value, 'row', pairs)  41.1 us
    pallas_call x10, Pallas kernels, run_segment(): pl.pallas_call(functools.partial(segment_kernel, source, target, len(args...  25 us
    ppermute x12, waiting for transfers between devices, shift_row(): return lax.ppermute(value, 'row', pairs)  17.6 us
    ppermute x8, starting transfers between devices, flip(): lax.ppermute(value, axis, [(s, s ^ mask) for s in range(lax.axis_size(axi...  13.8 us
  transfers between devices with their start and end apart: 20, of which 9 were waited for; matrix products, arithmetic and copies ran while one was open for 0% of the time, Pallas kernels for 15%

profile of v3, /device:TPU:32, one launch (start us, length us, event | category | flops | bytes accessed | tf_op | source)
XLA Modules:
  0.0 150.1 jit_solution(5187372699691837909)
XLA Ops:
  1.4 1.6 %copy-done.2 = f32[2,1,1,262144]{3,2,1,0:T(1,128)S(1)} copy-done((f32[2,1,1,262144]{3,2,1,0:T(1,128)S(1)}, f32[2,1,1,262144]{3,2,1,0:T(1,128)}, u32[]{:S(2)}) %copy-start.2) | copy-done | bytes 2097176
  3.0 2.3 %shard_map.48 = (f32[8,16,8,128]{3,2,1,0:T(8,128)S(1)}, f32[8,16,8,128]{3,2,1,0:T(8,128)S(1)}) custom-call(bf16[3,256,256]{2,1,0:T(8,128)(2,1)S(1)} %shard_map.41.refs_0_, f32[2,2048,128]{2,1,0:T(8,128)S(1)} %bitcast.2), custom_call_target="tpu_custom_call" | custom-call | flops 1207959552 | bytes 3145728 | tf_op jit(solution)/shard_map/pallas_call | solution.py:268
  5.4 2.3 %shard_map.42 = (f32[8,16,8,128]{3,2,1,0:T(8,128)S(1)}, f32[8,16,8,128]{3,2,1,0:T(8,128)S(1)}) custom-call(bf16[3,256,256]{2,1,0:T(8,128)(2,1)S(1)} %shard_map.41.refs_0_, f32[2,2048,128]{2,1,0:T(8,128)S(1)} %bitcast.3), custom_call_target="tpu_custom_call" | custom-call | flops 1207959552 | bytes 3145728 | tf_op jit(solution)/shard_map/pallas_call | solution.py:268
  8.7 2.0 %shard_map.49 = (f32[8,16,8,128]{3,2,1,0:T(8,128)S(1)}, f32[8,16,8,128]{3,2,1,0:T(8,128)S(1)}) custom-call(bf16[3,256,256]{2,1,0:T(8,128)(2,1)S(1)} %shard_map.40.refs_0_, f32[8,16,8,128]{3,2,1,0:T(8,128)S(1)} %get-tuple-element.53.refs_1_, f32[8,16,8,128]{3,2,1,0:T(8,128)S(1)} %collective-permute-done.10.refs_2_), custom_call_target="tpu_custom_call" | custom-call | flops 1207959552 | bytes 3145728 | tf_op jit(solution)/shard_map/pallas_call | solution.py:268
  10.7 6.4 %collective-permute-start.11 = (f32[8,16,8,128]{3,2,1,0:T(8,128)S(1)}, f32[8,16,8,128]{3,2,1,0:T(8,128)S(1)}, u32[]{:S(2)}, u32[]{:S(2)}) collective-permute-start(f32[8,16,8,128]{3,2,1,0:T(8,128)S(1)} %get-tuple-element.56), channel_id=1, source_target_pairs={{0,128},{8,136},{16,144},{24,152},{32,160},{40,168},{48,176},{56,1... | collective-permute-start | bytes 1572872 | tf_op jit(solution)/shard_map/ppermute | solution.py:305
  17.1 2.0 %shard_map.43 = (f32[8,16,8,128]{3,2,1,0:T(8,128)S(1)}, f32[8,16,8,128]{3,2,1,0:T(8,128)S(1)}) custom-call(bf16[3,256,256]{2,1,0:T(8,128)(2,1)S(1)} %shard_map.40.refs_0_, f32[8,16,8,128]{3,2,1,0:T(8,128)S(1)} %get-tuple-element.37.refs_1_, f32[8,16,8,128]{3,2,1,0:T(8,128)S(1)} %collective-permute-done.refs_2_), custom_call_target="tpu_custom_call" | custom-call | flops 1207959552 | bytes 3145728 | tf_op jit(solution)/shard_map/pallas_call | solution.py:268
  19.7 25.7 %collective-permute-done.11.refs_2_ = f32[8,16,8,128]{3,2,1,0:T(8,128)S(1)} collective-permute-done((f32[8,16,8,128]{3,2,1,0:T(8,128)S(1)}, f32[8,16,8,128]{3,2,1,0:T(8,128)S(1)}, u32[]{:S(2)}, u32[]{:S(2)}) %collective-permute-start.11) | collective-permute-done | bytes 524320 | tf_op jit(solution)/shard_map/ppermute | solution.py:305
  45.4 2.0 %shard_map.50 = (f32[16,8,8,128]{3,2,1,0:T(8,128)S(1)}, f32[16,8,8,128]{3,2,1,0:T(8,128)S(1)}) custom-call(bf16[3,256,256]{2,1,0:T(8,128)(2,1)S(1)} %shard_map.39.refs_0_, f32[8,16,8,128]{3,2,1,0:T(8,128)S(1)} %get-tuple-element.55.refs_1_, f32[8,16,8,128]{3,2,1,0:T(8,128)S(1)} %collective-permute-done.11.refs_2_), custom_call_target="tpu_custom_call" | custom-call | flops 1207959552 | bytes 3145728 | tf_op jit(solution)/shard_map/pallas_call | solution.py:268
  47.5 15.7 %collective-permute-done.1.refs_2_ = f32[8,16,8,128]{3,2,1,0:T(8,128)S(1)} collective-permute-done((f32[8,16,8,128]{3,2,1,0:T(8,128)S(1)}, f32[8,16,8,128]{3,2,1,0:T(8,128)S(1)}, u32[]{:S(2)}, u32[]{:S(2)}) %collective-permute-start.1) | collective-permute-done | bytes 524320 | tf_op jit(solution)/shard_map/ppermute | solution.py:305
  63.1 2.0 %shard_map.44 = (f32[16,8,8,128]{3,2,1,0:T(8,128)S(1)}, f32[16,8,8,128]{3,2,1,0:T(8,128)S(1)}) custom-call(bf16[3,256,256]{2,1,0:T(8,128)(2,1)S(1)} %shard_map.39.refs_0_, f32[8,16,8,128]{3,2,1,0:T(8,128)S(1)} %get-tuple-element.39.refs_1_, f32[8,16,8,128]{3,2,1,0:T(8,128)S(1)} %collective-permute-done.1.refs_2_), custom_call_target="tpu_custom_call" | custom-call | flops 1207959552 | bytes 3145728 | tf_op jit(solution)/shard_map/pallas_call | solution.py:268
  65.4 5.5 %collective-permute-start.14 = (f32[2,4,8,8,128]{4,3,2,1,0:T(8,128)S(1)}, f32[2,4,8,8,128]{4,3,2,1,0:T(8,128)S(1)}, u32[]{:S(2)}, u32[]{:S(2)}) collective-permute-start(f32[2,4,8,8,128]{4,3,2,1,0:T(8,128)S(1)} %get-tuple-element.61), channel_id=1, source_target_pairs={{0,128},{8,136},{16,144},{24,152},{32,160},{40,168},{48,176},{56,1... | collective-permute-start | bytes 786440 | tf_op jit(solution)/shard_map/ppermute | solution.py:313
  70.9 4.0 %collective-permute-start.15 = (f32[2,4,8,8,128]{4,3,2,1,0:T(8,128)S(1)}, f32[2,4,8,8,128]{4,3,2,1,0:T(8,128)S(1)}, u32[]{:S(2)}, u32[]{:S(2)}) collective-permute-start(f32[2,4,8,8,128]{4,3,2,1,0:T(8,128)S(1)} %get-tuple-element.62), channel_id=1, source_target_pairs={{0,192},{8,200},{16,208},{24,216},{32,224},{40,232},{48,240},{56,2... | collective-permute-start | bytes 786440 | tf_op jit(solution)/shard_map/ppermute | solution.py:313
  75.0 1.6 %collective-permute-start.3 = (f32[2,4,8,8,128]{4,3,2,1,0:T(8,128)S(1)}, f32[2,4,8,8,128]{4,3,2,1,0:T(8,128)S(1)}, u32[]{:S(2)}, u32[]{:S(2)}) collective-permute-start(f32[2,4,8,8,128]{4,3,2,1,0:T(8,128)S(1)} %get-tuple-element.44), channel_id=1, source_target_pairs={{0,16},{8,24},{16,32},{24,40},{32,48},{40,56},{48,0},{56,8},{64,80... | collective-permute-start | bytes 786440 | tf_op jit(solution)/shard_map/ppermute | solution.py:313
  76.6 2.7 %collective-permute-start.4 = (f32[2,4,8,8,128]{4,3,2,1,0:T(8,128)S(1)}, f32[2,4,8,8,128]{4,3,2,1,0:T(8,128)S(1)}, u32[]{:S(2)}, u32[]{:S(2)}) collective-permute-start(f32[2,4,8,8,128]{4,3,2,1,0:T(8,128)S(1)} %get-tuple-element.45), channel_id=1, source_target_pairs={{0,32},{8,40},{16,48},{24,56},{32,0},{40,8},{48,16},{56,24},{64,96... | collective-permute-start | bytes 786440 | tf_op jit(solution)/shard_map/ppermute | solution.py:313
  79.4 2.3 %collective-permute-done.13.refs_1_ = f32[2,4,8,8,128]{4,3,2,1,0:T(8,128)S(1)} collective-permute-done((f32[2,4,8,8,128]{4,3,2,1,0:T(8,128)S(1)}, f32[2,4,8,8,128]{4,3,2,1,0:T(8,128)S(1)}, u32[]{:S(2)}, u32[]{:S(2)}) %collective-permute-start.13) | collective-permute-done | bytes 262176 | tf_op jit(solution)/shard_map/ppermute | solution.py:313
  81.7 3.3 %collective-permute-start.5 = (f32[2,4,8,8,128]{4,3,2,1,0:T(8,128)S(1)}, f32[2,4,8,8,128]{4,3,2,1,0:T(8,128)S(1)}, u32[]{:S(2)}, u32[]{:S(2)}) collective-permute-start(f32[2,4,8,8,128]{4,3,2,1,0:T(8,128)S(1)} %get-tuple-element.46), channel_id=1, source_target_pairs={{0,48},{8,56},{16,0},{24,8},{32,16},{40,24},{48,32},{56,40},{64,11... | collective-permute-start | bytes 786440 | tf_op jit(solution)/shard_map/ppermute | solution.py:313
  85.2 8.6 %collective-permute-done.15.refs_3_ = f32[2,4,8,8,128]{4,3,2,1,0:T(8,128)S(1)} collective-permute-done((f32[2,4,8,8,128]{4,3,2,1,0:T(8,128)S(1)}, f32[2,4,8,8,128]{4,3,2,1,0:T(8,128)S(1)}, u32[]{:S(2)}, u32[]{:S(2)}) %collective-permute-start.15) | collective-permute-done | bytes 262176 | tf_op jit(solution)/shard_map/ppermute | solution.py:313
  94.0 2.7 %collective-permute-start.17 = (f32[2,4,8,8,128]{4,3,2,1,0:T(8,128)S(1)}, f32[2,4,8,8,128]{4,3,2,1,0:T(8,128)S(1)}, u32[]{:S(2)}, u32[]{:S(2)}) collective-permute-start(f32[2,4,8,8,128]{4,3,2,1,0:T(8,128)S(1)} %get-tuple-element.65), channel_id=1, source_target_pairs={{0,32},{8,40},{16,48},{24,56},{32,0},{40,8},{48,16},{56,24},{64,96... | collective-permute-start | bytes 786440 | tf_op jit(solution)/shard_map/ppermute | solution.py:313
  96.7 1.5 collective-permute-start.18
  98.2 11.4 %collective-permute-start.6 = (f32[2,4,8,8,128]{4,3,2,1,0:T(8,128)S(1)}, f32[2,4,8,8,128]{4,3,2,1,0:T(8,128)S(1)}, u32[]{:S(2)}, u32[]{:S(2)}) collective-permute-start(f32[2,4,8,8,128]{4,3,2,1,0:T(8,128)S(1)} %get-tuple-element.48), channel_id=1, source_target_pairs={{0,64},{8,72},{16,80},{24,88},{32,96},{40,104},{48,112},{56,120},{... | collective-permute-start | bytes 786440 | tf_op jit(solution)/shard_map/ppermute | solution.py:313
  109.6 4.3 %collective-permute-start.7 = (f32[2,4,8,8,128]{4,3,2,1,0:T(8,128)S(1)}, f32[2,4,8,8,128]{4,3,2,1,0:T(8,128)S(1)}, u32[]{:S(2)}, u32[]{:S(2)}) collective-permute-start(f32[2,4,8,8,128]{4,3,2,1,0:T(8,128)S(1)} %get-tuple-element.49), channel_id=1, source_target_pairs={{0,128},{8,136},{16,144},{24,152},{32,160},{40,168},{48,176},{56,1... | collective-permute-start | bytes 786440 | tf_op jit(solution)/shard_map/ppermute | solution.py:313
  114.0 3.8 %collective-permute-start.8 = (f32[2,4,8,8,128]{4,3,2,1,0:T(8,128)S(1)}, f32[2,4,8,8,128]{4,3,2,1,0:T(8,128)S(1)}, u32[]{:S(2)}, u32[]{:S(2)}) collective-permute-start(f32[2,4,8,8,128]{4,3,2,1,0:T(8,128)S(1)} %get-tuple-element.50), channel_id=1, source_target_pairs={{0,192},{8,200},{16,208},{24,216},{32,224},{40,232},{48,240},{56,2... | collective-permute-start | bytes 786440 | tf_op jit(solution)/shard_map/ppermute | solution.py:313
  118.7 2.0 %shard_map.53 = (f32[8,16,8,128]{3,2,1,0:T(8,128)S(1)}, f32[8,16,8,128]{3,2,1,0:T(8,128)S(1)}) custom-call(bf16[3,256,256]{2,1,0:T(8,128)(2,1)S(1)} %shard_map.38.refs_0_, f32[2,4,8,8,128]{4,3,2,1,0:T(8,128)S(1)} %get-tuple-element.63.refs_1_, f32[2,4,8,8,128]{4,3,2,1,0:T(8,128)S(1)} %collective-permute-done.16.refs_2_, ...), custom_call_target="tpu_custom_call" | custom-call | flops 1207959552 | bytes 3145728 | tf_op jit(solution)/shard_map/pallas_call | solution.py:268
  120.7 3.1 %collective-permute-start.19 = (f32[8,16,8,128]{3,2,1,0:T(8,128)S(1)}, f32[8,16,8,128]{3,2,1,0:T(8,128)S(1)}, u32[]{:S(2)}, u32[]{:S(2)}) collective-permute-start(f32[8,16,8,128]{3,2,1,0:T(8,128)S(1)} %get-tuple-element.68), channel_id=1, source_target_pairs={{0,4},{1,5},{2,6},{3,7},{4,0},{5,1},{6,2},{7,3},{8,12},{9,13},{10,... | collective-permute-start | bytes 1572872 | tf_op jit(solution)/shard_map/ppermute | solution.py:305
  124.8 2.6 %collective-permute-done.7.refs_3_ = f32[2,4,8,8,128]{4,3,2,1,0:T(8,128)S(1)} collective-permute-done((f32[2,4,8,8,128]{4,3,2,1,0:T(8,128)S(1)}, f32[2,4,8,8,128]{4,3,2,1,0:T(8,128)S(1)}, u32[]{:S(2)}, u32[]{:S(2)}) %collective-permute-start.7) | collective-permute-done | bytes 262176 | tf_op jit(solution)/shard_map/ppermute | solution.py:313
  127.4 2.9 %collective-permute-done.8.refs_4_ = f32[2,4,8,8,128]{4,3,2,1,0:T(8,128)S(1)} collective-permute-done((f32[2,4,8,8,128]{4,3,2,1,0:T(8,128)S(1)}, f32[2,4,8,8,128]{4,3,2,1,0:T(8,128)S(1)}, u32[]{:S(2)}, u32[]{:S(2)}) %collective-permute-start.8) | collective-permute-done | bytes 262176 | tf_op jit(solution)/shard_map/ppermute | solution.py:313
  130.3 2.0 %shard_map.47 = (f32[8,16,8,128]{3,2,1,0:T(8,128)S(1)}, f32[8,16,8,128]{3,2,1,0:T(8,128)S(1)}) custom-call(bf16[3,256,256]{2,1,0:T(8,128)(2,1)S(1)} %shard_map.38.refs_0_, f32[2,4,8,8,128]{4,3,2,1,0:T(8,128)S(1)} %get-tuple-element.47.refs_1_, f32[2,4,8,8,128]{4,3,2,1,0:T(8,128)S(1)} %collective-permute-done.6.refs_2_, ...), custom_call_target="tpu_custom_call" | custom-call | flops 1207959552 | bytes 3145728 | tf_op jit(solution)/shard_map/pallas_call | solution.py:268
  132.3 3.2 %collective-permute-start.9 = (f32[8,16,8,128]{3,2,1,0:T(8,128)S(1)}, f32[8,16,8,128]{3,2,1,0:T(8,128)S(1)}, u32[]{:S(2)}, u32[]{:S(2)}) collective-permute-start(f32[8,16,8,128]{3,2,1,0:T(8,128)S(1)} %get-tuple-element.52), channel_id=1, source_target_pairs={{0,4},{1,5},{2,6},{3,7},{4,0},{5,1},{6,2},{7,3},{8,12},{9,13},{10,... | collective-permute-start | bytes 1572872 | tf_op jit(solution)/shard_map/ppermute | solution.py:305
  135.8 1.8 %low_weights.1.refs_3_.refs_4_ = bf16[2,2,256,256]{3,2,1,0:T(8,128)(2,1)S(1)} custom-call(f32[5,4,2,128,128]{4,3,2,1,0:T(8,128)S(1)} %copy-done), custom_call_target="tpu_custom_call" | custom-call | flops 503316480 | bytes 1048576 | tf_op jit(solution)/shard_map/low_weights/pallas_call | solution.py:134
  137.6 4.1 %shard_map.54.refs_3_ = f32[4,512,256]{2,1,0:T(8,128)S(1)} custom-call(bf16[3,256,256]{2,1,0:T(8,128)(2,1)S(1)} %shard_map.37.refs_0_, f32[8,16,8,128]{3,2,1,0:T(8,128)S(1)} %get-tuple-element.67.refs_1_, f32[8,16,8,128]{3,2,1,0:T(8,128)S(1)} %collective-permute-done.19.refs_2_, bf16[2,2,256,256]{3,2,1,0:T(8,128)(2,1)S(1)} %low_weights.1.refs_3_.refs_4_), custom_call_target="tpu_custom_call" | custom-call | flops 1207959552 | bytes 3145728 | tf_op jit(solution)/shard_map/pallas_call | solution.py:268
  141.7 4.0 %collective-permute-done.9.refs_2_ = f32[8,16,8,128]{3,2,1,0:T(8,128)S(1)} collective-permute-done((f32[8,16,8,128]{3,2,1,0:T(8,128)S(1)}, f32[8,16,8,128]{3,2,1,0:T(8,128)S(1)}, u32[]{:S(2)}, u32[]{:S(2)}) %collective-permute-start.9) | collective-permute-done | bytes 524320 | tf_op jit(solution)/shard_map/ppermute | solution.py:305
  145.7 4.4 %shard_map.55 = f32[2,2048,128]{2,1,0:T(8,128)} custom-call(bf16[3,256,256]{2,1,0:T(8,128)(2,1)S(1)} %shard_map.37.refs_0_, f32[8,16,8,128]{3,2,1,0:T(8,128)S(1)} %get-tuple-element.51.refs_1_, f32[8,16,8,128]{3,2,1,0:T(8,128)S(1)} %collective-permute-done.9.refs_2_, f32[4,512,256]{2,1,0:T(8,128)S(1)} %shard_map.54.refs_3_, ...), custom_call_target="tpu_custom_call" | custom-call | flops 1207959552 | bytes 3145728 | tf_op jit(solution)/shard_map/pallas_call | solution.py:268
  (35 shorter events, 6.2 us)
Async XLA Ops:
  1.4 1.6 %copy-start.2 = (f32[2,1,1,262144]{3,2,1,0:T(1,128)S(1)}, f32[2,1,1,262144]{3,2,1,0:T(1,128)}, u32[]{:S(2)}) copy-start(f32[2,1,1,262144]{3,2,1,0:T(1,128)} %param.3) | copy-start | bytes 6291460
  5.3 3.0 %copy-start = (f32[5,4,2,128,128]{4,3,2,1,0:T(8,128)S(1)}, f32[5,4,2,128,128]{4,3,2,1,0:T(8,128)}, u32[]{:S(2)}) copy-start(f32[5,4,2,128,128]{4,3,2,1,0:T(8,128)} %gates_ref.1) | copy-start | bytes 7864324
  5.3 3.4 %collective-permute-start.10 = (f32[8,16,8,128]{3,2,1,0:T(8,128)S(1)}, f32[8,16,8,128]{3,2,1,0:T(8,128)S(1)}, u32[]{:S(2)}, u32[]{:S(2)}) collective-permute-start(f32[8,16,8,128]{3,2,1,0:T(8,128)S(1)} %get-tuple-element.54), channel_id=1, source_target_pairs={{0,8},{8,0},{16,24},{24,16},{32,40},{40,32},{48,56},{56,48},{64,72... | collective-permute-start | bytes 1572872 | tf_op jit(solution)/shard_map/ppermute | solution.py:305
  7.8 9.3 %collective-permute-start = (f32[8,16,8,128]{3,2,1,0:T(8,128)S(1)}, f32[8,16,8,128]{3,2,1,0:T(8,128)S(1)}, u32[]{:S(2)}, u32[]{:S(2)}) collective-permute-start(f32[8,16,8,128]{3,2,1,0:T(8,128)S(1)} %get-tuple-element.38), channel_id=1, source_target_pairs={{0,8},{8,0},{16,24},{24,16},{32,40},{40,32},{48,56},{56,48},{64,72... | collective-permute-start | bytes 1572872 | tf_op jit(solution)/shard_map/ppermute | solution.py:305
  10.7 34.7 %collective-permute-start.11 = (f32[8,16,8,128]{3,2,1,0:T(8,128)S(1)}, f32[8,16,8,128]{3,2,1,0:T(8,128)S(1)}, u32[]{:S(2)}, u32[]{:S(2)}) collective-permute-start(f32[8,16,8,128]{3,2,1,0:T(8,128)S(1)} %get-tuple-element.56), channel_id=1, source_target_pairs={{0,128},{8,136},{16,144},{24,152},{32,160},{40,168},{48,176},{56,1... | collective-permute-start | bytes 1572872 | tf_op jit(solution)/shard_map/ppermute | solution.py:305
  19.1 44.1 %collective-permute-start.1 = (f32[8,16,8,128]{3,2,1,0:T(8,128)S(1)}, f32[8,16,8,128]{3,2,1,0:T(8,128)S(1)}, u32[]{:S(2)}, u32[]{:S(2)}) collective-permute-start(f32[8,16,8,128]{3,2,1,0:T(8,128)S(1)} %get-tuple-element.40), channel_id=1, source_target_pairs={{0,128},{8,136},{16,144},{24,152},{32,160},{40,168},{48,176},{56,1... | collective-permute-start | bytes 1572872 | tf_op jit(solution)/shard_map/ppermute | solution.py:305
  47.4 17.9 %collective-permute-start.12 = (f32[16,8,8,128]{3,2,1,0:T(8,128)S(1)}, f32[16,8,8,128]{3,2,1,0:T(8,128)S(1)}, u32[]{:S(2)}, u32[]{:S(2)}) collective-permute-start(f32[16,8,8,128]{3,2,1,0:T(8,128)S(1)} %get-tuple-element.58), channel_id=1, source_target_pairs={{0,8},{8,0},{16,24},{24,16},{32,40},{40,32},{48,56},{56,48},{64,72... | collective-permute-start | bytes 1572872 | tf_op jit(solution)/shard_map/ppermute | solution.py:305
  65.1 9.8 %collective-permute-start.2 = (f32[16,8,8,128]{3,2,1,0:T(8,128)S(1)}, f32[16,8,8,128]{3,2,1,0:T(8,128)S(1)}, u32[]{:S(2)}, u32[]{:S(2)}) collective-permute-start(f32[16,8,8,128]{3,2,1,0:T(8,128)S(1)} %get-tuple-element.42), channel_id=1, source_target_pairs={{0,8},{8,0},{16,24},{24,16},{32,40},{40,32},{48,56},{56,48},{64,72... | collective-permute-start | bytes 1572872 | tf_op jit(solution)/shard_map/ppermute | solution.py:305
  65.2 52.6 %copy-start.1 = (s32[32]{0:T(128)S(1)}, s32[32]{0:T(128)}, u32[]{:S(2)}) copy-start(s32[32]{0:T(128)} %refs_0_.5) | copy-start | bytes 388
  65.3 16.3 %collective-permute-start.13 = (f32[2,4,8,8,128]{4,3,2,1,0:T(8,128)S(1)}, f32[2,4,8,8,128]{4,3,2,1,0:T(8,128)S(1)}, u32[]{:S(2)}, u32[]{:S(2)}) collective-permute-start(f32[2,4,8,8,128]{4,3,2,1,0:T(8,128)S(1)} %get-tuple-element.60), channel_id=1, source_target_pairs={{0,64},{8,72},{16,80},{24,88},{32,96},{40,104},{48,112},{56,120},{... | collective-permute-start | bytes 786440 | tf_op jit(solution)/shard_map/ppermute | solution.py:313
  65.4 19.8 %collective-permute-start.14 = (f32[2,4,8,8,128]{4,3,2,1,0:T(8,128)S(1)}, f32[2,4,8,8,128]{4,3,2,1,0:T(8,128)S(1)}, u32[]{:S(2)}, u32[]{:S(2)}) collective-permute-start(f32[2,4,8,8,128]{4,3,2,1,0:T(8,128)S(1)} %get-tuple-element.61), channel_id=1, source_target_pairs={{0,128},{8,136},{16,144},{24,152},{32,160},{40,168},{48,176},{56,1... | collective-permute-start | bytes 786440 | tf_op jit(solution)/shard_map/ppermute | solution.py:313
  70.9 22.8 %collective-permute-start.15 = (f32[2,4,8,8,128]{4,3,2,1,0:T(8,128)S(1)}, f32[2,4,8,8,128]{4,3,2,1,0:T(8,128)S(1)}, u32[]{:S(2)}, u32[]{:S(2)}) collective-permute-start(f32[2,4,8,8,128]{4,3,2,1,0:T(8,128)S(1)} %get-tuple-element.62), channel_id=1, source_target_pairs={{0,192},{8,200},{16,208},{24,216},{32,224},{40,232},{48,240},{56,2... | collective-permute-start | bytes 786440 | tf_op jit(solution)/shard_map/ppermute | solution.py:313
  75.0 21.6 %collective-permute-start.3 = (f32[2,4,8,8,128]{4,3,2,1,0:T(8,128)S(1)}, f32[2,4,8,8,128]{4,3,2,1,0:T(8,128)S(1)}, u32[]{:S(2)}, u32[]{:S(2)}) collective-permute-start(f32[2,4,8,8,128]{4,3,2,1,0:T(8,128)S(1)} %get-tuple-element.44), channel_id=1, source_target_pairs={{0,16},{8,24},{16,32},{24,40},{32,48},{40,56},{48,0},{56,8},{64,80... | collective-permute-start | bytes 786440 | tf_op jit(solution)/shard_map/ppermute | solution.py:313
  76.6 21.5 %collective-permute-start.4 = (f32[2,4,8,8,128]{4,3,2,1,0:T(8,128)S(1)}, f32[2,4,8,8,128]{4,3,2,1,0:T(8,128)S(1)}, u32[]{:S(2)}, u32[]{:S(2)}) collective-permute-start(f32[2,4,8,8,128]{4,3,2,1,0:T(8,128)S(1)} %get-tuple-element.45), channel_id=1, source_target_pairs={{0,32},{8,40},{16,48},{24,56},{32,0},{40,8},{48,16},{56,24},{64,96... | collective-permute-start | bytes 786440 | tf_op jit(solution)/shard_map/ppermute | solution.py:313
  81.7 16.4 %collective-permute-start.5 = (f32[2,4,8,8,128]{4,3,2,1,0:T(8,128)S(1)}, f32[2,4,8,8,128]{4,3,2,1,0:T(8,128)S(1)}, u32[]{:S(2)}, u32[]{:S(2)}) collective-permute-start(f32[2,4,8,8,128]{4,3,2,1,0:T(8,128)S(1)} %get-tuple-element.46), channel_id=1, source_target_pairs={{0,48},{8,56},{16,0},{24,8},{32,16},{40,24},{48,32},{56,40},{64,11... | collective-permute-start | bytes 786440 | tf_op jit(solution)/shard_map/ppermute | solution.py:313
  93.8 20.2 %collective-permute-start.16 = (f32[2,4,8,8,128]{4,3,2,1,0:T(8,128)S(1)}, f32[2,4,8,8,128]{4,3,2,1,0:T(8,128)S(1)}, u32[]{:S(2)}, u32[]{:S(2)}) collective-permute-start(f32[2,4,8,8,128]{4,3,2,1,0:T(8,128)S(1)} %get-tuple-element.64), channel_id=1, source_target_pairs={{0,16},{8,24},{16,32},{24,40},{32,48},{40,56},{48,0},{56,8},{64,80... | collective-permute-start | bytes 786440 | tf_op jit(solution)/shard_map/ppermute | solution.py:313
  94.0 24.7 %collective-permute-start.17 = (f32[2,4,8,8,128]{4,3,2,1,0:T(8,128)S(1)}, f32[2,4,8,8,128]{4,3,2,1,0:T(8,128)S(1)}, u32[]{:S(2)}, u32[]{:S(2)}) collective-permute-start(f32[2,4,8,8,128]{4,3,2,1,0:T(8,128)S(1)} %get-tuple-element.65), channel_id=1, source_target_pairs={{0,32},{8,40},{16,48},{24,56},{32,0},{40,8},{48,16},{56,24},{64,96... | collective-permute-start | bytes 786440 | tf_op jit(solution)/shard_map/ppermute | solution.py:313
  96.7 22.1 %collective-permute-start.18 = (f32[2,4,8,8,128]{4,3,2,1,0:T(8,128)S(1)}, f32[2,4,8,8,128]{4,3,2,1,0:T(8,128)S(1)}, u32[]{:S(2)}, u32[]{:S(2)}) collective-permute-start(f32[2,4,8,8,128]{4,3,2,1,0:T(8,128)S(1)} %get-tuple-element.66), channel_id=1, source_target_pairs={{0,48},{8,56},{16,0},{24,8},{32,16},{40,24},{48,32},{56,40},{64,11... | collective-permute-start | bytes 786440 | tf_op jit(solution)/shard_map/ppermute | solution.py:313
  98.2 26.6 %collective-permute-start.6 = (f32[2,4,8,8,128]{4,3,2,1,0:T(8,128)S(1)}, f32[2,4,8,8,128]{4,3,2,1,0:T(8,128)S(1)}, u32[]{:S(2)}, u32[]{:S(2)}) collective-permute-start(f32[2,4,8,8,128]{4,3,2,1,0:T(8,128)S(1)} %get-tuple-element.48), channel_id=1, source_target_pairs={{0,64},{8,72},{16,80},{24,88},{32,96},{40,104},{48,112},{56,120},{... | collective-permute-start | bytes 786440 | tf_op jit(solution)/shard_map/ppermute | solution.py:313
  109.6 17.8 %collective-permute-start.7 = (f32[2,4,8,8,128]{4,3,2,1,0:T(8,128)S(1)}, f32[2,4,8,8,128]{4,3,2,1,0:T(8,128)S(1)}, u32[]{:S(2)}, u32[]{:S(2)}) collective-permute-start(f32[2,4,8,8,128]{4,3,2,1,0:T(8,128)S(1)} %get-tuple-element.49), channel_id=1, source_target_pairs={{0,128},{8,136},{16,144},{24,152},{32,160},{40,168},{48,176},{56,1... | collective-permute-start | bytes 786440 | tf_op jit(solution)/shard_map/ppermute | solution.py:313
  114.0 16.3 %collective-permute-start.8 = (f32[2,4,8,8,128]{4,3,2,1,0:T(8,128)S(1)}, f32[2,4,8,8,128]{4,3,2,1,0:T(8,128)S(1)}, u32[]{:S(2)}, u32[]{:S(2)}) collective-permute-start(f32[2,4,8,8,128]{4,3,2,1,0:T(8,128)S(1)} %get-tuple-element.50), channel_id=1, source_target_pairs={{0,192},{8,200},{16,208},{24,216},{32,224},{40,232},{48,240},{56,2... | collective-permute-start | bytes 786440 | tf_op jit(solution)/shard_map/ppermute | solution.py:313
  120.7 16.9 %collective-permute-start.19 = (f32[8,16,8,128]{3,2,1,0:T(8,128)S(1)}, f32[8,16,8,128]{3,2,1,0:T(8,128)S(1)}, u32[]{:S(2)}, u32[]{:S(2)}) collective-permute-start(f32[8,16,8,128]{3,2,1,0:T(8,128)S(1)} %get-tuple-element.68), channel_id=1, source_target_pairs={{0,4},{1,5},{2,6},{3,7},{4,0},{5,1},{6,2},{7,3},{8,12},{9,13},{10,... | collective-permute-start | bytes 1572872 | tf_op jit(solution)/shard_map/ppermute | solution.py:305
  132.3 13.5 %collective-permute-start.9 = (f32[8,16,8,128]{3,2,1,0:T(8,128)S(1)}, f32[8,16,8,128]{3,2,1,0:T(8,128)S(1)}, u32[]{:S(2)}, u32[]{:S(2)}) collective-permute-start(f32[8,16,8,128]{3,2,1,0:T(8,128)S(1)} %get-tuple-element.52), channel_id=1, source_target_pairs={{0,4},{1,5},{2,6},{3,7},{4,0},{5,1},{6,2},{7,3},{8,12},{9,13},{10,... | collective-permute-start | bytes 1572872 | tf_op jit(solution)/shard_map/ppermute | solution.py:305

commit v4 on v3

--- a/solution.py
+++ b/solution.py
@@ -32,13 +32,13 @@
     if kind == "mid":
         want = ((new & 7) << 4) | (new >> 3)
     elif kind[:3] == "xor":
-        want = new ^ ({"xor2": c_own, "xor3": row >> 4, "xor4": col >> 2}[kind] << 6)
+        want = new ^ ({"xor2": c_own, "xor4": col >> 2}[kind] << 6)
     elif kind == "dest":
         x = ((block >> 2) + x_own) & 3
         z = ((block & 3) + z_own) & 3
         want = (((((z << 2) | x) << 1) | (core ^ c_own)) << 2) | rest
     else:
-        z = (z_own - (block >> 2)) & 3
+        z = ((block >> 3) << 1) | ((z_own - (block >> 2)) & 1)
         x = (x_own - (block & 3)) & 3
         want = (((((z << 2) | x) << 1) | (core ^ c_own)) << 2) | rest
         state = lax.broadcasted_iota(jnp.int32, (1, GD), 1)
@@ -110,7 +110,7 @@
     def _():
         new = lax.broadcasted_iota(jnp.int32, (256, 256), 0)
         old = lax.broadcasted_iota(jnp.int32, (256, 256), 1)
-        want = (((new >> 6) & 1) << 7) | ((new >> 7) << 6) | (new & 63)
+        want = (((new >> 6) & 1) << 7) | (((new >> 5) & 1) << 6) | ((new >> 7) << 5) | (new & 31)
         total_ref[...] = jnp.where(want == old, 1.0, 0.0)
 
     high, low = split(total_ref[...])
@@ -146,6 +146,51 @@
     )(gate_matrices)
 
 
+def cross(first, second, step):
+    axis = first.ndim - 1
+    lane = lax.broadcasted_iota(jnp.int32, (1,) * axis + (GD,), axis)
+    off = (lane & step) == 0
+    return (
+        jnp.where(off, first, pltpu.roll(second, step, axis)),
+        jnp.where(off, pltpu.roll(first, GD - step, axis), second),
+    )
+
+
+def in_order(swapped, first, second):
+    return jnp.where(swapped, second, first), jnp.where(swapped, first, second)
+
+
+def pack_kernel(state_ref, *outs):
+    own = lax.axis_index("row") >> 4 == 1
+
+    def some(p, carry):
+        tops = []
+        for top in range(2):
+            rows = [state_ref[c, pl.ds(1024 * top + p, HALF, stride=16), :] for c in range(2)]
+            tops.append(cross(rows[0], rows[1], 64))
+        sides = [cross(tops[0][b], tops[1][b], 32) for b in range(2)]
+        for h in range(2):
+            stays, leaves = in_order(own, sides[0][h], sides[1][h])
+            outs[2 * h][:, p] = stays.reshape(8, 8, GD)
+            outs[2 * h + 1][:, p] = leaves.reshape(8, 8, GD)
+        return carry
+
+    lax.fori_loop(0, 16, some, 0, unroll=8)
+
+
+def pack(state):
+    vmem = pl.BlockSpec(memory_space=pltpu.VMEM)
+    return pl.pallas_call(
+        pack_kernel,
+        out_shape=[jax.ShapeDtypeStruct(PART, F32)] * 4,
+        in_specs=[vmem],
+        out_specs=[vmem] * 4,
+        cost_estimate=pl.CostEstimate(flops=0, bytes_accessed=4 << 20, transcendentals=0),
+        compiler_params=pltpu.CompilerParams(vmem_limit_bytes=LIMIT),
+        name="pack",
+    )(state)
+
+
 def gate_step(first, second, w_high_low, w_high, sign):
     state = jnp.concatenate([first, second], axis=1)
     turned = jnp.concatenate(
@@ -167,14 +212,18 @@
     upper = lax.broadcasted_iota(jnp.int32, (1, 8, GD), 1) >= 4
 
     def load_start(i):
+        own = lax.axis_index("row") >> 4 == 1
         blocks = []
         for p in (2 * i, 2 * i + 1):
-            re = ins[0][0, pl.ds(p, GD, stride=16), :]
-            im = ins[0][1, pl.ds(p, GD, stride=16), :]
-            if source[1] == 0:
-                blocks.append(jnp.where(lane < HALF, re, pltpu.roll(im, HALF, 1)))
-            else:
-                blocks.append(jnp.where(lane < HALF, pltpu.roll(re, HALF, 1), im))
+            sides = in_order(own, ins[0][:, p].reshape(HALF, GD), ins[1][:, p].reshape(HALF, GD))
+            blocks.append(jnp.concatenate(cross(*sides, 32), axis=0))
+        return blocks
+
+    def load_turn(i):
+        blocks = []
+        for p in (2 * i, 2 * i + 1):
+            sides = ins[0][:8, p].reshape(HALF, GD), ins[0][8:, p].reshape(HALF, GD)
+            blocks.append(jnp.concatenate(cross(*sides, 32), axis=0))
         return blocks
 
     def load_pair(i):
@@ -194,9 +243,24 @@
         near, far = half(0), half(1)
         even = jnp.where(upper, pltpu.roll(far, 4, 1), near)
         odd = jnp.where(upper, far, pltpu.roll(near, 4, 1))
-        return [even.reshape(GD, GD), odd.reshape(GD, GD)]
-
-    load = {"start": load_start, "pair": load_pair, "remap": load_remap}[source[0]]
+        z_own = lax.axis_index("row") >> 3
+        blocks = []
+        for rows in (even, odd):
+            near_rows = [], []
+            for z in range(2):
+                swapped = ((z_own - z) & 3) >= 2
+                sides = in_order(swapped, rows[4 * z : 4 * z + 4], rows[4 * z + 8 : 4 * z + 12])
+                for k, side in enumerate(cross(*sides, 32)):
+                    near_rows[k].append(side)
+            blocks.append(jnp.concatenate(near_rows[0] + near_rows[1], axis=0).reshape(GD, GD))
+        return blocks
+
+    load = {
+        "start": load_start,
+        "pair": load_pair,
+        "turn": load_turn,
+        "remap": load_remap,
+    }[source[0]]
 
     def top_first(i, carry):
         first, second = load(i)
@@ -227,8 +291,9 @@
             outs[0][:, i] = jnp.where(upper, pltpu.roll(odd, 4, 1), even)
             outs[1][:, i] = jnp.where(upper, odd, pltpu.roll(even, 4, 1))
         else:
+            held = outs[0] if target == "plain" else one
             for p, piece in zip((2 * i, 2 * i + 1), pieces):
-                one[:, p] = piece.reshape(16, 8, GD)
+                held[:, p] = piece.reshape(16, 8, GD)
         return carry
 
     def low_gate(i, carry):
@@ -259,6 +324,8 @@
         out_shape = [jax.ShapeDtypeStruct(PART, F32)] * 2
     elif target == "remap":
         out_shape = [jax.ShapeDtypeStruct((16, 8, 8, 128), F32)] * 2
+    elif target == "plain":
+        out_shape = [jax.ShapeDtypeStruct(STATE, F32)]
     elif target == "share":
         out_shape = [jax.ShapeDtypeStruct((4, 512, 256), F32)]
     else:
@@ -332,8 +399,8 @@
     mid = ("mid", "mid")
     kinds = (
         ((None, None), mid, ("xor2", None)),
-        ((None, "xor2"), mid, ("xor3", None)),
-        ((None, "xor3"), mid, ("dest", None)),
+        ((None, "xor2"), mid, (None, None)),
+        ((None, None), mid, ("dest", None)),
         ((None, "src"), mid, ("xor4", None)),
         ((None, "xor4"), mid, (None, None)),
     )
@@ -343,16 +410,14 @@
     ]
     low = low_weights(gate_matrices)
     halves = (0, 1)
-    kept, sent = {}, {}
+    kept, sent, got = {}, {}, {}
+    stays_0, leaves_0, stays_1, leaves_1 = pack(state)
+    pairs = ([stays_0, flip(leaves_0, "row", 16)], [stays_1, flip(leaves_1, "row", 16)])
     for h in halves:
-        kept[h], out = run_segment(("start", h), "pair", w[0], [state])
+        kept[h], out = run_segment(("start",), "pair", w[0], pairs[h])
         sent[h] = flip(out, "row", 1)
-    for h in halves:
-        kept[h], out = run_segment(("pair",), "pair", w[1], [kept[h], sent[h]])
-        sent[h] = flip(out, "row", 16)
-    got = {}
-    for h in halves:
-        near, far = run_segment(("pair",), "remap", w[2], [kept[h], sent[h]])
+        (whole,) = run_segment(("pair",), "plain", w[1], [kept[h], sent[h]])
+        near, far = run_segment(("turn",), "remap", w[2], [whole])
         pair = [near, flip(far, "row", 1)]
         if h == 0:
             moved = shift_z(regroup("by_z", pair))

time: 150 us -> 154 us (1.027)
  the two profiles are of different devices: /device:TPU:32 before, /device:TPU:52 now
where the time goes in v4:
time: 154 us; the launch traced here: 153 us
  waiting for transfers between devices  78.1 us (51%)
  starting transfers between devices  40.1 us (26%)
  Pallas kernels  32.3 us (21%)
  local copies, waits for them, and re-layouts  2.67 us (2%)
    ppermute x8, waiting for transfers between devices, flip(): lax.ppermute(value, axis, [(s, s ^ mask) for s in range(lax.axis_size(axi...  49.8 us
    ppermute x12, starting transfers between devices, shift_row(): return lax.ppermute(value, 'row', pairs)  31.7 us
    ppermute x12, waiting for transfers between devices, shift_row(): return lax.ppermute(value, 'row', pairs)  28.3 us
    pallas_call x10, Pallas kernels, run_segment(): pl.pallas_call(functools.partial(segment_kernel, source, target, len(args...  25.8 us
    ppermute x8, starting transfers between devices, flip(): lax.ppermute(value, axis, [(s, s ^ mask) for s in range(lax.axis_size(axi...  8.38 us
  transfers between devices with their start and end apart: 20, of which 8 were waited for; matrix products, arithmetic and copies ran while one was open for 1% of the time, Pallas kernels for 17%

profile of v4, /device:TPU:52, one launch (start us, length us, event | category | flops | bytes accessed | tf_op | source)
XLA Modules:
  0.0 153.4 jit_solution(16254449561288524587)
XLA Ops:
  0.0 1.6 %copy-done.1 = f32[2,1,1,262144]{3,2,1,0:T(1,128)S(1)} copy-done((f32[2,1,1,262144]{3,2,1,0:T(1,128)S(1)}, f32[2,1,1,262144]{3,2,1,0:T(1,128)}, u32[]{:S(2)}) %copy-start.1) | copy-done | bytes 2097176
  1.6 2.2 %pack.1 = (f32[8,16,8,128]{3,2,1,0:T(8,128)S(1)}, f32[8,16,8,128]{3,2,1,0:T(8,128)S(1)}, f32[8,16,8,128]{3,2,1,0:T(8,128)S(1)}, f32[8,16,8,128]{3,2,1,0:T(8,128)S(1)}) custom-call(f32[2,2048,128]{2,1,0:T(8,128)S(1)} %bitcast.2), custom_call_target="tpu_custom_call" | custom-call | bytes 4194304 | tf_op jit(solution)/shard_map/pack/pallas_call | solution.py:183
  3.8 6.4 %collective-permute-start.10 = (f32[8,16,8,128]{3,2,1,0:T(8,128)S(1)}, f32[8,16,8,128]{3,2,1,0:T(8,128)S(1)}, u32[]{:S(2)}, u32[]{:S(2)}) collective-permute-start(f32[8,16,8,128]{3,2,1,0:T(8,128)S(1)} %get-tuple-element.54), channel_id=1, source_target_pairs={{0,128},{8,136},{16,144},{24,152},{32,160},{40,168},{48,176},{56,1... | collective-permute-start | bytes 1572872 | tf_op jit(solution)/shard_map/ppermute | solution.py:372
  10.3 1.1 slice.3.refs_0_
  11.7 26.8 %collective-permute-done.10.refs_2_ = f32[8,16,8,128]{3,2,1,0:T(8,128)S(1)} collective-permute-done((f32[8,16,8,128]{3,2,1,0:T(8,128)S(1)}, f32[8,16,8,128]{3,2,1,0:T(8,128)S(1)}, u32[]{:S(2)}, u32[]{:S(2)}) %collective-permute-start.10) | collective-permute-done | bytes 524320 | tf_op jit(solution)/shard_map/ppermute | solution.py:372
  38.5 2.2 %shard_map.48 = (f32[8,16,8,128]{3,2,1,0:T(8,128)S(1)}, f32[8,16,8,128]{3,2,1,0:T(8,128)S(1)}) custom-call(bf16[3,256,256]{2,1,0:T(8,128)(2,1)S(1)} %shard_map.41.refs_0_, f32[8,16,8,128]{3,2,1,0:T(8,128)S(1)} %get-tuple-element.53.refs_1_, f32[8,16,8,128]{3,2,1,0:T(8,128)S(1)} %collective-permute-done.10.refs_2_), custom_call_target="tpu_custom_call" | custom-call | flops 1207959552 | bytes 3145728 | tf_op jit(solution)/shard_map/pallas_call | solution.py:335
  40.8 15.3 %collective-permute-done.refs_2_ = f32[8,16,8,128]{3,2,1,0:T(8,128)S(1)} collective-permute-done((f32[8,16,8,128]{3,2,1,0:T(8,128)S(1)}, f32[8,16,8,128]{3,2,1,0:T(8,128)S(1)}, u32[]{:S(2)}, u32[]{:S(2)}) %collective-permute-start) | collective-permute-done | bytes 524320 | tf_op jit(solution)/shard_map/ppermute | solution.py:372
  56.0 2.2 %shard_map.42 = (f32[8,16,8,128]{3,2,1,0:T(8,128)S(1)}, f32[8,16,8,128]{3,2,1,0:T(8,128)S(1)}) custom-call(bf16[3,256,256]{2,1,0:T(8,128)(2,1)S(1)} %shard_map.41.refs_0_, f32[8,16,8,128]{3,2,1,0:T(8,128)S(1)} %get-tuple-element.37.refs_1_, f32[8,16,8,128]{3,2,1,0:T(8,128)S(1)} %collective-permute-done.refs_2_), custom_call_target="tpu_custom_call" | custom-call | flops 1207959552 | bytes 3145728 | tf_op jit(solution)/shard_map/pallas_call | solution.py:335
  59.1 2.0 %shard_map.49.refs_1_ = f32[16,16,8,128]{3,2,1,0:T(8,128)S(1)} custom-call(bf16[3,256,256]{2,1,0:T(8,128)(2,1)S(1)} %shard_map.40.refs_0_, f32[8,16,8,128]{3,2,1,0:T(8,128)S(1)} %get-tuple-element.55.refs_1_, f32[8,16,8,128]{3,2,1,0:T(8,128)S(1)} %collective-permute-done.11.refs_2_), custom_call_target="tpu_custom_call" | custom-call | flops 1207959552 | bytes 3145728 | tf_op jit(solution)/shard_map/pallas_call | solution.py:335
  61.1 2.2 %shard_map.50 = (f32[16,8,8,128]{3,2,1,0:T(8,128)S(1)}, f32[16,8,8,128]{3,2,1,0:T(8,128)S(1)}) custom-call(bf16[3,256,256]{2,1,0:T(8,128)(2,1)S(1)} %shard_map.39.refs_0_, f32[16,16,8,128]{3,2,1,0:T(8,128)S(1)} %shard_map.49.refs_1_), custom_call_target="tpu_custom_call" | custom-call | flops 1207959552 | bytes 3145728 | tf_op jit(solution)/shard_map/pallas_call | solution.py:335
  64.0 2.0 %shard_map.43.refs_1_ = f32[16,16,8,128]{3,2,1,0:T(8,128)S(1)} custom-call(bf16[3,256,256]{2,1,0:T(8,128)(2,1)S(1)} %shard_map.40.refs_0_, f32[8,16,8,128]{3,2,1,0:T(8,128)S(1)} %get-tuple-element.39.refs_1_, f32[8,16,8,128]{3,2,1,0:T(8,128)S(1)} %collective-permute-done.1.refs_2_), custom_call_target="tpu_custom_call" | custom-call | flops 1207959552 | bytes 3145728 | tf_op jit(solution)/shard_map/pallas_call | solution.py:335
  66.0 2.2 %shard_map.44 = (f32[16,8,8,128]{3,2,1,0:T(8,128)S(1)}, f32[16,8,8,128]{3,2,1,0:T(8,128)S(1)}) custom-call(bf16[3,256,256]{2,1,0:T(8,128)(2,1)S(1)} %shard_map.39.refs_0_, f32[16,16,8,128]{3,2,1,0:T(8,128)S(1)} %shard_map.43.refs_1_), custom_call_target="tpu_custom_call" | custom-call | flops 1207959552 | bytes 3145728 | tf_op jit(solution)/shard_map/pallas_call | solution.py:335
  68.5 5.5 %collective-permute-start.14 = (f32[2,4,8,8,128]{4,3,2,1,0:T(8,128)S(1)}, f32[2,4,8,8,128]{4,3,2,1,0:T(8,128)S(1)}, u32[]{:S(2)}, u32[]{:S(2)}) collective-permute-start(f32[2,4,8,8,128]{4,3,2,1,0:T(8,128)S(1)} %get-tuple-element.61), channel_id=1, source_target_pairs={{0,128},{8,136},{16,144},{24,152},{32,160},{40,168},{48,176},{56,1... | collective-permute-start | bytes 786440 | tf_op jit(solution)/shard_map/ppermute | solution.py:380
  74.0 4.0 %collective-permute-start.15 = (f32[2,4,8,8,128]{4,3,2,1,0:T(8,128)S(1)}, f32[2,4,8,8,128]{4,3,2,1,0:T(8,128)S(1)}, u32[]{:S(2)}, u32[]{:S(2)}) collective-permute-start(f32[2,4,8,8,128]{4,3,2,1,0:T(8,128)S(1)} %get-tuple-element.62), channel_id=1, source_target_pairs={{0,192},{8,200},{16,208},{24,216},{32,224},{40,232},{48,240},{56,2... | collective-permute-start | bytes 786440 | tf_op jit(solution)/shard_map/ppermute | solution.py:380
  78.2 1.3 collective-permute-start.3
  80.2 5.0 %collective-permute-done.13.refs_1_ = f32[2,4,8,8,128]{4,3,2,1,0:T(8,128)S(1)} collective-permute-done((f32[2,4,8,8,128]{4,3,2,1,0:T(8,128)S(1)}, f32[2,4,8,8,128]{4,3,2,1,0:T(8,128)S(1)}, u32[]{:S(2)}, u32[]{:S(2)}) %collective-permute-start.13) | collective-permute-done | bytes 262176 | tf_op jit(solution)/shard_map/ppermute | solution.py:380
  85.8 2.2 %collective-permute-done.14.refs_2_ = f32[2,4,8,8,128]{4,3,2,1,0:T(8,128)S(1)} collective-permute-done((f32[2,4,8,8,128]{4,3,2,1,0:T(8,128)S(1)}, f32[2,4,8,8,128]{4,3,2,1,0:T(8,128)S(1)}, u32[]{:S(2)}, u32[]{:S(2)}) %collective-permute-start.14) | collective-permute-done | bytes 262176 | tf_op jit(solution)/shard_map/ppermute | solution.py:380
  88.1 7.4 %collective-permute-done.15.refs_3_ = f32[2,4,8,8,128]{4,3,2,1,0:T(8,128)S(1)} collective-permute-done((f32[2,4,8,8,128]{4,3,2,1,0:T(8,128)S(1)}, f32[2,4,8,8,128]{4,3,2,1,0:T(8,128)S(1)}, u32[]{:S(2)}, u32[]{:S(2)}) %collective-permute-start.15) | collective-permute-done | bytes 262176 | tf_op jit(solution)/shard_map/ppermute | solution.py:380
  95.5 1.3 collective-permute-start.16
  96.8 2.1 %collective-permute-start.17 = (f32[2,4,8,8,128]{4,3,2,1,0:T(8,128)S(1)}, f32[2,4,8,8,128]{4,3,2,1,0:T(8,128)S(1)}, u32[]{:S(2)}, u32[]{:S(2)}) collective-permute-start(f32[2,4,8,8,128]{4,3,2,1,0:T(8,128)S(1)} %get-tuple-element.65), channel_id=1, source_target_pairs={{0,32},{8,40},{16,48},{24,56},{32,0},{40,8},{48,16},{56,24},{64,96... | collective-permute-start | bytes 786440 | tf_op jit(solution)/shard_map/ppermute | solution.py:380
  98.9 2.5 %collective-permute-start.18 = (f32[2,4,8,8,128]{4,3,2,1,0:T(8,128)S(1)}, f32[2,4,8,8,128]{4,3,2,1,0:T(8,128)S(1)}, u32[]{:S(2)}, u32[]{:S(2)}) collective-permute-start(f32[2,4,8,8,128]{4,3,2,1,0:T(8,128)S(1)} %get-tuple-element.66), channel_id=1, source_target_pairs={{0,48},{8,56},{16,0},{24,8},{32,16},{40,24},{48,32},{56,40},{64,11... | collective-permute-start | bytes 786440 | tf_op jit(solution)/shard_map/ppermute | solution.py:380
  101.5 5.3 %collective-permute-start.6 = (f32[2,4,8,8,128]{4,3,2,1,0:T(8,128)S(1)}, f32[2,4,8,8,128]{4,3,2,1,0:T(8,128)S(1)}, u32[]{:S(2)}, u32[]{:S(2)}) collective-permute-start(f32[2,4,8,8,128]{4,3,2,1,0:T(8,128)S(1)} %get-tuple-element.48), channel_id=1, source_target_pairs={{0,64},{8,72},{16,80},{24,88},{32,96},{40,104},{48,112},{56,120},{... | collective-permute-start | bytes 786440 | tf_op jit(solution)/shard_map/ppermute | solution.py:380
  106.8 4.1 %collective-permute-start.7 = (f32[2,4,8,8,128]{4,3,2,1,0:T(8,128)S(1)}, f32[2,4,8,8,128]{4,3,2,1,0:T(8,128)S(1)}, u32[]{:S(2)}, u32[]{:S(2)}) collective-permute-start(f32[2,4,8,8,128]{4,3,2,1,0:T(8,128)S(1)} %get-tuple-element.49), channel_id=1, source_target_pairs={{0,128},{8,136},{16,144},{24,152},{32,160},{40,168},{48,176},{56,1... | collective-permute-start | bytes 786440 | tf_op jit(solution)/shard_map/ppermute | solution.py:380
  111.0 4.0 %collective-permute-start.8 = (f32[2,4,8,8,128]{4,3,2,1,0:T(8,128)S(1)}, f32[2,4,8,8,128]{4,3,2,1,0:T(8,128)S(1)}, u32[]{:S(2)}, u32[]{:S(2)}) collective-permute-start(f32[2,4,8,8,128]{4,3,2,1,0:T(8,128)S(1)} %get-tuple-element.50), channel_id=1, source_target_pairs={{0,192},{8,200},{16,208},{24,216},{32,224},{40,232},{48,240},{56,2... | collective-permute-start | bytes 786440 | tf_op jit(solution)/shard_map/ppermute | solution.py:380
  115.9 2.3 %shard_map.53 = (f32[8,16,8,128]{3,2,1,0:T(8,128)S(1)}, f32[8,16,8,128]{3,2,1,0:T(8,128)S(1)}) custom-call(bf16[3,256,256]{2,1,0:T(8,128)(2,1)S(1)} %shard_map.38.refs_0_, f32[2,4,8,8,128]{4,3,2,1,0:T(8,128)S(1)} %get-tuple-element.63.refs_1_, f32[2,4,8,8,128]{4,3,2,1,0:T(8,128)S(1)} %collective-permute-done.16.refs_2_, ...), custom_call_target="tpu_custom_call" | custom-call | flops 1207959552 | bytes 3145728 | tf_op jit(solution)/shard_map/pallas_call | solution.py:335
  118.6 8.3 %collective-permute-done.6.refs_2_ = f32[2,4,8,8,128]{4,3,2,1,0:T(8,128)S(1)} collective-permute-done((f32[2,4,8,8,128]{4,3,2,1,0:T(8,128)S(1)}, f32[2,4,8,8,128]{4,3,2,1,0:T(8,128)S(1)}, u32[]{:S(2)}, u32[]{:S(2)}) %collective-permute-start.6) | collective-permute-done | bytes 262176 | tf_op jit(solution)/shard_map/ppermute | solution.py:380
  126.9 5.4 %collective-permute-done.8.refs_4_ = f32[2,4,8,8,128]{4,3,2,1,0:T(8,128)S(1)} collective-permute-done((f32[2,4,8,8,128]{4,3,2,1,0:T(8,128)S(1)}, f32[2,4,8,8,128]{4,3,2,1,0:T(8,128)S(1)}, u32[]{:S(2)}, u32[]{:S(2)}) %collective-permute-start.8) | collective-permute-done | bytes 262176 | tf_op jit(solution)/shard_map/ppermute | solution.py:380
  132.3 2.2 %shard_map.47 = (f32[8,16,8,128]{3,2,1,0:T(8,128)S(1)}, f32[8,16,8,128]{3,2,1,0:T(8,128)S(1)}) custom-call(bf16[3,256,256]{2,1,0:T(8,128)(2,1)S(1)} %shard_map.38.refs_0_, f32[2,4,8,8,128]{4,3,2,1,0:T(8,128)S(1)} %get-tuple-element.47.refs_1_, f32[2,4,8,8,128]{4,3,2,1,0:T(8,128)S(1)} %collective-permute-done.6.refs_2_, ...), custom_call_target="tpu_custom_call" | custom-call | flops 1207959552 | bytes 3145728 | tf_op jit(solution)/shard_map/pallas_call | solution.py:335
  135.3 1.8 %low_weights.1.refs_3_.refs_4_ = bf16[2,2,256,256]{3,2,1,0:T(8,128)(2,1)S(1)} custom-call(f32[5,4,2,128,128]{4,3,2,1,0:T(8,128)S(1)} %copy-done), custom_call_target="tpu_custom_call" | custom-call | flops 503316480 | bytes 1048576 | tf_op jit(solution)/shard_map/low_weights/pallas_call | solution.py:134
  137.2 4.1 %shard_map.54.refs_3_ = f32[4,512,256]{2,1,0:T(8,128)S(1)} custom-call(bf16[3,256,256]{2,1,0:T(8,128)(2,1)S(1)} %shard_map.37.refs_0_, f32[8,16,8,128]{3,2,1,0:T(8,128)S(1)} %get-tuple-element.67.refs_1_, f32[8,16,8,128]{3,2,1,0:T(8,128)S(1)} %collective-permute-done.19.refs_2_, bf16[2,2,256,256]{3,2,1,0:T(8,128)(2,1)S(1)} %low_weights.1.refs_3_.refs_4_), custom_call_target="tpu_custom_call" | custom-call | flops 1207959552 | bytes 3145728 | tf_op jit(solution)/shard_map/pallas_call | solution.py:335
  141.3 7.8 %collective-permute-done.9.refs_2_ = f32[8,16,8,128]{3,2,1,0:T(8,128)S(1)} collective-permute-done((f32[8,16,8,128]{3,2,1,0:T(8,128)S(1)}, f32[8,16,8,128]{3,2,1,0:T(8,128)S(1)}, u32[]{:S(2)}, u32[]{:S(2)}) %collective-permute-start.9) | collective-permute-done | bytes 524320 | tf_op jit(solution)/shard_map/ppermute | solution.py:372
  149.0 4.4 %shard_map.55 = f32[2,2048,128]{2,1,0:T(8,128)} custom-call(bf16[3,256,256]{2,1,0:T(8,128)(2,1)S(1)} %shard_map.37.refs_0_, f32[8,16,8,128]{3,2,1,0:T(8,128)S(1)} %get-tuple-element.51.refs_1_, f32[8,16,8,128]{3,2,1,0:T(8,128)S(1)} %collective-permute-done.9.refs_2_, f32[4,512,256]{2,1,0:T(8,128)S(1)} %shard_map.54.refs_3_, ...), custom_call_target="tpu_custom_call" | custom-call | flops 1207959552 | bytes 3145728 | tf_op jit(solution)/shard_map/pallas_call | solution.py:335
  (36 shorter events, 6.0 us)
Async XLA Ops:
  0.0 1.6 %copy-start.1 = (f32[2,1,1,262144]{3,2,1,0:T(1,128)S(1)}, f32[2,1,1,262144]{3,2,1,0:T(1,128)}, u32[]{:S(2)}) copy-start(f32[2,1,1,262144]{3,2,1,0:T(1,128)} %param.3) | copy-start | bytes 6291460
  3.8 34.7 %collective-permute-start.10 = (f32[8,16,8,128]{3,2,1,0:T(8,128)S(1)}, f32[8,16,8,128]{3,2,1,0:T(8,128)S(1)}, u32[]{:S(2)}, u32[]{:S(2)}) collective-permute-start(f32[8,16,8,128]{3,2,1,0:T(8,128)S(1)} %get-tuple-element.54), channel_id=1, source_target_pairs={{0,128},{8,136},{16,144},{24,152},{32,160},{40,168},{48,176},{56,1... | collective-permute-start | bytes 1572872 | tf_op jit(solution)/shard_map/ppermute | solution.py:372
  10.2 45.9 %collective-permute-start = (f32[8,16,8,128]{3,2,1,0:T(8,128)S(1)}, f32[8,16,8,128]{3,2,1,0:T(8,128)S(1)}, u32[]{:S(2)}, u32[]{:S(2)}) collective-permute-start(f32[8,16,8,128]{3,2,1,0:T(8,128)S(1)} %get-tuple-element.38), channel_id=1, source_target_pairs={{0,128},{8,136},{16,144},{24,152},{32,160},{40,168},{48,176},{56,1... | collective-permute-start | bytes 1572872 | tf_op jit(solution)/shard_map/ppermute | solution.py:372
  40.7 18.4 %collective-permute-start.11 = (f32[8,16,8,128]{3,2,1,0:T(8,128)S(1)}, f32[8,16,8,128]{3,2,1,0:T(8,128)S(1)}, u32[]{:S(2)}, u32[]{:S(2)}) collective-permute-start(f32[8,16,8,128]{3,2,1,0:T(8,128)S(1)} %get-tuple-element.56), channel_id=1, source_target_pairs={{0,8},{8,0},{16,24},{24,16},{32,40},{40,32},{48,56},{56,48},{64,72... | collective-permute-start | bytes 1572872 | tf_op jit(solution)/shard_map/ppermute | solution.py:372
  56.0 2.3 %copy-start = (f32[5,4,2,128,128]{4,3,2,1,0:T(8,128)S(1)}, f32[5,4,2,128,128]{4,3,2,1,0:T(8,128)}, u32[]{:S(2)}) copy-start(f32[5,4,2,128,128]{4,3,2,1,0:T(8,128)} %gates_ref.1) | copy-start | bytes 7864324
  58.3 5.8 %collective-permute-start.1 = (f32[8,16,8,128]{3,2,1,0:T(8,128)S(1)}, f32[8,16,8,128]{3,2,1,0:T(8,128)S(1)}, u32[]{:S(2)}, u32[]{:S(2)}) collective-permute-start(f32[8,16,8,128]{3,2,1,0:T(8,128)S(1)} %get-tuple-element.40), channel_id=1, source_target_pairs={{0,8},{8,0},{16,24},{24,16},{32,40},{40,32},{48,56},{56,48},{64,72... | collective-permute-start | bytes 1572872 | tf_op jit(solution)/shard_map/ppermute | solution.py:372
  63.3 5.1 %collective-permute-start.12 = (f32[16,8,8,128]{3,2,1,0:T(8,128)S(1)}, f32[16,8,8,128]{3,2,1,0:T(8,128)S(1)}, u32[]{:S(2)}, u32[]{:S(2)}) collective-permute-start(f32[16,8,8,128]{3,2,1,0:T(8,128)S(1)} %get-tuple-element.58), channel_id=1, source_target_pairs={{0,8},{8,0},{16,24},{24,16},{32,40},{40,32},{48,56},{56,48},{64,72... | collective-permute-start | bytes 1572872 | tf_op jit(solution)/shard_map/ppermute | solution.py:372
  68.2 9.8 %collective-permute-start.2 = (f32[16,8,8,128]{3,2,1,0:T(8,128)S(1)}, f32[16,8,8,128]{3,2,1,0:T(8,128)S(1)}, u32[]{:S(2)}, u32[]{:S(2)}) collective-permute-start(f32[16,8,8,128]{3,2,1,0:T(8,128)S(1)} %get-tuple-element.42), channel_id=1, source_target_pairs={{0,8},{8,0},{16,24},{24,16},{32,40},{40,32},{48,56},{56,48},{64,72... | collective-permute-start | bytes 1572872 | tf_op jit(solution)/shard_map/ppermute | solution.py:372
  68.4 46.7 %copy-start.2 = (s32[32]{0:T(128)S(1)}, s32[32]{0:T(128)}, u32[]{:S(2)}) copy-start(s32[32]{0:T(128)} %refs_0_.5) | copy-start | bytes 388
  68.4 16.8 %collective-permute-start.13 = (f32[2,4,8,8,128]{4,3,2,1,0:T(8,128)S(1)}, f32[2,4,8,8,128]{4,3,2,1,0:T(8,128)S(1)}, u32[]{:S(2)}, u32[]{:S(2)}) collective-permute-start(f32[2,4,8,8,128]{4,3,2,1,0:T(8,128)S(1)} %get-tuple-element.60), channel_id=1, source_target_pairs={{0,64},{8,72},{16,80},{24,88},{32,96},{40,104},{48,112},{56,120},{... | collective-permute-start | bytes 786440 | tf_op jit(solution)/shard_map/ppermute | solution.py:380
  68.5 19.5 %collective-permute-start.14 = (f32[2,4,8,8,128]{4,3,2,1,0:T(8,128)S(1)}, f32[2,4,8,8,128]{4,3,2,1,0:T(8,128)S(1)}, u32[]{:S(2)}, u32[]{:S(2)}) collective-permute-start(f32[2,4,8,8,128]{4,3,2,1,0:T(8,128)S(1)} %get-tuple-element.61), channel_id=1, source_target_pairs={{0,128},{8,136},{16,144},{24,152},{32,160},{40,168},{48,176},{56,1... | collective-permute-start | bytes 786440 | tf_op jit(solution)/shard_map/ppermute | solution.py:380
  74.0 21.4 %collective-permute-start.15 = (f32[2,4,8,8,128]{4,3,2,1,0:T(8,128)S(1)}, f32[2,4,8,8,128]{4,3,2,1,0:T(8,128)S(1)}, u32[]{:S(2)}, u32[]{:S(2)}) collective-permute-start(f32[2,4,8,8,128]{4,3,2,1,0:T(8,128)S(1)} %get-tuple-element.62), channel_id=1, source_target_pairs={{0,192},{8,200},{16,208},{24,216},{32,224},{40,232},{48,240},{56,2... | collective-permute-start | bytes 786440 | tf_op jit(solution)/shard_map/ppermute | solution.py:380
  78.2 20.8 %collective-permute-start.3 = (f32[2,4,8,8,128]{4,3,2,1,0:T(8,128)S(1)}, f32[2,4,8,8,128]{4,3,2,1,0:T(8,128)S(1)}, u32[]{:S(2)}, u32[]{:S(2)}) collective-permute-start(f32[2,4,8,8,128]{4,3,2,1,0:T(8,128)S(1)} %get-tuple-element.44), channel_id=1, source_target_pairs={{0,16},{8,24},{16,32},{24,40},{32,48},{40,56},{48,0},{56,8},{64,80... | collective-permute-start | bytes 786440 | tf_op jit(solution)/shard_map/ppermute | solution.py:380
  79.4 22.0 %collective-permute-start.4 = (f32[2,4,8,8,128]{4,3,2,1,0:T(8,128)S(1)}, f32[2,4,8,8,128]{4,3,2,1,0:T(8,128)S(1)}, u32[]{:S(2)}, u32[]{:S(2)}) collective-permute-start(f32[2,4,8,8,128]{4,3,2,1,0:T(8,128)S(1)} %get-tuple-element.45), channel_id=1, source_target_pairs={{0,32},{8,40},{16,48},{24,56},{32,0},{40,8},{48,16},{56,24},{64,96... | collective-permute-start | bytes 786440 | tf_op jit(solution)/shard_map/ppermute | solution.py:380
  85.3 16.2 %collective-permute-start.5 = (f32[2,4,8,8,128]{4,3,2,1,0:T(8,128)S(1)}, f32[2,4,8,8,128]{4,3,2,1,0:T(8,128)S(1)}, u32[]{:S(2)}, u32[]{:S(2)}) collective-permute-start(f32[2,4,8,8,128]{4,3,2,1,0:T(8,128)S(1)} %get-tuple-element.46), channel_id=1, source_target_pairs={{0,48},{8,56},{16,0},{24,8},{32,16},{40,24},{48,32},{56,40},{64,11... | collective-permute-start | bytes 786440 | tf_op jit(solution)/shard_map/ppermute | solution.py:380
  95.5 15.5 %collective-permute-start.16 = (f32[2,4,8,8,128]{4,3,2,1,0:T(8,128)S(1)}, f32[2,4,8,8,128]{4,3,2,1,0:T(8,128)S(1)}, u32[]{:S(2)}, u32[]{:S(2)}) collective-permute-start(f32[2,4,8,8,128]{4,3,2,1,0:T(8,128)S(1)} %get-tuple-element.64), channel_id=1, source_target_pairs={{0,16},{8,24},{16,32},{24,40},{32,48},{40,56},{48,0},{56,8},{64,80... | collective-permute-start | bytes 786440 | tf_op jit(solution)/shard_map/ppermute | solution.py:380
  96.8 19.1 %collective-permute-start.17 = (f32[2,4,8,8,128]{4,3,2,1,0:T(8,128)S(1)}, f32[2,4,8,8,128]{4,3,2,1,0:T(8,128)S(1)}, u32[]{:S(2)}, u32[]{:S(2)}) collective-permute-start(f32[2,4,8,8,128]{4,3,2,1,0:T(8,128)S(1)} %get-tuple-element.65), channel_id=1, source_target_pairs={{0,32},{8,40},{16,48},{24,56},{32,0},{40,8},{48,16},{56,24},{64,96... | collective-permute-start | bytes 786440 | tf_op jit(solution)/shard_map/ppermute | solution.py:380
  98.9 17.0 %collective-permute-start.18 = (f32[2,4,8,8,128]{4,3,2,1,0:T(8,128)S(1)}, f32[2,4,8,8,128]{4,3,2,1,0:T(8,128)S(1)}, u32[]{:S(2)}, u32[]{:S(2)}) collective-permute-start(f32[2,4,8,8,128]{4,3,2,1,0:T(8,128)S(1)} %get-tuple-element.66), channel_id=1, source_target_pairs={{0,48},{8,56},{16,0},{24,8},{32,16},{40,24},{48,32},{56,40},{64,11... | collective-permute-start | bytes 786440 | tf_op jit(solution)/shard_map/ppermute | solution.py:380
  101.5 25.4 %collective-permute-start.6 = (f32[2,4,8,8,128]{4,3,2,1,0:T(8,128)S(1)}, f32[2,4,8,8,128]{4,3,2,1,0:T(8,128)S(1)}, u32[]{:S(2)}, u32[]{:S(2)}) collective-permute-start(f32[2,4,8,8,128]{4,3,2,1,0:T(8,128)S(1)} %get-tuple-element.48), channel_id=1, source_target_pairs={{0,64},{8,72},{16,80},{24,88},{32,96},{40,104},{48,112},{56,120},{... | collective-permute-start | bytes 786440 | tf_op jit(solution)/shard_map/ppermute | solution.py:380
  106.8 20.0 %collective-permute-start.7 = (f32[2,4,8,8,128]{4,3,2,1,0:T(8,128)S(1)}, f32[2,4,8,8,128]{4,3,2,1,0:T(8,128)S(1)}, u32[]{:S(2)}, u32[]{:S(2)}) collective-permute-start(f32[2,4,8,8,128]{4,3,2,1,0:T(8,128)S(1)} %get-tuple-element.49), channel_id=1, source_target_pairs={{0,128},{8,136},{16,144},{24,152},{32,160},{40,168},{48,176},{56,1... | collective-permute-start | bytes 786440 | tf_op jit(solution)/shard_map/ppermute | solution.py:380
  111.0 21.3 %collective-permute-start.8 = (f32[2,4,8,8,128]{4,3,2,1,0:T(8,128)S(1)}, f32[2,4,8,8,128]{4,3,2,1,0:T(8,128)S(1)}, u32[]{:S(2)}, u32[]{:S(2)}) collective-permute-start(f32[2,4,8,8,128]{4,3,2,1,0:T(8,128)S(1)} %get-tuple-element.50), channel_id=1, source_target_pairs={{0,192},{8,200},{16,208},{24,216},{32,224},{40,232},{48,240},{56,2... | collective-permute-start | bytes 786440 | tf_op jit(solution)/shard_map/ppermute | solution.py:380
  118.2 19.0 %collective-permute-start.19 = (f32[8,16,8,128]{3,2,1,0:T(8,128)S(1)}, f32[8,16,8,128]{3,2,1,0:T(8,128)S(1)}, u32[]{:S(2)}, u32[]{:S(2)}) collective-permute-start(f32[8,16,8,128]{3,2,1,0:T(8,128)S(1)} %get-tuple-element.68), channel_id=1, source_target_pairs={{0,4},{1,5},{2,6},{3,7},{4,0},{5,1},{6,2},{7,3},{8,12},{9,13},{10,... | collective-permute-start | bytes 1572872 | tf_op jit(solution)/shard_map/ppermute | solution.py:372
  134.6 14.5 %collective-permute-start.9 = (f32[8,16,8,128]{3,2,1,0:T(8,128)S(1)}, f32[8,16,8,128]{3,2,1,0:T(8,128)S(1)}, u32[]{:S(2)}, u32[]{:S(2)}) collective-permute-start(f32[8,16,8,128]{3,2,1,0:T(8,128)S(1)} %get-tuple-element.52), channel_id=1, source_target_pairs={{0,4},{1,5},{2,6},{3,7},{4,0},{5,1},{6,2},{7,3},{8,12},{9,13},{10,... | collective-permute-start | bytes 1572872 | tf_op jit(solution)/shard_map/ppermute | solution.py:372

commit v5 on v4

--- a/solution.py
+++ b/solution.py
@@ -168,11 +168,11 @@
         for top in range(2):
             rows = [state_ref[c, pl.ds(1024 * top + p, HALF, stride=16), :] for c in range(2)]
             tops.append(cross(rows[0], rows[1], 64))
-        sides = [cross(tops[0][b], tops[1][b], 32) for b in range(2)]
-        for h in range(2):
-            stays, leaves = in_order(own, sides[0][h], sides[1][h])
-            outs[2 * h][:, p] = stays.reshape(8, 8, GD)
-            outs[2 * h + 1][:, p] = leaves.reshape(8, 8, GD)
+        sides = [cross(tops[0][b], tops[1][b], 32)[0] for b in range(2)]
+        for out, side in zip(outs[:2], in_order(own, *sides)):
+            out[:, p] = side.reshape(8, 8, GD)
+        for top in range(2):
+            outs[2][8 * top : 8 * top + 8, p] = cross(*tops[top], 32)[1].reshape(8, 8, GD)
         return carry
 
     lax.fori_loop(0, 16, some, 0, unroll=8)
@@ -182,9 +182,9 @@
     vmem = pl.BlockSpec(memory_space=pltpu.VMEM)
     return pl.pallas_call(
         pack_kernel,
-        out_shape=[jax.ShapeDtypeStruct(PART, F32)] * 4,
+        out_shape=[jax.ShapeDtypeStruct(shape, F32) for shape in (PART, PART, STATE)],
         in_specs=[vmem],
-        out_specs=[vmem] * 4,
+        out_specs=[vmem] * 3,
         cost_estimate=pl.CostEstimate(flops=0, bytes_accessed=4 << 20, transcendentals=0),
         compiler_params=pltpu.CompilerParams(vmem_limit_bytes=LIMIT),
         name="pack",
@@ -211,12 +211,23 @@
     sign = jnp.where(lane < HALF, -1.0, 1.0)
     upper = lax.broadcasted_iota(jnp.int32, (1, 8, GD), 1) >= 4
 
+    own = lax.axis_index("row") >> 4 == 1
+
     def load_start(i):
-        own = lax.axis_index("row") >> 4 == 1
         blocks = []
         for p in (2 * i, 2 * i + 1):
             sides = in_order(own, ins[0][:, p].reshape(HALF, GD), ins[1][:, p].reshape(HALF, GD))
             blocks.append(jnp.concatenate(cross(*sides, 32), axis=0))
+        return blocks
+
+    def load_whole(i):
+        return [ins[0][:, p].reshape(GD, GD) for p in (2 * i, 2 * i + 1)]
+
+    def load_join(i):
+        blocks = []
+        for p in (2 * i, 2 * i + 1):
+            sides = in_order(own, ins[0][:, p].reshape(HALF, GD), ins[1][:, p].reshape(HALF, GD))
+            blocks.append(jnp.concatenate(sides, axis=0))
         return blocks
 
     def load_turn(i):
@@ -259,6 +270,8 @@
         "start": load_start,
         "pair": load_pair,
         "turn": load_turn,
+        "whole": load_whole,
+        "join": load_join,
         "remap": load_remap,
     }[source[0]]
 
@@ -286,6 +299,11 @@
             for p, piece in zip((2 * i, 2 * i + 1), pieces):
                 outs[0][:, p] = piece[:HALF].reshape(8, 8, GD)
                 outs[1][:, p] = piece[HALF:].reshape(8, 8, GD)
+        elif target == "leave":
+            for p, piece in zip((2 * i, 2 * i + 1), pieces):
+                sides = in_order(own, *cross(piece[:HALF], piece[HALF:], 32))
+                for out, side in zip(outs, sides):
+                    out[:, p] = side.reshape(8, 8, GD)
         elif target == "remap":
             even, odd = (piece.reshape(16, 8, GD) for piece in pieces)
             outs[0][:, i] = jnp.where(upper, pltpu.roll(odd, 4, 1), even)
@@ -320,7 +338,7 @@
 
 
 def run_segment(source, target, w, ins, extra=(), unroll=8):
-    if target == "pair":
+    if target in ("pair", "leave"):
         out_shape = [jax.ShapeDtypeStruct(PART, F32)] * 2
     elif target == "remap":
         out_shape = [jax.ShapeDtypeStruct((16, 8, 8, 128), F32)] * 2
@@ -411,13 +429,19 @@
     low = low_weights(gate_matrices)
     halves = (0, 1)
     kept, sent, got = {}, {}, {}
-    stays_0, leaves_0, stays_1, leaves_1 = pack(state)
-    pairs = ([stays_0, flip(leaves_0, "row", 16)], [stays_1, flip(leaves_1, "row", 16)])
+    stays, leaves, whole = pack(state)
+    firsts = ("start",), [stays, flip(leaves, "row", 16)]
     for h in halves:
-        kept[h], out = run_segment(("start",), "pair", w[0], pairs[h])
+        source, ins = firsts if h == 0 else (("whole",), [whole])
+        kept[h], out = run_segment(source, "pair", w[0], ins)
         sent[h] = flip(out, "row", 1)
-        (whole,) = run_segment(("pair",), "plain", w[1], [kept[h], sent[h]])
-        near, far = run_segment(("turn",), "remap", w[2], [whole])
+        pair = [kept[h], sent[h]]
+        if h == 0:
+            pair = run_segment(("pair",), "plain", w[1], pair)
+        else:
+            stays, leaves = run_segment(("pair",), "leave", w[1], pair)
+            pair = [stays, flip(leaves, "row", 16)]
+        near, far = run_segment(("turn", "join")[h : h + 1], "remap", w[2], pair)
         pair = [near, flip(far, "row", 1)]
         if h == 0:
             moved = shift_z(regroup("by_z", pair))

time: 154 us -> 155 us (level)
  the two profiles are of different devices: /device:TPU:52 before, /device:TPU:1 now
where the time goes in v5:
time: 155 us; the launch traced here: 154 us
  starting transfers between devices  68.8 us (44%)
  waiting for transfers between devices  50.2 us (32%)
  Pallas kernels  32.1 us (21%)
  local copies, waits for them, and re-layouts  2.67 us (2%)
    ppermute x12, starting transfers between devices, shift_row(): return lax.ppermute(value, 'row', pairs)  36.5 us
    ppermute x8, starting transfers between devices, flip(): lax.ppermute(value, axis, [(s, s ^ mask) for s in range(lax.axis_size(axi...  32.3 us
    ppermute x12, waiting for transfers between devices, shift_row(): return lax.ppermute(value, 'row', pairs)  27.5 us
    pallas_call x10, Pallas kernels, run_segment(): pl.pallas_call(functools.partial(segment_kernel, source, target, len(args...  25.5 us
    ppermute x8, waiting for transfers between devices, flip(): lax.ppermute(value, axis, [(s, s ^ mask) for s in range(lax.axis_size(axi...  22.7 us
  transfers between devices with their start and end apart: 20, of which 9 were waited for; matrix products, arithmetic and copies ran while one was open for 1% of the time, Pallas kernels for 17%

profile of v5, /device:TPU:1, one launch (start us, length us, event | category | flops | bytes accessed | tf_op | source)
XLA Modules:
  0.0 153.9 jit_solution(12176535265263202263)
XLA Ops:
  1.6 2.2 %pack.1 = (f32[8,16,8,128]{3,2,1,0:T(8,128)S(1)}, f32[8,16,8,128]{3,2,1,0:T(8,128)S(1)}, f32[16,16,8,128]{3,2,1,0:T(8,128)S(1)}) custom-call(f32[2,2048,128]{2,1,0:T(8,128)S(1)} %bitcast.2), custom_call_target="tpu_custom_call" | custom-call | bytes 4194304 | tf_op jit(solution)/shard_map/pack/pallas_call | solution.py:183
  3.8 7.8 %collective-permute-start.10 = (f32[8,16,8,128]{3,2,1,0:T(8,128)S(1)}, f32[8,16,8,128]{3,2,1,0:T(8,128)S(1)}, u32[]{:S(2)}, u32[]{:S(2)}) collective-permute-start(f32[8,16,8,128]{3,2,1,0:T(8,128)S(1)} %get-tuple-element.56), channel_id=1, source_target_pairs={{0,128},{8,136},{16,144},{24,152},{32,160},{40,168},{48,176},{56,1... | collective-permute-start | bytes 1572872 | tf_op jit(solution)/shard_map/ppermute | solution.py:390
  13.1 2.0 %shard_map.42 = (f32[8,16,8,128]{3,2,1,0:T(8,128)S(1)}, f32[8,16,8,128]{3,2,1,0:T(8,128)S(1)}) custom-call(bf16[3,256,256]{2,1,0:T(8,128)(2,1)S(1)} %shard_map.41.refs_0_, f32[16,16,8,128]{3,2,1,0:T(8,128)S(1)} %get-tuple-element.38.refs_1_), custom_call_target="tpu_custom_call" | custom-call | flops 1207959552 | bytes 3145728 | tf_op jit(solution)/shard_map/pallas_call | solution.py:353
  16.1 8.8 %collective-permute-done.10.refs_2_ = f32[8,16,8,128]{3,2,1,0:T(8,128)S(1)} collective-permute-done((f32[8,16,8,128]{3,2,1,0:T(8,128)S(1)}, f32[8,16,8,128]{3,2,1,0:T(8,128)S(1)}, u32[]{:S(2)}, u32[]{:S(2)}) %collective-permute-start.10) | collective-permute-done | bytes 524320 | tf_op jit(solution)/shard_map/ppermute | solution.py:390
  24.9 2.2 %shard_map.48 = (f32[8,16,8,128]{3,2,1,0:T(8,128)S(1)}, f32[8,16,8,128]{3,2,1,0:T(8,128)S(1)}) custom-call(bf16[3,256,256]{2,1,0:T(8,128)(2,1)S(1)} %shard_map.41.refs_0_, f32[8,16,8,128]{3,2,1,0:T(8,128)S(1)} %get-tuple-element.55.refs_1_, f32[8,16,8,128]{3,2,1,0:T(8,128)S(1)} %collective-permute-done.10.refs_2_), custom_call_target="tpu_custom_call" | custom-call | flops 1207959552 | bytes 3145728 | tf_op jit(solution)/shard_map/pallas_call | solution.py:353
  27.2 1.9 %collective-permute-start.11 = (f32[8,16,8,128]{3,2,1,0:T(8,128)S(1)}, f32[8,16,8,128]{3,2,1,0:T(8,128)S(1)}, u32[]{:S(2)}, u32[]{:S(2)}) collective-permute-start(f32[8,16,8,128]{3,2,1,0:T(8,128)S(1)} %get-tuple-element.58), channel_id=1, source_target_pairs={{0,8},{8,0},{16,24},{24,16},{32,40},{40,32},{48,56},{56,48},{64,72... | collective-permute-start | bytes 1572872 | tf_op jit(solution)/shard_map/ppermute | solution.py:390
  29.4 2.1 %shard_map.43 = (f32[8,16,8,128]{3,2,1,0:T(8,128)S(1)}, f32[8,16,8,128]{3,2,1,0:T(8,128)S(1)}) custom-call(bf16[3,256,256]{2,1,0:T(8,128)(2,1)S(1)} %shard_map.40.refs_0_, f32[8,16,8,128]{3,2,1,0:T(8,128)S(1)} %get-tuple-element.39.refs_1_, f32[8,16,8,128]{3,2,1,0:T(8,128)S(1)} %collective-permute-done.refs_2_), custom_call_target="tpu_custom_call" | custom-call | flops 1207959552 | bytes 3145728 | tf_op jit(solution)/shard_map/pallas_call | solution.py:353
  31.6 14.0 %collective-permute-start.1 = (f32[8,16,8,128]{3,2,1,0:T(8,128)S(1)}, f32[8,16,8,128]{3,2,1,0:T(8,128)S(1)}, u32[]{:S(2)}, u32[]{:S(2)}) collective-permute-start(f32[8,16,8,128]{3,2,1,0:T(8,128)S(1)} %get-tuple-element.42), channel_id=1, source_target_pairs={{0,128},{8,136},{16,144},{24,152},{32,160},{40,168},{48,176},{56,1... | collective-permute-start | bytes 1572872 | tf_op jit(solution)/shard_map/ppermute | solution.py:390
  46.0 2.0 %shard_map.49.refs_1_ = f32[16,16,8,128]{3,2,1,0:T(8,128)S(1)} custom-call(bf16[3,256,256]{2,1,0:T(8,128)(2,1)S(1)} %shard_map.40.refs_0_, f32[8,16,8,128]{3,2,1,0:T(8,128)S(1)} %get-tuple-element.57.refs_1_, f32[8,16,8,128]{3,2,1,0:T(8,128)S(1)} %collective-permute-done.11.refs_2_), custom_call_target="tpu_custom_call" | custom-call | flops 1207959552 | bytes 3145728 | tf_op jit(solution)/shard_map/pallas_call | solution.py:353
  48.0 2.2 %shard_map.50 = (f32[16,8,8,128]{3,2,1,0:T(8,128)S(1)}, f32[16,8,8,128]{3,2,1,0:T(8,128)S(1)}) custom-call(bf16[3,256,256]{2,1,0:T(8,128)(2,1)S(1)} %shard_map.39.refs_0_, f32[16,16,8,128]{3,2,1,0:T(8,128)S(1)} %shard_map.49.refs_1_), custom_call_target="tpu_custom_call" | custom-call | flops 1207959552 | bytes 3145728 | tf_op jit(solution)/shard_map/pallas_call | solution.py:353
  50.6 8.6 %collective-permute-done.1.refs_2_ = f32[8,16,8,128]{3,2,1,0:T(8,128)S(1)} collective-permute-done((f32[8,16,8,128]{3,2,1,0:T(8,128)S(1)}, f32[8,16,8,128]{3,2,1,0:T(8,128)S(1)}, u32[]{:S(2)}, u32[]{:S(2)}) %collective-permute-start.1) | collective-permute-done | bytes 524320 | tf_op jit(solution)/shard_map/ppermute | solution.py:390
  59.1 2.0 %shard_map.44 = (f32[16,8,8,128]{3,2,1,0:T(8,128)S(1)}, f32[16,8,8,128]{3,2,1,0:T(8,128)S(1)}) custom-call(bf16[3,256,256]{2,1,0:T(8,128)(2,1)S(1)} %shard_map.39.refs_0_, f32[8,16,8,128]{3,2,1,0:T(8,128)S(1)} %get-tuple-element.41.refs_1_, f32[8,16,8,128]{3,2,1,0:T(8,128)S(1)} %collective-permute-done.1.refs_2_), custom_call_target="tpu_custom_call" | custom-call | flops 1207959552 | bytes 3145728 | tf_op jit(solution)/shard_map/pallas_call | solution.py:353
  62.1 12.2 %collective-permute-start.13 = (f32[2,4,8,8,128]{4,3,2,1,0:T(8,128)S(1)}, f32[2,4,8,8,128]{4,3,2,1,0:T(8,128)S(1)}, u32[]{:S(2)}, u32[]{:S(2)}) collective-permute-start(f32[2,4,8,8,128]{4,3,2,1,0:T(8,128)S(1)} %get-tuple-element.62), channel_id=1, source_target_pairs={{0,64},{8,72},{16,80},{24,88},{32,96},{40,104},{48,112},{56,120},{... | collective-permute-start | bytes 786440 | tf_op jit(solution)/shard_map/ppermute | solution.py:398
  74.3 4.6 %collective-permute-start.14 = (f32[2,4,8,8,128]{4,3,2,1,0:T(8,128)S(1)}, f32[2,4,8,8,128]{4,3,2,1,0:T(8,128)S(1)}, u32[]{:S(2)}, u32[]{:S(2)}) collective-permute-start(f32[2,4,8,8,128]{4,3,2,1,0:T(8,128)S(1)} %get-tuple-element.63), channel_id=1, source_target_pairs={{0,128},{8,136},{16,144},{24,152},{32,160},{40,168},{48,176},{56,1... | collective-permute-start | bytes 786440 | tf_op jit(solution)/shard_map/ppermute | solution.py:398
  78.8 2.2 %collective-permute-start.15 = (f32[2,4,8,8,128]{4,3,2,1,0:T(8,128)S(1)}, f32[2,4,8,8,128]{4,3,2,1,0:T(8,128)S(1)}, u32[]{:S(2)}, u32[]{:S(2)}) collective-permute-start(f32[2,4,8,8,128]{4,3,2,1,0:T(8,128)S(1)} %get-tuple-element.64), channel_id=1, source_target_pairs={{0,192},{8,200},{16,208},{24,216},{32,224},{40,232},{48,240},{56,2... | collective-permute-start | bytes 786440 | tf_op jit(solution)/shard_map/ppermute | solution.py:398
  82.3 2.5 %collective-permute-start.4 = (f32[2,4,8,8,128]{4,3,2,1,0:T(8,128)S(1)}, f32[2,4,8,8,128]{4,3,2,1,0:T(8,128)S(1)}, u32[]{:S(2)}, u32[]{:S(2)}) collective-permute-start(f32[2,4,8,8,128]{4,3,2,1,0:T(8,128)S(1)} %get-tuple-element.47), channel_id=1, source_target_pairs={{0,32},{8,40},{16,48},{24,56},{32,0},{40,8},{48,16},{56,24},{64,96... | collective-permute-start | bytes 786440 | tf_op jit(solution)/shard_map/ppermute | solution.py:398
  84.8 2.4 %collective-permute-done.13.refs_1_ = f32[2,4,8,8,128]{4,3,2,1,0:T(8,128)S(1)} collective-permute-done((f32[2,4,8,8,128]{4,3,2,1,0:T(8,128)S(1)}, f32[2,4,8,8,128]{4,3,2,1,0:T(8,128)S(1)}, u32[]{:S(2)}, u32[]{:S(2)}) %collective-permute-start.13) | collective-permute-done | bytes 262176 | tf_op jit(solution)/shard_map/ppermute | solution.py:398
  87.2 2.5 %collective-permute-start.5 = (f32[2,4,8,8,128]{4,3,2,1,0:T(8,128)S(1)}, f32[2,4,8,8,128]{4,3,2,1,0:T(8,128)S(1)}, u32[]{:S(2)}, u32[]{:S(2)}) collective-permute-start(f32[2,4,8,8,128]{4,3,2,1,0:T(8,128)S(1)} %get-tuple-element.48), channel_id=1, source_target_pairs={{0,48},{8,56},{16,0},{24,8},{32,16},{40,24},{48,32},{56,40},{64,11... | collective-permute-start | bytes 786440 | tf_op jit(solution)/shard_map/ppermute | solution.py:398
  89.6 11.7 %collective-permute-done.14.refs_2_ = f32[2,4,8,8,128]{4,3,2,1,0:T(8,128)S(1)} collective-permute-done((f32[2,4,8,8,128]{4,3,2,1,0:T(8,128)S(1)}, f32[2,4,8,8,128]{4,3,2,1,0:T(8,128)S(1)}, u32[]{:S(2)}, u32[]{:S(2)}) %collective-permute-start.14) | collective-permute-done | bytes 262176 | tf_op jit(solution)/shard_map/ppermute | solution.py:398
  102.7 2.5 %collective-permute-start.17 = (f32[2,4,8,8,128]{4,3,2,1,0:T(8,128)S(1)}, f32[2,4,8,8,128]{4,3,2,1,0:T(8,128)S(1)}, u32[]{:S(2)}, u32[]{:S(2)}) collective-permute-start(f32[2,4,8,8,128]{4,3,2,1,0:T(8,128)S(1)} %get-tuple-element.67), channel_id=1, source_target_pairs={{0,32},{8,40},{16,48},{24,56},{32,0},{40,8},{48,16},{56,24},{64,96... | collective-permute-start | bytes 786440 | tf_op jit(solution)/shard_map/ppermute | solution.py:398
  106.4 3.4 %collective-permute-start.7 = (f32[2,4,8,8,128]{4,3,2,1,0:T(8,128)S(1)}, f32[2,4,8,8,128]{4,3,2,1,0:T(8,128)S(1)}, u32[]{:S(2)}, u32[]{:S(2)}) collective-permute-start(f32[2,4,8,8,128]{4,3,2,1,0:T(8,128)S(1)} %get-tuple-element.51), channel_id=1, source_target_pairs={{0,128},{8,136},{16,144},{24,152},{32,160},{40,168},{48,176},{56,1... | collective-permute-start | bytes 786440 | tf_op jit(solution)/shard_map/ppermute | solution.py:398
  110.1 3.0 %collective-permute-start.8 = (f32[2,4,8,8,128]{4,3,2,1,0:T(8,128)S(1)}, f32[2,4,8,8,128]{4,3,2,1,0:T(8,128)S(1)}, u32[]{:S(2)}, u32[]{:S(2)}) collective-permute-start(f32[2,4,8,8,128]{4,3,2,1,0:T(8,128)S(1)} %get-tuple-element.52), channel_id=1, source_target_pairs={{0,192},{8,200},{16,208},{24,216},{32,224},{40,232},{48,240},{56,2... | collective-permute-start | bytes 786440 | tf_op jit(solution)/shard_map/ppermute | solution.py:398
  114.0 2.6 %collective-permute-done.17.refs_3_ = f32[2,4,8,8,128]{4,3,2,1,0:T(8,128)S(1)} collective-permute-done((f32[2,4,8,8,128]{4,3,2,1,0:T(8,128)S(1)}, f32[2,4,8,8,128]{4,3,2,1,0:T(8,128)S(1)}, u32[]{:S(2)}, u32[]{:S(2)}) %collective-permute-start.17) | collective-permute-done | bytes 262176 | tf_op jit(solution)/shard_map/ppermute | solution.py:398
  116.6 2.2 %shard_map.53 = (f32[8,16,8,128]{3,2,1,0:T(8,128)S(1)}, f32[8,16,8,128]{3,2,1,0:T(8,128)S(1)}) custom-call(bf16[3,256,256]{2,1,0:T(8,128)(2,1)S(1)} %shard_map.38.refs_0_, f32[2,4,8,8,128]{4,3,2,1,0:T(8,128)S(1)} %get-tuple-element.65.refs_1_, f32[2,4,8,8,128]{4,3,2,1,0:T(8,128)S(1)} %collective-permute-done.16.refs_2_, ...), custom_call_target="tpu_custom_call" | custom-call | flops 1207959552 | bytes 3145728 | tf_op jit(solution)/shard_map/pallas_call | solution.py:353
  118.9 3.0 %collective-permute-start.19 = (f32[8,16,8,128]{3,2,1,0:T(8,128)S(1)}, f32[8,16,8,128]{3,2,1,0:T(8,128)S(1)}, u32[]{:S(2)}, u32[]{:S(2)}) collective-permute-start(f32[8,16,8,128]{3,2,1,0:T(8,128)S(1)} %get-tuple-element.70), channel_id=1, source_target_pairs={{0,4},{1,5},{2,6},{3,7},{4,0},{5,1},{6,2},{7,3},{8,12},{9,13},{10,... | collective-permute-start | bytes 1572872 | tf_op jit(solution)/shard_map/ppermute | solution.py:390
  121.9 4.8 %collective-permute-done.7.refs_3_ = f32[2,4,8,8,128]{4,3,2,1,0:T(8,128)S(1)} collective-permute-done((f32[2,4,8,8,128]{4,3,2,1,0:T(8,128)S(1)}, f32[2,4,8,8,128]{4,3,2,1,0:T(8,128)S(1)}, u32[]{:S(2)}, u32[]{:S(2)}) %collective-permute-start.7) | collective-permute-done | bytes 262176 | tf_op jit(solution)/shard_map/ppermute | solution.py:398
  126.7 5.8 %collective-permute-done.8.refs_4_ = f32[2,4,8,8,128]{4,3,2,1,0:T(8,128)S(1)} collective-permute-done((f32[2,4,8,8,128]{4,3,2,1,0:T(8,128)S(1)}, f32[2,4,8,8,128]{4,3,2,1,0:T(8,128)S(1)}, u32[]{:S(2)}, u32[]{:S(2)}) %collective-permute-start.8) | collective-permute-done | bytes 262176 | tf_op jit(solution)/shard_map/ppermute | solution.py:398
  132.5 2.2 %shard_map.47 = (f32[8,16,8,128]{3,2,1,0:T(8,128)S(1)}, f32[8,16,8,128]{3,2,1,0:T(8,128)S(1)}) custom-call(bf16[3,256,256]{2,1,0:T(8,128)(2,1)S(1)} %shard_map.38.refs_0_, f32[2,4,8,8,128]{4,3,2,1,0:T(8,128)S(1)} %get-tuple-element.49.refs_1_, f32[2,4,8,8,128]{4,3,2,1,0:T(8,128)S(1)} %collective-permute-done.6.refs_2_, ...), custom_call_target="tpu_custom_call" | custom-call | flops 1207959552 | bytes 3145728 | tf_op jit(solution)/shard_map/pallas_call | solution.py:353
  134.7 3.3 %collective-permute-start.9 = (f32[8,16,8,128]{3,2,1,0:T(8,128)S(1)}, f32[8,16,8,128]{3,2,1,0:T(8,128)S(1)}, u32[]{:S(2)}, u32[]{:S(2)}) collective-permute-start(f32[8,16,8,128]{3,2,1,0:T(8,128)S(1)} %get-tuple-element.54), channel_id=1, source_target_pairs={{0,4},{1,5},{2,6},{3,7},{4,0},{5,1},{6,2},{7,3},{8,12},{9,13},{10,... | collective-permute-start | bytes 1572872 | tf_op jit(solution)/shard_map/ppermute | solution.py:390
  140.1 4.1 %shard_map.54.refs_3_ = f32[4,512,256]{2,1,0:T(8,128)S(1)} custom-call(bf16[3,256,256]{2,1,0:T(8,128)(2,1)S(1)} %shard_map.37.refs_0_, f32[8,16,8,128]{3,2,1,0:T(8,128)S(1)} %get-tuple-element.69.refs_1_, f32[8,16,8,128]{3,2,1,0:T(8,128)S(1)} %collective-permute-done.19.refs_2_, bf16[2,2,256,256]{3,2,1,0:T(8,128)(2,1)S(1)} %low_weights.1.refs_3_.refs_4_), custom_call_target="tpu_custom_call" | custom-call | flops 1207959552 | bytes 3145728 | tf_op jit(solution)/shard_map/pallas_call | solution.py:353
  144.3 5.3 %collective-permute-done.9.refs_2_ = f32[8,16,8,128]{3,2,1,0:T(8,128)S(1)} collective-permute-done((f32[8,16,8,128]{3,2,1,0:T(8,128)S(1)}, f32[8,16,8,128]{3,2,1,0:T(8,128)S(1)}, u32[]{:S(2)}, u32[]{:S(2)}) %collective-permute-start.9) | collective-permute-done | bytes 524320 | tf_op jit(solution)/shard_map/ppermute | solution.py:390
  149.5 4.4 %shard_map.55 = f32[2,2048,128]{2,1,0:T(8,128)} custom-call(bf16[3,256,256]{2,1,0:T(8,128)(2,1)S(1)} %shard_map.37.refs_0_, f32[8,16,8,128]{3,2,1,0:T(8,128)S(1)} %get-tuple-element.53.refs_1_, f32[8,16,8,128]{3,2,1,0:T(8,128)S(1)} %collective-permute-done.9.refs_2_, f32[4,512,256]{2,1,0:T(8,128)S(1)} %shard_map.54.refs_3_, ...), custom_call_target="tpu_custom_call" | custom-call | flops 1207959552 | bytes 3145728 | tf_op jit(solution)/shard_map/pallas_call | solution.py:353
  (36 shorter events, 13.4 us)
Async XLA Ops:
  0.0 1.6 %copy-start.1 = (f32[2,1,1,262144]{3,2,1,0:T(1,128)S(1)}, f32[2,1,1,262144]{3,2,1,0:T(1,128)}, u32[]{:S(2)}) copy-start(f32[2,1,1,262144]{3,2,1,0:T(1,128)} %param.3) | copy-start | bytes 6291460
  3.8 21.1 %collective-permute-start.10 = (f32[8,16,8,128]{3,2,1,0:T(8,128)S(1)}, f32[8,16,8,128]{3,2,1,0:T(8,128)S(1)}, u32[]{:S(2)}, u32[]{:S(2)}) collective-permute-start(f32[8,16,8,128]{3,2,1,0:T(8,128)S(1)} %get-tuple-element.56), channel_id=1, source_target_pairs={{0,128},{8,136},{16,144},{24,152},{32,160},{40,168},{48,176},{56,1... | collective-permute-start | bytes 1572872 | tf_op jit(solution)/shard_map/ppermute | solution.py:390
  15.1 14.4 %collective-permute-start = (f32[8,16,8,128]{3,2,1,0:T(8,128)S(1)}, f32[8,16,8,128]{3,2,1,0:T(8,128)S(1)}, u32[]{:S(2)}, u32[]{:S(2)}) collective-permute-start(f32[8,16,8,128]{3,2,1,0:T(8,128)S(1)} %get-tuple-element.40), channel_id=1, source_target_pairs={{0,8},{8,0},{16,24},{24,16},{32,40},{40,32},{48,56},{56,48},{64,72... | collective-permute-start | bytes 1572872 | tf_op jit(solution)/shard_map/ppermute | solution.py:390
  24.9 4.2 %copy-start = (f32[5,4,2,128,128]{4,3,2,1,0:T(8,128)S(1)}, f32[5,4,2,128,128]{4,3,2,1,0:T(8,128)}, u32[]{:S(2)}) copy-start(f32[5,4,2,128,128]{4,3,2,1,0:T(8,128)} %gates_ref.1) | copy-start | bytes 7864324
  27.2 18.8 %collective-permute-start.11 = (f32[8,16,8,128]{3,2,1,0:T(8,128)S(1)}, f32[8,16,8,128]{3,2,1,0:T(8,128)S(1)}, u32[]{:S(2)}, u32[]{:S(2)}) collective-permute-start(f32[8,16,8,128]{3,2,1,0:T(8,128)S(1)} %get-tuple-element.58), channel_id=1, source_target_pairs={{0,8},{8,0},{16,24},{24,16},{32,40},{40,32},{48,56},{56,48},{64,72... | collective-permute-start | bytes 1572872 | tf_op jit(solution)/shard_map/ppermute | solution.py:390
  31.6 27.6 %collective-permute-start.1 = (f32[8,16,8,128]{3,2,1,0:T(8,128)S(1)}, f32[8,16,8,128]{3,2,1,0:T(8,128)S(1)}, u32[]{:S(2)}, u32[]{:S(2)}) collective-permute-start(f32[8,16,8,128]{3,2,1,0:T(8,128)S(1)} %get-tuple-element.42), channel_id=1, source_target_pairs={{0,128},{8,136},{16,144},{24,152},{32,160},{40,168},{48,176},{56,1... | collective-permute-start | bytes 1572872 | tf_op jit(solution)/shard_map/ppermute | solution.py:390
  50.2 11.8 %collective-permute-start.12 = (f32[16,8,8,128]{3,2,1,0:T(8,128)S(1)}, f32[16,8,8,128]{3,2,1,0:T(8,128)S(1)}, u32[]{:S(2)}, u32[]{:S(2)}) collective-permute-start(f32[16,8,8,128]{3,2,1,0:T(8,128)S(1)} %get-tuple-element.60), channel_id=1, source_target_pairs={{0,8},{8,0},{16,24},{24,16},{32,40},{40,32},{48,56},{56,48},{64,72... | collective-permute-start | bytes 1572872 | tf_op jit(solution)/shard_map/ppermute | solution.py:390
  61.2 19.8 %collective-permute-start.2 = (f32[16,8,8,128]{3,2,1,0:T(8,128)S(1)}, f32[16,8,8,128]{3,2,1,0:T(8,128)S(1)}, u32[]{:S(2)}, u32[]{:S(2)}) collective-permute-start(f32[16,8,8,128]{3,2,1,0:T(8,128)S(1)} %get-tuple-element.44), channel_id=1, source_target_pairs={{0,8},{8,0},{16,24},{24,16},{32,40},{40,32},{48,56},{56,48},{64,72... | collective-permute-start | bytes 1572872 | tf_op jit(solution)/shard_map/ppermute | solution.py:390
  62.0 51.1 %copy-start.2 = (s32[32]{0:T(128)S(1)}, s32[32]{0:T(128)}, u32[]{:S(2)}) copy-start(s32[32]{0:T(128)} %refs_0_.5) | copy-start | bytes 388
  62.1 25.1 %collective-permute-start.13 = (f32[2,4,8,8,128]{4,3,2,1,0:T(8,128)S(1)}, f32[2,4,8,8,128]{4,3,2,1,0:T(8,128)S(1)}, u32[]{:S(2)}, u32[]{:S(2)}) collective-permute-start(f32[2,4,8,8,128]{4,3,2,1,0:T(8,128)S(1)} %get-tuple-element.62), channel_id=1, source_target_pairs={{0,64},{8,72},{16,80},{24,88},{32,96},{40,104},{48,112},{56,120},{... | collective-permute-start | bytes 786440 | tf_op jit(solution)/shard_map/ppermute | solution.py:398
  74.3 27.1 %collective-permute-start.14 = (f32[2,4,8,8,128]{4,3,2,1,0:T(8,128)S(1)}, f32[2,4,8,8,128]{4,3,2,1,0:T(8,128)S(1)}, u32[]{:S(2)}, u32[]{:S(2)}) collective-permute-start(f32[2,4,8,8,128]{4,3,2,1,0:T(8,128)S(1)} %get-tuple-element.63), channel_id=1, source_target_pairs={{0,128},{8,136},{16,144},{24,152},{32,160},{40,168},{48,176},{56,1... | collective-permute-start | bytes 786440 | tf_op jit(solution)/shard_map/ppermute | solution.py:398
  78.8 22.5 %collective-permute-start.15 = (f32[2,4,8,8,128]{4,3,2,1,0:T(8,128)S(1)}, f32[2,4,8,8,128]{4,3,2,1,0:T(8,128)S(1)}, u32[]{:S(2)}, u32[]{:S(2)}) collective-permute-start(f32[2,4,8,8,128]{4,3,2,1,0:T(8,128)S(1)} %get-tuple-element.64), channel_id=1, source_target_pairs={{0,192},{8,200},{16,208},{24,216},{32,224},{40,232},{48,240},{56,2... | collective-permute-start | bytes 786440 | tf_op jit(solution)/shard_map/ppermute | solution.py:398
  81.1 24.1 %collective-permute-start.3 = (f32[2,4,8,8,128]{4,3,2,1,0:T(8,128)S(1)}, f32[2,4,8,8,128]{4,3,2,1,0:T(8,128)S(1)}, u32[]{:S(2)}, u32[]{:S(2)}) collective-permute-start(f32[2,4,8,8,128]{4,3,2,1,0:T(8,128)S(1)} %get-tuple-element.46), channel_id=1, source_target_pairs={{0,16},{8,24},{16,32},{24,40},{32,48},{40,56},{48,0},{56,8},{64,80... | collective-permute-start | bytes 786440 | tf_op jit(solution)/shard_map/ppermute | solution.py:398
  82.3 23.9 %collective-permute-start.4 = (f32[2,4,8,8,128]{4,3,2,1,0:T(8,128)S(1)}, f32[2,4,8,8,128]{4,3,2,1,0:T(8,128)S(1)}, u32[]{:S(2)}, u32[]{:S(2)}) collective-permute-start(f32[2,4,8,8,128]{4,3,2,1,0:T(8,128)S(1)} %get-tuple-element.47), channel_id=1, source_target_pairs={{0,32},{8,40},{16,48},{24,56},{32,0},{40,8},{48,16},{56,24},{64,96... | collective-permute-start | bytes 786440 | tf_op jit(solution)/shard_map/ppermute | solution.py:398
  87.2 19.1 %collective-permute-start.5 = (f32[2,4,8,8,128]{4,3,2,1,0:T(8,128)S(1)}, f32[2,4,8,8,128]{4,3,2,1,0:T(8,128)S(1)}, u32[]{:S(2)}, u32[]{:S(2)}) collective-permute-start(f32[2,4,8,8,128]{4,3,2,1,0:T(8,128)S(1)} %get-tuple-element.48), channel_id=1, source_target_pairs={{0,48},{8,56},{16,0},{24,8},{32,16},{40,24},{48,32},{56,40},{64,11... | collective-permute-start | bytes 786440 | tf_op jit(solution)/shard_map/ppermute | solution.py:398
  101.4 8.7 %collective-permute-start.16 = (f32[2,4,8,8,128]{4,3,2,1,0:T(8,128)S(1)}, f32[2,4,8,8,128]{4,3,2,1,0:T(8,128)S(1)}, u32[]{:S(2)}, u32[]{:S(2)}) collective-permute-start(f32[2,4,8,8,128]{4,3,2,1,0:T(8,128)S(1)} %get-tuple-element.66), channel_id=1, source_target_pairs={{0,16},{8,24},{16,32},{24,40},{32,48},{40,56},{48,0},{56,8},{64,80... | collective-permute-start | bytes 786440 | tf_op jit(solution)/shard_map/ppermute | solution.py:398
  102.7 13.9 %collective-permute-start.17 = (f32[2,4,8,8,128]{4,3,2,1,0:T(8,128)S(1)}, f32[2,4,8,8,128]{4,3,2,1,0:T(8,128)S(1)}, u32[]{:S(2)}, u32[]{:S(2)}) collective-permute-start(f32[2,4,8,8,128]{4,3,2,1,0:T(8,128)S(1)} %get-tuple-element.67), channel_id=1, source_target_pairs={{0,32},{8,40},{16,48},{24,56},{32,0},{40,8},{48,16},{56,24},{64,96... | collective-permute-start | bytes 786440 | tf_op jit(solution)/shard_map/ppermute | solution.py:398
  105.1 11.5 %collective-permute-start.18 = (f32[2,4,8,8,128]{4,3,2,1,0:T(8,128)S(1)}, f32[2,4,8,8,128]{4,3,2,1,0:T(8,128)S(1)}, u32[]{:S(2)}, u32[]{:S(2)}) collective-permute-start(f32[2,4,8,8,128]{4,3,2,1,0:T(8,128)S(1)} %get-tuple-element.68), channel_id=1, source_target_pairs={{0,48},{8,56},{16,0},{24,8},{32,16},{40,24},{48,32},{56,40},{64,11... | collective-permute-start | bytes 786440 | tf_op jit(solution)/shard_map/ppermute | solution.py:398
  106.4 15.5 %collective-permute-start.6 = (f32[2,4,8,8,128]{4,3,2,1,0:T(8,128)S(1)}, f32[2,4,8,8,128]{4,3,2,1,0:T(8,128)S(1)}, u32[]{:S(2)}, u32[]{:S(2)}) collective-permute-start(f32[2,4,8,8,128]{4,3,2,1,0:T(8,128)S(1)} %get-tuple-element.50), channel_id=1, source_target_pairs={{0,64},{8,72},{16,80},{24,88},{32,96},{40,104},{48,112},{56,120},{... | collective-permute-start | bytes 786440 | tf_op jit(solution)/shard_map/ppermute | solution.py:398
  106.4 20.2 %collective-permute-start.7 = (f32[2,4,8,8,128]{4,3,2,1,0:T(8,128)S(1)}, f32[2,4,8,8,128]{4,3,2,1,0:T(8,128)S(1)}, u32[]{:S(2)}, u32[]{:S(2)}) collective-permute-start(f32[2,4,8,8,128]{4,3,2,1,0:T(8,128)S(1)} %get-tuple-element.51), channel_id=1, source_target_pairs={{0,128},{8,136},{16,144},{24,152},{32,160},{40,168},{48,176},{56,1... | collective-permute-start | bytes 786440 | tf_op jit(solution)/shard_map/ppermute | solution.py:398
  110.1 22.4 %collective-permute-start.8 = (f32[2,4,8,8,128]{4,3,2,1,0:T(8,128)S(1)}, f32[2,4,8,8,128]{4,3,2,1,0:T(8,128)S(1)}, u32[]{:S(2)}, u32[]{:S(2)}) collective-permute-start(f32[2,4,8,8,128]{4,3,2,1,0:T(8,128)S(1)} %get-tuple-element.52), channel_id=1, source_target_pairs={{0,192},{8,200},{16,208},{24,216},{32,224},{40,232},{48,240},{56,2... | collective-permute-start | bytes 786440 | tf_op jit(solution)/shard_map/ppermute | solution.py:398
  118.9 21.3 %collective-permute-start.19 = (f32[8,16,8,128]{3,2,1,0:T(8,128)S(1)}, f32[8,16,8,128]{3,2,1,0:T(8,128)S(1)}, u32[]{:S(2)}, u32[]{:S(2)}) collective-permute-start(f32[8,16,8,128]{3,2,1,0:T(8,128)S(1)} %get-tuple-element.70), channel_id=1, source_target_pairs={{0,4},{1,5},{2,6},{3,7},{4,0},{5,1},{6,2},{7,3},{8,12},{9,13},{10,... | collective-permute-start | bytes 1572872 | tf_op jit(solution)/shard_map/ppermute | solution.py:390
  134.7 14.8 %collective-permute-start.9 = (f32[8,16,8,128]{3,2,1,0:T(8,128)S(1)}, f32[8,16,8,128]{3,2,1,0:T(8,128)S(1)}, u32[]{:S(2)}, u32[]{:S(2)}) collective-permute-start(f32[8,16,8,128]{3,2,1,0:T(8,128)S(1)} %get-tuple-element.54), channel_id=1, source_target_pairs={{0,4},{1,5},{2,6},{3,7},{4,0},{5,1},{6,2},{7,3},{8,12},{9,13},{10,... | collective-permute-start | bytes 1572872 | tf_op jit(solution)/shard_map/ppermute | solution.py:390

commit v6 on v5

--- a/solution.py
+++ b/solution.py
@@ -160,22 +160,44 @@
     return jnp.where(swapped, second, first), jnp.where(swapped, first, second)
 
 
+def turned(blocks):
+    sub = lax.broadcasted_iota(jnp.int32, (1, 8, 1), 1)
+    for step in (1, 2, 4):
+        off = (sub & step) == 0
+        made = [None] * 8
+        for k in range(8):
+            if k & step:
+                continue
+            first, second = blocks[k], blocks[k + step]
+            made[k] = jnp.where(off, first, pltpu.roll(second, step, 1))
+            made[k + step] = jnp.where(off, pltpu.roll(first, 8 - step, 1), second)
+        blocks = made
+    return blocks
+
+
 def pack_kernel(state_ref, *outs):
     own = lax.axis_index("row") >> 4 == 1
 
-    def some(p, carry):
-        tops = []
-        for top in range(2):
-            rows = [state_ref[c, pl.ds(1024 * top + p, HALF, stride=16), :] for c in range(2)]
-            tops.append(cross(rows[0], rows[1], 64))
-        sides = [cross(tops[0][b], tops[1][b], 32)[0] for b in range(2)]
-        for out, side in zip(outs[:2], in_order(own, *sides)):
-            out[:, p] = side.reshape(8, 8, GD)
-        for top in range(2):
-            outs[2][8 * top : 8 * top + 8, p] = cross(*tops[top], 32)[1].reshape(8, 8, GD)
+    def some(a, carry):
+        made = [[], [], [], []]
+        for o in range(8):
+            tops = [cross(state_ref[0, t, a, o], state_ref[1, t, a, o], 64) for t in range(2)]
+            sides = [cross(tops[0][b], tops[1][b], 32)[0] for b in range(2)]
+            for k, side in enumerate(in_order(own, *sides)):
+                made[k].append(side)
+            for t in range(2):
+                made[2 + t].append(cross(*tops[t], 32)[1])
+        for k, blocks in enumerate(made):
+            for low, block in enumerate(turned(blocks)):
+                for high in range(2):
+                    p = 8 * high + low
+                    if k < 2:
+                        outs[k][a, p] = block[high]
+                    else:
+                        outs[2][8 * (k - 2) + a, p] = block[high]
         return carry
 
-    lax.fori_loop(0, 16, some, 0, unroll=8)
+    lax.fori_loop(0, 8, some, 0, unroll=2)
 
 
 def pack(state):
@@ -247,8 +269,6 @@
 
     def load_remap(i):
         def half(c):
-            if source[1] == "by_x":
-                return jnp.stack([ins[x][c, z, i] for z in range(4) for x in range(4)], axis=0)
             return jnp.concatenate([ins[z][c, :, i] for z in range(4)], axis=0)
 
         near, far = half(0), half(1)
@@ -316,7 +336,7 @@
 
     def low_gate(i, carry):
         low_ref = ins[-1]
-        rows = jnp.concatenate([one[:, 4 * i + k].reshape(GD, GD) for k in range(4)], axis=0)
+        rows = one[pl.ds(4 * i, 4)].reshape(512, GD)
         pair = jnp.concatenate(split(rows), axis=1)
         done = jnp.dot(pair, low_ref[source[1], 0], preferred_element_type=F32) + jnp.dot(
             pair, low_ref[source[1], 1], preferred_element_type=F32
@@ -325,10 +345,11 @@
             outs[0][i] = done
             return carry
         done = done + ins[-2][i]
-        for k in range(4):
-            piece = done[GD * k : GD * (k + 1)]
-            outs[0][0, pl.ds(4 * i + k, GD, stride=16), :] = piece[:, :GD]
-            outs[0][1, pl.ds(4 * i + k, GD, stride=16), :] = piece[:, GD:]
+        for c in range(2):
+            part = done[:, GD * c : GD * (c + 1)].reshape(4, 2, 8, 8, GD)
+            blocks = [part[:, :, k].reshape(8, 8, GD) for k in range(8)]
+            for o, block in enumerate(turned(blocks)):
+                outs[0][c, pl.ds(4 * i, 4), o] = block.reshape(4, 2, 8, GD)
         return carry
 
     for step in (top_first, mid, top_last):
@@ -347,7 +368,7 @@
     elif target == "share":
         out_shape = [jax.ShapeDtypeStruct((4, 512, 256), F32)]
     else:
-        out_shape = [jax.ShapeDtypeStruct((2, 2048, 128), F32)]
+        out_shape = [jax.ShapeDtypeStruct((2, 16, 8, 2, 8, 128), F32)]
     args = list(ins) + list(extra)
     vmem = pl.BlockSpec(memory_space=pltpu.VMEM)
     return pl.pallas_call(
@@ -371,7 +392,7 @@
                 if order == "swap":
                     outs[j][c, k] = ins[k][c, j]
                 else:
-                    outs[j][c, k] = ins[c][4 * j + k if order == "by_x" else 4 * k + j]
+                    outs[j][c, k] = ins[c][4 * j + k]
 
 
 def regroup(order, blocks):
@@ -413,7 +434,7 @@
 
 
 def circuit(amplitudes, gate_matrices, permutation):
-    state = amplitudes.reshape(2, 2048, 128)
+    state = amplitudes.reshape(2, 2, 8, 8, 2, 8, 128)
     mid = ("mid", "mid")
     kinds = (
         ((None, None), mid, ("xor2", None)),
@@ -443,14 +464,10 @@
             pair = [stays, flip(leaves, "row", 16)]
         near, far = run_segment(("turn", "join")[h : h + 1], "remap", w[2], pair)
         pair = [near, flip(far, "row", 1)]
-        if h == 0:
-            moved = shift_z(regroup("by_z", pair))
-            got[h] = shift_x(regroup("swap", moved))
-        else:
-            moved = shift_x(regroup("by_x", pair))
-            got[h] = shift_z(regroup("swap", moved))
+        moved = shift_x(regroup("by_x", pair))
+        got[h] = shift_z(regroup("swap", moved))
     for h in halves:
-        kept[h], out = run_segment(("remap", ("by_x", "by_z")[h]), "pair", w[3], got[h])
+        kept[h], out = run_segment(("remap",), "pair", w[3], got[h])
         sent[h] = flip(out, "col", 4)
     (share,) = run_segment(("pair", 0), "share", w[4], [kept[0], sent[0]], [low], unroll=4)
     (out,) = run_segment(("pair", 1), "low", w[4], [kept[1], sent[1]], [share, low])

time: 155 us -> 163 us (1.052)
  the two profiles are of different devices: /device:TPU:1 before, /device:TPU:2 now
where the time goes in v6:
time: 163 us; the launch traced here: 162 us
  starting transfers between devices  66.7 us (41%)
  waiting for transfers between devices  59.5 us (37%)
  Pallas kernels  33.3 us (20%)
  local copies, waits for them, and re-layouts  2.68 us (2%)
    ppermute x12, starting transfers between devices, shift_row(): return lax.ppermute(value, 'row', pairs)  37.8 us
    ppermute x8, waiting for transfers between devices, flip(): lax.ppermute(value, axis, [(s, s ^ mask) for s in range(lax.axis_size(axi...  31 us
    ppermute x8, starting transfers between devices, flip(): lax.ppermute(value, axis, [(s, s ^ mask) for s in range(lax.axis_size(axi...  28.9 us
    ppermute x12, waiting for transfers between devices, shift_row(): return lax.ppermute(value, 'row', pairs)  28.5 us
    pallas_call x10, Pallas kernels, run_segment(): pl.pallas_call(functools.partial(segment_kernel, source, target, len(args...  25.2 us
    pallas_call x1, Pallas kernels, pack(): pl.pallas_call(pack_kernel, out_shape=[jax.ShapeDtypeStruct(shape, F32) f...  3.74 us
  transfers between devices with their start and end apart: 20, of which 8 were waited for; matrix products, arithmetic and copies ran while one was open for 1% of the time, Pallas kernels for 16%

profile of v6, /device:TPU:2, one launch (start us, length us, event | category | flops | bytes accessed | tf_op | source)
XLA Modules:
  0.0 162.4 jit_solution(13530077311341907105)
XLA Ops:
  1.6 3.7 %pack.1 = (f32[8,16,8,128]{3,2,1,0:T(8,128)S(1)}, f32[8,16,8,128]{3,2,1,0:T(8,128)S(1)}, f32[16,16,8,128]{3,2,1,0:T(8,128)S(1)}) custom-call(f32[2,2,8,8,2,8,128]{6,5,4,3,2,1,0:T(8,128)S(1)} %bitcast.2), custom_call_target="tpu_custom_call" | custom-call | bytes 4194304 | tf_op jit(solution)/shard_map/pack/pallas_call | solution.py:205
  5.3 7.3 %collective-permute-start.10 = (f32[8,16,8,128]{3,2,1,0:T(8,128)S(1)}, f32[8,16,8,128]{3,2,1,0:T(8,128)S(1)}, u32[]{:S(2)}, u32[]{:S(2)}) collective-permute-start(f32[8,16,8,128]{3,2,1,0:T(8,128)S(1)} %get-tuple-element.56), channel_id=1, source_target_pairs={{0,128},{8,136},{16,144},{24,152},{32,160},{40,168},{48,176},{56,1... | collective-permute-start | bytes 1572872 | tf_op jit(solution)/shard_map/ppermute | solution.py:411
  14.0 2.0 %shard_map.42 = (f32[8,16,8,128]{3,2,1,0:T(8,128)S(1)}, f32[8,16,8,128]{3,2,1,0:T(8,128)S(1)}) custom-call(bf16[3,256,256]{2,1,0:T(8,128)(2,1)S(1)} %shard_map.41.refs_0_, f32[16,16,8,128]{3,2,1,0:T(8,128)S(1)} %get-tuple-element.38.refs_1_), custom_call_target="tpu_custom_call" | custom-call | flops 1207959552 | bytes 3145728 | tf_op jit(solution)/shard_map/pallas_call | solution.py:374
  16.1 10.7 %collective-permute-done.10.refs_2_ = f32[8,16,8,128]{3,2,1,0:T(8,128)S(1)} collective-permute-done((f32[8,16,8,128]{3,2,1,0:T(8,128)S(1)}, f32[8,16,8,128]{3,2,1,0:T(8,128)S(1)}, u32[]{:S(2)}, u32[]{:S(2)}) %collective-permute-start.10) | collective-permute-done | bytes 524320 | tf_op jit(solution)/shard_map/ppermute | solution.py:411
  26.8 2.2 %shard_map.48 = (f32[8,16,8,128]{3,2,1,0:T(8,128)S(1)}, f32[8,16,8,128]{3,2,1,0:T(8,128)S(1)}) custom-call(bf16[3,256,256]{2,1,0:T(8,128)(2,1)S(1)} %shard_map.41.refs_0_, f32[8,16,8,128]{3,2,1,0:T(8,128)S(1)} %get-tuple-element.55.refs_1_, f32[8,16,8,128]{3,2,1,0:T(8,128)S(1)} %collective-permute-done.10.refs_2_), custom_call_target="tpu_custom_call" | custom-call | flops 1207959552 | bytes 3145728 | tf_op jit(solution)/shard_map/pallas_call | solution.py:374
  29.5 2.1 %shard_map.43 = (f32[8,16,8,128]{3,2,1,0:T(8,128)S(1)}, f32[8,16,8,128]{3,2,1,0:T(8,128)S(1)}) custom-call(bf16[3,256,256]{2,1,0:T(8,128)(2,1)S(1)} %shard_map.40.refs_0_, f32[8,16,8,128]{3,2,1,0:T(8,128)S(1)} %get-tuple-element.39.refs_1_, f32[8,16,8,128]{3,2,1,0:T(8,128)S(1)} %collective-permute-done.refs_2_), custom_call_target="tpu_custom_call" | custom-call | flops 1207959552 | bytes 3145728 | tf_op jit(solution)/shard_map/pallas_call | solution.py:374
  31.6 14.3 %collective-permute-start.1 = (f32[8,16,8,128]{3,2,1,0:T(8,128)S(1)}, f32[8,16,8,128]{3,2,1,0:T(8,128)S(1)}, u32[]{:S(2)}, u32[]{:S(2)}) collective-permute-start(f32[8,16,8,128]{3,2,1,0:T(8,128)S(1)} %get-tuple-element.42), channel_id=1, source_target_pairs={{0,128},{8,136},{16,144},{24,152},{32,160},{40,168},{48,176},{56,1... | collective-permute-start | bytes 1572872 | tf_op jit(solution)/shard_map/ppermute | solution.py:411
  46.3 2.0 %shard_map.49.refs_1_ = f32[16,16,8,128]{3,2,1,0:T(8,128)S(1)} custom-call(bf16[3,256,256]{2,1,0:T(8,128)(2,1)S(1)} %shard_map.40.refs_0_, f32[8,16,8,128]{3,2,1,0:T(8,128)S(1)} %get-tuple-element.57.refs_1_, f32[8,16,8,128]{3,2,1,0:T(8,128)S(1)} %collective-permute-done.11.refs_2_), custom_call_target="tpu_custom_call" | custom-call | flops 1207959552 | bytes 3145728 | tf_op jit(solution)/shard_map/pallas_call | solution.py:374
  48.3 2.2 %shard_map.50 = (f32[16,8,8,128]{3,2,1,0:T(8,128)S(1)}, f32[16,8,8,128]{3,2,1,0:T(8,128)S(1)}) custom-call(bf16[3,256,256]{2,1,0:T(8,128)(2,1)S(1)} %shard_map.39.refs_0_, f32[16,16,8,128]{3,2,1,0:T(8,128)S(1)} %shard_map.49.refs_1_), custom_call_target="tpu_custom_call" | custom-call | flops 1207959552 | bytes 3145728 | tf_op jit(solution)/shard_map/pallas_call | solution.py:374
  50.8 9.1 %collective-permute-done.1.refs_2_ = f32[8,16,8,128]{3,2,1,0:T(8,128)S(1)} collective-permute-done((f32[8,16,8,128]{3,2,1,0:T(8,128)S(1)}, f32[8,16,8,128]{3,2,1,0:T(8,128)S(1)}, u32[]{:S(2)}, u32[]{:S(2)}) %collective-permute-start.1) | collective-permute-done | bytes 524320 | tf_op jit(solution)/shard_map/ppermute | solution.py:411
  59.9 2.0 %shard_map.44 = (f32[16,8,8,128]{3,2,1,0:T(8,128)S(1)}, f32[16,8,8,128]{3,2,1,0:T(8,128)S(1)}) custom-call(bf16[3,256,256]{2,1,0:T(8,128)(2,1)S(1)} %shard_map.39.refs_0_, f32[8,16,8,128]{3,2,1,0:T(8,128)S(1)} %get-tuple-element.41.refs_1_, f32[8,16,8,128]{3,2,1,0:T(8,128)S(1)} %collective-permute-done.1.refs_2_), custom_call_target="tpu_custom_call" | custom-call | flops 1207959552 | bytes 3145728 | tf_op jit(solution)/shard_map/pallas_call | solution.py:374
  64.8 2.2 %collective-permute-start.15 = (f32[2,4,8,8,128]{4,3,2,1,0:T(8,128)S(1)}, f32[2,4,8,8,128]{4,3,2,1,0:T(8,128)S(1)}, u32[]{:S(2)}, u32[]{:S(2)}) collective-permute-start(f32[2,4,8,8,128]{4,3,2,1,0:T(8,128)S(1)} %get-tuple-element.64), channel_id=1, source_target_pairs={{0,48},{8,56},{16,0},{24,8},{32,16},{40,24},{48,32},{56,40},{64,11... | collective-permute-start | bytes 786440 | tf_op jit(solution)/shard_map/ppermute | solution.py:419
  67.1 3.4 %collective-permute-start.4 = (f32[2,4,8,8,128]{4,3,2,1,0:T(8,128)S(1)}, f32[2,4,8,8,128]{4,3,2,1,0:T(8,128)S(1)}, u32[]{:S(2)}, u32[]{:S(2)}) collective-permute-start(f32[2,4,8,8,128]{4,3,2,1,0:T(8,128)S(1)} %get-tuple-element.47), channel_id=1, source_target_pairs={{0,32},{8,40},{16,48},{24,56},{32,0},{40,8},{48,16},{56,24},{64,96... | collective-permute-start | bytes 786440 | tf_op jit(solution)/shard_map/ppermute | solution.py:419
  70.5 4.8 %collective-permute-done.13.refs_1_ = f32[2,4,8,8,128]{4,3,2,1,0:T(8,128)S(1)} collective-permute-done((f32[2,4,8,8,128]{4,3,2,1,0:T(8,128)S(1)}, f32[2,4,8,8,128]{4,3,2,1,0:T(8,128)S(1)}, u32[]{:S(2)}, u32[]{:S(2)}) %collective-permute-start.13) | collective-permute-done | bytes 262176 | tf_op jit(solution)/shard_map/ppermute | solution.py:419
  75.4 4.6 %collective-permute-done.15.refs_3_ = f32[2,4,8,8,128]{4,3,2,1,0:T(8,128)S(1)} collective-permute-done((f32[2,4,8,8,128]{4,3,2,1,0:T(8,128)S(1)}, f32[2,4,8,8,128]{4,3,2,1,0:T(8,128)S(1)}, u32[]{:S(2)}, u32[]{:S(2)}) %collective-permute-start.15) | collective-permute-done | bytes 262176 | tf_op jit(solution)/shard_map/ppermute | solution.py:419
  80.1 12.5 %collective-permute-start.16 = (f32[2,4,8,8,128]{4,3,2,1,0:T(8,128)S(1)}, f32[2,4,8,8,128]{4,3,2,1,0:T(8,128)S(1)}, u32[]{:S(2)}, u32[]{:S(2)}) collective-permute-start(f32[2,4,8,8,128]{4,3,2,1,0:T(8,128)S(1)} %get-tuple-element.66), channel_id=1, source_target_pairs={{0,64},{8,72},{16,80},{24,88},{32,96},{40,104},{48,112},{56,120},{... | collective-permute-start | bytes 786440 | tf_op jit(solution)/shard_map/ppermute | solution.py:419
  92.6 4.9 %collective-permute-start.17 = (f32[2,4,8,8,128]{4,3,2,1,0:T(8,128)S(1)}, f32[2,4,8,8,128]{4,3,2,1,0:T(8,128)S(1)}, u32[]{:S(2)}, u32[]{:S(2)}) collective-permute-start(f32[2,4,8,8,128]{4,3,2,1,0:T(8,128)S(1)} %get-tuple-element.67), channel_id=1, source_target_pairs={{0,128},{8,136},{16,144},{24,152},{32,160},{40,168},{48,176},{56,1... | collective-permute-start | bytes 786440 | tf_op jit(solution)/shard_map/ppermute | solution.py:419
  97.5 2.4 %collective-permute-start.18 = (f32[2,4,8,8,128]{4,3,2,1,0:T(8,128)S(1)}, f32[2,4,8,8,128]{4,3,2,1,0:T(8,128)S(1)}, u32[]{:S(2)}, u32[]{:S(2)}) collective-permute-start(f32[2,4,8,8,128]{4,3,2,1,0:T(8,128)S(1)} %get-tuple-element.68), channel_id=1, source_target_pairs={{0,192},{8,200},{16,208},{24,216},{32,224},{40,232},{48,240},{56,2... | collective-permute-start | bytes 786440 | tf_op jit(solution)/shard_map/ppermute | solution.py:419
  100.0 2.3 %collective-permute-start.6 = (f32[2,4,8,8,128]{4,3,2,1,0:T(8,128)S(1)}, f32[2,4,8,8,128]{4,3,2,1,0:T(8,128)S(1)}, u32[]{:S(2)}, u32[]{:S(2)}) collective-permute-start(f32[2,4,8,8,128]{4,3,2,1,0:T(8,128)S(1)} %get-tuple-element.50), channel_id=1, source_target_pairs={{0,64},{8,72},{16,80},{24,88},{32,96},{40,104},{48,112},{56,120},{... | collective-permute-start | bytes 786440 | tf_op jit(solution)/shard_map/ppermute | solution.py:419
  102.3 4.9 %collective-permute-start.7 = (f32[2,4,8,8,128]{4,3,2,1,0:T(8,128)S(1)}, f32[2,4,8,8,128]{4,3,2,1,0:T(8,128)S(1)}, u32[]{:S(2)}, u32[]{:S(2)}) collective-permute-start(f32[2,4,8,8,128]{4,3,2,1,0:T(8,128)S(1)} %get-tuple-element.51), channel_id=1, source_target_pairs={{0,128},{8,136},{16,144},{24,152},{32,160},{40,168},{48,176},{56,1... | collective-permute-start | bytes 786440 | tf_op jit(solution)/shard_map/ppermute | solution.py:419
  107.2 2.4 %collective-permute-start.8 = (f32[2,4,8,8,128]{4,3,2,1,0:T(8,128)S(1)}, f32[2,4,8,8,128]{4,3,2,1,0:T(8,128)S(1)}, u32[]{:S(2)}, u32[]{:S(2)}) collective-permute-start(f32[2,4,8,8,128]{4,3,2,1,0:T(8,128)S(1)} %get-tuple-element.52), channel_id=1, source_target_pairs={{0,192},{8,200},{16,208},{24,216},{32,224},{40,232},{48,240},{56,2... | collective-permute-start | bytes 786440 | tf_op jit(solution)/shard_map/ppermute | solution.py:419
  110.5 5.1 %collective-permute-done.17.refs_3_ = f32[2,4,8,8,128]{4,3,2,1,0:T(8,128)S(1)} collective-permute-done((f32[2,4,8,8,128]{4,3,2,1,0:T(8,128)S(1)}, f32[2,4,8,8,128]{4,3,2,1,0:T(8,128)S(1)}, u32[]{:S(2)}, u32[]{:S(2)}) %collective-permute-start.17) | collective-permute-done | bytes 262176 | tf_op jit(solution)/shard_map/ppermute | solution.py:419
  115.6 13.8 %collective-permute-done.18.refs_4_ = f32[2,4,8,8,128]{4,3,2,1,0:T(8,128)S(1)} collective-permute-done((f32[2,4,8,8,128]{4,3,2,1,0:T(8,128)S(1)}, f32[2,4,8,8,128]{4,3,2,1,0:T(8,128)S(1)}, u32[]{:S(2)}, u32[]{:S(2)}) %collective-permute-start.18) | collective-permute-done | bytes 262176 | tf_op jit(solution)/shard_map/ppermute | solution.py:419
  129.5 2.2 %shard_map.53 = (f32[8,16,8,128]{3,2,1,0:T(8,128)S(1)}, f32[8,16,8,128]{3,2,1,0:T(8,128)S(1)}) custom-call(bf16[3,256,256]{2,1,0:T(8,128)(2,1)S(1)} %shard_map.38.refs_0_, f32[2,4,8,8,128]{4,3,2,1,0:T(8,128)S(1)} %get-tuple-element.65.refs_1_, f32[2,4,8,8,128]{4,3,2,1,0:T(8,128)S(1)} %collective-permute-done.16.refs_2_, ...), custom_call_target="tpu_custom_call" | custom-call | flops 1207959552 | bytes 3145728 | tf_op jit(solution)/shard_map/pallas_call | solution.py:374
  131.7 3.3 %collective-permute-start.19 = (f32[8,16,8,128]{3,2,1,0:T(8,128)S(1)}, f32[8,16,8,128]{3,2,1,0:T(8,128)S(1)}, u32[]{:S(2)}, u32[]{:S(2)}) collective-permute-start(f32[8,16,8,128]{3,2,1,0:T(8,128)S(1)} %get-tuple-element.70), channel_id=1, source_target_pairs={{0,4},{1,5},{2,6},{3,7},{4,0},{5,1},{6,2},{7,3},{8,12},{9,13},{10,... | collective-permute-start | bytes 1572872 | tf_op jit(solution)/shard_map/ppermute | solution.py:411
  135.0 2.2 %shard_map.47 = (f32[8,16,8,128]{3,2,1,0:T(8,128)S(1)}, f32[8,16,8,128]{3,2,1,0:T(8,128)S(1)}) custom-call(bf16[3,256,256]{2,1,0:T(8,128)(2,1)S(1)} %shard_map.38.refs_0_, f32[2,4,8,8,128]{4,3,2,1,0:T(8,128)S(1)} %get-tuple-element.49.refs_1_, f32[2,4,8,8,128]{4,3,2,1,0:T(8,128)S(1)} %collective-permute-done.6.refs_2_, ...), custom_call_target="tpu_custom_call" | custom-call | flops 1207959552 | bytes 3145728 | tf_op jit(solution)/shard_map/pallas_call | solution.py:374
  137.2 3.5 %collective-permute-start.9 = (f32[8,16,8,128]{3,2,1,0:T(8,128)S(1)}, f32[8,16,8,128]{3,2,1,0:T(8,128)S(1)}, u32[]{:S(2)}, u32[]{:S(2)}) collective-permute-start(f32[8,16,8,128]{3,2,1,0:T(8,128)S(1)} %get-tuple-element.54), channel_id=1, source_target_pairs={{0,4},{1,5},{2,6},{3,7},{4,0},{5,1},{6,2},{7,3},{8,12},{9,13},{10,... | collective-permute-start | bytes 1572872 | tf_op jit(solution)/shard_map/ppermute | solution.py:411
  141.1 1.8 %low_weights.1.refs_3_.refs_4_ = bf16[2,2,256,256]{3,2,1,0:T(8,128)(2,1)S(1)} custom-call(f32[5,4,2,128,128]{4,3,2,1,0:T(8,128)S(1)} %copy-done), custom_call_target="tpu_custom_call" | custom-call | flops 503316480 | bytes 1048576 | tf_op jit(solution)/shard_map/low_weights/pallas_call | solution.py:134
  142.9 5.2 %collective-permute-done.19.refs_2_ = f32[8,16,8,128]{3,2,1,0:T(8,128)S(1)} collective-permute-done((f32[8,16,8,128]{3,2,1,0:T(8,128)S(1)}, f32[8,16,8,128]{3,2,1,0:T(8,128)S(1)}, u32[]{:S(2)}, u32[]{:S(2)}) %collective-permute-start.19) | collective-permute-done | bytes 524320 | tf_op jit(solution)/shard_map/ppermute | solution.py:411
  148.1 4.1 %shard_map.54.refs_3_ = f32[4,512,256]{2,1,0:T(8,128)S(1)} custom-call(bf16[3,256,256]{2,1,0:T(8,128)(2,1)S(1)} %shard_map.37.refs_0_, f32[8,16,8,128]{3,2,1,0:T(8,128)S(1)} %get-tuple-element.69.refs_1_, f32[8,16,8,128]{3,2,1,0:T(8,128)S(1)} %collective-permute-done.19.refs_2_, bf16[2,2,256,256]{3,2,1,0:T(8,128)(2,1)S(1)} %low_weights.1.refs_3_.refs_4_), custom_call_target="tpu_custom_call" | custom-call | flops 1207959552 | bytes 3145728 | tf_op jit(solution)/shard_map/pallas_call | solution.py:374
  152.2 6.1 %collective-permute-done.9.refs_2_ = f32[8,16,8,128]{3,2,1,0:T(8,128)S(1)} collective-permute-done((f32[8,16,8,128]{3,2,1,0:T(8,128)S(1)}, f32[8,16,8,128]{3,2,1,0:T(8,128)S(1)}, u32[]{:S(2)}, u32[]{:S(2)}) %collective-permute-start.9) | collective-permute-done | bytes 524320 | tf_op jit(solution)/shard_map/ppermute | solution.py:411
  158.3 4.1 %shard_map.55 = f32[2,16,8,2,8,128]{5,4,3,2,1,0:T(8,128)} custom-call(bf16[3,256,256]{2,1,0:T(8,128)(2,1)S(1)} %shard_map.37.refs_0_, f32[8,16,8,128]{3,2,1,0:T(8,128)S(1)} %get-tuple-element.53.refs_1_, f32[8,16,8,128]{3,2,1,0:T(8,128)S(1)} %collective-permute-done.9.refs_2_, f32[4,512,256]{2,1,0:T(8,128)S(1)} %shard_map.54.refs_3_, ...), custom_call_target="tpu_custom_call" | custom-call | flops 1207959552 | bytes 3145728 | tf_op jit(solution)/shard_map/pallas_call | solution.py:374
  (36 shorter events, 8.5 us)
Async XLA Ops:
  0.0 1.6 copy-start.1
  5.3 21.5 %collective-permute-start.10 = (f32[8,16,8,128]{3,2,1,0:T(8,128)S(1)}, f32[8,16,8,128]{3,2,1,0:T(8,128)S(1)}, u32[]{:S(2)}, u32[]{:S(2)}) collective-permute-start(f32[8,16,8,128]{3,2,1,0:T(8,128)S(1)} %get-tuple-element.56), channel_id=1, source_target_pairs={{0,128},{8,136},{16,144},{24,152},{32,160},{40,168},{48,176},{56,1... | collective-permute-start | bytes 1572872 | tf_op jit(solution)/shard_map/ppermute | solution.py:411
  16.0 13.4 %collective-permute-start = (f32[8,16,8,128]{3,2,1,0:T(8,128)S(1)}, f32[8,16,8,128]{3,2,1,0:T(8,128)S(1)}, u32[]{:S(2)}, u32[]{:S(2)}) collective-permute-start(f32[8,16,8,128]{3,2,1,0:T(8,128)S(1)} %get-tuple-element.40), channel_id=1, source_target_pairs={{0,8},{8,0},{16,24},{24,16},{32,40},{40,32},{48,56},{56,48},{64,72... | collective-permute-start | bytes 1572872 | tf_op jit(solution)/shard_map/ppermute | solution.py:411
  26.8 2.3 %copy-start = (f32[5,4,2,128,128]{4,3,2,1,0:T(8,128)S(1)}, f32[5,4,2,128,128]{4,3,2,1,0:T(8,128)}, u32[]{:S(2)}) copy-start(f32[5,4,2,128,128]{4,3,2,1,0:T(8,128)} %gates_ref.1) | copy-start | bytes 7864324
  29.0 17.3 %collective-permute-start.11 = (f32[8,16,8,128]{3,2,1,0:T(8,128)S(1)}, f32[8,16,8,128]{3,2,1,0:T(8,128)S(1)}, u32[]{:S(2)}, u32[]{:S(2)}) collective-permute-start(f32[8,16,8,128]{3,2,1,0:T(8,128)S(1)} %get-tuple-element.58), channel_id=1, source_target_pairs={{0,8},{8,0},{16,24},{24,16},{32,40},{40,32},{48,56},{56,48},{64,72... | collective-permute-start | bytes 1572872 | tf_op jit(solution)/shard_map/ppermute | solution.py:411
  31.6 28.3 %collective-permute-start.1 = (f32[8,16,8,128]{3,2,1,0:T(8,128)S(1)}, f32[8,16,8,128]{3,2,1,0:T(8,128)S(1)}, u32[]{:S(2)}, u32[]{:S(2)}) collective-permute-start(f32[8,16,8,128]{3,2,1,0:T(8,128)S(1)} %get-tuple-element.42), channel_id=1, source_target_pairs={{0,128},{8,136},{16,144},{24,152},{32,160},{40,168},{48,176},{56,1... | collective-permute-start | bytes 1572872 | tf_op jit(solution)/shard_map/ppermute | solution.py:411
  50.5 11.5 %collective-permute-start.12 = (f32[16,8,8,128]{3,2,1,0:T(8,128)S(1)}, f32[16,8,8,128]{3,2,1,0:T(8,128)S(1)}, u32[]{:S(2)}, u32[]{:S(2)}) collective-permute-start(f32[16,8,8,128]{3,2,1,0:T(8,128)S(1)} %get-tuple-element.60), channel_id=1, source_target_pairs={{0,8},{8,0},{16,24},{24,16},{32,40},{40,32},{48,56},{56,48},{64,72... | collective-permute-start | bytes 1572872 | tf_op jit(solution)/shard_map/ppermute | solution.py:411
  61.9 5.1 %collective-permute-start.2 = (f32[16,8,8,128]{3,2,1,0:T(8,128)S(1)}, f32[16,8,8,128]{3,2,1,0:T(8,128)S(1)}, u32[]{:S(2)}, u32[]{:S(2)}) collective-permute-start(f32[16,8,8,128]{3,2,1,0:T(8,128)S(1)} %get-tuple-element.44), channel_id=1, source_target_pairs={{0,8},{8,0},{16,24},{24,16},{32,40},{40,32},{48,56},{56,48},{64,72... | collective-permute-start | bytes 1572872 | tf_op jit(solution)/shard_map/ppermute | solution.py:411
  62.0 47.6 %copy-start.2 = (s32[32]{0:T(128)S(1)}, s32[32]{0:T(128)}, u32[]{:S(2)}) copy-start(s32[32]{0:T(128)} %refs_0_.5) | copy-start | bytes 388
  62.1 13.3 %collective-permute-start.13 = (f32[2,4,8,8,128]{4,3,2,1,0:T(8,128)S(1)}, f32[2,4,8,8,128]{4,3,2,1,0:T(8,128)S(1)}, u32[]{:S(2)}, u32[]{:S(2)}) collective-permute-start(f32[2,4,8,8,128]{4,3,2,1,0:T(8,128)S(1)} %get-tuple-element.62), channel_id=1, source_target_pairs={{0,16},{8,24},{16,32},{24,40},{32,48},{40,56},{48,0},{56,8},{64,80... | collective-permute-start | bytes 786440 | tf_op jit(solution)/shard_map/ppermute | solution.py:419
  63.6 11.8 %collective-permute-start.14 = (f32[2,4,8,8,128]{4,3,2,1,0:T(8,128)S(1)}, f32[2,4,8,8,128]{4,3,2,1,0:T(8,128)S(1)}, u32[]{:S(2)}, u32[]{:S(2)}) collective-permute-start(f32[2,4,8,8,128]{4,3,2,1,0:T(8,128)S(1)} %get-tuple-element.63), channel_id=1, source_target_pairs={{0,32},{8,40},{16,48},{24,56},{32,0},{40,8},{48,16},{56,24},{64,96... | collective-permute-start | bytes 786440 | tf_op jit(solution)/shard_map/ppermute | solution.py:419
  64.8 15.3 %collective-permute-start.15 = (f32[2,4,8,8,128]{4,3,2,1,0:T(8,128)S(1)}, f32[2,4,8,8,128]{4,3,2,1,0:T(8,128)S(1)}, u32[]{:S(2)}, u32[]{:S(2)}) collective-permute-start(f32[2,4,8,8,128]{4,3,2,1,0:T(8,128)S(1)} %get-tuple-element.64), channel_id=1, source_target_pairs={{0,48},{8,56},{16,0},{24,8},{32,16},{40,24},{48,32},{56,40},{64,11... | collective-permute-start | bytes 786440 | tf_op jit(solution)/shard_map/ppermute | solution.py:419
  67.0 30.4 %collective-permute-start.3 = (f32[2,4,8,8,128]{4,3,2,1,0:T(8,128)S(1)}, f32[2,4,8,8,128]{4,3,2,1,0:T(8,128)S(1)}, u32[]{:S(2)}, u32[]{:S(2)}) collective-permute-start(f32[2,4,8,8,128]{4,3,2,1,0:T(8,128)S(1)} %get-tuple-element.46), channel_id=1, source_target_pairs={{0,16},{8,24},{16,32},{24,40},{32,48},{40,56},{48,0},{56,8},{64,80... | collective-permute-start | bytes 786440 | tf_op jit(solution)/shard_map/ppermute | solution.py:419
  67.1 32.8 %collective-permute-start.4 = (f32[2,4,8,8,128]{4,3,2,1,0:T(8,128)S(1)}, f32[2,4,8,8,128]{4,3,2,1,0:T(8,128)S(1)}, u32[]{:S(2)}, u32[]{:S(2)}) collective-permute-start(f32[2,4,8,8,128]{4,3,2,1,0:T(8,128)S(1)} %get-tuple-element.47), channel_id=1, source_target_pairs={{0,32},{8,40},{16,48},{24,56},{32,0},{40,8},{48,16},{56,24},{64,96... | collective-permute-start | bytes 786440 | tf_op jit(solution)/shard_map/ppermute | solution.py:419
  75.4 24.5 %collective-permute-start.5 = (f32[2,4,8,8,128]{4,3,2,1,0:T(8,128)S(1)}, f32[2,4,8,8,128]{4,3,2,1,0:T(8,128)S(1)}, u32[]{:S(2)}, u32[]{:S(2)}) collective-permute-start(f32[2,4,8,8,128]{4,3,2,1,0:T(8,128)S(1)} %get-tuple-element.48), channel_id=1, source_target_pairs={{0,48},{8,56},{16,0},{24,8},{32,16},{40,24},{48,32},{56,40},{64,11... | collective-permute-start | bytes 786440 | tf_op jit(solution)/shard_map/ppermute | solution.py:419
  80.1 27.1 %collective-permute-start.16 = (f32[2,4,8,8,128]{4,3,2,1,0:T(8,128)S(1)}, f32[2,4,8,8,128]{4,3,2,1,0:T(8,128)S(1)}, u32[]{:S(2)}, u32[]{:S(2)}) collective-permute-start(f32[2,4,8,8,128]{4,3,2,1,0:T(8,128)S(1)} %get-tuple-element.66), channel_id=1, source_target_pairs={{0,64},{8,72},{16,80},{24,88},{32,96},{40,104},{48,112},{56,120},{... | collective-permute-start | bytes 786440 | tf_op jit(solution)/shard_map/ppermute | solution.py:419
  92.6 23.0 %collective-permute-start.17 = (f32[2,4,8,8,128]{4,3,2,1,0:T(8,128)S(1)}, f32[2,4,8,8,128]{4,3,2,1,0:T(8,128)S(1)}, u32[]{:S(2)}, u32[]{:S(2)}) collective-permute-start(f32[2,4,8,8,128]{4,3,2,1,0:T(8,128)S(1)} %get-tuple-element.67), channel_id=1, source_target_pairs={{0,128},{8,136},{16,144},{24,152},{32,160},{40,168},{48,176},{56,1... | collective-permute-start | bytes 786440 | tf_op jit(solution)/shard_map/ppermute | solution.py:419
  97.5 32.0 %collective-permute-start.18 = (f32[2,4,8,8,128]{4,3,2,1,0:T(8,128)S(1)}, f32[2,4,8,8,128]{4,3,2,1,0:T(8,128)S(1)}, u32[]{:S(2)}, u32[]{:S(2)}) collective-permute-start(f32[2,4,8,8,128]{4,3,2,1,0:T(8,128)S(1)} %get-tuple-element.68), channel_id=1, source_target_pairs={{0,192},{8,200},{16,208},{24,216},{32,224},{40,232},{48,240},{56,2... | collective-permute-start | bytes 786440 | tf_op jit(solution)/shard_map/ppermute | solution.py:419
  100.0 35.0 %collective-permute-start.6 = (f32[2,4,8,8,128]{4,3,2,1,0:T(8,128)S(1)}, f32[2,4,8,8,128]{4,3,2,1,0:T(8,128)S(1)}, u32[]{:S(2)}, u32[]{:S(2)}) collective-permute-start(f32[2,4,8,8,128]{4,3,2,1,0:T(8,128)S(1)} %get-tuple-element.50), channel_id=1, source_target_pairs={{0,64},{8,72},{16,80},{24,88},{32,96},{40,104},{48,112},{56,120},{... | collective-permute-start | bytes 786440 | tf_op jit(solution)/shard_map/ppermute | solution.py:419
  102.3 32.7 %collective-permute-start.7 = (f32[2,4,8,8,128]{4,3,2,1,0:T(8,128)S(1)}, f32[2,4,8,8,128]{4,3,2,1,0:T(8,128)S(1)}, u32[]{:S(2)}, u32[]{:S(2)}) collective-permute-start(f32[2,4,8,8,128]{4,3,2,1,0:T(8,128)S(1)} %get-tuple-element.51), channel_id=1, source_target_pairs={{0,128},{8,136},{16,144},{24,152},{32,160},{40,168},{48,176},{56,1... | collective-permute-start | bytes 786440 | tf_op jit(solution)/shard_map/ppermute | solution.py:419
  107.2 27.8 %collective-permute-start.8 = (f32[2,4,8,8,128]{4,3,2,1,0:T(8,128)S(1)}, f32[2,4,8,8,128]{4,3,2,1,0:T(8,128)S(1)}, u32[]{:S(2)}, u32[]{:S(2)}) collective-permute-start(f32[2,4,8,8,128]{4,3,2,1,0:T(8,128)S(1)} %get-tuple-element.52), channel_id=1, source_target_pairs={{0,192},{8,200},{16,208},{24,216},{32,224},{40,232},{48,240},{56,2... | collective-permute-start | bytes 786440 | tf_op jit(solution)/shard_map/ppermute | solution.py:419
  131.7 16.4 %collective-permute-start.19 = (f32[8,16,8,128]{3,2,1,0:T(8,128)S(1)}, f32[8,16,8,128]{3,2,1,0:T(8,128)S(1)}, u32[]{:S(2)}, u32[]{:S(2)}) collective-permute-start(f32[8,16,8,128]{3,2,1,0:T(8,128)S(1)} %get-tuple-element.70), channel_id=1, source_target_pairs={{0,4},{1,5},{2,6},{3,7},{4,0},{5,1},{6,2},{7,3},{8,12},{9,13},{10,... | collective-permute-start | bytes 1572872 | tf_op jit(solution)/shard_map/ppermute | solution.py:411
  137.2 21.0 %collective-permute-start.9 = (f32[8,16,8,128]{3,2,1,0:T(8,128)S(1)}, f32[8,16,8,128]{3,2,1,0:T(8,128)S(1)}, u32[]{:S(2)}, u32[]{:S(2)}) collective-permute-start(f32[8,16,8,128]{3,2,1,0:T(8,128)S(1)} %get-tuple-element.54), channel_id=1, source_target_pairs={{0,4},{1,5},{2,6},{3,7},{4,0},{5,1},{6,2},{7,3},{8,12},{9,13},{10,... | collective-permute-start | bytes 1572872 | tf_op jit(solution)/shard_map/ppermute | solution.py:411

commit v7 on v5

--- a/solution.py
+++ b/solution.py
@@ -160,6 +160,21 @@
     return jnp.where(swapped, second, first), jnp.where(swapped, first, second)
 
 
+def turned(blocks):
+    sub = lax.broadcasted_iota(jnp.int32, (1, 8, 1), 1)
+    for step in (1, 2, 4):
+        off = (sub & step) == 0
+        made = [None] * 8
+        for k in range(8):
+            if k & step:
+                continue
+            first, second = blocks[k], blocks[k + step]
+            made[k] = jnp.where(off, first, pltpu.roll(second, step, 1))
+            made[k + step] = jnp.where(off, pltpu.roll(first, 8 - step, 1), second)
+        blocks = made
+    return blocks
+
+
 def pack_kernel(state_ref, *outs):
     own = lax.axis_index("row") >> 4 == 1
 
@@ -316,7 +331,7 @@
 
     def low_gate(i, carry):
         low_ref = ins[-1]
-        rows = jnp.concatenate([one[:, 4 * i + k].reshape(GD, GD) for k in range(4)], axis=0)
+        rows = one[pl.ds(4 * i, 4)].reshape(512, GD)
         pair = jnp.concatenate(split(rows), axis=1)
         done = jnp.dot(pair, low_ref[source[1], 0], preferred_element_type=F32) + jnp.dot(
             pair, low_ref[source[1], 1], preferred_element_type=F32
@@ -325,10 +340,11 @@
             outs[0][i] = done
             return carry
         done = done + ins[-2][i]
-        for k in range(4):
-            piece = done[GD * k : GD * (k + 1)]
-            outs[0][0, pl.ds(4 * i + k, GD, stride=16), :] = piece[:, :GD]
-            outs[0][1, pl.ds(4 * i + k, GD, stride=16), :] = piece[:, GD:]
+        for c in range(2):
+            part = done[:, GD * c : GD * (c + 1)].reshape(4, 2, 8, 8, GD)
+            blocks = [part[:, :, k].reshape(8, 8, GD) for k in range(8)]
+            for o, block in enumerate(turned(blocks)):
+                outs[0][c, pl.ds(4 * i, 4), o] = block.reshape(4, 2, 8, GD)
         return carry
 
     for step in (top_first, mid, top_last):
@@ -347,7 +363,7 @@
     elif target == "share":
         out_shape = [jax.ShapeDtypeStruct((4, 512, 256), F32)]
     else:
-        out_shape = [jax.ShapeDtypeStruct((2, 2048, 128), F32)]
+        out_shape = [jax.ShapeDtypeStruct((2, 16, 8, 2, 8, 128), F32)]
     args = list(ins) + list(extra)
     vmem = pl.BlockSpec(memory_space=pltpu.VMEM)
     return pl.pallas_call(

time: 155 us -> 155 us (level)
  no operation moved by 1% of the time
where the time goes in v7:
time: 155 us; the launch traced here: 154 us
  starting transfers between devices  68.8 us (44%)
  waiting for transfers between devices  50.2 us (32%)
  Pallas kernels  31.7 us (20%)
  local copies, waits for them, and re-layouts  2.67 us (2%)
    ppermute x12, starting transfers between devices, shift_row(): return lax.ppermute(value, 'row', pairs)  36.5 us
    ppermute x8, starting transfers between devices, flip(): lax.ppermute(value, axis, [(s, s ^ mask) for s in range(lax.axis_size(axi...  32.3 us
    ppermute x12, waiting for transfers between devices, shift_row(): return lax.ppermute(value, 'row', pairs)  27.5 us
    pallas_call x10, Pallas kernels, run_segment(): pl.pallas_call(functools.partial(segment_kernel, source, target, len(args...  25.2 us
    ppermute x8, waiting for transfers between devices, flip(): lax.ppermute(value, axis, [(s, s ^ mask) for s in range(lax.axis_size(axi...  22.7 us
  transfers between devices with their start and end apart: 20, of which 9 were waited for; matrix products, arithmetic and copies ran while one was open for 1% of the time, Pallas kernels for 17%

profile of v7, /device:TPU:1, one launch (start us, length us, event | category | flops | bytes accessed | tf_op | source)
XLA Modules:
  0.0 153.6 jit_solution(14160591320488074575)
XLA Ops:
  1.6 2.2 %pack.1 = (f32[8,16,8,128]{3,2,1,0:T(8,128)S(1)}, f32[8,16,8,128]{3,2,1,0:T(8,128)S(1)}, f32[16,16,8,128]{3,2,1,0:T(8,128)S(1)}) custom-call(f32[2,2048,128]{2,1,0:T(8,128)S(1)} %bitcast.2), custom_call_target="tpu_custom_call" | custom-call | bytes 4194304 | tf_op jit(solution)/shard_map/pack/pallas_call | solution.py:198
  3.8 7.8 %collective-permute-start.10 = (f32[8,16,8,128]{3,2,1,0:T(8,128)S(1)}, f32[8,16,8,128]{3,2,1,0:T(8,128)S(1)}, u32[]{:S(2)}, u32[]{:S(2)}) collective-permute-start(f32[8,16,8,128]{3,2,1,0:T(8,128)S(1)} %get-tuple-element.56), channel_id=1, source_target_pairs={{0,128},{8,136},{16,144},{24,152},{32,160},{40,168},{48,176},{56,1... | collective-permute-start | bytes 1572872 | tf_op jit(solution)/shard_map/ppermute | solution.py:406
  13.1 2.0 %shard_map.42 = (f32[8,16,8,128]{3,2,1,0:T(8,128)S(1)}, f32[8,16,8,128]{3,2,1,0:T(8,128)S(1)}) custom-call(bf16[3,256,256]{2,1,0:T(8,128)(2,1)S(1)} %shard_map.41.refs_0_, f32[16,16,8,128]{3,2,1,0:T(8,128)S(1)} %get-tuple-element.38.refs_1_), custom_call_target="tpu_custom_call" | custom-call | flops 1207959552 | bytes 3145728 | tf_op jit(solution)/shard_map/pallas_call | solution.py:369
  16.1 8.8 %collective-permute-done.10.refs_2_ = f32[8,16,8,128]{3,2,1,0:T(8,128)S(1)} collective-permute-done((f32[8,16,8,128]{3,2,1,0:T(8,128)S(1)}, f32[8,16,8,128]{3,2,1,0:T(8,128)S(1)}, u32[]{:S(2)}, u32[]{:S(2)}) %collective-permute-start.10) | collective-permute-done | bytes 524320 | tf_op jit(solution)/shard_map/ppermute | solution.py:406
  24.9 2.2 %shard_map.48 = (f32[8,16,8,128]{3,2,1,0:T(8,128)S(1)}, f32[8,16,8,128]{3,2,1,0:T(8,128)S(1)}) custom-call(bf16[3,256,256]{2,1,0:T(8,128)(2,1)S(1)} %shard_map.41.refs_0_, f32[8,16,8,128]{3,2,1,0:T(8,128)S(1)} %get-tuple-element.55.refs_1_, f32[8,16,8,128]{3,2,1,0:T(8,128)S(1)} %collective-permute-done.10.refs_2_), custom_call_target="tpu_custom_call" | custom-call | flops 1207959552 | bytes 3145728 | tf_op jit(solution)/shard_map/pallas_call | solution.py:369
  27.2 1.9 %collective-permute-start.11 = (f32[8,16,8,128]{3,2,1,0:T(8,128)S(1)}, f32[8,16,8,128]{3,2,1,0:T(8,128)S(1)}, u32[]{:S(2)}, u32[]{:S(2)}) collective-permute-start(f32[8,16,8,128]{3,2,1,0:T(8,128)S(1)} %get-tuple-element.58), channel_id=1, source_target_pairs={{0,8},{8,0},{16,24},{24,16},{32,40},{40,32},{48,56},{56,48},{64,72... | collective-permute-start | bytes 1572872 | tf_op jit(solution)/shard_map/ppermute | solution.py:406
  29.4 2.1 %shard_map.43 = (f32[8,16,8,128]{3,2,1,0:T(8,128)S(1)}, f32[8,16,8,128]{3,2,1,0:T(8,128)S(1)}) custom-call(bf16[3,256,256]{2,1,0:T(8,128)(2,1)S(1)} %shard_map.40.refs_0_, f32[8,16,8,128]{3,2,1,0:T(8,128)S(1)} %get-tuple-element.39.refs_1_, f32[8,16,8,128]{3,2,1,0:T(8,128)S(1)} %collective-permute-done.refs_2_), custom_call_target="tpu_custom_call" | custom-call | flops 1207959552 | bytes 3145728 | tf_op jit(solution)/shard_map/pallas_call | solution.py:369
  31.6 14.0 %collective-permute-start.1 = (f32[8,16,8,128]{3,2,1,0:T(8,128)S(1)}, f32[8,16,8,128]{3,2,1,0:T(8,128)S(1)}, u32[]{:S(2)}, u32[]{:S(2)}) collective-permute-start(f32[8,16,8,128]{3,2,1,0:T(8,128)S(1)} %get-tuple-element.42), channel_id=1, source_target_pairs={{0,128},{8,136},{16,144},{24,152},{32,160},{40,168},{48,176},{56,1... | collective-permute-start | bytes 1572872 | tf_op jit(solution)/shard_map/ppermute | solution.py:406
  46.0 2.0 %shard_map.49.refs_1_ = f32[16,16,8,128]{3,2,1,0:T(8,128)S(1)} custom-call(bf16[3,256,256]{2,1,0:T(8,128)(2,1)S(1)} %shard_map.40.refs_0_, f32[8,16,8,128]{3,2,1,0:T(8,128)S(1)} %get-tuple-element.57.refs_1_, f32[8,16,8,128]{3,2,1,0:T(8,128)S(1)} %collective-permute-done.11.refs_2_), custom_call_target="tpu_custom_call" | custom-call | flops 1207959552 | bytes 3145728 | tf_op jit(solution)/shard_map/pallas_call | solution.py:369
  48.0 2.2 %shard_map.50 = (f32[16,8,8,128]{3,2,1,0:T(8,128)S(1)}, f32[16,8,8,128]{3,2,1,0:T(8,128)S(1)}) custom-call(bf16[3,256,256]{2,1,0:T(8,128)(2,1)S(1)} %shard_map.39.refs_0_, f32[16,16,8,128]{3,2,1,0:T(8,128)S(1)} %shard_map.49.refs_1_), custom_call_target="tpu_custom_call" | custom-call | flops 1207959552 | bytes 3145728 | tf_op jit(solution)/shard_map/pallas_call | solution.py:369
  50.6 8.6 %collective-permute-done.1.refs_2_ = f32[8,16,8,128]{3,2,1,0:T(8,128)S(1)} collective-permute-done((f32[8,16,8,128]{3,2,1,0:T(8,128)S(1)}, f32[8,16,8,128]{3,2,1,0:T(8,128)S(1)}, u32[]{:S(2)}, u32[]{:S(2)}) %collective-permute-start.1) | collective-permute-done | bytes 524320 | tf_op jit(solution)/shard_map/ppermute | solution.py:406
  59.1 2.0 %shard_map.44 = (f32[16,8,8,128]{3,2,1,0:T(8,128)S(1)}, f32[16,8,8,128]{3,2,1,0:T(8,128)S(1)}) custom-call(bf16[3,256,256]{2,1,0:T(8,128)(2,1)S(1)} %shard_map.39.refs_0_, f32[8,16,8,128]{3,2,1,0:T(8,128)S(1)} %get-tuple-element.41.refs_1_, f32[8,16,8,128]{3,2,1,0:T(8,128)S(1)} %collective-permute-done.1.refs_2_), custom_call_target="tpu_custom_call" | custom-call | flops 1207959552 | bytes 3145728 | tf_op jit(solution)/shard_map/pallas_call | solution.py:369
  62.1 12.2 %collective-permute-start.13 = (f32[2,4,8,8,128]{4,3,2,1,0:T(8,128)S(1)}, f32[2,4,8,8,128]{4,3,2,1,0:T(8,128)S(1)}, u32[]{:S(2)}, u32[]{:S(2)}) collective-permute-start(f32[2,4,8,8,128]{4,3,2,1,0:T(8,128)S(1)} %get-tuple-element.62), channel_id=1, source_target_pairs={{0,64},{8,72},{16,80},{24,88},{32,96},{40,104},{48,112},{56,120},{... | collective-permute-start | bytes 786440 | tf_op jit(solution)/shard_map/ppermute | solution.py:414
  74.3 4.6 %collective-permute-start.14 = (f32[2,4,8,8,128]{4,3,2,1,0:T(8,128)S(1)}, f32[2,4,8,8,128]{4,3,2,1,0:T(8,128)S(1)}, u32[]{:S(2)}, u32[]{:S(2)}) collective-permute-start(f32[2,4,8,8,128]{4,3,2,1,0:T(8,128)S(1)} %get-tuple-element.63), channel_id=1, source_target_pairs={{0,128},{8,136},{16,144},{24,152},{32,160},{40,168},{48,176},{56,1... | collective-permute-start | bytes 786440 | tf_op jit(solution)/shard_map/ppermute | solution.py:414
  78.8 2.2 %collective-permute-start.15 = (f32[2,4,8,8,128]{4,3,2,1,0:T(8,128)S(1)}, f32[2,4,8,8,128]{4,3,2,1,0:T(8,128)S(1)}, u32[]{:S(2)}, u32[]{:S(2)}) collective-permute-start(f32[2,4,8,8,128]{4,3,2,1,0:T(8,128)S(1)} %get-tuple-element.64), channel_id=1, source_target_pairs={{0,192},{8,200},{16,208},{24,216},{32,224},{40,232},{48,240},{56,2... | collective-permute-start | bytes 786440 | tf_op jit(solution)/shard_map/ppermute | solution.py:414
  82.3 2.5 %collective-permute-start.4 = (f32[2,4,8,8,128]{4,3,2,1,0:T(8,128)S(1)}, f32[2,4,8,8,128]{4,3,2,1,0:T(8,128)S(1)}, u32[]{:S(2)}, u32[]{:S(2)}) collective-permute-start(f32[2,4,8,8,128]{4,3,2,1,0:T(8,128)S(1)} %get-tuple-element.47), channel_id=1, source_target_pairs={{0,32},{8,40},{16,48},{24,56},{32,0},{40,8},{48,16},{56,24},{64,96... | collective-permute-start | bytes 786440 | tf_op jit(solution)/shard_map/ppermute | solution.py:414
  84.8 2.4 %collective-permute-done.13.refs_1_ = f32[2,4,8,8,128]{4,3,2,1,0:T(8,128)S(1)} collective-permute-done((f32[2,4,8,8,128]{4,3,2,1,0:T(8,128)S(1)}, f32[2,4,8,8,128]{4,3,2,1,0:T(8,128)S(1)}, u32[]{:S(2)}, u32[]{:S(2)}) %collective-permute-start.13) | collective-permute-done | bytes 262176 | tf_op jit(solution)/shard_map/ppermute | solution.py:414
  87.2 2.5 %collective-permute-start.5 = (f32[2,4,8,8,128]{4,3,2,1,0:T(8,128)S(1)}, f32[2,4,8,8,128]{4,3,2,1,0:T(8,128)S(1)}, u32[]{:S(2)}, u32[]{:S(2)}) collective-permute-start(f32[2,4,8,8,128]{4,3,2,1,0:T(8,128)S(1)} %get-tuple-element.48), channel_id=1, source_target_pairs={{0,48},{8,56},{16,0},{24,8},{32,16},{40,24},{48,32},{56,40},{64,11... | collective-permute-start | bytes 786440 | tf_op jit(solution)/shard_map/ppermute | solution.py:414
  89.6 11.7 %collective-permute-done.14.refs_2_ = f32[2,4,8,8,128]{4,3,2,1,0:T(8,128)S(1)} collective-permute-done((f32[2,4,8,8,128]{4,3,2,1,0:T(8,128)S(1)}, f32[2,4,8,8,128]{4,3,2,1,0:T(8,128)S(1)}, u32[]{:S(2)}, u32[]{:S(2)}) %collective-permute-start.14) | collective-permute-done | bytes 262176 | tf_op jit(solution)/shard_map/ppermute | solution.py:414
  102.7 2.5 %collective-permute-start.17 = (f32[2,4,8,8,128]{4,3,2,1,0:T(8,128)S(1)}, f32[2,4,8,8,128]{4,3,2,1,0:T(8,128)S(1)}, u32[]{:S(2)}, u32[]{:S(2)}) collective-permute-start(f32[2,4,8,8,128]{4,3,2,1,0:T(8,128)S(1)} %get-tuple-element.67), channel_id=1, source_target_pairs={{0,32},{8,40},{16,48},{24,56},{32,0},{40,8},{48,16},{56,24},{64,96... | collective-permute-start | bytes 786440 | tf_op jit(solution)/shard_map/ppermute | solution.py:414
  106.4 3.4 %collective-permute-start.7 = (f32[2,4,8,8,128]{4,3,2,1,0:T(8,128)S(1)}, f32[2,4,8,8,128]{4,3,2,1,0:T(8,128)S(1)}, u32[]{:S(2)}, u32[]{:S(2)}) collective-permute-start(f32[2,4,8,8,128]{4,3,2,1,0:T(8,128)S(1)} %get-tuple-element.51), channel_id=1, source_target_pairs={{0,128},{8,136},{16,144},{24,152},{32,160},{40,168},{48,176},{56,1... | collective-permute-start | bytes 786440 | tf_op jit(solution)/shard_map/ppermute | solution.py:414
  110.1 3.0 %collective-permute-start.8 = (f32[2,4,8,8,128]{4,3,2,1,0:T(8,128)S(1)}, f32[2,4,8,8,128]{4,3,2,1,0:T(8,128)S(1)}, u32[]{:S(2)}, u32[]{:S(2)}) collective-permute-start(f32[2,4,8,8,128]{4,3,2,1,0:T(8,128)S(1)} %get-tuple-element.52), channel_id=1, source_target_pairs={{0,192},{8,200},{16,208},{24,216},{32,224},{40,232},{48,240},{56,2... | collective-permute-start | bytes 786440 | tf_op jit(solution)/shard_map/ppermute | solution.py:414
  114.0 2.6 %collective-permute-done.17.refs_3_ = f32[2,4,8,8,128]{4,3,2,1,0:T(8,128)S(1)} collective-permute-done((f32[2,4,8,8,128]{4,3,2,1,0:T(8,128)S(1)}, f32[2,4,8,8,128]{4,3,2,1,0:T(8,128)S(1)}, u32[]{:S(2)}, u32[]{:S(2)}) %collective-permute-start.17) | collective-permute-done | bytes 262176 | tf_op jit(solution)/shard_map/ppermute | solution.py:414
  116.6 2.2 %shard_map.53 = (f32[8,16,8,128]{3,2,1,0:T(8,128)S(1)}, f32[8,16,8,128]{3,2,1,0:T(8,128)S(1)}) custom-call(bf16[3,256,256]{2,1,0:T(8,128)(2,1)S(1)} %shard_map.38.refs_0_, f32[2,4,8,8,128]{4,3,2,1,0:T(8,128)S(1)} %get-tuple-element.65.refs_1_, f32[2,4,8,8,128]{4,3,2,1,0:T(8,128)S(1)} %collective-permute-done.16.refs_2_, ...), custom_call_target="tpu_custom_call" | custom-call | flops 1207959552 | bytes 3145728 | tf_op jit(solution)/shard_map/pallas_call | solution.py:369
  118.9 3.0 %collective-permute-start.19 = (f32[8,16,8,128]{3,2,1,0:T(8,128)S(1)}, f32[8,16,8,128]{3,2,1,0:T(8,128)S(1)}, u32[]{:S(2)}, u32[]{:S(2)}) collective-permute-start(f32[8,16,8,128]{3,2,1,0:T(8,128)S(1)} %get-tuple-element.70), channel_id=1, source_target_pairs={{0,4},{1,5},{2,6},{3,7},{4,0},{5,1},{6,2},{7,3},{8,12},{9,13},{10,... | collective-permute-start | bytes 1572872 | tf_op jit(solution)/shard_map/ppermute | solution.py:406
  121.9 4.8 %collective-permute-done.7.refs_3_ = f32[2,4,8,8,128]{4,3,2,1,0:T(8,128)S(1)} collective-permute-done((f32[2,4,8,8,128]{4,3,2,1,0:T(8,128)S(1)}, f32[2,4,8,8,128]{4,3,2,1,0:T(8,128)S(1)}, u32[]{:S(2)}, u32[]{:S(2)}) %collective-permute-start.7) | collective-permute-done | bytes 262176 | tf_op jit(solution)/shard_map/ppermute | solution.py:414
  126.7 5.8 %collective-permute-done.8.refs_4_ = f32[2,4,8,8,128]{4,3,2,1,0:T(8,128)S(1)} collective-permute-done((f32[2,4,8,8,128]{4,3,2,1,0:T(8,128)S(1)}, f32[2,4,8,8,128]{4,3,2,1,0:T(8,128)S(1)}, u32[]{:S(2)}, u32[]{:S(2)}) %collective-permute-start.8) | collective-permute-done | bytes 262176 | tf_op jit(solution)/shard_map/ppermute | solution.py:414
  132.5 2.2 %shard_map.47 = (f32[8,16,8,128]{3,2,1,0:T(8,128)S(1)}, f32[8,16,8,128]{3,2,1,0:T(8,128)S(1)}) custom-call(bf16[3,256,256]{2,1,0:T(8,128)(2,1)S(1)} %shard_map.38.refs_0_, f32[2,4,8,8,128]{4,3,2,1,0:T(8,128)S(1)} %get-tuple-element.49.refs_1_, f32[2,4,8,8,128]{4,3,2,1,0:T(8,128)S(1)} %collective-permute-done.6.refs_2_, ...), custom_call_target="tpu_custom_call" | custom-call | flops 1207959552 | bytes 3145728 | tf_op jit(solution)/shard_map/pallas_call | solution.py:369
  134.7 3.3 %collective-permute-start.9 = (f32[8,16,8,128]{3,2,1,0:T(8,128)S(1)}, f32[8,16,8,128]{3,2,1,0:T(8,128)S(1)}, u32[]{:S(2)}, u32[]{:S(2)}) collective-permute-start(f32[8,16,8,128]{3,2,1,0:T(8,128)S(1)} %get-tuple-element.54), channel_id=1, source_target_pairs={{0,4},{1,5},{2,6},{3,7},{4,0},{5,1},{6,2},{7,3},{8,12},{9,13},{10,... | collective-permute-start | bytes 1572872 | tf_op jit(solution)/shard_map/ppermute | solution.py:406
  140.1 4.1 %shard_map.54.refs_3_ = f32[4,512,256]{2,1,0:T(8,128)S(1)} custom-call(bf16[3,256,256]{2,1,0:T(8,128)(2,1)S(1)} %shard_map.37.refs_0_, f32[8,16,8,128]{3,2,1,0:T(8,128)S(1)} %get-tuple-element.69.refs_1_, f32[8,16,8,128]{3,2,1,0:T(8,128)S(1)} %collective-permute-done.19.refs_2_, bf16[2,2,256,256]{3,2,1,0:T(8,128)(2,1)S(1)} %low_weights.1.refs_3_.refs_4_), custom_call_target="tpu_custom_call" | custom-call | flops 1207959552 | bytes 3145728 | tf_op jit(solution)/shard_map/pallas_call | solution.py:369
  144.3 5.3 %collective-permute-done.9.refs_2_ = f32[8,16,8,128]{3,2,1,0:T(8,128)S(1)} collective-permute-done((f32[8,16,8,128]{3,2,1,0:T(8,128)S(1)}, f32[8,16,8,128]{3,2,1,0:T(8,128)S(1)}, u32[]{:S(2)}, u32[]{:S(2)}) %collective-permute-start.9) | collective-permute-done | bytes 524320 | tf_op jit(solution)/shard_map/ppermute | solution.py:406
  149.5 4.1 %shard_map.55 = f32[2,16,8,2,8,128]{5,4,3,2,1,0:T(8,128)} custom-call(bf16[3,256,256]{2,1,0:T(8,128)(2,1)S(1)} %shard_map.37.refs_0_, f32[8,16,8,128]{3,2,1,0:T(8,128)S(1)} %get-tuple-element.53.refs_1_, f32[8,16,8,128]{3,2,1,0:T(8,128)S(1)} %collective-permute-done.9.refs_2_, f32[4,512,256]{2,1,0:T(8,128)S(1)} %shard_map.54.refs_3_, ...), custom_call_target="tpu_custom_call" | custom-call | flops 1207959552 | bytes 3145728 | tf_op jit(solution)/shard_map/pallas_call | solution.py:369
  (36 shorter events, 13.4 us)
Async XLA Ops:
  0.0 1.6 %copy-start.1 = (f32[2,1,1,262144]{3,2,1,0:T(1,128)S(1)}, f32[2,1,1,262144]{3,2,1,0:T(1,128)}, u32[]{:S(2)}) copy-start(f32[2,1,1,262144]{3,2,1,0:T(1,128)} %param.3) | copy-start | bytes 6291460
  3.8 21.1 %collective-permute-start.10 = (f32[8,16,8,128]{3,2,1,0:T(8,128)S(1)}, f32[8,16,8,128]{3,2,1,0:T(8,128)S(1)}, u32[]{:S(2)}, u32[]{:S(2)}) collective-permute-start(f32[8,16,8,128]{3,2,1,0:T(8,128)S(1)} %get-tuple-element.56), channel_id=1, source_target_pairs={{0,128},{8,136},{16,144},{24,152},{32,160},{40,168},{48,176},{56,1... | collective-permute-start | bytes 1572872 | tf_op jit(solution)/shard_map/ppermute | solution.py:406
  15.1 14.4 %collective-permute-start = (f32[8,16,8,128]{3,2,1,0:T(8,128)S(1)}, f32[8,16,8,128]{3,2,1,0:T(8,128)S(1)}, u32[]{:S(2)}, u32[]{:S(2)}) collective-permute-start(f32[8,16,8,128]{3,2,1,0:T(8,128)S(1)} %get-tuple-element.40), channel_id=1, source_target_pairs={{0,8},{8,0},{16,24},{24,16},{32,40},{40,32},{48,56},{56,48},{64,72... | collective-permute-start | bytes 1572872 | tf_op jit(solution)/shard_map/ppermute | solution.py:406
  24.9 4.2 %copy-start = (f32[5,4,2,128,128]{4,3,2,1,0:T(8,128)S(1)}, f32[5,4,2,128,128]{4,3,2,1,0:T(8,128)}, u32[]{:S(2)}) copy-start(f32[5,4,2,128,128]{4,3,2,1,0:T(8,128)} %gates_ref.1) | copy-start | bytes 7864324
  27.2 18.8 %collective-permute-start.11 = (f32[8,16,8,128]{3,2,1,0:T(8,128)S(1)}, f32[8,16,8,128]{3,2,1,0:T(8,128)S(1)}, u32[]{:S(2)}, u32[]{:S(2)}) collective-permute-start(f32[8,16,8,128]{3,2,1,0:T(8,128)S(1)} %get-tuple-element.58), channel_id=1, source_target_pairs={{0,8},{8,0},{16,24},{24,16},{32,40},{40,32},{48,56},{56,48},{64,72... | collective-permute-start | bytes 1572872 | tf_op jit(solution)/shard_map/ppermute | solution.py:406
  31.6 27.6 %collective-permute-start.1 = (f32[8,16,8,128]{3,2,1,0:T(8,128)S(1)}, f32[8,16,8,128]{3,2,1,0:T(8,128)S(1)}, u32[]{:S(2)}, u32[]{:S(2)}) collective-permute-start(f32[8,16,8,128]{3,2,1,0:T(8,128)S(1)} %get-tuple-element.42), channel_id=1, source_target_pairs={{0,128},{8,136},{16,144},{24,152},{32,160},{40,168},{48,176},{56,1... | collective-permute-start | bytes 1572872 | tf_op jit(solution)/shard_map/ppermute | solution.py:406
  50.2 11.8 %collective-permute-start.12 = (f32[16,8,8,128]{3,2,1,0:T(8,128)S(1)}, f32[16,8,8,128]{3,2,1,0:T(8,128)S(1)}, u32[]{:S(2)}, u32[]{:S(2)}) collective-permute-start(f32[16,8,8,128]{3,2,1,0:T(8,128)S(1)} %get-tuple-element.60), channel_id=1, source_target_pairs={{0,8},{8,0},{16,24},{24,16},{32,40},{40,32},{48,56},{56,48},{64,72... | collective-permute-start | bytes 1572872 | tf_op jit(solution)/shard_map/ppermute | solution.py:406
  61.2 19.8 %collective-permute-start.2 = (f32[16,8,8,128]{3,2,1,0:T(8,128)S(1)}, f32[16,8,8,128]{3,2,1,0:T(8,128)S(1)}, u32[]{:S(2)}, u32[]{:S(2)}) collective-permute-start(f32[16,8,8,128]{3,2,1,0:T(8,128)S(1)} %get-tuple-element.44), channel_id=1, source_target_pairs={{0,8},{8,0},{16,24},{24,16},{32,40},{40,32},{48,56},{56,48},{64,72... | collective-permute-start | bytes 1572872 | tf_op jit(solution)/shard_map/ppermute | solution.py:406
  62.0 51.1 %copy-start.2 = (s32[32]{0:T(128)S(1)}, s32[32]{0:T(128)}, u32[]{:S(2)}) copy-start(s32[32]{0:T(128)} %refs_0_.5) | copy-start | bytes 388
  62.1 25.1 %collective-permute-start.13 = (f32[2,4,8,8,128]{4,3,2,1,0:T(8,128)S(1)}, f32[2,4,8,8,128]{4,3,2,1,0:T(8,128)S(1)}, u32[]{:S(2)}, u32[]{:S(2)}) collective-permute-start(f32[2,4,8,8,128]{4,3,2,1,0:T(8,128)S(1)} %get-tuple-element.62), channel_id=1, source_target_pairs={{0,64},{8,72},{16,80},{24,88},{32,96},{40,104},{48,112},{56,120},{... | collective-permute-start | bytes 786440 | tf_op jit(solution)/shard_map/ppermute | solution.py:414
  74.3 27.1 %collective-permute-start.14 = (f32[2,4,8,8,128]{4,3,2,1,0:T(8,128)S(1)}, f32[2,4,8,8,128]{4,3,2,1,0:T(8,128)S(1)}, u32[]{:S(2)}, u32[]{:S(2)}) collective-permute-start(f32[2,4,8,8,128]{4,3,2,1,0:T(8,128)S(1)} %get-tuple-element.63), channel_id=1, source_target_pairs={{0,128},{8,136},{16,144},{24,152},{32,160},{40,168},{48,176},{56,1... | collective-permute-start | bytes 786440 | tf_op jit(solution)/shard_map/ppermute | solution.py:414
  78.8 22.5 %collective-permute-start.15 = (f32[2,4,8,8,128]{4,3,2,1,0:T(8,128)S(1)}, f32[2,4,8,8,128]{4,3,2,1,0:T(8,128)S(1)}, u32[]{:S(2)}, u32[]{:S(2)}) collective-permute-start(f32[2,4,8,8,128]{4,3,2,1,0:T(8,128)S(1)} %get-tuple-element.64), channel_id=1, source_target_pairs={{0,192},{8,200},{16,208},{24,216},{32,224},{40,232},{48,240},{56,2... | collective-permute-start | bytes 786440 | tf_op jit(solution)/shard_map/ppermute | solution.py:414
  81.1 24.1 %collective-permute-start.3 = (f32[2,4,8,8,128]{4,3,2,1,0:T(8,128)S(1)}, f32[2,4,8,8,128]{4,3,2,1,0:T(8,128)S(1)}, u32[]{:S(2)}, u32[]{:S(2)}) collective-permute-start(f32[2,4,8,8,128]{4,3,2,1,0:T(8,128)S(1)} %get-tuple-element.46), channel_id=1, source_target_pairs={{0,16},{8,24},{16,32},{24,40},{32,48},{40,56},{48,0},{56,8},{64,80... | collective-permute-start | bytes 786440 | tf_op jit(solution)/shard_map/ppermute | solution.py:414
  82.3 23.9 %collective-permute-start.4 = (f32[2,4,8,8,128]{4,3,2,1,0:T(8,128)S(1)}, f32[2,4,8,8,128]{4,3,2,1,0:T(8,128)S(1)}, u32[]{:S(2)}, u32[]{:S(2)}) collective-permute-start(f32[2,4,8,8,128]{4,3,2,1,0:T(8,128)S(1)} %get-tuple-element.47), channel_id=1, source_target_pairs={{0,32},{8,40},{16,48},{24,56},{32,0},{40,8},{48,16},{56,24},{64,96... | collective-permute-start | bytes 786440 | tf_op jit(solution)/shard_map/ppermute | solution.py:414
  87.2 19.1 %collective-permute-start.5 = (f32[2,4,8,8,128]{4,3,2,1,0:T(8,128)S(1)}, f32[2,4,8,8,128]{4,3,2,1,0:T(8,128)S(1)}, u32[]{:S(2)}, u32[]{:S(2)}) collective-permute-start(f32[2,4,8,8,128]{4,3,2,1,0:T(8,128)S(1)} %get-tuple-element.48), channel_id=1, source_target_pairs={{0,48},{8,56},{16,0},{24,8},{32,16},{40,24},{48,32},{56,40},{64,11... | collective-permute-start | bytes 786440 | tf_op jit(solution)/shard_map/ppermute | solution.py:414
  101.4 8.7 %collective-permute-start.16 = (f32[2,4,8,8,128]{4,3,2,1,0:T(8,128)S(1)}, f32[2,4,8,8,128]{4,3,2,1,0:T(8,128)S(1)}, u32[]{:S(2)}, u32[]{:S(2)}) collective-permute-start(f32[2,4,8,8,128]{4,3,2,1,0:T(8,128)S(1)} %get-tuple-element.66), channel_id=1, source_target_pairs={{0,16},{8,24},{16,32},{24,40},{32,48},{40,56},{48,0},{56,8},{64,80... | collective-permute-start | bytes 786440 | tf_op jit(solution)/shard_map/ppermute | solution.py:414
  102.7 13.9 %collective-permute-start.17 = (f32[2,4,8,8,128]{4,3,2,1,0:T(8,128)S(1)}, f32[2,4,8,8,128]{4,3,2,1,0:T(8,128)S(1)}, u32[]{:S(2)}, u32[]{:S(2)}) collective-permute-start(f32[2,4,8,8,128]{4,3,2,1,0:T(8,128)S(1)} %get-tuple-element.67), channel_id=1, source_target_pairs={{0,32},{8,40},{16,48},{24,56},{32,0},{40,8},{48,16},{56,24},{64,96... | collective-permute-start | bytes 786440 | tf_op jit(solution)/shard_map/ppermute | solution.py:414
  105.1 11.5 %collective-permute-start.18 = (f32[2,4,8,8,128]{4,3,2,1,0:T(8,128)S(1)}, f32[2,4,8,8,128]{4,3,2,1,0:T(8,128)S(1)}, u32[]{:S(2)}, u32[]{:S(2)}) collective-permute-start(f32[2,4,8,8,128]{4,3,2,1,0:T(8,128)S(1)} %get-tuple-element.68), channel_id=1, source_target_pairs={{0,48},{8,56},{16,0},{24,8},{32,16},{40,24},{48,32},{56,40},{64,11... | collective-permute-start | bytes 786440 | tf_op jit(solution)/shard_map/ppermute | solution.py:414
  106.4 15.5 %collective-permute-start.6 = (f32[2,4,8,8,128]{4,3,2,1,0:T(8,128)S(1)}, f32[2,4,8,8,128]{4,3,2,1,0:T(8,128)S(1)}, u32[]{:S(2)}, u32[]{:S(2)}) collective-permute-start(f32[2,4,8,8,128]{4,3,2,1,0:T(8,128)S(1)} %get-tuple-element.50), channel_id=1, source_target_pairs={{0,64},{8,72},{16,80},{24,88},{32,96},{40,104},{48,112},{56,120},{... | collective-permute-start | bytes 786440 | tf_op jit(solution)/shard_map/ppermute | solution.py:414
  106.4 20.2 %collective-permute-start.7 = (f32[2,4,8,8,128]{4,3,2,1,0:T(8,128)S(1)}, f32[2,4,8,8,128]{4,3,2,1,0:T(8,128)S(1)}, u32[]{:S(2)}, u32[]{:S(2)}) collective-permute-start(f32[2,4,8,8,128]{4,3,2,1,0:T(8,128)S(1)} %get-tuple-element.51), channel_id=1, source_target_pairs={{0,128},{8,136},{16,144},{24,152},{32,160},{40,168},{48,176},{56,1... | collective-permute-start | bytes 786440 | tf_op jit(solution)/shard_map/ppermute | solution.py:414
  110.1 22.4 %collective-permute-start.8 = (f32[2,4,8,8,128]{4,3,2,1,0:T(8,128)S(1)}, f32[2,4,8,8,128]{4,3,2,1,0:T(8,128)S(1)}, u32[]{:S(2)}, u32[]{:S(2)}) collective-permute-start(f32[2,4,8,8,128]{4,3,2,1,0:T(8,128)S(1)} %get-tuple-element.52), channel_id=1, source_target_pairs={{0,192},{8,200},{16,208},{24,216},{32,224},{40,232},{48,240},{56,2... | collective-permute-start | bytes 786440 | tf_op jit(solution)/shard_map/ppermute | solution.py:414
  118.9 21.3 %collective-permute-start.19 = (f32[8,16,8,128]{3,2,1,0:T(8,128)S(1)}, f32[8,16,8,128]{3,2,1,0:T(8,128)S(1)}, u32[]{:S(2)}, u32[]{:S(2)}) collective-permute-start(f32[8,16,8,128]{3,2,1,0:T(8,128)S(1)} %get-tuple-element.70), channel_id=1, source_target_pairs={{0,4},{1,5},{2,6},{3,7},{4,0},{5,1},{6,2},{7,3},{8,12},{9,13},{10,... | collective-permute-start | bytes 1572872 | tf_op jit(solution)/shard_map/ppermute | solution.py:406
  134.7 14.8 %collective-permute-start.9 = (f32[8,16,8,128]{3,2,1,0:T(8,128)S(1)}, f32[8,16,8,128]{3,2,1,0:T(8,128)S(1)}, u32[]{:S(2)}, u32[]{:S(2)}) collective-permute-start(f32[8,16,8,128]{3,2,1,0:T(8,128)S(1)} %get-tuple-element.54), channel_id=1, source_target_pairs={{0,4},{1,5},{2,6},{3,7},{4,0},{5,1},{6,2},{7,3},{8,12},{9,13},{10,... | collective-permute-start | bytes 1572872 | tf_op jit(solution)/shard_map/ppermute | solution.py:406

commit v8 on v7

--- a/solution.py
+++ b/solution.py
@@ -178,26 +178,27 @@
 def pack_kernel(state_ref, *outs):
     own = lax.axis_index("row") >> 4 == 1
 
-    def some(p, carry):
-        tops = []
-        for top in range(2):
-            rows = [state_ref[c, pl.ds(1024 * top + p, HALF, stride=16), :] for c in range(2)]
-            tops.append(cross(rows[0], rows[1], 64))
+    def some(i, carry):
+        rows = pl.ds(GD * i, GD)
+        tops = [cross(state_ref[0, t, rows], state_ref[1, t, rows], 64) for t in range(2)]
         sides = [cross(tops[0][b], tops[1][b], 32)[0] for b in range(2)]
         for out, side in zip(outs[:2], in_order(own, *sides)):
-            out[:, p] = side.reshape(8, 8, GD)
-        for top in range(2):
-            outs[2][8 * top : 8 * top + 8, p] = cross(*tops[top], 32)[1].reshape(8, 8, GD)
+            out[rows] = side
+        for t in range(2):
+            outs[2][t, rows] = cross(*tops[t], 32)[1]
         return carry
 
-    lax.fori_loop(0, 16, some, 0, unroll=8)
+    lax.fori_loop(0, 8, some, 0, unroll=4)
 
 
 def pack(state):
     vmem = pl.BlockSpec(memory_space=pltpu.VMEM)
     return pl.pallas_call(
         pack_kernel,
-        out_shape=[jax.ShapeDtypeStruct(shape, F32) for shape in (PART, PART, STATE)],
+        out_shape=[
+            jax.ShapeDtypeStruct(shape, F32)
+            for shape in ((1024, 128), (1024, 128), (2, 1024, 128))
+        ],
         in_specs=[vmem],
         out_specs=[vmem] * 3,
         cost_estimate=pl.CostEstimate(flops=0, bytes_accessed=4 << 20, transcendentals=0),
@@ -231,12 +232,17 @@
     def load_start(i):
         blocks = []
         for p in (2 * i, 2 * i + 1):
-            sides = in_order(own, ins[0][:, p].reshape(HALF, GD), ins[1][:, p].reshape(HALF, GD))
+            rows = pl.ds(p, HALF, stride=16)
+            sides = in_order(own, ins[0][rows, :], ins[1][rows, :])
             blocks.append(jnp.concatenate(cross(*sides, 32), axis=0))
         return blocks
 
     def load_whole(i):
-        return [ins[0][:, p].reshape(GD, GD) for p in (2 * i, 2 * i + 1)]
+        blocks = []
+        for p in (2 * i, 2 * i + 1):
+            rows = pl.ds(p, HALF, stride=16)
+            blocks.append(jnp.concatenate([ins[0][0, rows, :], ins[0][1, rows, :]], axis=0))
+        return blocks
 
     def load_join(i):
         blocks = []
@@ -429,7 +435,7 @@
 
 
 def circuit(amplitudes, gate_matrices, permutation):
-    state = amplitudes.reshape(2, 2048, 128)
+    state = amplitudes.reshape(2, 2, 1024, 128)
     mid = ("mid", "mid")
     kinds = (
         ((None, None), mid, ("xor2", None)),

time: 155 us -> 154 us (level)
  no operation moved by 1% of the time
where the time goes in v8:
time: 154 us; the launch traced here: 153 us
  starting transfers between devices  68.7 us (45%)
  waiting for transfers between devices  50.2 us (33%)
  Pallas kernels  31.3 us (20%)
  local copies, waits for them, and re-layouts  2.67 us (2%)
    ppermute x12, starting transfers between devices, shift_row(): return lax.ppermute(value, 'row', pairs)  36.6 us
    ppermute x8, starting transfers between devices, flip(): lax.ppermute(value, axis, [(s, s ^ mask) for s in range(lax.axis_size(axi...  32.1 us
    ppermute x12, waiting for transfers between devices, shift_row(): return lax.ppermute(value, 'row', pairs)  27.5 us
    pallas_call x10, Pallas kernels, run_segment(): pl.pallas_call(functools.partial(segment_kernel, source, target, len(args...  25.4 us
    ppermute x8, waiting for transfers between devices, flip(): lax.ppermute(value, axis, [(s, s ^ mask) for s in range(lax.axis_size(axi...  22.7 us
  transfers between devices with their start and end apart: 20, of which 9 were waited for; matrix products, arithmetic and copies ran while one was open for 1% of the time, Pallas kernels for 17%

profile of v8, /device:TPU:1, one launch (start us, length us, event | category | flops | bytes accessed | tf_op | source)
XLA Modules:
  0.0 153.0 jit_solution(5669133393406292796)
XLA Ops:
  3.1 7.8 %collective-permute-start.10 = (f32[1024,128]{1,0:T(8,128)S(1)}, f32[1024,128]{1,0:T(8,128)S(1)}, u32[]{:S(2)}, u32[]{:S(2)}) collective-permute-start(f32[1024,128]{1,0:T(8,128)S(1)} %get-tuple-element.56), channel_id=1, source_target_pairs={{0,128},{8,136},{16,144},{24,152},{32,160},{40,168},{48,176},{56,1... | collective-permute-start | bytes 1572872 | tf_op jit(solution)/shard_map/ppermute | solution.py:412
  12.3 2.1 %shard_map.42 = (f32[8,16,8,128]{3,2,1,0:T(8,128)S(1)}, f32[8,16,8,128]{3,2,1,0:T(8,128)S(1)}) custom-call(bf16[3,256,256]{2,1,0:T(8,128)(2,1)S(1)} %shard_map.41.refs_0_, f32[2,1024,128]{2,1,0:T(8,128)S(1)} %get-tuple-element.38.refs_1_), custom_call_target="tpu_custom_call" | custom-call | flops 1207959552 | bytes 3145728 | tf_op jit(solution)/shard_map/pallas_call | solution.py:375
  15.5 8.7 %collective-permute-done.10.refs_2_ = f32[1024,128]{1,0:T(8,128)S(1)} collective-permute-done((f32[1024,128]{1,0:T(8,128)S(1)}, f32[1024,128]{1,0:T(8,128)S(1)}, u32[]{:S(2)}, u32[]{:S(2)}) %collective-permute-start.10) | collective-permute-done | bytes 524320 | tf_op jit(solution)/shard_map/ppermute | solution.py:412
  24.2 2.3 %shard_map.48 = (f32[8,16,8,128]{3,2,1,0:T(8,128)S(1)}, f32[8,16,8,128]{3,2,1,0:T(8,128)S(1)}) custom-call(bf16[3,256,256]{2,1,0:T(8,128)(2,1)S(1)} %shard_map.41.refs_0_, f32[1024,128]{1,0:T(8,128)S(1)} %get-tuple-element.55.refs_1_, f32[1024,128]{1,0:T(8,128)S(1)} %collective-permute-done.10.refs_2_), custom_call_target="tpu_custom_call" | custom-call | flops 1207959552 | bytes 3145728 | tf_op jit(solution)/shard_map/pallas_call | solution.py:375
  26.5 1.9 %collective-permute-start.11 = (f32[8,16,8,128]{3,2,1,0:T(8,128)S(1)}, f32[8,16,8,128]{3,2,1,0:T(8,128)S(1)}, u32[]{:S(2)}, u32[]{:S(2)}) collective-permute-start(f32[8,16,8,128]{3,2,1,0:T(8,128)S(1)} %get-tuple-element.58), channel_id=1, source_target_pairs={{0,8},{8,0},{16,24},{24,16},{32,40},{40,32},{48,56},{56,48},{64,72... | collective-permute-start | bytes 1572872 | tf_op jit(solution)/shard_map/ppermute | solution.py:412
  28.8 2.1 %shard_map.43 = (f32[8,16,8,128]{3,2,1,0:T(8,128)S(1)}, f32[8,16,8,128]{3,2,1,0:T(8,128)S(1)}) custom-call(bf16[3,256,256]{2,1,0:T(8,128)(2,1)S(1)} %shard_map.40.refs_0_, f32[8,16,8,128]{3,2,1,0:T(8,128)S(1)} %get-tuple-element.39.refs_1_, f32[8,16,8,128]{3,2,1,0:T(8,128)S(1)} %collective-permute-done.refs_2_), custom_call_target="tpu_custom_call" | custom-call | flops 1207959552 | bytes 3145728 | tf_op jit(solution)/shard_map/pallas_call | solution.py:375
  31.0 14.0 %collective-permute-start.1 = (f32[8,16,8,128]{3,2,1,0:T(8,128)S(1)}, f32[8,16,8,128]{3,2,1,0:T(8,128)S(1)}, u32[]{:S(2)}, u32[]{:S(2)}) collective-permute-start(f32[8,16,8,128]{3,2,1,0:T(8,128)S(1)} %get-tuple-element.42), channel_id=1, source_target_pairs={{0,128},{8,136},{16,144},{24,152},{32,160},{40,168},{48,176},{56,1... | collective-permute-start | bytes 1572872 | tf_op jit(solution)/shard_map/ppermute | solution.py:412
  45.4 2.0 %shard_map.49.refs_1_ = f32[16,16,8,128]{3,2,1,0:T(8,128)S(1)} custom-call(bf16[3,256,256]{2,1,0:T(8,128)(2,1)S(1)} %shard_map.40.refs_0_, f32[8,16,8,128]{3,2,1,0:T(8,128)S(1)} %get-tuple-element.57.refs_1_, f32[8,16,8,128]{3,2,1,0:T(8,128)S(1)} %collective-permute-done.11.refs_2_), custom_call_target="tpu_custom_call" | custom-call | flops 1207959552 | bytes 3145728 | tf_op jit(solution)/shard_map/pallas_call | solution.py:375
  47.3 2.2 %shard_map.50 = (f32[16,8,8,128]{3,2,1,0:T(8,128)S(1)}, f32[16,8,8,128]{3,2,1,0:T(8,128)S(1)}) custom-call(bf16[3,256,256]{2,1,0:T(8,128)(2,1)S(1)} %shard_map.39.refs_0_, f32[16,16,8,128]{3,2,1,0:T(8,128)S(1)} %shard_map.49.refs_1_), custom_call_target="tpu_custom_call" | custom-call | flops 1207959552 | bytes 3145728 | tf_op jit(solution)/shard_map/pallas_call | solution.py:375
  49.9 8.5 %collective-permute-done.1.refs_2_ = f32[8,16,8,128]{3,2,1,0:T(8,128)S(1)} collective-permute-done((f32[8,16,8,128]{3,2,1,0:T(8,128)S(1)}, f32[8,16,8,128]{3,2,1,0:T(8,128)S(1)}, u32[]{:S(2)}, u32[]{:S(2)}) %collective-permute-start.1) | collective-permute-done | bytes 524320 | tf_op jit(solution)/shard_map/ppermute | solution.py:412
  58.5 2.0 %shard_map.44 = (f32[16,8,8,128]{3,2,1,0:T(8,128)S(1)}, f32[16,8,8,128]{3,2,1,0:T(8,128)S(1)}) custom-call(bf16[3,256,256]{2,1,0:T(8,128)(2,1)S(1)} %shard_map.39.refs_0_, f32[8,16,8,128]{3,2,1,0:T(8,128)S(1)} %get-tuple-element.41.refs_1_, f32[8,16,8,128]{3,2,1,0:T(8,128)S(1)} %collective-permute-done.1.refs_2_), custom_call_target="tpu_custom_call" | custom-call | flops 1207959552 | bytes 3145728 | tf_op jit(solution)/shard_map/pallas_call | solution.py:375
  61.4 12.2 %collective-permute-start.13 = (f32[2,4,8,8,128]{4,3,2,1,0:T(8,128)S(1)}, f32[2,4,8,8,128]{4,3,2,1,0:T(8,128)S(1)}, u32[]{:S(2)}, u32[]{:S(2)}) collective-permute-start(f32[2,4,8,8,128]{4,3,2,1,0:T(8,128)S(1)} %get-tuple-element.62), channel_id=1, source_target_pairs={{0,64},{8,72},{16,80},{24,88},{32,96},{40,104},{48,112},{56,120},{... | collective-permute-start | bytes 786440 | tf_op jit(solution)/shard_map/ppermute | solution.py:420
  73.6 4.6 %collective-permute-start.14 = (f32[2,4,8,8,128]{4,3,2,1,0:T(8,128)S(1)}, f32[2,4,8,8,128]{4,3,2,1,0:T(8,128)S(1)}, u32[]{:S(2)}, u32[]{:S(2)}) collective-permute-start(f32[2,4,8,8,128]{4,3,2,1,0:T(8,128)S(1)} %get-tuple-element.63), channel_id=1, source_target_pairs={{0,128},{8,136},{16,144},{24,152},{32,160},{40,168},{48,176},{56,1... | collective-permute-start | bytes 786440 | tf_op jit(solution)/shard_map/ppermute | solution.py:420
  78.2 2.2 %collective-permute-start.15 = (f32[2,4,8,8,128]{4,3,2,1,0:T(8,128)S(1)}, f32[2,4,8,8,128]{4,3,2,1,0:T(8,128)S(1)}, u32[]{:S(2)}, u32[]{:S(2)}) collective-permute-start(f32[2,4,8,8,128]{4,3,2,1,0:T(8,128)S(1)} %get-tuple-element.64), channel_id=1, source_target_pairs={{0,192},{8,200},{16,208},{24,216},{32,224},{40,232},{48,240},{56,2... | collective-permute-start | bytes 786440 | tf_op jit(solution)/shard_map/ppermute | solution.py:420
  81.7 2.5 %collective-permute-start.4 = (f32[2,4,8,8,128]{4,3,2,1,0:T(8,128)S(1)}, f32[2,4,8,8,128]{4,3,2,1,0:T(8,128)S(1)}, u32[]{:S(2)}, u32[]{:S(2)}) collective-permute-start(f32[2,4,8,8,128]{4,3,2,1,0:T(8,128)S(1)} %get-tuple-element.47), channel_id=1, source_target_pairs={{0,32},{8,40},{16,48},{24,56},{32,0},{40,8},{48,16},{56,24},{64,96... | collective-permute-start | bytes 786440 | tf_op jit(solution)/shard_map/ppermute | solution.py:420
  84.2 2.3 %collective-permute-done.13.refs_1_ = f32[2,4,8,8,128]{4,3,2,1,0:T(8,128)S(1)} collective-permute-done((f32[2,4,8,8,128]{4,3,2,1,0:T(8,128)S(1)}, f32[2,4,8,8,128]{4,3,2,1,0:T(8,128)S(1)}, u32[]{:S(2)}, u32[]{:S(2)}) %collective-permute-start.13) | collective-permute-done | bytes 262176 | tf_op jit(solution)/shard_map/ppermute | solution.py:420
  86.5 2.5 %collective-permute-start.5 = (f32[2,4,8,8,128]{4,3,2,1,0:T(8,128)S(1)}, f32[2,4,8,8,128]{4,3,2,1,0:T(8,128)S(1)}, u32[]{:S(2)}, u32[]{:S(2)}) collective-permute-start(f32[2,4,8,8,128]{4,3,2,1,0:T(8,128)S(1)} %get-tuple-element.48), channel_id=1, source_target_pairs={{0,48},{8,56},{16,0},{24,8},{32,16},{40,24},{48,32},{56,40},{64,11... | collective-permute-start | bytes 786440 | tf_op jit(solution)/shard_map/ppermute | solution.py:420
  89.0 11.7 %collective-permute-done.14.refs_2_ = f32[2,4,8,8,128]{4,3,2,1,0:T(8,128)S(1)} collective-permute-done((f32[2,4,8,8,128]{4,3,2,1,0:T(8,128)S(1)}, f32[2,4,8,8,128]{4,3,2,1,0:T(8,128)S(1)}, u32[]{:S(2)}, u32[]{:S(2)}) %collective-permute-start.14) | collective-permute-done | bytes 262176 | tf_op jit(solution)/shard_map/ppermute | solution.py:420
  102.0 2.4 %collective-permute-start.17 = (f32[2,4,8,8,128]{4,3,2,1,0:T(8,128)S(1)}, f32[2,4,8,8,128]{4,3,2,1,0:T(8,128)S(1)}, u32[]{:S(2)}, u32[]{:S(2)}) collective-permute-start(f32[2,4,8,8,128]{4,3,2,1,0:T(8,128)S(1)} %get-tuple-element.67), channel_id=1, source_target_pairs={{0,32},{8,40},{16,48},{24,56},{32,0},{40,8},{48,16},{56,24},{64,96... | collective-permute-start | bytes 786440 | tf_op jit(solution)/shard_map/ppermute | solution.py:420
  105.8 3.4 %collective-permute-start.7 = (f32[2,4,8,8,128]{4,3,2,1,0:T(8,128)S(1)}, f32[2,4,8,8,128]{4,3,2,1,0:T(8,128)S(1)}, u32[]{:S(2)}, u32[]{:S(2)}) collective-permute-start(f32[2,4,8,8,128]{4,3,2,1,0:T(8,128)S(1)} %get-tuple-element.51), channel_id=1, source_target_pairs={{0,128},{8,136},{16,144},{24,152},{32,160},{40,168},{48,176},{56,1... | collective-permute-start | bytes 786440 | tf_op jit(solution)/shard_map/ppermute | solution.py:420
  109.5 3.0 %collective-permute-start.8 = (f32[2,4,8,8,128]{4,3,2,1,0:T(8,128)S(1)}, f32[2,4,8,8,128]{4,3,2,1,0:T(8,128)S(1)}, u32[]{:S(2)}, u32[]{:S(2)}) collective-permute-start(f32[2,4,8,8,128]{4,3,2,1,0:T(8,128)S(1)} %get-tuple-element.52), channel_id=1, source_target_pairs={{0,192},{8,200},{16,208},{24,216},{32,224},{40,232},{48,240},{56,2... | collective-permute-start | bytes 786440 | tf_op jit(solution)/shard_map/ppermute | solution.py:420
  113.4 2.6 %collective-permute-done.17.refs_3_ = f32[2,4,8,8,128]{4,3,2,1,0:T(8,128)S(1)} collective-permute-done((f32[2,4,8,8,128]{4,3,2,1,0:T(8,128)S(1)}, f32[2,4,8,8,128]{4,3,2,1,0:T(8,128)S(1)}, u32[]{:S(2)}, u32[]{:S(2)}) %collective-permute-start.17) | collective-permute-done | bytes 262176 | tf_op jit(solution)/shard_map/ppermute | solution.py:420
  116.0 2.2 %shard_map.53 = (f32[8,16,8,128]{3,2,1,0:T(8,128)S(1)}, f32[8,16,8,128]{3,2,1,0:T(8,128)S(1)}) custom-call(bf16[3,256,256]{2,1,0:T(8,128)(2,1)S(1)} %shard_map.38.refs_0_, f32[2,4,8,8,128]{4,3,2,1,0:T(8,128)S(1)} %get-tuple-element.65.refs_1_, f32[2,4,8,8,128]{4,3,2,1,0:T(8,128)S(1)} %collective-permute-done.16.refs_2_, ...), custom_call_target="tpu_custom_call" | custom-call | flops 1207959552 | bytes 3145728 | tf_op jit(solution)/shard_map/pallas_call | solution.py:375
  118.2 3.0 %collective-permute-start.19 = (f32[8,16,8,128]{3,2,1,0:T(8,128)S(1)}, f32[8,16,8,128]{3,2,1,0:T(8,128)S(1)}, u32[]{:S(2)}, u32[]{:S(2)}) collective-permute-start(f32[8,16,8,128]{3,2,1,0:T(8,128)S(1)} %get-tuple-element.70), channel_id=1, source_target_pairs={{0,4},{1,5},{2,6},{3,7},{4,0},{5,1},{6,2},{7,3},{8,12},{9,13},{10,... | collective-permute-start | bytes 1572872 | tf_op jit(solution)/shard_map/ppermute | solution.py:412
  121.2 5.0 %collective-permute-done.7.refs_3_ = f32[2,4,8,8,128]{4,3,2,1,0:T(8,128)S(1)} collective-permute-done((f32[2,4,8,8,128]{4,3,2,1,0:T(8,128)S(1)}, f32[2,4,8,8,128]{4,3,2,1,0:T(8,128)S(1)}, u32[]{:S(2)}, u32[]{:S(2)}) %collective-permute-start.7) | collective-permute-done | bytes 262176 | tf_op jit(solution)/shard_map/ppermute | solution.py:420
  126.2 5.6 %collective-permute-done.8.refs_4_ = f32[2,4,8,8,128]{4,3,2,1,0:T(8,128)S(1)} collective-permute-done((f32[2,4,8,8,128]{4,3,2,1,0:T(8,128)S(1)}, f32[2,4,8,8,128]{4,3,2,1,0:T(8,128)S(1)}, u32[]{:S(2)}, u32[]{:S(2)}) %collective-permute-start.8) | collective-permute-done | bytes 262176 | tf_op jit(solution)/shard_map/ppermute | solution.py:420
  131.8 2.2 %shard_map.47 = (f32[8,16,8,128]{3,2,1,0:T(8,128)S(1)}, f32[8,16,8,128]{3,2,1,0:T(8,128)S(1)}) custom-call(bf16[3,256,256]{2,1,0:T(8,128)(2,1)S(1)} %shard_map.38.refs_0_, f32[2,4,8,8,128]{4,3,2,1,0:T(8,128)S(1)} %get-tuple-element.49.refs_1_, f32[2,4,8,8,128]{4,3,2,1,0:T(8,128)S(1)} %collective-permute-done.6.refs_2_, ...), custom_call_target="tpu_custom_call" | custom-call | flops 1207959552 | bytes 3145728 | tf_op jit(solution)/shard_map/pallas_call | solution.py:375
  134.1 3.1 %collective-permute-start.9 = (f32[8,16,8,128]{3,2,1,0:T(8,128)S(1)}, f32[8,16,8,128]{3,2,1,0:T(8,128)S(1)}, u32[]{:S(2)}, u32[]{:S(2)}) collective-permute-start(f32[8,16,8,128]{3,2,1,0:T(8,128)S(1)} %get-tuple-element.54), channel_id=1, source_target_pairs={{0,4},{1,5},{2,6},{3,7},{4,0},{5,1},{6,2},{7,3},{8,12},{9,13},{10,... | collective-permute-start | bytes 1572872 | tf_op jit(solution)/shard_map/ppermute | solution.py:412
  137.5 1.8 %low_weights.1.refs_3_.refs_4_ = bf16[2,2,256,256]{3,2,1,0:T(8,128)(2,1)S(1)} custom-call(f32[5,4,2,128,128]{4,3,2,1,0:T(8,128)S(1)} %copy-done), custom_call_target="tpu_custom_call" | custom-call | flops 503316480 | bytes 1048576 | tf_op jit(solution)/shard_map/low_weights/pallas_call | solution.py:134
  139.3 4.1 %shard_map.54.refs_3_ = f32[4,512,256]{2,1,0:T(8,128)S(1)} custom-call(bf16[3,256,256]{2,1,0:T(8,128)(2,1)S(1)} %shard_map.37.refs_0_, f32[8,16,8,128]{3,2,1,0:T(8,128)S(1)} %get-tuple-element.69.refs_1_, f32[8,16,8,128]{3,2,1,0:T(8,128)S(1)} %collective-permute-done.19.refs_2_, bf16[2,2,256,256]{3,2,1,0:T(8,128)(2,1)S(1)} %low_weights.1.refs_3_.refs_4_), custom_call_target="tpu_custom_call" | custom-call | flops 1207959552 | bytes 3145728 | tf_op jit(solution)/shard_map/pallas_call | solution.py:375
  143.5 5.5 %collective-permute-done.9.refs_2_ = f32[8,16,8,128]{3,2,1,0:T(8,128)S(1)} collective-permute-done((f32[8,16,8,128]{3,2,1,0:T(8,128)S(1)}, f32[8,16,8,128]{3,2,1,0:T(8,128)S(1)}, u32[]{:S(2)}, u32[]{:S(2)}) %collective-permute-start.9) | collective-permute-done | bytes 524320 | tf_op jit(solution)/shard_map/ppermute | solution.py:412
  148.9 4.1 %shard_map.55 = f32[2,16,8,2,8,128]{5,4,3,2,1,0:T(8,128)} custom-call(bf16[3,256,256]{2,1,0:T(8,128)(2,1)S(1)} %shard_map.37.refs_0_, f32[8,16,8,128]{3,2,1,0:T(8,128)S(1)} %get-tuple-element.53.refs_1_, f32[8,16,8,128]{3,2,1,0:T(8,128)S(1)} %collective-permute-done.9.refs_2_, f32[4,512,256]{2,1,0:T(8,128)S(1)} %shard_map.54.refs_3_, ...), custom_call_target="tpu_custom_call" | custom-call | flops 1207959552 | bytes 3145728 | tf_op jit(solution)/shard_map/pallas_call | solution.py:375
  (36 shorter events, 13.0 us)
Async XLA Ops:
  0.0 1.6 %copy-start.1 = (f32[2,1,1,262144]{3,2,1,0:T(1,128)S(1)}, f32[2,1,1,262144]{3,2,1,0:T(1,128)}, u32[]{:S(2)}) copy-start(f32[2,1,1,262144]{3,2,1,0:T(1,128)} %param.3) | copy-start | bytes 6291460
  3.1 21.1 %collective-permute-start.10 = (f32[1024,128]{1,0:T(8,128)S(1)}, f32[1024,128]{1,0:T(8,128)S(1)}, u32[]{:S(2)}, u32[]{:S(2)}) collective-permute-start(f32[1024,128]{1,0:T(8,128)S(1)} %get-tuple-element.56), channel_id=1, source_target_pairs={{0,128},{8,136},{16,144},{24,152},{32,160},{40,168},{48,176},{56,1... | collective-permute-start | bytes 1572872 | tf_op jit(solution)/shard_map/ppermute | solution.py:412
  14.4 14.4 %collective-permute-start = (f32[8,16,8,128]{3,2,1,0:T(8,128)S(1)}, f32[8,16,8,128]{3,2,1,0:T(8,128)S(1)}, u32[]{:S(2)}, u32[]{:S(2)}) collective-permute-start(f32[8,16,8,128]{3,2,1,0:T(8,128)S(1)} %get-tuple-element.40), channel_id=1, source_target_pairs={{0,8},{8,0},{16,24},{24,16},{32,40},{40,32},{48,56},{56,48},{64,72... | collective-permute-start | bytes 1572872 | tf_op jit(solution)/shard_map/ppermute | solution.py:412
  24.2 4.3 %copy-start = (f32[5,4,2,128,128]{4,3,2,1,0:T(8,128)S(1)}, f32[5,4,2,128,128]{4,3,2,1,0:T(8,128)}, u32[]{:S(2)}) copy-start(f32[5,4,2,128,128]{4,3,2,1,0:T(8,128)} %gates_ref.1) | copy-start | bytes 7864324
  26.5 18.8 %collective-permute-start.11 = (f32[8,16,8,128]{3,2,1,0:T(8,128)S(1)}, f32[8,16,8,128]{3,2,1,0:T(8,128)S(1)}, u32[]{:S(2)}, u32[]{:S(2)}) collective-permute-start(f32[8,16,8,128]{3,2,1,0:T(8,128)S(1)} %get-tuple-element.58), channel_id=1, source_target_pairs={{0,8},{8,0},{16,24},{24,16},{32,40},{40,32},{48,56},{56,48},{64,72... | collective-permute-start | bytes 1572872 | tf_op jit(solution)/shard_map/ppermute | solution.py:412
  31.0 27.5 %collective-permute-start.1 = (f32[8,16,8,128]{3,2,1,0:T(8,128)S(1)}, f32[8,16,8,128]{3,2,1,0:T(8,128)S(1)}, u32[]{:S(2)}, u32[]{:S(2)}) collective-permute-start(f32[8,16,8,128]{3,2,1,0:T(8,128)S(1)} %get-tuple-element.42), channel_id=1, source_target_pairs={{0,128},{8,136},{16,144},{24,152},{32,160},{40,168},{48,176},{56,1... | collective-permute-start | bytes 1572872 | tf_op jit(solution)/shard_map/ppermute | solution.py:412
  49.6 11.8 %collective-permute-start.12 = (f32[16,8,8,128]{3,2,1,0:T(8,128)S(1)}, f32[16,8,8,128]{3,2,1,0:T(8,128)S(1)}, u32[]{:S(2)}, u32[]{:S(2)}) collective-permute-start(f32[16,8,8,128]{3,2,1,0:T(8,128)S(1)} %get-tuple-element.60), channel_id=1, source_target_pairs={{0,8},{8,0},{16,24},{24,16},{32,40},{40,32},{48,56},{56,48},{64,72... | collective-permute-start | bytes 1572872 | tf_op jit(solution)/shard_map/ppermute | solution.py:412
  60.5 19.9 %collective-permute-start.2 = (f32[16,8,8,128]{3,2,1,0:T(8,128)S(1)}, f32[16,8,8,128]{3,2,1,0:T(8,128)S(1)}, u32[]{:S(2)}, u32[]{:S(2)}) collective-permute-start(f32[16,8,8,128]{3,2,1,0:T(8,128)S(1)} %get-tuple-element.44), channel_id=1, source_target_pairs={{0,8},{8,0},{16,24},{24,16},{32,40},{40,32},{48,56},{56,48},{64,72... | collective-permute-start | bytes 1572872 | tf_op jit(solution)/shard_map/ppermute | solution.py:412
  61.3 51.2 %copy-start.2 = (s32[32]{0:T(128)S(1)}, s32[32]{0:T(128)}, u32[]{:S(2)}) copy-start(s32[32]{0:T(128)} %refs_0_.5) | copy-start | bytes 388
  61.4 25.1 %collective-permute-start.13 = (f32[2,4,8,8,128]{4,3,2,1,0:T(8,128)S(1)}, f32[2,4,8,8,128]{4,3,2,1,0:T(8,128)S(1)}, u32[]{:S(2)}, u32[]{:S(2)}) collective-permute-start(f32[2,4,8,8,128]{4,3,2,1,0:T(8,128)S(1)} %get-tuple-element.62), channel_id=1, source_target_pairs={{0,64},{8,72},{16,80},{24,88},{32,96},{40,104},{48,112},{56,120},{... | collective-permute-start | bytes 786440 | tf_op jit(solution)/shard_map/ppermute | solution.py:420
  73.6 27.1 %collective-permute-start.14 = (f32[2,4,8,8,128]{4,3,2,1,0:T(8,128)S(1)}, f32[2,4,8,8,128]{4,3,2,1,0:T(8,128)S(1)}, u32[]{:S(2)}, u32[]{:S(2)}) collective-permute-start(f32[2,4,8,8,128]{4,3,2,1,0:T(8,128)S(1)} %get-tuple-element.63), channel_id=1, source_target_pairs={{0,128},{8,136},{16,144},{24,152},{32,160},{40,168},{48,176},{56,1... | collective-permute-start | bytes 786440 | tf_op jit(solution)/shard_map/ppermute | solution.py:420
  78.2 22.5 %collective-permute-start.15 = (f32[2,4,8,8,128]{4,3,2,1,0:T(8,128)S(1)}, f32[2,4,8,8,128]{4,3,2,1,0:T(8,128)S(1)}, u32[]{:S(2)}, u32[]{:S(2)}) collective-permute-start(f32[2,4,8,8,128]{4,3,2,1,0:T(8,128)S(1)} %get-tuple-element.64), channel_id=1, source_target_pairs={{0,192},{8,200},{16,208},{24,216},{32,224},{40,232},{48,240},{56,2... | collective-permute-start | bytes 786440 | tf_op jit(solution)/shard_map/ppermute | solution.py:420
  80.4 24.0 %collective-permute-start.3 = (f32[2,4,8,8,128]{4,3,2,1,0:T(8,128)S(1)}, f32[2,4,8,8,128]{4,3,2,1,0:T(8,128)S(1)}, u32[]{:S(2)}, u32[]{:S(2)}) collective-permute-start(f32[2,4,8,8,128]{4,3,2,1,0:T(8,128)S(1)} %get-tuple-element.46), channel_id=1, source_target_pairs={{0,16},{8,24},{16,32},{24,40},{32,48},{40,56},{48,0},{56,8},{64,80... | collective-permute-start | bytes 786440 | tf_op jit(solution)/shard_map/ppermute | solution.py:420
  81.7 23.9 %collective-permute-start.4 = (f32[2,4,8,8,128]{4,3,2,1,0:T(8,128)S(1)}, f32[2,4,8,8,128]{4,3,2,1,0:T(8,128)S(1)}, u32[]{:S(2)}, u32[]{:S(2)}) collective-permute-start(f32[2,4,8,8,128]{4,3,2,1,0:T(8,128)S(1)} %get-tuple-element.47), channel_id=1, source_target_pairs={{0,32},{8,40},{16,48},{24,56},{32,0},{40,8},{48,16},{56,24},{64,96... | collective-permute-start | bytes 786440 | tf_op jit(solution)/shard_map/ppermute | solution.py:420
  86.5 19.1 %collective-permute-start.5 = (f32[2,4,8,8,128]{4,3,2,1,0:T(8,128)S(1)}, f32[2,4,8,8,128]{4,3,2,1,0:T(8,128)S(1)}, u32[]{:S(2)}, u32[]{:S(2)}) collective-permute-start(f32[2,4,8,8,128]{4,3,2,1,0:T(8,128)S(1)} %get-tuple-element.48), channel_id=1, source_target_pairs={{0,48},{8,56},{16,0},{24,8},{32,16},{40,24},{48,32},{56,40},{64,11... | collective-permute-start | bytes 786440 | tf_op jit(solution)/shard_map/ppermute | solution.py:420
  100.8 8.7 %collective-permute-start.16 = (f32[2,4,8,8,128]{4,3,2,1,0:T(8,128)S(1)}, f32[2,4,8,8,128]{4,3,2,1,0:T(8,128)S(1)}, u32[]{:S(2)}, u32[]{:S(2)}) collective-permute-start(f32[2,4,8,8,128]{4,3,2,1,0:T(8,128)S(1)} %get-tuple-element.66), channel_id=1, source_target_pairs={{0,16},{8,24},{16,32},{24,40},{32,48},{40,56},{48,0},{56,8},{64,80... | collective-permute-start | bytes 786440 | tf_op jit(solution)/shard_map/ppermute | solution.py:420
  102.0 13.9 %collective-permute-start.17 = (f32[2,4,8,8,128]{4,3,2,1,0:T(8,128)S(1)}, f32[2,4,8,8,128]{4,3,2,1,0:T(8,128)S(1)}, u32[]{:S(2)}, u32[]{:S(2)}) collective-permute-start(f32[2,4,8,8,128]{4,3,2,1,0:T(8,128)S(1)} %get-tuple-element.67), channel_id=1, source_target_pairs={{0,32},{8,40},{16,48},{24,56},{32,0},{40,8},{48,16},{56,24},{64,96... | collective-permute-start | bytes 786440 | tf_op jit(solution)/shard_map/ppermute | solution.py:420
  104.5 11.5 %collective-permute-start.18 = (f32[2,4,8,8,128]{4,3,2,1,0:T(8,128)S(1)}, f32[2,4,8,8,128]{4,3,2,1,0:T(8,128)S(1)}, u32[]{:S(2)}, u32[]{:S(2)}) collective-permute-start(f32[2,4,8,8,128]{4,3,2,1,0:T(8,128)S(1)} %get-tuple-element.68), channel_id=1, source_target_pairs={{0,48},{8,56},{16,0},{24,8},{32,16},{40,24},{48,32},{56,40},{64,11... | collective-permute-start | bytes 786440 | tf_op jit(solution)/shard_map/ppermute | solution.py:420
  105.8 15.5 %collective-permute-start.6 = (f32[2,4,8,8,128]{4,3,2,1,0:T(8,128)S(1)}, f32[2,4,8,8,128]{4,3,2,1,0:T(8,128)S(1)}, u32[]{:S(2)}, u32[]{:S(2)}) collective-permute-start(f32[2,4,8,8,128]{4,3,2,1,0:T(8,128)S(1)} %get-tuple-element.50), channel_id=1, source_target_pairs={{0,64},{8,72},{16,80},{24,88},{32,96},{40,104},{48,112},{56,120},{... | collective-permute-start | bytes 786440 | tf_op jit(solution)/shard_map/ppermute | solution.py:420
  105.8 20.4 %collective-permute-start.7 = (f32[2,4,8,8,128]{4,3,2,1,0:T(8,128)S(1)}, f32[2,4,8,8,128]{4,3,2,1,0:T(8,128)S(1)}, u32[]{:S(2)}, u32[]{:S(2)}) collective-permute-start(f32[2,4,8,8,128]{4,3,2,1,0:T(8,128)S(1)} %get-tuple-element.51), channel_id=1, source_target_pairs={{0,128},{8,136},{16,144},{24,152},{32,160},{40,168},{48,176},{56,1... | collective-permute-start | bytes 786440 | tf_op jit(solution)/shard_map/ppermute | solution.py:420
  109.5 22.4 %collective-permute-start.8 = (f32[2,4,8,8,128]{4,3,2,1,0:T(8,128)S(1)}, f32[2,4,8,8,128]{4,3,2,1,0:T(8,128)S(1)}, u32[]{:S(2)}, u32[]{:S(2)}) collective-permute-start(f32[2,4,8,8,128]{4,3,2,1,0:T(8,128)S(1)} %get-tuple-element.52), channel_id=1, source_target_pairs={{0,192},{8,200},{16,208},{24,216},{32,224},{40,232},{48,240},{56,2... | collective-permute-start | bytes 786440 | tf_op jit(solution)/shard_map/ppermute | solution.py:420
  118.2 21.1 %collective-permute-start.19 = (f32[8,16,8,128]{3,2,1,0:T(8,128)S(1)}, f32[8,16,8,128]{3,2,1,0:T(8,128)S(1)}, u32[]{:S(2)}, u32[]{:S(2)}) collective-permute-start(f32[8,16,8,128]{3,2,1,0:T(8,128)S(1)} %get-tuple-element.70), channel_id=1, source_target_pairs={{0,4},{1,5},{2,6},{3,7},{4,0},{5,1},{6,2},{7,3},{8,12},{9,13},{10,... | collective-permute-start | bytes 1572872 | tf_op jit(solution)/shard_map/ppermute | solution.py:412
  134.1 14.8 %collective-permute-start.9 = (f32[8,16,8,128]{3,2,1,0:T(8,128)S(1)}, f32[8,16,8,128]{3,2,1,0:T(8,128)S(1)}, u32[]{:S(2)}, u32[]{:S(2)}) collective-permute-start(f32[8,16,8,128]{3,2,1,0:T(8,128)S(1)} %get-tuple-element.54), channel_id=1, source_target_pairs={{0,4},{1,5},{2,6},{3,7},{4,0},{5,1},{6,2},{7,3},{8,12},{9,13},{10,... | collective-permute-start | bytes 1572872 | tf_op jit(solution)/shard_map/ppermute | solution.py:412

commit v9 on v8

--- a/solution.py
+++ b/solution.py
@@ -178,31 +178,27 @@
 def pack_kernel(state_ref, *outs):
     own = lax.axis_index("row") >> 4 == 1
 
-    def some(i, carry):
-        rows = pl.ds(GD * i, GD)
-        tops = [cross(state_ref[0, t, rows], state_ref[1, t, rows], 64) for t in range(2)]
-        sides = [cross(tops[0][b], tops[1][b], 32)[0] for b in range(2)]
-        for out, side in zip(outs[:2], in_order(own, *sides)):
-            out[rows] = side
-        for t in range(2):
-            outs[2][t, rows] = cross(*tops[t], 32)[1]
-        return carry
-
-    lax.fori_loop(0, 8, some, 0, unroll=4)
+    tops = [cross(state_ref[0, t], state_ref[1, t], 64) for t in range(2)]
+    sides = [cross(tops[0][b], tops[1][b], 32)[0] for b in range(2)]
+    for out, side in zip(outs[:2], in_order(own, *sides)):
+        out[...] = side
+    for t in range(2):
+        outs[2][t] = cross(*tops[t], 32)[1]
 
 
 def pack(state):
-    vmem = pl.BlockSpec(memory_space=pltpu.VMEM)
+    part = pl.BlockSpec((256, GD), lambda i: (i, 0))
     return pl.pallas_call(
         pack_kernel,
         out_shape=[
             jax.ShapeDtypeStruct(shape, F32)
             for shape in ((1024, 128), (1024, 128), (2, 1024, 128))
         ],
-        in_specs=[vmem],
-        out_specs=[vmem] * 3,
+        grid=(4,),
+        in_specs=[pl.BlockSpec((2, 2, 256, GD), lambda i: (0, 0, i, 0))],
+        out_specs=[part, part, pl.BlockSpec((2, 256, GD), lambda i: (0, i, 0))],
         cost_estimate=pl.CostEstimate(flops=0, bytes_accessed=4 << 20, transcendentals=0),
-        compiler_params=pltpu.CompilerParams(vmem_limit_bytes=LIMIT),
+        compiler_params=pltpu.CompilerParams(vmem_limit_bytes=60 << 20),
         name="pack",
     )(state)
 

time: 154 us -> 156 us (1.013)
  Pallas kernels: 31.3 us -> 34 us
    pallas_call x1, Pallas kernels: 1.48 us -> 4.24 us  [pack(): pl.pallas_call(pack_kernel, out_shape=[jax.ShapeDtypeStruct(shape, F32) f...]
where the time goes in v9:
time: 156 us; the launch traced here: 154 us
  starting transfers between devices  68.7 us (44%)
  waiting for transfers between devices  49.2 us (32%)
  Pallas kernels  34 us (22%)
  local copies, waits for them, and re-layouts  2.31 us (1%)
    ppermute x12, starting transfers between devices, shift_row(): return lax.ppermute(value, 'row', pairs)  36.5 us
    ppermute x8, starting transfers between devices, flip(): lax.ppermute(value, axis, [(s, s ^ mask) for s in range(lax.axis_size(axi...  32.2 us
    ppermute x12, waiting for transfers between devices, shift_row(): return lax.ppermute(value, 'row', pairs)  27.5 us
    pallas_call x10, Pallas kernels, run_segment(): pl.pallas_call(functools.partial(segment_kernel, source, target, len(args...  25.4 us
    ppermute x8, waiting for transfers between devices, flip(): lax.ppermute(value, axis, [(s, s ^ mask) for s in range(lax.axis_size(axi...  21.6 us
    pallas_call x1, Pallas kernels, pack(): pl.pallas_call(pack_kernel, out_shape=[jax.ShapeDtypeStruct(shape, F32) f...  4.24 us
  transfers between devices with their start and end apart: 20, of which 9 were waited for; matrix products, arithmetic and copies ran while one was open for 1% of the time, Pallas kernels for 17%

profile of v9, /device:TPU:1, one launch (start us, length us, event | category | flops | bytes accessed | tf_op | source)
XLA Modules:
  0.0 154.3 jit_solution(13384779534224067272)
XLA Ops:
  0.0 4.2 %pack.1 = (f32[1024,128]{1,0:T(8,128)}, f32[1024,128]{1,0:T(8,128)}, f32[2,1024,128]{2,1,0:T(8,128)}) custom-call(f32[2,2,1024,128]{3,2,1,0:T(8,128)} %bitcast.2), custom_call_target="tpu_custom_call" | custom-call | bytes 4194304 | tf_op jit(solution)/shard_map/pack/pallas_call | solution.py:191
  4.2 7.7 %collective-permute-start.10 = (f32[1024,128]{1,0:T(8,128)}, f32[1024,128]{1,0:T(8,128)S(1)}, u32[]{:S(2)}, u32[]{:S(2)}) collective-permute-start(f32[1024,128]{1,0:T(8,128)} %get-tuple-element.56), channel_id=1, source_target_pairs={{0,128},{8,136},{16,144},{24,152},{32,160},{40,168},{48,176},{56,1... | collective-permute-start | bytes 1572872 | tf_op jit(solution)/shard_map/ppermute | solution.py:408
  14.6 2.1 %shard_map.42 = (f32[8,16,8,128]{3,2,1,0:T(8,128)S(1)}, f32[8,16,8,128]{3,2,1,0:T(8,128)S(1)}) custom-call(bf16[3,256,256]{2,1,0:T(8,128)(2,1)S(1)} %shard_map.41.refs_0_, f32[2,1024,128]{2,1,0:T(8,128)S(1)} %copy-done.2), custom_call_target="tpu_custom_call" | custom-call | flops 1207959552 | bytes 3145728 | tf_op jit(solution)/shard_map/pallas_call | solution.py:371
  17.8 7.7 %collective-permute-done.10.refs_2_ = f32[1024,128]{1,0:T(8,128)S(1)} collective-permute-done((f32[1024,128]{1,0:T(8,128)}, f32[1024,128]{1,0:T(8,128)S(1)}, u32[]{:S(2)}, u32[]{:S(2)}) %collective-permute-start.10) | collective-permute-done | bytes 524320 | tf_op jit(solution)/shard_map/ppermute | solution.py:408
  25.5 2.3 %shard_map.48 = (f32[8,16,8,128]{3,2,1,0:T(8,128)S(1)}, f32[8,16,8,128]{3,2,1,0:T(8,128)S(1)}) custom-call(bf16[3,256,256]{2,1,0:T(8,128)(2,1)S(1)} %shard_map.41.refs_0_, f32[1024,128]{1,0:T(8,128)S(1)} %copy-done.3, f32[1024,128]{1,0:T(8,128)S(1)} %collective-permute-done.10.refs_2_), custom_call_target="tpu_custom_call" | custom-call | flops 1207959552 | bytes 3145728 | tf_op jit(solution)/shard_map/pallas_call | solution.py:371
  27.8 1.9 %collective-permute-start.11 = (f32[8,16,8,128]{3,2,1,0:T(8,128)S(1)}, f32[8,16,8,128]{3,2,1,0:T(8,128)S(1)}, u32[]{:S(2)}, u32[]{:S(2)}) collective-permute-start(f32[8,16,8,128]{3,2,1,0:T(8,128)S(1)} %get-tuple-element.58), channel_id=1, source_target_pairs={{0,8},{8,0},{16,24},{24,16},{32,40},{40,32},{48,56},{56,48},{64,72... | collective-permute-start | bytes 1572872 | tf_op jit(solution)/shard_map/ppermute | solution.py:408
  30.1 2.1 %shard_map.43 = (f32[8,16,8,128]{3,2,1,0:T(8,128)S(1)}, f32[8,16,8,128]{3,2,1,0:T(8,128)S(1)}) custom-call(bf16[3,256,256]{2,1,0:T(8,128)(2,1)S(1)} %shard_map.40.refs_0_, f32[8,16,8,128]{3,2,1,0:T(8,128)S(1)} %get-tuple-element.39.refs_1_, f32[8,16,8,128]{3,2,1,0:T(8,128)S(1)} %collective-permute-done.refs_2_), custom_call_target="tpu_custom_call" | custom-call | flops 1207959552 | bytes 3145728 | tf_op jit(solution)/shard_map/pallas_call | solution.py:371
  32.2 14.0 %collective-permute-start.1 = (f32[8,16,8,128]{3,2,1,0:T(8,128)S(1)}, f32[8,16,8,128]{3,2,1,0:T(8,128)S(1)}, u32[]{:S(2)}, u32[]{:S(2)}) collective-permute-start(f32[8,16,8,128]{3,2,1,0:T(8,128)S(1)} %get-tuple-element.42), channel_id=1, source_target_pairs={{0,128},{8,136},{16,144},{24,152},{32,160},{40,168},{48,176},{56,1... | collective-permute-start | bytes 1572872 | tf_op jit(solution)/shard_map/ppermute | solution.py:408
  46.6 2.0 %shard_map.49.refs_1_ = f32[16,16,8,128]{3,2,1,0:T(8,128)S(1)} custom-call(bf16[3,256,256]{2,1,0:T(8,128)(2,1)S(1)} %shard_map.40.refs_0_, f32[8,16,8,128]{3,2,1,0:T(8,128)S(1)} %get-tuple-element.57.refs_1_, f32[8,16,8,128]{3,2,1,0:T(8,128)S(1)} %collective-permute-done.11.refs_2_), custom_call_target="tpu_custom_call" | custom-call | flops 1207959552 | bytes 3145728 | tf_op jit(solution)/shard_map/pallas_call | solution.py:371
  48.6 2.2 %shard_map.50 = (f32[16,8,8,128]{3,2,1,0:T(8,128)S(1)}, f32[16,8,8,128]{3,2,1,0:T(8,128)S(1)}) custom-call(bf16[3,256,256]{2,1,0:T(8,128)(2,1)S(1)} %shard_map.39.refs_0_, f32[16,16,8,128]{3,2,1,0:T(8,128)S(1)} %shard_map.49.refs_1_), custom_call_target="tpu_custom_call" | custom-call | flops 1207959552 | bytes 3145728 | tf_op jit(solution)/shard_map/pallas_call | solution.py:371
  51.2 8.6 %collective-permute-done.1.refs_2_ = f32[8,16,8,128]{3,2,1,0:T(8,128)S(1)} collective-permute-done((f32[8,16,8,128]{3,2,1,0:T(8,128)S(1)}, f32[8,16,8,128]{3,2,1,0:T(8,128)S(1)}, u32[]{:S(2)}, u32[]{:S(2)}) %collective-permute-start.1) | collective-permute-done | bytes 524320 | tf_op jit(solution)/shard_map/ppermute | solution.py:408
  59.8 2.0 %shard_map.44 = (f32[16,8,8,128]{3,2,1,0:T(8,128)S(1)}, f32[16,8,8,128]{3,2,1,0:T(8,128)S(1)}) custom-call(bf16[3,256,256]{2,1,0:T(8,128)(2,1)S(1)} %shard_map.39.refs_0_, f32[8,16,8,128]{3,2,1,0:T(8,128)S(1)} %get-tuple-element.41.refs_1_, f32[8,16,8,128]{3,2,1,0:T(8,128)S(1)} %collective-permute-done.1.refs_2_), custom_call_target="tpu_custom_call" | custom-call | flops 1207959552 | bytes 3145728 | tf_op jit(solution)/shard_map/pallas_call | solution.py:371
  62.7 12.2 %collective-permute-start.13 = (f32[2,4,8,8,128]{4,3,2,1,0:T(8,128)S(1)}, f32[2,4,8,8,128]{4,3,2,1,0:T(8,128)S(1)}, u32[]{:S(2)}, u32[]{:S(2)}) collective-permute-start(f32[2,4,8,8,128]{4,3,2,1,0:T(8,128)S(1)} %get-tuple-element.62), channel_id=1, source_target_pairs={{0,64},{8,72},{16,80},{24,88},{32,96},{40,104},{48,112},{56,120},{... | collective-permute-start | bytes 786440 | tf_op jit(solution)/shard_map/ppermute | solution.py:416
  74.9 4.6 %collective-permute-start.14 = (f32[2,4,8,8,128]{4,3,2,1,0:T(8,128)S(1)}, f32[2,4,8,8,128]{4,3,2,1,0:T(8,128)S(1)}, u32[]{:S(2)}, u32[]{:S(2)}) collective-permute-start(f32[2,4,8,8,128]{4,3,2,1,0:T(8,128)S(1)} %get-tuple-element.63), channel_id=1, source_target_pairs={{0,128},{8,136},{16,144},{24,152},{32,160},{40,168},{48,176},{56,1... | collective-permute-start | bytes 786440 | tf_op jit(solution)/shard_map/ppermute | solution.py:416
  79.5 2.2 %collective-permute-start.15 = (f32[2,4,8,8,128]{4,3,2,1,0:T(8,128)S(1)}, f32[2,4,8,8,128]{4,3,2,1,0:T(8,128)S(1)}, u32[]{:S(2)}, u32[]{:S(2)}) collective-permute-start(f32[2,4,8,8,128]{4,3,2,1,0:T(8,128)S(1)} %get-tuple-element.64), channel_id=1, source_target_pairs={{0,192},{8,200},{16,208},{24,216},{32,224},{40,232},{48,240},{56,2... | collective-permute-start | bytes 786440 | tf_op jit(solution)/shard_map/ppermute | solution.py:416
  83.0 2.5 %collective-permute-start.4 = (f32[2,4,8,8,128]{4,3,2,1,0:T(8,128)S(1)}, f32[2,4,8,8,128]{4,3,2,1,0:T(8,128)S(1)}, u32[]{:S(2)}, u32[]{:S(2)}) collective-permute-start(f32[2,4,8,8,128]{4,3,2,1,0:T(8,128)S(1)} %get-tuple-element.47), channel_id=1, source_target_pairs={{0,32},{8,40},{16,48},{24,56},{32,0},{40,8},{48,16},{56,24},{64,96... | collective-permute-start | bytes 786440 | tf_op jit(solution)/shard_map/ppermute | solution.py:416
  85.5 2.3 %collective-permute-done.13.refs_1_ = f32[2,4,8,8,128]{4,3,2,1,0:T(8,128)S(1)} collective-permute-done((f32[2,4,8,8,128]{4,3,2,1,0:T(8,128)S(1)}, f32[2,4,8,8,128]{4,3,2,1,0:T(8,128)S(1)}, u32[]{:S(2)}, u32[]{:S(2)}) %collective-permute-start.13) | collective-permute-done | bytes 262176 | tf_op jit(solution)/shard_map/ppermute | solution.py:416
  87.8 2.5 %collective-permute-start.5 = (f32[2,4,8,8,128]{4,3,2,1,0:T(8,128)S(1)}, f32[2,4,8,8,128]{4,3,2,1,0:T(8,128)S(1)}, u32[]{:S(2)}, u32[]{:S(2)}) collective-permute-start(f32[2,4,8,8,128]{4,3,2,1,0:T(8,128)S(1)} %get-tuple-element.48), channel_id=1, source_target_pairs={{0,48},{8,56},{16,0},{24,8},{32,16},{40,24},{48,32},{56,40},{64,11... | collective-permute-start | bytes 786440 | tf_op jit(solution)/shard_map/ppermute | solution.py:416
  90.3 11.7 %collective-permute-done.14.refs_2_ = f32[2,4,8,8,128]{4,3,2,1,0:T(8,128)S(1)} collective-permute-done((f32[2,4,8,8,128]{4,3,2,1,0:T(8,128)S(1)}, f32[2,4,8,8,128]{4,3,2,1,0:T(8,128)S(1)}, u32[]{:S(2)}, u32[]{:S(2)}) %collective-permute-start.14) | collective-permute-done | bytes 262176 | tf_op jit(solution)/shard_map/ppermute | solution.py:416
  103.3 2.5 %collective-permute-start.17 = (f32[2,4,8,8,128]{4,3,2,1,0:T(8,128)S(1)}, f32[2,4,8,8,128]{4,3,2,1,0:T(8,128)S(1)}, u32[]{:S(2)}, u32[]{:S(2)}) collective-permute-start(f32[2,4,8,8,128]{4,3,2,1,0:T(8,128)S(1)} %get-tuple-element.67), channel_id=1, source_target_pairs={{0,32},{8,40},{16,48},{24,56},{32,0},{40,8},{48,16},{56,24},{64,96... | collective-permute-start | bytes 786440 | tf_op jit(solution)/shard_map/ppermute | solution.py:416
  107.1 3.4 %collective-permute-start.7 = (f32[2,4,8,8,128]{4,3,2,1,0:T(8,128)S(1)}, f32[2,4,8,8,128]{4,3,2,1,0:T(8,128)S(1)}, u32[]{:S(2)}, u32[]{:S(2)}) collective-permute-start(f32[2,4,8,8,128]{4,3,2,1,0:T(8,128)S(1)} %get-tuple-element.51), channel_id=1, source_target_pairs={{0,128},{8,136},{16,144},{24,152},{32,160},{40,168},{48,176},{56,1... | collective-permute-start | bytes 786440 | tf_op jit(solution)/shard_map/ppermute | solution.py:416
  110.7 3.0 %collective-permute-start.8 = (f32[2,4,8,8,128]{4,3,2,1,0:T(8,128)S(1)}, f32[2,4,8,8,128]{4,3,2,1,0:T(8,128)S(1)}, u32[]{:S(2)}, u32[]{:S(2)}) collective-permute-start(f32[2,4,8,8,128]{4,3,2,1,0:T(8,128)S(1)} %get-tuple-element.52), channel_id=1, source_target_pairs={{0,192},{8,200},{16,208},{24,216},{32,224},{40,232},{48,240},{56,2... | collective-permute-start | bytes 786440 | tf_op jit(solution)/shard_map/ppermute | solution.py:416
  114.7 2.6 %collective-permute-done.17.refs_3_ = f32[2,4,8,8,128]{4,3,2,1,0:T(8,128)S(1)} collective-permute-done((f32[2,4,8,8,128]{4,3,2,1,0:T(8,128)S(1)}, f32[2,4,8,8,128]{4,3,2,1,0:T(8,128)S(1)}, u32[]{:S(2)}, u32[]{:S(2)}) %collective-permute-start.17) | collective-permute-done | bytes 262176 | tf_op jit(solution)/shard_map/ppermute | solution.py:416
  117.3 2.2 %shard_map.53 = (f32[8,16,8,128]{3,2,1,0:T(8,128)S(1)}, f32[8,16,8,128]{3,2,1,0:T(8,128)S(1)}) custom-call(bf16[3,256,256]{2,1,0:T(8,128)(2,1)S(1)} %shard_map.38.refs_0_, f32[2,4,8,8,128]{4,3,2,1,0:T(8,128)S(1)} %get-tuple-element.65.refs_1_, f32[2,4,8,8,128]{4,3,2,1,0:T(8,128)S(1)} %collective-permute-done.16.refs_2_, ...), custom_call_target="tpu_custom_call" | custom-call | flops 1207959552 | bytes 3145728 | tf_op jit(solution)/shard_map/pallas_call | solution.py:371
  119.5 3.0 %collective-permute-start.19 = (f32[8,16,8,128]{3,2,1,0:T(8,128)S(1)}, f32[8,16,8,128]{3,2,1,0:T(8,128)S(1)}, u32[]{:S(2)}, u32[]{:S(2)}) collective-permute-start(f32[8,16,8,128]{3,2,1,0:T(8,128)S(1)} %get-tuple-element.70), channel_id=1, source_target_pairs={{0,4},{1,5},{2,6},{3,7},{4,0},{5,1},{6,2},{7,3},{8,12},{9,13},{10,... | collective-permute-start | bytes 1572872 | tf_op jit(solution)/shard_map/ppermute | solution.py:408
  122.5 4.8 %collective-permute-done.7.refs_3_ = f32[2,4,8,8,128]{4,3,2,1,0:T(8,128)S(1)} collective-permute-done((f32[2,4,8,8,128]{4,3,2,1,0:T(8,128)S(1)}, f32[2,4,8,8,128]{4,3,2,1,0:T(8,128)S(1)}, u32[]{:S(2)}, u32[]{:S(2)}) %collective-permute-start.7) | collective-permute-done | bytes 262176 | tf_op jit(solution)/shard_map/ppermute | solution.py:416
  127.3 5.8 %collective-permute-done.8.refs_4_ = f32[2,4,8,8,128]{4,3,2,1,0:T(8,128)S(1)} collective-permute-done((f32[2,4,8,8,128]{4,3,2,1,0:T(8,128)S(1)}, f32[2,4,8,8,128]{4,3,2,1,0:T(8,128)S(1)}, u32[]{:S(2)}, u32[]{:S(2)}) %collective-permute-start.8) | collective-permute-done | bytes 262176 | tf_op jit(solution)/shard_map/ppermute | solution.py:416
  133.1 2.2 %shard_map.47 = (f32[8,16,8,128]{3,2,1,0:T(8,128)S(1)}, f32[8,16,8,128]{3,2,1,0:T(8,128)S(1)}) custom-call(bf16[3,256,256]{2,1,0:T(8,128)(2,1)S(1)} %shard_map.38.refs_0_, f32[2,4,8,8,128]{4,3,2,1,0:T(8,128)S(1)} %get-tuple-element.49.refs_1_, f32[2,4,8,8,128]{4,3,2,1,0:T(8,128)S(1)} %collective-permute-done.6.refs_2_, ...), custom_call_target="tpu_custom_call" | custom-call | flops 1207959552 | bytes 3145728 | tf_op jit(solution)/shard_map/pallas_call | solution.py:371
  135.4 3.2 %collective-permute-start.9 = (f32[8,16,8,128]{3,2,1,0:T(8,128)S(1)}, f32[8,16,8,128]{3,2,1,0:T(8,128)S(1)}, u32[]{:S(2)}, u32[]{:S(2)}) collective-permute-start(f32[8,16,8,128]{3,2,1,0:T(8,128)S(1)} %get-tuple-element.54), channel_id=1, source_target_pairs={{0,4},{1,5},{2,6},{3,7},{4,0},{5,1},{6,2},{7,3},{8,12},{9,13},{10,... | collective-permute-start | bytes 1572872 | tf_op jit(solution)/shard_map/ppermute | solution.py:408
  140.8 4.1 %shard_map.54.refs_3_ = f32[4,512,256]{2,1,0:T(8,128)S(1)} custom-call(bf16[3,256,256]{2,1,0:T(8,128)(2,1)S(1)} %shard_map.37.refs_0_, f32[8,16,8,128]{3,2,1,0:T(8,128)S(1)} %get-tuple-element.69.refs_1_, f32[8,16,8,128]{3,2,1,0:T(8,128)S(1)} %collective-permute-done.19.refs_2_, bf16[2,2,256,256]{3,2,1,0:T(8,128)(2,1)S(1)} %low_weights.1.refs_3_.refs_4_), custom_call_target="tpu_custom_call" | custom-call | flops 1207959552 | bytes 3145728 | tf_op jit(solution)/shard_map/pallas_call | solution.py:371
  144.9 5.4 %collective-permute-done.9.refs_2_ = f32[8,16,8,128]{3,2,1,0:T(8,128)S(1)} collective-permute-done((f32[8,16,8,128]{3,2,1,0:T(8,128)S(1)}, f32[8,16,8,128]{3,2,1,0:T(8,128)S(1)}, u32[]{:S(2)}, u32[]{:S(2)}) %collective-permute-start.9) | collective-permute-done | bytes 524320 | tf_op jit(solution)/shard_map/ppermute | solution.py:408
  150.2 4.1 %shard_map.55 = f32[2,16,8,2,8,128]{5,4,3,2,1,0:T(8,128)} custom-call(bf16[3,256,256]{2,1,0:T(8,128)(2,1)S(1)} %shard_map.37.refs_0_, f32[8,16,8,128]{3,2,1,0:T(8,128)S(1)} %get-tuple-element.53.refs_1_, f32[8,16,8,128]{3,2,1,0:T(8,128)S(1)} %collective-permute-done.9.refs_2_, f32[4,512,256]{2,1,0:T(8,128)S(1)} %shard_map.54.refs_3_, ...), custom_call_target="tpu_custom_call" | custom-call | flops 1207959552 | bytes 3145728 | tf_op jit(solution)/shard_map/pallas_call | solution.py:371
  (38 shorter events, 13.0 us)
Async XLA Ops:
  4.2 21.2 %collective-permute-start.10 = (f32[1024,128]{1,0:T(8,128)}, f32[1024,128]{1,0:T(8,128)S(1)}, u32[]{:S(2)}, u32[]{:S(2)}) collective-permute-start(f32[1024,128]{1,0:T(8,128)} %get-tuple-element.56), channel_id=1, source_target_pairs={{0,128},{8,136},{16,144},{24,152},{32,160},{40,168},{48,176},{56,1... | collective-permute-start | bytes 1572872 | tf_op jit(solution)/shard_map/ppermute | solution.py:408
  13.4 1.2 copy-start.2
  14.6 10.8 %copy-start.3 = (f32[1024,128]{1,0:T(8,128)S(1)}, f32[1024,128]{1,0:T(8,128)}, u32[]{:S(2)}) copy-start(f32[1024,128]{1,0:T(8,128)} %get-tuple-element.55.refs_1_) | copy-start | bytes 1572868
  16.7 13.4 %collective-permute-start = (f32[8,16,8,128]{3,2,1,0:T(8,128)S(1)}, f32[8,16,8,128]{3,2,1,0:T(8,128)S(1)}, u32[]{:S(2)}, u32[]{:S(2)}) collective-permute-start(f32[8,16,8,128]{3,2,1,0:T(8,128)S(1)} %get-tuple-element.40), channel_id=1, source_target_pairs={{0,8},{8,0},{16,24},{24,16},{32,40},{40,32},{48,56},{56,48},{64,72... | collective-permute-start | bytes 1572872 | tf_op jit(solution)/shard_map/ppermute | solution.py:408
  25.5 4.3 %copy-start = (f32[5,4,2,128,128]{4,3,2,1,0:T(8,128)S(1)}, f32[5,4,2,128,128]{4,3,2,1,0:T(8,128)}, u32[]{:S(2)}) copy-start(f32[5,4,2,128,128]{4,3,2,1,0:T(8,128)} %gates_ref.1) | copy-start | bytes 7864324
  27.8 18.8 %collective-permute-start.11 = (f32[8,16,8,128]{3,2,1,0:T(8,128)S(1)}, f32[8,16,8,128]{3,2,1,0:T(8,128)S(1)}, u32[]{:S(2)}, u32[]{:S(2)}) collective-permute-start(f32[8,16,8,128]{3,2,1,0:T(8,128)S(1)} %get-tuple-element.58), channel_id=1, source_target_pairs={{0,8},{8,0},{16,24},{24,16},{32,40},{40,32},{48,56},{56,48},{64,72... | collective-permute-start | bytes 1572872 | tf_op jit(solution)/shard_map/ppermute | solution.py:408
  32.2 27.5 %collective-permute-start.1 = (f32[8,16,8,128]{3,2,1,0:T(8,128)S(1)}, f32[8,16,8,128]{3,2,1,0:T(8,128)S(1)}, u32[]{:S(2)}, u32[]{:S(2)}) collective-permute-start(f32[8,16,8,128]{3,2,1,0:T(8,128)S(1)} %get-tuple-element.42), channel_id=1, source_target_pairs={{0,128},{8,136},{16,144},{24,152},{32,160},{40,168},{48,176},{56,1... | collective-permute-start | bytes 1572872 | tf_op jit(solution)/shard_map/ppermute | solution.py:408
  50.8 11.8 %collective-permute-start.12 = (f32[16,8,8,128]{3,2,1,0:T(8,128)S(1)}, f32[16,8,8,128]{3,2,1,0:T(8,128)S(1)}, u32[]{:S(2)}, u32[]{:S(2)}) collective-permute-start(f32[16,8,8,128]{3,2,1,0:T(8,128)S(1)} %get-tuple-element.60), channel_id=1, source_target_pairs={{0,8},{8,0},{16,24},{24,16},{32,40},{40,32},{48,56},{56,48},{64,72... | collective-permute-start | bytes 1572872 | tf_op jit(solution)/shard_map/ppermute | solution.py:408
  61.8 19.8 %collective-permute-start.2 = (f32[16,8,8,128]{3,2,1,0:T(8,128)S(1)}, f32[16,8,8,128]{3,2,1,0:T(8,128)S(1)}, u32[]{:S(2)}, u32[]{:S(2)}) collective-permute-start(f32[16,8,8,128]{3,2,1,0:T(8,128)S(1)} %get-tuple-element.44), channel_id=1, source_target_pairs={{0,8},{8,0},{16,24},{24,16},{32,40},{40,32},{48,56},{56,48},{64,72... | collective-permute-start | bytes 1572872 | tf_op jit(solution)/shard_map/ppermute | solution.py:408
  62.7 51.1 %copy-start.1 = (s32[32]{0:T(128)S(1)}, s32[32]{0:T(128)}, u32[]{:S(2)}) copy-start(s32[32]{0:T(128)} %refs_0_.5) | copy-start | bytes 388
  62.7 25.1 %collective-permute-start.13 = (f32[2,4,8,8,128]{4,3,2,1,0:T(8,128)S(1)}, f32[2,4,8,8,128]{4,3,2,1,0:T(8,128)S(1)}, u32[]{:S(2)}, u32[]{:S(2)}) collective-permute-start(f32[2,4,8,8,128]{4,3,2,1,0:T(8,128)S(1)} %get-tuple-element.62), channel_id=1, source_target_pairs={{0,64},{8,72},{16,80},{24,88},{32,96},{40,104},{48,112},{56,120},{... | collective-permute-start | bytes 786440 | tf_op jit(solution)/shard_map/ppermute | solution.py:416
  74.9 27.1 %collective-permute-start.14 = (f32[2,4,8,8,128]{4,3,2,1,0:T(8,128)S(1)}, f32[2,4,8,8,128]{4,3,2,1,0:T(8,128)S(1)}, u32[]{:S(2)}, u32[]{:S(2)}) collective-permute-start(f32[2,4,8,8,128]{4,3,2,1,0:T(8,128)S(1)} %get-tuple-element.63), channel_id=1, source_target_pairs={{0,128},{8,136},{16,144},{24,152},{32,160},{40,168},{48,176},{56,1... | collective-permute-start | bytes 786440 | tf_op jit(solution)/shard_map/ppermute | solution.py:416
  79.5 22.5 %collective-permute-start.15 = (f32[2,4,8,8,128]{4,3,2,1,0:T(8,128)S(1)}, f32[2,4,8,8,128]{4,3,2,1,0:T(8,128)S(1)}, u32[]{:S(2)}, u32[]{:S(2)}) collective-permute-start(f32[2,4,8,8,128]{4,3,2,1,0:T(8,128)S(1)} %get-tuple-element.64), channel_id=1, source_target_pairs={{0,192},{8,200},{16,208},{24,216},{32,224},{40,232},{48,240},{56,2... | collective-permute-start | bytes 786440 | tf_op jit(solution)/shard_map/ppermute | solution.py:416
  81.7 24.1 %collective-permute-start.3 = (f32[2,4,8,8,128]{4,3,2,1,0:T(8,128)S(1)}, f32[2,4,8,8,128]{4,3,2,1,0:T(8,128)S(1)}, u32[]{:S(2)}, u32[]{:S(2)}) collective-permute-start(f32[2,4,8,8,128]{4,3,2,1,0:T(8,128)S(1)} %get-tuple-element.46), channel_id=1, source_target_pairs={{0,16},{8,24},{16,32},{24,40},{32,48},{40,56},{48,0},{56,8},{64,80... | collective-permute-start | bytes 786440 | tf_op jit(solution)/shard_map/ppermute | solution.py:416
  83.0 23.9 %collective-permute-start.4 = (f32[2,4,8,8,128]{4,3,2,1,0:T(8,128)S(1)}, f32[2,4,8,8,128]{4,3,2,1,0:T(8,128)S(1)}, u32[]{:S(2)}, u32[]{:S(2)}) collective-permute-start(f32[2,4,8,8,128]{4,3,2,1,0:T(8,128)S(1)} %get-tuple-element.47), channel_id=1, source_target_pairs={{0,32},{8,40},{16,48},{24,56},{32,0},{40,8},{48,16},{56,24},{64,96... | collective-permute-start | bytes 786440 | tf_op jit(solution)/shard_map/ppermute | solution.py:416
  87.8 19.1 %collective-permute-start.5 = (f32[2,4,8,8,128]{4,3,2,1,0:T(8,128)S(1)}, f32[2,4,8,8,128]{4,3,2,1,0:T(8,128)S(1)}, u32[]{:S(2)}, u32[]{:S(2)}) collective-permute-start(f32[2,4,8,8,128]{4,3,2,1,0:T(8,128)S(1)} %get-tuple-element.48), channel_id=1, source_target_pairs={{0,48},{8,56},{16,0},{24,8},{32,16},{40,24},{48,32},{56,40},{64,11... | collective-permute-start | bytes 786440 | tf_op jit(solution)/shard_map/ppermute | solution.py:416
  102.0 8.7 %collective-permute-start.16 = (f32[2,4,8,8,128]{4,3,2,1,0:T(8,128)S(1)}, f32[2,4,8,8,128]{4,3,2,1,0:T(8,128)S(1)}, u32[]{:S(2)}, u32[]{:S(2)}) collective-permute-start(f32[2,4,8,8,128]{4,3,2,1,0:T(8,128)S(1)} %get-tuple-element.66), channel_id=1, source_target_pairs={{0,16},{8,24},{16,32},{24,40},{32,48},{40,56},{48,0},{56,8},{64,80... | collective-permute-start | bytes 786440 | tf_op jit(solution)/shard_map/ppermute | solution.py:416
  103.3 13.9 %collective-permute-start.17 = (f32[2,4,8,8,128]{4,3,2,1,0:T(8,128)S(1)}, f32[2,4,8,8,128]{4,3,2,1,0:T(8,128)S(1)}, u32[]{:S(2)}, u32[]{:S(2)}) collective-permute-start(f32[2,4,8,8,128]{4,3,2,1,0:T(8,128)S(1)} %get-tuple-element.67), channel_id=1, source_target_pairs={{0,32},{8,40},{16,48},{24,56},{32,0},{40,8},{48,16},{56,24},{64,96... | collective-permute-start | bytes 786440 | tf_op jit(solution)/shard_map/ppermute | solution.py:416
  105.8 11.5 %collective-permute-start.18 = (f32[2,4,8,8,128]{4,3,2,1,0:T(8,128)S(1)}, f32[2,4,8,8,128]{4,3,2,1,0:T(8,128)S(1)}, u32[]{:S(2)}, u32[]{:S(2)}) collective-permute-start(f32[2,4,8,8,128]{4,3,2,1,0:T(8,128)S(1)} %get-tuple-element.68), channel_id=1, source_target_pairs={{0,48},{8,56},{16,0},{24,8},{32,16},{40,24},{48,32},{56,40},{64,11... | collective-permute-start | bytes 786440 | tf_op jit(solution)/shard_map/ppermute | solution.py:416
  107.0 15.5 %collective-permute-start.6 = (f32[2,4,8,8,128]{4,3,2,1,0:T(8,128)S(1)}, f32[2,4,8,8,128]{4,3,2,1,0:T(8,128)S(1)}, u32[]{:S(2)}, u32[]{:S(2)}) collective-permute-start(f32[2,4,8,8,128]{4,3,2,1,0:T(8,128)S(1)} %get-tuple-element.50), channel_id=1, source_target_pairs={{0,64},{8,72},{16,80},{24,88},{32,96},{40,104},{48,112},{56,120},{... | collective-permute-start | bytes 786440 | tf_op jit(solution)/shard_map/ppermute | solution.py:416
  107.1 20.2 %collective-permute-start.7 = (f32[2,4,8,8,128]{4,3,2,1,0:T(8,128)S(1)}, f32[2,4,8,8,128]{4,3,2,1,0:T(8,128)S(1)}, u32[]{:S(2)}, u32[]{:S(2)}) collective-permute-start(f32[2,4,8,8,128]{4,3,2,1,0:T(8,128)S(1)} %get-tuple-element.51), channel_id=1, source_target_pairs={{0,128},{8,136},{16,144},{24,152},{32,160},{40,168},{48,176},{56,1... | collective-permute-start | bytes 786440 | tf_op jit(solution)/shard_map/ppermute | solution.py:416
  110.7 22.4 %collective-permute-start.8 = (f32[2,4,8,8,128]{4,3,2,1,0:T(8,128)S(1)}, f32[2,4,8,8,128]{4,3,2,1,0:T(8,128)S(1)}, u32[]{:S(2)}, u32[]{:S(2)}) collective-permute-start(f32[2,4,8,8,128]{4,3,2,1,0:T(8,128)S(1)} %get-tuple-element.52), channel_id=1, source_target_pairs={{0,192},{8,200},{16,208},{24,216},{32,224},{40,232},{48,240},{56,2... | collective-permute-start | bytes 786440 | tf_op jit(solution)/shard_map/ppermute | solution.py:416
  119.5 21.2 %collective-permute-start.19 = (f32[8,16,8,128]{3,2,1,0:T(8,128)S(1)}, f32[8,16,8,128]{3,2,1,0:T(8,128)S(1)}, u32[]{:S(2)}, u32[]{:S(2)}) collective-permute-start(f32[8,16,8,128]{3,2,1,0:T(8,128)S(1)} %get-tuple-element.70), channel_id=1, source_target_pairs={{0,4},{1,5},{2,6},{3,7},{4,0},{5,1},{6,2},{7,3},{8,12},{9,13},{10,... | collective-permute-start | bytes 1572872 | tf_op jit(solution)/shard_map/ppermute | solution.py:408
  135.4 14.8 %collective-permute-start.9 = (f32[8,16,8,128]{3,2,1,0:T(8,128)S(1)}, f32[8,16,8,128]{3,2,1,0:T(8,128)S(1)}, u32[]{:S(2)}, u32[]{:S(2)}) collective-permute-start(f32[8,16,8,128]{3,2,1,0:T(8,128)S(1)} %get-tuple-element.54), channel_id=1, source_target_pairs={{0,4},{1,5},{2,6},{3,7},{4,0},{5,1},{6,2},{7,3},{8,12},{9,13},{10,... | collective-permute-start | bytes 1572872 | tf_op jit(solution)/shard_map/ppermute | solution.py:408
